TPU v7x, 32 devices: a whole 2x2x4 slice. The times are simulated.
32 devices in a mesh: space: 4 (over y, core), chan: 8 (over z, x).
Axes of the slice: x: 2, y: 2, z: 4, core: 2. Of those that a mesh axis runs over, the one named last changes fastest.
Arguments:
- volume: bfloat16 [4, 32, 32, 64, 128], P(None, 'space', 'chan'), may hold values from -6 to 6
- w_first: bfloat16 [3, 3, 3, 128, 256], P(None, None, None, None, 'chan'), may hold values from -0.109375 to 0.109375
- w_second: bfloat16 [3, 3, 3, 256, 256], P(None, None, None, None, 'chan'), may hold values from -0.078125 to 0.078125
- cotangent: bfloat16 [4, 8, 8, 16, 256], P(None, 'space', None, None, 'chan'), may hold values from -6 to 6
Outputs:
- second_out: bfloat16 [4, 8, 8, 16, 256], P(None, 'space', None, None, 'chan')
- volume_grad: bfloat16 [4, 32, 32, 64, 128], P(None, 'space', 'chan')
- first_grad: float32 [3, 3, 3, 128, 256], P(None, None, None, None, 'chan')
- second_grad: float32 [3, 3, 3, 256, 256], P(None, None, None, None, 'chan')
All inputs are finite; a program needn't handle non-finite values.
Results may differ from a plain program's by a relative error of at most 0.018.
Values may be sent and summed in bfloat16 or wider, within the bound.
No kernel may reach another device: no remote copies, remote signals or barrier semaphores. Data moves between devices by JAX's collectives and lax.ppermute only.
A program may use at most 64 MiB of HBM per device.

v0:
```python
import functools

import jax
import jax.numpy as jnp
from jax import lax
from jax.experimental import pallas as pl
from jax.experimental.pallas import tpu as pltpu
from jax.sharding import PartitionSpec as P

BF16 = jnp.bfloat16
F32 = jnp.float32
LANES = 128
PAD = 8
NT = (((1,), (1,)), ((), ()))
NN = (((1,), (0,)), ((), ()))
REACH = (((1, 0),), ((0, 1), (2, 0)))


def dot(left, right, dims):
    return lax.dot_general(left, right, dims, preferred_element_type=F32)


def bits(axis):
    return lax.axis_size(axis).bit_length() - 1


def gather_order(axis):
    return list(reversed(range(bits(axis))))


def chan_gather_order():
    return [bit for bit in reversed(range(bits("chan"))) if bit] + [0]


def chan_sum_order():
    return [0] + [bit for bit in reversed(range(bits("chan"))) if bit]


def shifted(value, steps):
    pairs = []
    sizes = (lax.axis_size("space"), lax.axis_size("chan"))
    for a in range(sizes[0]):
        for b in range(sizes[1]):
            to = (a + steps[0], b + steps[1])
            if 0 <= to[0] < sizes[0] and 0 <= to[1] < sizes[1]:
                pairs.append((a * sizes[1] + b, to[0] * sizes[1] + to[1]))
    return lax.ppermute(value, ("space", "chan"), pairs)


def swapped(value, axis, bit):
    count = lax.axis_size(axis)
    return lax.ppermute(value, axis, [(i, i ^ (1 << bit)) for i in range(count)])


def doubled(value, axis, bit):
    return jnp.stack([value, swapped(value, axis, bit)])


def position():
    return jnp.stack([lax.axis_index("space"), lax.axis_index("chan")]).astype(jnp.int32)


def gather_filters(shard):
    space = lax.axis_size("space")
    edge, inputs, mine = shard.shape[0], shard.shape[3], shard.shape[4]
    taps = edge**3
    each = -(-taps // space)
    flat = jnp.transpose(shard.reshape(taps, inputs, mine), (0, 2, 1))
    flat = jnp.pad(flat, ((0, each * space - taps), (0, 0), (0, 0)))
    part = lax.dynamic_slice_in_dim(flat, lax.axis_index("space") * each, each, 0)
    for bit in chan_gather_order():
        part = doubled(part, "chan", bit)
    for bit in gather_order("space"):
        part = doubled(part, "space", bit)
    return part.reshape(space, lax.axis_size("chan"), each, mine, inputs)


def relative(index, mine, order):
    apart = index ^ mine
    place = 0
    for bit in order:
        place = place * 2 + ((apart >> bit) & 1)
    return place


def filter_tap(ref, here, tap, orders):
    each = ref.shape[2]
    owner = relative(tap // each, here[0], orders[0])
    rows = [
        ref[owner, relative(chan, here[1], orders[1]), tap % each]
        for chan in range(ref.shape[1])
    ]
    return jnp.concatenate(rows, axis=0)


def call(kernel, outs, args, scratch=(), grid=None, in_specs=None, out_specs=None, flops=0):
    moved = sum(a.size * a.dtype.itemsize for a in args)
    moved += sum(o.size * o.dtype.itemsize for o in outs)
    whole = pl.BlockSpec(memory_space=pltpu.VMEM)
    smem = pl.BlockSpec(memory_space=pltpu.SMEM)
    specs = in_specs or [smem if a.dtype == jnp.int32 else whole for a in args]
    return pl.pallas_call(
        kernel,
        out_shape=outs,
        grid=grid or (),
        in_specs=specs,
        out_specs=out_specs or [whole] * len(outs),
        scratch_shapes=scratch,
        cost_estimate=pl.CostEstimate(flops=flops, bytes_accessed=moved, transcendentals=0),
        compiler_params=pltpu.CompilerParams(vmem_limit_bytes=56 * 2**20),
    )(*args)


def parted_tile(tile, wide, base, store):
    depth, lanes = tile.shape
    for part in range(lanes // LANES):
        rows = wide.at[part]
        rows[pl.ds(base, PAD), :] = jnp.zeros((PAD, LANES), F32)
        rows[pl.ds(base + PAD, depth), :] = tile[:, part * LANES : (part + 1) * LANES].astype(F32)
        for k in range(3):
            piece = rows[pl.ds(base + PAD - 1 + k, depth // 2, stride=2), :]
            store(k, part, piece.astype(BF16))


def part_kernel(own, plane, row, out, wide):
    _, wide_a, wide_b, depth, _ = (1, out.shape[2], out.shape[3], own.shape[3], own.shape[4])
    for a in range(wide_a):
        for b in range(wide_b):
            if b == 0:
                tile = row[0, a, 0]
            elif a == 0:
                tile = plane[0, 0, b - 1]
            else:
                tile = own[0, a - 1, b - 1]
            slot = ((a * wide_b + b) % 8) * (PAD + depth)

            def store(k, part, piece):
                out[k, 0, a, b, :, part * LANES : (part + 1) * LANES] = piece

            parted_tile(tile, wide, slot, store)


def parted(own, plane, row):
    vols, side_a, side_b, depth, lanes = own.shape
    out = jax.ShapeDtypeStruct((3, vols, side_a + 1, side_b + 1, depth // 2, lanes), BF16)

    def block(shape):
        return pl.BlockSpec((1,) + shape[1:], lambda n: (n, 0, 0, 0, 0))

    return call(
        part_kernel,
        [out],
        (own, plane, row),
        [pltpu.VMEM((lanes // LANES, 8 * (PAD + depth), LANES), F32)],
        (vols,),
        [block(own.shape), block(plane.shape), block(row.shape)],
        [pl.BlockSpec((3, 1) + out.shape[2:], lambda n: (0, n, 0, 0, 0, 0))],
    )[0]


def window(ref, i, j, sides):
    vols, side_a, side_b = sides
    rows = []
    for n in range(vols):
        for a in range(side_a):
            for b in range(side_b):
                rows.append(
                    jnp.concatenate([ref[k, n, 2 * a + i, 2 * b + j] for k in range(3)], axis=1)
                )
    return jnp.concatenate(rows, axis=0)


def forward_kernel(orders, sides, here, ref, filters, *rest):
    outs, acc = rest[:-1], rest[-1]

    def step(ij, carry):
        i, j = ij // 3, ij % 3
        left = window(ref, i, j, sides)
        right = jnp.concatenate(
            [filter_tap(filters, here, ij * 3 + k, orders) for k in range(3)], axis=1
        )
        part = dot(left, right, NT)
        acc[...] = jnp.where(ij == 0, part, acc[...] + part)
        return carry

    lax.fori_loop(0, 9, step, 0)
    total = acc[...]
    depth = ref.shape[4]
    vols, side_a, side_b = sides
    if len(outs) == 1:
        outs[0][...] = total.astype(BF16).reshape(outs[0].shape)
        return
    hidden, plane, row = outs
    act = jnp.where(total > 0, total, 0.3 * total).astype(BF16)
    act = act.reshape(vols, side_a, side_b, depth, total.shape[1])
    hidden[...] = act
    plane[...] = act[:, side_a - 1 :]
    row[...] = act[:, :, side_b - 1 :]


def forward(here, ref, filters, orders, split):
    _, vols, wide_a, wide_b, depth, inputs = ref.shape
    sides = (vols, (wide_a - 1) // 2, (wide_b - 1) // 2)
    count = filters.shape[1] * filters.shape[3]
    cells = vols * sides[1] * sides[2] * depth
    shape = sides + (depth, count)
    outs = [jax.ShapeDtypeStruct(shape, BF16)]
    if split:
        outs.append(jax.ShapeDtypeStruct((vols, 1) + shape[2:], BF16))
        outs.append(jax.ShapeDtypeStruct(shape[:2] + (1,) + shape[3:], BF16))
    return call(
        functools.partial(forward_kernel, orders, sides),
        outs,
        (here, ref, filters),
        [pltpu.VMEM((cells, count), F32)],
        flops=2 * cells * 27 * inputs * count,
    )


def grads_kernel(orders, sides, here, ref, grads, keep, send, turned):
    cells, count = turned.shape[1], turned.shape[0]
    inputs = ref.shape[5]
    chans = 2 ** len(orders[1])
    mine = count // chans
    each = keep.shape[2]
    turned[...] = jnp.transpose(grads[...].reshape(cells, count).astype(F32), (1, 0)).astype(BF16)

    def step(ij, carry):
        part = dot(turned[...], window(ref, ij // 3, ij % 3, sides), NN).astype(BF16)
        for k in range(3):
            tap = ij * 3 + k
            place = relative(tap // each, here[0], orders[0])
            half = keep.shape[0]
            for chan in range(chans):
                block = part[chan * mine : (chan + 1) * mine, k * inputs : (k + 1) * inputs]
                to = relative(chan, here[1], orders[1])

                @pl.when(place < half)
                def _():
                    keep[place, to, tap % each] = block

                @pl.when(place >= half)
                def _():
                    send[place - half, to, tap % each] = block

        return carry

    lax.fori_loop(0, 9, step, 0)
    for tap in range(27, each * 2 * keep.shape[0]):
        place = relative(tap // each, here[0], orders[0])
        blank = jnp.zeros((chans, mine, inputs), BF16)

        @pl.when(place < keep.shape[0])
        def _():
            keep[place, :, tap % each] = blank

        @pl.when(place >= keep.shape[0])
        def _():
            send[place - keep.shape[0], :, tap % each] = blank


def filter_grads(here, ref, grads, orders):
    _, vols, wide_a, wide_b, depth, inputs = ref.shape
    sides = (vols, (wide_a - 1) // 2, (wide_b - 1) // 2)
    cells = vols * sides[1] * sides[2] * depth
    count = grads.shape[-1]
    space, chans = 2 ** len(orders[0]), 2 ** len(orders[1])
    each = -(-27 // space)
    out = jax.ShapeDtypeStruct((space // 2, chans, each, count // chans, inputs), BF16)
    return call(
        functools.partial(grads_kernel, orders, sides),
        [out, out],
        (here, ref, grads),
        [pltpu.VMEM((count, cells), BF16)],
        flops=2 * cells * 27 * inputs * count,
    )


def sum_filters(keep, send):
    each, mine, inputs = keep.shape[2:]
    total = None
    order = [("space", bit) for bit in range(bits("space"))]
    order += [("chan", bit) for bit in chan_sum_order()]
    for axis, bit in order:
        if total is not None:
            half = total.shape[0] // 2
            keep, send = total[:half], total[half:]
        else:
            keep = keep.reshape(-1, each, mine, inputs)
            send = send.reshape(-1, each, mine, inputs)
        total = keep.astype(F32) + swapped(send.astype(BF16), axis, bit).astype(F32)
    part = total[0].astype(BF16)
    for bit in gather_order("space"):
        part = doubled(part, "space", bit)
    space = lax.axis_size("space")
    part = part.reshape(space, each, mine, inputs)
    places = jnp.arange(space) ^ lax.axis_index("space")
    taps = [lax.dynamic_index_in_dim(part, space_order(places[s]), 0, keepdims=False) for s in range(space)]
    full = jnp.concatenate(taps, axis=0)[:27].astype(F32)
    return jnp.transpose(full, (0, 2, 1)).reshape(3, 3, 3, inputs, mine)


def space_order(apart):
    place = 0
    for bit in range(bits("space")):
        place = place * 2 + ((apart >> bit) & 1)
    return place


def stepped_tile(tile, wide, base, store):
    depth, lanes = tile.shape
    for part in range(lanes // LANES):
        rows = wide.at[part]
        rows[pl.ds(base + depth, PAD), :] = jnp.zeros((PAD, LANES), F32)
        rows[pl.ds(base, depth), :] = tile[:, part * LANES : (part + 1) * LANES].astype(F32)
        store(part, rows[pl.ds(base + 1, depth), :].astype(BF16))


def back_kernel(orders, here, cells, filters, hidden, out, plane, row, wide, moved, spread):
    vols, wide_a, wide_b, depth, count = cells.shape
    side_a, side_b = wide_a - 1, wide_b - 1
    inputs = filters.shape[4]
    for n in range(vols):
        for a in range(wide_a):
            for b in range(wide_b):
                slot = ((n * wide_a + a) * wide_b + b) % 8 * (PAD + depth)

                def store(part, piece):
                    moved[n, a, b, :, part * LANES : (part + 1) * LANES] = piece

                stepped_tile(cells[n, a, b], wide, slot, store)

    def lefts(ref, da, db):
        return ref[:, da : da + side_a, db : db + side_b].reshape(-1, count)

    for sa in range(2):
        for sb in range(2):
            even = odd = None
            for i, da in REACH[sa]:
                for j, db in REACH[sb]:
                    tap = (i * 3 + j) * 3
                    here_cells = lefts(cells, da, db)
                    first = dot(here_cells, filter_tap(filters, here, tap + 1, orders), NN)
                    second = dot(here_cells, filter_tap(filters, here, tap + 2, orders), NN)
                    second += dot(lefts(moved, da, db), filter_tap(filters, here, tap, orders), NN)
                    even = first if even is None else even + first
                    odd = second if odd is None else odd + second
            for parity, value in enumerate((even, odd)):
                value = value.reshape(vols, side_a, side_b, depth, inputs)
                for n in range(vols):
                    for a in range(side_a):
                        for b in range(side_b):
                            for part in range(inputs // LANES):
                                spread[
                                    part, n, 2 * a + sa, 2 * b + sb, pl.ds(parity, depth, stride=2), :
                                ] = value[n, a, b, :, part * LANES : (part + 1) * LANES]
    for part in range(inputs // LANES):
        lanes = slice(part * LANES, (part + 1) * LANES)
        act = hidden[:, :, :, :, lanes].astype(F32)
        value = (spread[part] * jnp.where(act > 0, 1.0, 0.3)).astype(BF16)
        out[:, :, :, :, lanes] = value
        plane[:, :, :, :, lanes] = value[:, :1]
        row[:, :, :, :, lanes] = value[:, :, :1]


def hidden_back(here, cells, filters, hidden, orders):
    vols, wide_a, wide_b, depth, count = cells.shape
    inputs = hidden.shape[-1]
    shape = hidden.shape
    outs = [
        jax.ShapeDtypeStruct(shape, BF16),
        jax.ShapeDtypeStruct((vols, 1) + shape[2:], BF16),
        jax.ShapeDtypeStruct(shape[:2] + (1,) + shape[3:], BF16),
    ]
    return call(
        functools.partial(back_kernel, orders),
        outs,
        (here, cells, filters, hidden),
        [
            pltpu.VMEM((count // LANES, 8 * (PAD + depth), LANES), F32),
            pltpu.VMEM(cells.shape, BF16),
            pltpu.VMEM((inputs // LANES,) + shape[:4] + (LANES,), F32),
        ],
        flops=2 * vols * (wide_a - 1) * (wide_b - 1) * depth * 27 * inputs * count,
    )


def volume_kernel(orders, here, cells, plane, row, filters, out, wide, ext, moved, spread):
    _, side_a, side_b, depth, count = cells.shape
    inputs = filters.shape[4]
    for a in range(side_a + 1):
        for b in range(side_b + 1):
            if b == side_b:
                tile = row[0, a, 0]
            elif a == side_a:
                tile = plane[0, 0, b]
            else:
                tile = cells[0, a, b]
            ext[a, b] = tile
            slot = ((a * (side_b + 1) + b) % 8) * (PAD + depth)

            def store(part, piece):
                moved[a, b, :, part * LANES : (part + 1) * LANES] = piece

            stepped_tile(tile, wide, slot, store)

    def lefts(ref, da, db):
        return ref[da : da + side_a, db : db + side_b].reshape(-1, count)

    for sa in range(2):
        for sb in range(2):
            both = late = None
            for i, da in REACH[sa]:
                for j, db in REACH[sb]:
                    tap = (i * 3 + j) * 3
                    pair = jnp.concatenate(
                        [filter_tap(filters, here, tap + k, orders) for k in (1, 2)], axis=1
                    )
                    first = dot(lefts(ext, da, db), pair, NN)
                    second = dot(lefts(moved, da, db), filter_tap(filters, here, tap, orders), NN)
                    both = first if both is None else both + first
                    late = second if late is None else late + second
            halves = (both[:, :inputs], both[:, inputs:] + late)
            for parity, value in enumerate(halves):
                value = value.reshape(side_a, side_b, depth, inputs)
                for a in range(side_a):
                    for b in range(side_b):
                        spread[2 * a + sa, 2 * b + sb, pl.ds(parity, depth, stride=2), :] = value[a, b]
    out[0] = spread[...].astype(BF16)


def volume_grads(here, cells, plane, row, filters, orders):
    vols, side_a, side_b, depth, count = cells.shape
    inputs = filters.shape[4]
    out = jax.ShapeDtypeStruct((vols, 2 * side_a, 2 * side_b, 2 * depth, inputs), BF16)

    def block(shape):
        return pl.BlockSpec((1,) + shape[1:], lambda n: (n, 0, 0, 0, 0))

    return call(
        functools.partial(volume_kernel, orders),
        [out],
        (here, cells, plane, row, filters),
        [
            pltpu.VMEM((count // LANES, 8 * (PAD + depth), LANES), F32),
            pltpu.VMEM((side_a + 1, side_b + 1, depth, count), BF16),
            pltpu.VMEM((side_a + 1, side_b + 1, depth, count), BF16),
            pltpu.VMEM((2 * side_a, 2 * side_b, 2 * depth, inputs), F32),
        ],
        (vols,),
        [
            pl.BlockSpec(memory_space=pltpu.SMEM),
            block(cells.shape),
            block(plane.shape),
            block(row.shape),
            pl.BlockSpec(memory_space=pltpu.VMEM),
        ],
        [block(out.shape)],
        flops=2 * vols * side_a * side_b * depth * 27 * inputs * count,
    )[0]


def spread_cells(cotangent):
    chan = lax.axis_size("chan")
    vols, side_a, side_b, side_c, mine = cotangent.shape
    rows = side_b // chan
    flat = cotangent.reshape(vols, side_a, side_b, side_c * mine)
    for step, bit in enumerate(gather_order("chan")):
        other = swapped(flat, "chan", bit)
        high = (lax.axis_index("chan") >> bit) & 1 == 1
        flat = jnp.stack([jnp.where(high, other, flat), jnp.where(high, flat, other)], axis=step)
    flat = flat.reshape(chan, vols, side_a, side_b, side_c * mine)
    flat = jnp.pad(flat, ((0, 0), (0, 0), (0, 0), (0, 1), (0, 0)))
    near = lax.dynamic_slice_in_dim(flat, lax.axis_index("chan") * rows, rows + 1, 3)
    near = near.reshape(chan, vols, side_a, rows + 1, side_c, mine)
    near = jnp.transpose(near, (1, 2, 3, 4, 0, 5))
    near = near.reshape(vols, side_a, rows + 1, side_c, chan * mine)
    plane = shifted(near[:, :1], (-1, 0))
    return jnp.concatenate([near, plane], axis=1)


def local(volume, w_first, w_second, cotangent):
    here = position()
    gathered = (list(range(bits("space"))), [0] + [b for b in range(1, bits("chan"))])
    summed = (list(range(bits("space"))), chan_sum_order())
    plane = shifted(volume[:, -1:], (1, 0))
    row = shifted(jnp.concatenate([plane, volume], axis=1)[:, :, -1:], (0, 1))
    first_full = gather_filters(w_first)
    second_full = gather_filters(w_second)
    grad_ext = spread_cells(cotangent)
    grad_cells = grad_ext[:, :-1, :-1]
    vol_parts = parted(volume, plane, row)
    hidden, hid_plane, hid_row = forward(here, vol_parts, first_full, gathered, True)
    plane = shifted(hid_plane, (1, 0))
    row = shifted(hid_row, (0, 1))
    corner = shifted(hid_row[:, -1:], (1, 1))
    act_parts = parted(hidden, plane, jnp.concatenate([corner, row], axis=1))
    second_grad = sum_filters(*filter_grads(here, act_parts, grad_cells, summed))
    pre_back, pre_plane, pre_row = hidden_back(here, grad_ext, second_full, hidden, gathered)
    first_grad = sum_filters(*filter_grads(here, vol_parts, pre_back, summed))
    local_out = forward(here, act_parts, second_full, gathered, False)[0]
    second_out = lax.all_to_all(local_out, "chan", split_axis=4, concat_axis=2, tiled=True)
    plane = shifted(pre_plane, (-1, 0))
    row = shifted(jnp.concatenate([pre_row, plane[:, :, :1]], axis=1), (0, -1))
    volume_grad = volume_grads(here, pre_back, plane, row, first_full, gathered)
    return (second_out, volume_grad, first_grad, second_grad)


def solution(mesh):
    return jax.shard_map(
        local,
        mesh=mesh,
        in_specs=(
            P(None, "space", "chan", None, None),
            P(None, None, None, None, "chan"),
            P(None, None, None, None, "chan"),
            P(None, "space", None, None, "chan"),
        ),
        out_specs=(
            P(None, "space", None, None, "chan"),
            P(None, "space", "chan", None, None),
            P(None, None, None, None, "chan"),
            P(None, None, None, None, "chan"),
        ),
        check_vma=False,
    )
```

profile of v0, /device:TPU:0, one launch (start us, length us, event | category | flops | bytes accessed | tf_op | source)
XLA Modules:
  0.0 218.5 jit_solution(14877277197786486819)
XLA Ops:
  1.5 4.1 %collective-permute-start.2 = (bf16[7,32,128]{2,1,0:T(8,128)(2,1)S(1)}, bf16[7,32,128]{2,1,0:T(8,128)(2,1)S(1)}, u32[]{:S(2)}, u32[]{:S(2)}) collective-permute-start(bf16[7,32,128]{2,1,0:T(8,128)(2,1)S(1)} %pad_dynamic-slice_fusion.2), channel_id=1, source_target_pairs={{0,4},{1,5},{2,6},{3,7},{4,0},{5,1},{6,2},{7,3},{8,12},{9,13},{10,... | collective-permute-start | bytes 172040 | tf_op jit(solution)/shard_map/ppermute | solution.py:52
  8.3 4.0 %collective-permute-start.3 = (bf16[2,7,32,128]{3,2,1,0:T(8,128)(2,1)S(1)}, bf16[2,7,32,128]{3,2,1,0:T(8,128)(2,1)S(1)}, u32[]{:S(2)}, u32[]{:S(2)}) collective-permute-start(bf16[2,7,32,128]{3,2,1,0:T(8,128)(2,1)S(1)} %get-tuple-element.65), channel_id=1, source_target_pairs={{0,2},{1,3},{2,0},{3,1},{4,6},{5,7},{6,4},{7,5},{8,10},{9,11},{10,... | collective-permute-start | bytes 344072 | tf_op jit(solution)/shard_map/ppermute | solution.py:52
  17.3 3.8 %collective-permute-done.11 = bf16[2,7,32,256]{3,2,1,0:T(8,128)(2,1)S(1)} collective-permute-done((bf16[2,7,32,256]{3,2,1,0:T(8,128)(2,1)S(1)}, bf16[2,7,32,256]{3,2,1,0:T(8,128)(2,1)S(1)}, u32[]{:S(2)}, u32[]{:S(2)}) %collective-permute-start.11) | collective-permute-done | bytes 229408 | tf_op jit(solution)/shard_map/ppermute | solution.py:52
  41.3 3.4 %collective-permute-start.1 = (bf16[4,9,1,64,128]{4,3,2,1,0:T(8,128)(2,1)}, bf16[4,9,1,64,128]{4,3,2,1,0:T(8,128)(2,1)S(1)}, u32[]{:S(2)}, u32[]{:S(2)}) collective-permute-start(bf16[4,9,1,64,128]{4,3,2,1,0:T(8,128)(2,1)} %pad_maximum_fusion.5), channel_id=1, source_target_pairs={{0,1},{1,2},{2,3},{3,4},{4,5},{5,6},{6,7},{8,9},{9,10},{10,11},{11... | collective-permute-start | bytes 1769480 | tf_op jit(solution)/shard_map/ppermute | solution.py:47
  47.4 3.2 %collective-permute-done.16 = bf16[2,4,2,8,512]{4,3,2,1,0:T(8,128)(2,1)S(1)} collective-permute-done((bf16[2,4,2,8,512]{4,3,2,1,0:T(8,128)(2,1)S(1)}, bf16[2,4,2,8,512]{4,3,2,1,0:T(8,128)(2,1)S(1)}, u32[]{:S(2)}, u32[]{:S(2)}) %collective-permute-start.16) | collective-permute-done | bytes 131104 | tf_op jit(solution)/shard_map/ppermute | solution.py:52
  50.7 12.3 %collective-permute-start.17 = (bf16[2,2,4,2,8,512]{5,4,3,2,1,0:T(8,128)(2,1)S(1)}, bf16[2,2,4,2,8,512]{5,4,3,2,1,0:T(8,128)(2,1)S(1)}, u32[]{:S(2)}, u32[]{:S(2)}) collective-permute-start(bf16[2,2,4,2,8,512]{5,4,3,2,1,0:T(8,128)(2,1)S(1)} %pad_maximum_fusion.15), channel_id=1, source_target_pairs={{0,1},{1,0},{2,3},{3,2},{4,5},{5,4},{6,7},{7,6},{8,9},{9,8},{10,11... | collective-permute-start | bytes 786440 | tf_op jit(solution)/shard_map/ppermute | solution.py:52
  63.8 4.7 %shard_map.75.ref = bf16[3,4,9,5,32,128]{5,4,3,2,1,0:T(8,128)(2,1)} custom-call(bf16[4,8,4,64,128]{4,3,2,1,0:T(8,128)(2,1)} %own.1, bf16[4,1,4,64,128]{4,3,2,1,0:T(8,128)(2,1)} %collective-permute-done.plane, bf16[4,9,1,64,128]{4,3,2,1,0:T(8,128)(2,1)} %copy-done.5), custom_call_target="tpu_custom_call" | custom-call | bytes 7372800 | tf_op jit(solution)/shard_map/pallas_call | solution.py:102
  68.5 2.6 %fusion.13 = (bf16[1,2,2,2,2,7,32,256]{7,6,5,4,3,2,1,0:T(8,128)(2,1)S(1)}, bf16[2,2,2,2,7,32,256]{6,5,4,3,2,1,0:T(8,128)(2,1)}) fusion(bf16[1,2,2,2,7,32,256]{6,5,4,3,2,1,0:T(8,128)(2,1)} %bitcast.24, bf16[1,2,2,2,7,32,256]{6,5,4,3,2,1,0:T(8,128)(2,1)S(1)} %copy-done.2), kind=kLoop, calls=%fused_computation.77 | loop fusion | flops 917504 | bytes 5505024 | tf_op jit(solution)/shard_map/stack | solution.py:56
  71.2 2.6 %pad_maximum_fusion.1 = bf16[2,2,2,2,2,7,32,128]{7,6,5,4,3,2,1,0:T(8,128)(2,1)} fusion(bf16[1,2,2,2,2,7,32,128]{7,6,5,4,3,2,1,0:T(8,128)(2,1)} %bitcast.13, bf16[1,2,2,2,2,7,32,128]{7,6,5,4,3,2,1,0:T(8,128)(2,1)S(1)} %get-tuple-element.36), kind=kLoop, calls=%fused_computation.4 | loop fusion | flops 917504 | bytes 3670016 | tf_op jit(solution)/shard_map/stack | solution.py:56
  73.8 8.2 %shard_map.76 = (bf16[4,4,2,32,256]{4,3,2,1,0:T(8,128)(2,1)}, bf16[4,1,2,32,256]{4,3,2,1,0:T(8,128)(2,1)}, bf16[4,4,1,32,256]{4,3,2,1,0:T(8,128)(2,1)}) custom-call(s32[2]{0:T(128)} %pad_add_fusion.here, bf16[3,4,9,5,32,128]{5,4,3,2,1,0:T(8,128)(2,1)} %shard_map.75.ref, bf16[4,8,7,32,128]{4,3,2,1,0:T(8,128)(2,1)} %bitcast.124), custom_call_target="tpu_custom_call" | custom-call | flops 1811939328 | bytes 7176200 | tf_op jit(solution)/shard_map/pallas_call | solution.py:102
  85.1 5.6 %collective-permute-start.8 = (bf16[4,1,1,32,256]{4,3,2,1,0:T(8,128)(2,1)S(1)}, bf16[4,1,1,32,256]{4,3,2,1,0:T(8,128)(2,1)S(1)}, u32[]{:S(2)}, u32[]{:S(2)}) collective-permute-start(bf16[4,1,1,32,256]{4,3,2,1,0:T(8,128)(2,1)S(1)} %slice.98), channel_id=1, source_target_pairs={{0,9},{1,10},{2,11},{3,12},{4,13},{5,14},{6,15},{8,17},{9,18},{10,... | collective-permute-start | bytes 196616 | tf_op jit(solution)/shard_map/ppermute | solution.py:47
  95.9 3.7 %shard_map.77.ref = bf16[3,4,5,3,16,256]{5,4,3,2,1,0:T(8,128)(2,1)} custom-call(bf16[4,4,2,32,256]{4,3,2,1,0:T(8,128)(2,1)} %get-tuple-element.14.own.hidden, bf16[4,1,2,32,256]{4,3,2,1,0:T(8,128)(2,1)} %copy-done.6, bf16[4,5,1,32,256]{4,3,2,1,0:T(8,128)(2,1)} %pad_maximum_fusion.13.row), custom_call_target="tpu_custom_call" | custom-call | bytes 2457600 | tf_op jit(solution)/shard_map/pallas_call | solution.py:102
  99.6 8.7 %shard_map.82 = (bf16[2,8,7,32,256]{4,3,2,1,0:T(8,128)(2,1)}, bf16[2,8,7,32,256]{4,3,2,1,0:T(8,128)(2,1)}) custom-call(s32[2]{0:T(128)} %pad_add_fusion.here, bf16[3,4,5,3,16,256]{5,4,3,2,1,0:T(8,128)(2,1)} %shard_map.77.ref, bf16[4,2,1,16,256]{4,3,2,1,0:T(8,128)(2,1)} %slice.134.grads), custom_call_target="tpu_custom_call" | custom-call | flops 452984832 | bytes 5210120 | tf_op jit(solution)/shard_map/pallas_call | solution.py:102
  113.1 3.7 %pad_maximum_fusion = bf16[2,2,2,2,2,7,32,256]{7,6,5,4,3,2,1,0:T(8,128)(2,1)} fusion(bf16[1,2,2,2,2,7,32,256]{7,6,5,4,3,2,1,0:T(8,128)(2,1)} %bitcast.26, bf16[1,2,2,2,2,7,32,256]{7,6,5,4,3,2,1,0:T(8,128)(2,1)S(1)} %get-tuple-element.32), kind=kLoop, calls=%fused_computation | loop fusion | flops 1835008 | bytes 7340032 | tf_op jit(solution)/shard_map/stack | solution.py:56
  116.8 3.8 %shard_map.79 = (bf16[4,4,2,32,256]{4,3,2,1,0:T(8,128)(2,1)}, bf16[4,1,2,32,256]{4,3,2,1,0:T(8,128)(2,1)}, bf16[4,4,1,32,256]{4,3,2,1,0:T(8,128)(2,1)}) custom-call(s32[2]{0:T(128)} %pad_add_fusion.here, bf16[4,3,2,16,256]{4,3,2,1,0:T(8,128)(2,1)} %pad_maximum_fusion.23.cells, bf16[4,8,7,32,256]{4,3,2,1,0:T(8,128)(2,1)} %bitcast.118, ...), custom_call_target="tpu_custom_call" | custom-call | flops 452984832 | bytes 5308424 | tf_op jit(solution)/shard_map/pallas_call | solution.py:102
  120.6 11.0 %shard_map.81 = (bf16[2,8,7,32,128]{4,3,2,1,0:T(8,128)(2,1)}, bf16[2,8,7,32,128]{4,3,2,1,0:T(8,128)(2,1)}) custom-call(s32[2]{0:T(128)} %pad_add_fusion.here, bf16[3,4,9,5,32,128]{5,4,3,2,1,0:T(8,128)(2,1)} %shard_map.75.ref, bf16[4,4,2,32,256]{4,3,2,1,0:T(8,128)(2,1)} %get-tuple-element.17.cells.grads), custom_call_target="tpu_custom_call" | custom-call | flops 1811939328 | bytes 6782984 | tf_op jit(solution)/shard_map/pallas_call | solution.py:102
  139.3 5.9 %shard_map.78 = bf16[4,2,1,16,256]{4,3,2,1,0:T(8,128)(2,1)} custom-call(s32[2]{0:T(128)} %pad_add_fusion.here, bf16[3,4,5,3,16,256]{5,4,3,2,1,0:T(8,128)(2,1)} %shard_map.77.ref, bf16[4,8,7,32,256]{4,3,2,1,0:T(8,128)(2,1)} %bitcast.119), custom_call_target="tpu_custom_call" | custom-call | flops 452984832 | bytes 5210120 | tf_op jit(solution)/shard_map/pallas_call | solution.py:102
  147.6 6.8 %all-to-all-start = ((bf16[8,2,2048]{2,1,0:T(2,128)(2,1)}), bf16[8,2,2048]{2,1,0:T(2,128)(2,1)S(1)}, u32[]{:S(2)}, u32[]{:S(2)}) async-start(bf16[8,2,2048]{2,1,0:T(2,128)(2,1)} %reshape.134), calls=%async_computation | async-start | bytes 131072 | tf_op jit(solution)/shard_map/all_to_all | solution.py:502
  172.6 5.6 %collective-permute-done.23 = bf16[4,7,32,128]{3,2,1,0:T(8,128)(2,1)S(1)} collective-permute-done((bf16[4,7,32,128]{3,2,1,0:T(8,128)(2,1)S(1)}, bf16[4,7,32,128]{3,2,1,0:T(8,128)(2,1)S(1)}, u32[]{:S(2)}, u32[]{:S(2)}) %collective-permute-start.23) | collective-permute-done | bytes 229408 | tf_op jit(solution)/shard_map/ppermute | solution.py:52
  180.4 6.6 %shard_map.80 = bf16[4,8,4,64,128]{4,3,2,1,0:T(8,128)(2,1)} custom-call(s32[2]{0:T(128)} %pad_add_fusion.here, bf16[4,4,2,32,256]{4,3,2,1,0:T(8,128)(2,1)} %get-tuple-element.17.cells.grads, bf16[4,1,2,32,256]{4,3,2,1,0:T(8,128)(2,1)} %copy-done.7, bf16[4,5,1,32,256]{4,3,2,1,0:T(8,128)(2,1)} %copy-done.8, bf16[4,8,7,32,128]{4,3,2,1,0:T(8,128)(2,1)} %bitcast.125), custom_call_target="tpu_custom_call" | custom-call | flops 1811939328 | bytes 4915208 | tf_op jit(solution)/shard_map/pallas_call | solution.py:102
  192.2 9.5 %collective-permute-start.26 = (bf16[7,32,128]{2,1,0:T(8,128)(2,1)S(1)}, bf16[7,32,128]{2,1,0:T(8,128)(2,1)S(1)}, u32[]{:S(2)}, u32[]{:S(2)}) collective-permute-start(bf16[7,32,128]{2,1,0:T(8,128)(2,1)S(1)} %bitcast.137), channel_id=1, source_target_pairs={{0,16},{8,24},{16,0},{24,8},{1,17},{9,25},{17,1},{25,9},{2,18},{10... | collective-permute-start | bytes 172040 | tf_op jit(solution)/shard_map/ppermute | solution.py:52
  204.5 2.5 %collective-permute-start.27 = (bf16[2,7,32,128]{3,2,1,0:T(8,128)(2,1)S(1)}, bf16[2,7,32,128]{3,2,1,0:T(8,128)(2,1)S(1)}, u32[]{:S(2)}, u32[]{:S(2)}) collective-permute-start(bf16[2,7,32,128]{3,2,1,0:T(8,128)(2,1)S(1)} %get-tuple-element.63), channel_id=1, source_target_pairs={{0,8},{8,0},{16,24},{24,16},{1,9},{9,1},{17,25},{25,17},{2,10},{10... | collective-permute-start | bytes 344072 | tf_op jit(solution)/shard_map/ppermute | solution.py:52
  208.1 4.9 %collective-permute-start.33 = (bf16[7,32,256]{2,1,0:T(8,128)(2,1)S(1)}, bf16[7,32,256]{2,1,0:T(8,128)(2,1)S(1)}, u32[]{:S(2)}, u32[]{:S(2)}) collective-permute-start(bf16[7,32,256]{2,1,0:T(8,128)(2,1)S(1)} %bitcast.133), channel_id=1, source_target_pairs={{0,16},{8,24},{16,0},{24,8},{1,17},{9,25},{17,1},{25,9},{2,18},{10... | collective-permute-start | bytes 344072 | tf_op jit(solution)/shard_map/ppermute | solution.py:52
  213.1 2.7 %collective-permute-done.33 = bf16[7,32,256]{2,1,0:T(8,128)(2,1)S(1)} collective-permute-done((bf16[7,32,256]{2,1,0:T(8,128)(2,1)S(1)}, bf16[7,32,256]{2,1,0:T(8,128)(2,1)S(1)}, u32[]{:S(2)}, u32[]{:S(2)}) %collective-permute-start.33) | collective-permute-done | bytes 114720 | tf_op jit(solution)/shard_map/ppermute | solution.py:52
  (144 shorter events, 82.0 us)
Async XLA Ops:
  6.4 8.1 %collective-permute-start.10 = (bf16[7,32,256]{2,1,0:T(8,128)(2,1)S(1)}, bf16[7,32,256]{2,1,0:T(8,128)(2,1)S(1)}, u32[]{:S(2)}, u32[]{:S(2)}) collective-permute-start(bf16[7,32,256]{2,1,0:T(8,128)(2,1)S(1)} %pad_dynamic-slice_fusion.1), channel_id=1, source_target_pairs={{0,4},{1,5},{2,6},{3,7},{4,0},{5,1},{6,2},{7,3},{8,12},{9,13},{10,... | collective-permute-start | bytes 344072 | tf_op jit(solution)/shard_map/ppermute | solution.py:52
  21.9 10.9 %collective-permute-start.12 = (bf16[2,2,7,32,256]{4,3,2,1,0:T(8,128)(2,1)}, bf16[2,2,7,32,256]{4,3,2,1,0:T(8,128)(2,1)}, u32[]{:S(2)}, u32[]{:S(2)}) collective-permute-start(bf16[2,2,7,32,256]{4,3,2,1,0:T(8,128)(2,1)} %get-tuple-element.45), channel_id=1, source_target_pairs={{0,1},{1,0},{2,3},{3,2},{4,5},{5,4},{6,7},{7,6},{8,9},{9,8},{10,11... | collective-permute-start | bytes 1376264 | tf_op jit(solution)/shard_map/ppermute | solution.py:52
  24.2 12.4 %collective-permute-start.5 = (bf16[2,2,2,7,32,128]{5,4,3,2,1,0:T(8,128)(2,1)}, bf16[2,2,2,7,32,128]{5,4,3,2,1,0:T(8,128)(2,1)}, u32[]{:S(2)}, u32[]{:S(2)}) collective-permute-start(bf16[2,2,2,7,32,128]{5,4,3,2,1,0:T(8,128)(2,1)} %get-tuple-element.47), channel_id=1, source_target_pairs={{0,16},{8,24},{16,0},{24,8},{1,17},{9,25},{17,1},{25,9},{2,18},{10... | collective-permute-start | bytes 1376264 | tf_op jit(solution)/shard_map/ppermute | solution.py:52
  26.9 11.8 %collective-permute-start.15 = (bf16[4,2,8,512]{3,2,1,0:T(8,128)(2,1)S(1)}, bf16[4,2,8,512]{3,2,1,0:T(8,128)(2,1)}, u32[]{:S(2)}, u32[]{:S(2)}) collective-permute-start(bf16[4,2,8,512]{3,2,1,0:T(8,128)(2,1)S(1)} %reshape.112), channel_id=1, source_target_pairs={{0,4},{1,5},{2,6},{3,7},{4,0},{5,1},{6,2},{7,3},{8,12},{9,13},{10,... | collective-permute-start | bytes 196616 | tf_op jit(solution)/shard_map/ppermute | solution.py:52
  30.1 9.5 %collective-permute-start = (bf16[4,1,4,64,128]{4,3,2,1,0:T(8,128)(2,1)}, bf16[4,1,4,64,128]{4,3,2,1,0:T(8,128)(2,1)}, u32[]{:S(2)}, u32[]{:S(2)}) collective-permute-start(bf16[4,1,4,64,128]{4,3,2,1,0:T(8,128)(2,1)} %slice.96), channel_id=1, source_target_pairs={{0,8},{1,9},{2,10},{3,11},{4,12},{5,13},{6,14},{7,15},{8,16},{9,17... | collective-permute-start | bytes 786440 | tf_op jit(solution)/shard_map/ppermute | solution.py:47
  35.2 33.3 %collective-permute-start.13 = (bf16[2,2,2,7,32,256]{5,4,3,2,1,0:T(8,128)(2,1)}, bf16[2,2,2,7,32,256]{5,4,3,2,1,0:T(8,128)(2,1)}, u32[]{:S(2)}, u32[]{:S(2)}) collective-permute-start(bf16[2,2,2,7,32,256]{5,4,3,2,1,0:T(8,128)(2,1)} %get-tuple-element.35), channel_id=1, source_target_pairs={{0,16},{8,24},{16,0},{24,8},{1,17},{9,25},{17,1},{25,9},{2,18},{10... | collective-permute-start | bytes 2752520 | tf_op jit(solution)/shard_map/ppermute | solution.py:52
  38.7 32.5 %collective-permute-start.6 = (bf16[2,2,2,2,7,32,128]{6,5,4,3,2,1,0:T(8,128)(2,1)}, bf16[2,2,2,2,7,32,128]{6,5,4,3,2,1,0:T(8,128)(2,1)}, u32[]{:S(2)}, u32[]{:S(2)}) collective-permute-start(bf16[2,2,2,2,7,32,128]{6,5,4,3,2,1,0:T(8,128)(2,1)} %get-tuple-element.37), channel_id=1, source_target_pairs={{0,8},{8,0},{16,24},{24,16},{1,9},{9,1},{17,25},{25,17},{2,10},{10... | collective-permute-start | bytes 2752520 | tf_op jit(solution)/shard_map/ppermute | solution.py:52
  41.3 21.7 %collective-permute-start.1 = (bf16[4,9,1,64,128]{4,3,2,1,0:T(8,128)(2,1)}, bf16[4,9,1,64,128]{4,3,2,1,0:T(8,128)(2,1)S(1)}, u32[]{:S(2)}, u32[]{:S(2)}) collective-permute-start(bf16[4,9,1,64,128]{4,3,2,1,0:T(8,128)(2,1)} %pad_maximum_fusion.5), channel_id=1, source_target_pairs={{0,1},{1,2},{2,3},{3,4},{4,5},{5,6},{6,7},{8,9},{9,10},{10,11},{11... | collective-permute-start | bytes 1769480 | tf_op jit(solution)/shard_map/ppermute | solution.py:47
  50.7 33.4 %collective-permute-start.17 = (bf16[2,2,4,2,8,512]{5,4,3,2,1,0:T(8,128)(2,1)S(1)}, bf16[2,2,4,2,8,512]{5,4,3,2,1,0:T(8,128)(2,1)S(1)}, u32[]{:S(2)}, u32[]{:S(2)}) collective-permute-start(bf16[2,2,4,2,8,512]{5,4,3,2,1,0:T(8,128)(2,1)S(1)} %pad_maximum_fusion.15), channel_id=1, source_target_pairs={{0,1},{1,0},{2,3},{3,2},{4,5},{5,4},{6,7},{7,6},{8,9},{9,8},{10,11... | collective-permute-start | bytes 786440 | tf_op jit(solution)/shard_map/ppermute | solution.py:52
  71.2 41.9 %collective-permute-start.14 = (bf16[2,2,2,2,7,32,256]{6,5,4,3,2,1,0:T(8,128)(2,1)}, bf16[2,2,2,2,7,32,256]{6,5,4,3,2,1,0:T(8,128)(2,1)}, u32[]{:S(2)}, u32[]{:S(2)}) collective-permute-start(bf16[2,2,2,2,7,32,256]{6,5,4,3,2,1,0:T(8,128)(2,1)} %get-tuple-element.33), channel_id=1, source_target_pairs={{0,8},{8,0},{16,24},{24,16},{1,9},{9,1},{17,25},{25,17},{2,10},{10... | collective-permute-start | bytes 5505032 | tf_op jit(solution)/shard_map/ppermute | solution.py:52
  82.0 12.5 %collective-permute-start.9 = (bf16[4,4,1,32,256]{4,3,2,1,0:T(8,128)(2,1)}, bf16[4,4,1,32,256]{4,3,2,1,0:T(8,128)(2,1)S(1)}, u32[]{:S(2)}, u32[]{:S(2)}) collective-permute-start(bf16[4,4,1,32,256]{4,3,2,1,0:T(8,128)(2,1)} %get-tuple-element.16), channel_id=1, source_target_pairs={{0,1},{1,2},{2,3},{3,4},{4,5},{5,6},{6,7},{8,9},{9,10},{10,11},{11... | collective-permute-start | bytes 786440 | tf_op jit(solution)/shard_map/ppermute | solution.py:47
  85.1 9.4 %collective-permute-start.8 = (bf16[4,1,1,32,256]{4,3,2,1,0:T(8,128)(2,1)S(1)}, bf16[4,1,1,32,256]{4,3,2,1,0:T(8,128)(2,1)S(1)}, u32[]{:S(2)}, u32[]{:S(2)}) collective-permute-start(bf16[4,1,1,32,256]{4,3,2,1,0:T(8,128)(2,1)S(1)} %slice.98), channel_id=1, source_target_pairs={{0,9},{1,10},{2,11},{3,12},{4,13},{5,14},{6,15},{8,17},{9,18},{10,... | collective-permute-start | bytes 196616 | tf_op jit(solution)/shard_map/ppermute | solution.py:47
  108.3 25.4 %collective-permute-start.28 = (bf16[16,7,32,256]{3,2,1,0:T(8,128)(2,1)}, bf16[16,7,32,256]{3,2,1,0:T(8,128)(2,1)S(1)}, u32[]{:S(2)}, u32[]{:S(2)}) collective-permute-start(bf16[16,7,32,256]{3,2,1,0:T(8,128)(2,1)} %bitcast.146), channel_id=1, source_target_pairs={{0,8},{8,0},{16,24},{24,16},{1,9},{9,1},{17,25},{25,17},{2,10},{10... | collective-permute-start | bytes 5505032 | tf_op jit(solution)/shard_map/ppermute | solution.py:52
  134.8 34.9 %collective-permute-start.29 = (bf16[8,7,32,256]{3,2,1,0:T(8,128)(2,1)S(1)}, bf16[8,7,32,256]{3,2,1,0:T(8,128)(2,1)}, u32[]{:S(2)}, u32[]{:S(2)}) collective-permute-start(bf16[8,7,32,256]{3,2,1,0:T(8,128)(2,1)S(1)} %slice.163), channel_id=1, source_target_pairs={{0,16},{8,24},{16,0},{24,8},{1,17},{9,25},{17,1},{25,9},{2,18},{10... | collective-permute-start | bytes 2752520 | tf_op jit(solution)/shard_map/ppermute | solution.py:52
  137.7 29.4 %collective-permute-start.22 = (bf16[8,7,32,128]{3,2,1,0:T(8,128)(2,1)}, bf16[8,7,32,128]{3,2,1,0:T(8,128)(2,1)}, u32[]{:S(2)}, u32[]{:S(2)}) collective-permute-start(bf16[8,7,32,128]{3,2,1,0:T(8,128)(2,1)} %slice.165), channel_id=1, source_target_pairs={{0,16},{8,24},{16,0},{24,8},{1,17},{9,25},{17,1},{25,9},{2,18},{10... | collective-permute-start | bytes 1376264 | tf_op jit(solution)/shard_map/ppermute | solution.py:52
  138.0 25.1 %collective-permute-start.19 = (bf16[4,1,2,32,256]{4,3,2,1,0:T(8,128)(2,1)}, bf16[4,1,2,32,256]{4,3,2,1,0:T(8,128)(2,1)S(1)}, u32[]{:S(2)}, u32[]{:S(2)}) collective-permute-start(bf16[4,1,2,32,256]{4,3,2,1,0:T(8,128)(2,1)} %get-tuple-element.18), channel_id=1, source_target_pairs={{8,0},{9,1},{10,2},{11,3},{12,4},{13,5},{14,6},{15,7},{16,8},{17,9... | collective-permute-start | bytes 393224 | tf_op jit(solution)/shard_map/ppermute | solution.py:47
  147.6 14.1 %all-to-all-start = ((bf16[8,2,2048]{2,1,0:T(2,128)(2,1)}), bf16[8,2,2048]{2,1,0:T(2,128)(2,1)S(1)}, u32[]{:S(2)}, u32[]{:S(2)}) async-start(bf16[8,2,2048]{2,1,0:T(2,128)(2,1)} %reshape.134), calls=%async_computation | async-start | bytes 131072 | tf_op jit(solution)/shard_map/all_to_all | solution.py:502
  164.2 15.4 %collective-permute-start.20 = (bf16[4,5,1,32,256]{4,3,2,1,0:T(8,128)(2,1)S(1)}, bf16[4,5,1,32,256]{4,3,2,1,0:T(8,128)(2,1)S(1)}, u32[]{:S(2)}, u32[]{:S(2)}) collective-permute-start(bf16[4,5,1,32,256]{4,3,2,1,0:T(8,128)(2,1)S(1)} %pad_maximum_fusion.14), channel_id=1, source_target_pairs={{1,0},{2,1},{3,2},{4,3},{5,4},{6,5},{7,6},{9,8},{10,9},{11,10},{12... | collective-permute-start | bytes 983048 | tf_op jit(solution)/shard_map/ppermute | solution.py:47
  168.2 10.0 %collective-permute-start.23 = (bf16[4,7,32,128]{3,2,1,0:T(8,128)(2,1)S(1)}, bf16[4,7,32,128]{3,2,1,0:T(8,128)(2,1)S(1)}, u32[]{:S(2)}, u32[]{:S(2)}) collective-permute-start(bf16[4,7,32,128]{3,2,1,0:T(8,128)(2,1)S(1)} %slice.167), channel_id=1, source_target_pairs={{0,1},{1,0},{2,3},{3,2},{4,5},{5,4},{6,7},{7,6},{8,9},{9,8},{10,11... | collective-permute-start | bytes 688136 | tf_op jit(solution)/shard_map/ppermute | solution.py:52
  171.9 16.5 %collective-permute-start.30 = (bf16[4,7,32,256]{3,2,1,0:T(8,128)(2,1)S(1)}, bf16[4,7,32,256]{3,2,1,0:T(8,128)(2,1)S(1)}, u32[]{:S(2)}, u32[]{:S(2)}) collective-permute-start(bf16[4,7,32,256]{3,2,1,0:T(8,128)(2,1)S(1)} %slice.164), channel_id=1, source_target_pairs={{0,1},{1,0},{2,3},{3,2},{4,5},{5,4},{6,7},{7,6},{8,9},{9,8},{10,11... | collective-permute-start | bytes 1376264 | tf_op jit(solution)/shard_map/ppermute | solution.py:52
  178.3 8.6 %collective-permute-start.24 = (bf16[2,7,32,128]{3,2,1,0:T(8,128)(2,1)S(1)}, bf16[2,7,32,128]{3,2,1,0:T(8,128)(2,1)S(1)}, u32[]{:S(2)}, u32[]{:S(2)}) collective-permute-start(bf16[2,7,32,128]{3,2,1,0:T(8,128)(2,1)S(1)} %slice.169), channel_id=1, source_target_pairs={{0,4},{1,5},{2,6},{3,7},{4,0},{5,1},{6,2},{7,3},{8,12},{9,13},{10,... | collective-permute-start | bytes 344072 | tf_op jit(solution)/shard_map/ppermute | solution.py:52
  188.6 13.2 %collective-permute-start.31 = (bf16[2,7,32,256]{3,2,1,0:T(8,128)(2,1)S(1)}, bf16[2,7,32,256]{3,2,1,0:T(8,128)(2,1)S(1)}, u32[]{:S(2)}, u32[]{:S(2)}) collective-permute-start(bf16[2,7,32,256]{3,2,1,0:T(8,128)(2,1)S(1)} %slice.166), channel_id=1, source_target_pairs={{0,4},{1,5},{2,6},{3,7},{4,0},{5,1},{6,2},{7,3},{8,12},{9,13},{10,... | collective-permute-start | bytes 688136 | tf_op jit(solution)/shard_map/ppermute | solution.py:52
  192.2 12.3 %collective-permute-start.26 = (bf16[7,32,128]{2,1,0:T(8,128)(2,1)S(1)}, bf16[7,32,128]{2,1,0:T(8,128)(2,1)S(1)}, u32[]{:S(2)}, u32[]{:S(2)}) collective-permute-start(bf16[7,32,128]{2,1,0:T(8,128)(2,1)S(1)} %bitcast.137), channel_id=1, source_target_pairs={{0,16},{8,24},{16,0},{24,8},{1,17},{9,25},{17,1},{25,9},{2,18},{10... | collective-permute-start | bytes 172040 | tf_op jit(solution)/shard_map/ppermute | solution.py:52
  204.5 8.5 %collective-permute-start.27 = (bf16[2,7,32,128]{3,2,1,0:T(8,128)(2,1)S(1)}, bf16[2,7,32,128]{3,2,1,0:T(8,128)(2,1)S(1)}, u32[]{:S(2)}, u32[]{:S(2)}) collective-permute-start(bf16[2,7,32,128]{3,2,1,0:T(8,128)(2,1)S(1)} %get-tuple-element.63), channel_id=1, source_target_pairs={{0,8},{8,0},{16,24},{24,16},{1,9},{9,1},{17,25},{25,17},{2,10},{10... | collective-permute-start | bytes 344072 | tf_op jit(solution)/shard_map/ppermute | solution.py:52
  (22 other events, 135.2 us)
where the time goes:
time: 220 us; the launch traced here: 218 us
  starting transfers between devices  84.7 us (38%)
  Pallas kernels  52.7 us (24%)
  waiting for transfers between devices  30.8 us (14%)
  other arithmetic  27.8 us (13%)
  local copies, waits for them, and re-layouts  16.3 us (7%)
  between operations  6.19 us (3%)
    ppermute x27, starting transfers between devices, swapped(): return lax.ppermute(value, axis, [(i, i ^ 1 << bit) for i in range(count)])  58.7 us
    pallas_call x8, Pallas kernels, call(): pl.pallas_call(kernel, out_shape=outs, grid=grid or (), in_specs=specs, o...  52.7 us
    ppermute x27, waiting for transfers between devices, swapped(): return lax.ppermute(value, axis, [(i, i ^ 1 << bit) for i in range(count)])  26.9 us
    ppermute x8, starting transfers between devices, shifted(): return lax.ppermute(value, ('space', 'chan'), pairs)  19.2 us
    another operation x14, other arithmetic, doubled(): return jnp.stack([value, swapped(value, axis, bit)])  15.3 us
    all_to_all x1, starting transfers between devices, local(): lax.all_to_all(local_out, 'chan', split_axis=4, concat_axis=2, tiled=True)  6.83 us
    add x8, other arithmetic, sum_filters(): total = keep.astype(F32) + swapped(send.astype(BF16), axis, bit).astype(F32)  4.8 us
  transfers between devices with their start and end apart: 36, of which 15 were waited for; matrix products, arithmetic and copies ran while one was open for 18% of the time, Pallas kernels for 24%

commit v1 on v0

--- a/solution.py
+++ b/solution.py
@@ -22,14 +22,6 @@
 
 def bits(axis):
     return lax.axis_size(axis).bit_length() - 1
-
-
-def gather_order(axis):
-    return list(reversed(range(bits(axis))))
-
-
-def chan_gather_order():
-    return [bit for bit in reversed(range(bits("chan"))) if bit] + [0]
 
 
 def chan_sum_order():
@@ -52,27 +44,65 @@
     return lax.ppermute(value, axis, [(i, i ^ (1 << bit)) for i in range(count)])
 
 
-def doubled(value, axis, bit):
-    return jnp.stack([value, swapped(value, axis, bit)])
+def doubled(value, axis, bit, name):
+    with jax.named_scope(name):
+        other = swapped(value, axis, bit)
+    return jnp.stack([value, other])
 
 
 def position():
     return jnp.stack([lax.axis_index("space"), lax.axis_index("chan")]).astype(jnp.int32)
 
 
-def gather_filters(shard):
+def own_part(shard):
     space = lax.axis_size("space")
     edge, inputs, mine = shard.shape[0], shard.shape[3], shard.shape[4]
     taps = edge**3
     each = -(-taps // space)
     flat = jnp.transpose(shard.reshape(taps, inputs, mine), (0, 2, 1))
     flat = jnp.pad(flat, ((0, each * space - taps), (0, 0), (0, 0)))
-    part = lax.dynamic_slice_in_dim(flat, lax.axis_index("space") * each, each, 0)
-    for bit in chan_gather_order():
-        part = doubled(part, "chan", bit)
-    for bit in gather_order("space"):
-        part = doubled(part, "space", bit)
-    return part.reshape(space, lax.axis_size("chan"), each, mine, inputs)
+    return lax.dynamic_slice_in_dim(flat, lax.axis_index("space") * each, each, 0)
+
+
+def far_bits():
+    return list(reversed(range(1, bits("chan"))))
+
+
+def high_bits():
+    return list(reversed(range(1, bits("space"))))
+
+
+def after(value, other):
+    return lax.optimization_barrier((value, other))[0]
+
+
+def finish_gather(part, name, gate=None):
+    each, mine, inputs = part.shape[-3:]
+    for bit in high_bits():
+        part = doubled(part, "space", bit, f"{name}_y")
+    part = doubled(part, "space", 0, f"{name}_core")
+    return part.reshape(lax.axis_size("space"), lax.axis_size("chan"), each, mine, inputs)
+
+
+def mixed_gather(part, name):
+    each, mine, inputs = part.shape
+    for bit in far_bits():
+        part = doubled(part, "chan", bit, f"{name}_z")
+    far = part.shape[:-3]
+    highs = len(high_bits())
+    cut = (each + 1) // 2
+    one, two = part[..., :cut, :, :], part[..., cut:, :, :]
+    one = doubled(one, "chan", 0, f"{name}_x1")
+    for bit in high_bits():
+        two = doubled(two, "space", bit, f"{name}_y1")
+    for bit in high_bits():
+        one = doubled(one, "space", bit, f"{name}_y2")
+    two = doubled(two, "chan", 0, f"{name}_x2")
+    one = doubled(one, "space", 0, f"{name}_core")
+    two = doubled(two, "space", 0, f"{name}_core")
+    two = jnp.moveaxis(two, 1, 1 + highs)
+    whole = jnp.concatenate([one, two], axis=-3)
+    return whole.reshape(lax.axis_size("space"), lax.axis_size("chan"), each, mine, inputs)
 
 
 def relative(index, mine, order):
@@ -276,22 +306,42 @@
     )
 
 
-def sum_filters(keep, send):
-    each, mine, inputs = keep.shape[2:]
-    total = None
-    order = [("space", bit) for bit in range(bits("space"))]
-    order += [("chan", bit) for bit in chan_sum_order()]
-    for axis, bit in order:
-        if total is not None:
-            half = total.shape[0] // 2
-            keep, send = total[:half], total[half:]
-        else:
-            keep = keep.reshape(-1, each, mine, inputs)
-            send = send.reshape(-1, each, mine, inputs)
-        total = keep.astype(F32) + swapped(send.astype(BF16), axis, bit).astype(F32)
-    part = total[0].astype(BF16)
-    for bit in gather_order("space"):
-        part = doubled(part, "space", bit)
+def core_sum(keep, send, name):
+    tail = keep.shape[2:]
+    with jax.named_scope(f"{name}_core"):
+        other = swapped(send, "space", 0)
+    total = keep.astype(F32) + other.astype(F32)
+    highs = bits("space") - 1
+    return total.reshape((2,) * highs + (2, -1) + tail)
+
+
+def half_sum(value, axis, bit, dim, name):
+    keep = lax.index_in_dim(value, 0, dim, keepdims=False)
+    send = lax.index_in_dim(value, 1, dim, keepdims=False)
+    with jax.named_scope(name):
+        other = swapped(send.astype(BF16), axis, bit)
+    return keep.astype(F32) + other.astype(F32)
+
+
+def sum_filters(total, name):
+    each, mine, inputs = total.shape[-3:]
+    highs = list(range(1, bits("space")))
+    cut = (each + 1) // 2
+    one, two = total[..., :cut, :, :], total[..., cut:, :, :]
+    two = half_sum(two, "chan", 0, len(highs), f"{name}_x1")
+    for bit in highs:
+        one = half_sum(one, "space", bit, 0, f"{name}_y1")
+    one = half_sum(one, "chan", 0, 0, f"{name}_x2")
+    for bit in highs:
+        two = half_sum(two, "space", bit, 0, f"{name}_y2")
+    part = jnp.concatenate([one, two], axis=-3)
+    for bit in far_bits():
+        part = part.reshape((2, -1, each, mine, inputs))
+        part = half_sum(part, "chan", bit, 0, f"{name}_z")
+    part = part.reshape(each, mine, inputs).astype(BF16)
+    for bit in high_bits():
+        part = doubled(part, "space", bit, f"{name}_end")
+    part = doubled(part, "space", 0, f"{name}_end")
     space = lax.axis_size("space")
     part = part.reshape(space, each, mine, inputs)
     places = jnp.arange(space) ^ lax.axis_index("space")
@@ -460,48 +510,77 @@
     )[0]
 
 
-def spread_cells(cotangent):
-    chan = lax.axis_size("chan")
-    vols, side_a, side_b, side_c, mine = cotangent.shape
-    rows = side_b // chan
-    flat = cotangent.reshape(vols, side_a, side_b, side_c * mine)
-    for step, bit in enumerate(gather_order("chan")):
-        other = swapped(flat, "chan", bit)
-        high = (lax.axis_index("chan") >> bit) & 1 == 1
-        flat = jnp.stack([jnp.where(high, other, flat), jnp.where(high, flat, other)], axis=step)
-    flat = flat.reshape(chan, vols, side_a, side_b, side_c * mine)
-    flat = jnp.pad(flat, ((0, 0), (0, 0), (0, 0), (0, 1), (0, 0)))
-    near = lax.dynamic_slice_in_dim(flat, lax.axis_index("chan") * rows, rows + 1, 3)
-    near = near.reshape(chan, vols, side_a, rows + 1, side_c, mine)
-    near = jnp.transpose(near, (1, 2, 3, 4, 0, 5))
-    near = near.reshape(vols, side_a, rows + 1, side_c, chan * mine)
-    plane = shifted(near[:, :1], (-1, 0))
-    return jnp.concatenate([near, plane], axis=1)
+class CellExchange:
+    def __init__(self, cotangent):
+        vols, side_a, side_b, side_c, mine = cotangent.shape
+        self.count = bits("chan")
+        self.tail = (side_b // 2**self.count, vols, side_a, side_c, mine)
+        flat = cotangent.reshape(vols, side_a, side_b, side_c * mine)
+        flat = jnp.transpose(flat, (2, 0, 1, 3))
+        self.value = flat.reshape((2,) * self.count + (-1,) + flat.shape[1:])
+
+    def stage(self, step):
+        bit = self.count - 1 - step
+        mine = (lax.axis_index("chan") >> bit) & 1
+        keep = lax.dynamic_index_in_dim(self.value, mine, 0, keepdims=False)
+        send = lax.dynamic_index_in_dim(self.value, 1 - mine, 0, keepdims=False)
+        with jax.named_scope("cells"):
+            other = swapped(send, "chan", bit)
+        low, high = jnp.where(mine == 1, other, keep), jnp.where(mine == 1, keep, other)
+        self.value = jnp.stack([low, high], axis=self.count - 1)
+
+    def finish(self):
+        rows, vols, side_a, side_c, mine = self.tail
+        chan = 2**self.count
+        value = self.value.reshape((chan, rows, vols, side_a, side_c, mine))
+        value = jnp.transpose(value, (2, 3, 1, 4, 0, 5))
+        own = value.reshape(vols, side_a, rows, side_c, chan * mine)
+        with jax.named_scope("cells_row"):
+            row = shifted(own[:, :, :1], (0, -1))
+        near = jnp.concatenate([own, row], axis=2)
+        with jax.named_scope("cells_plane"):
+            plane = shifted(near[:, :1], (-1, 0))
+        return own, jnp.concatenate([near, plane], axis=1)
 
 
 def local(volume, w_first, w_second, cotangent):
     here = position()
-    gathered = (list(range(bits("space"))), [0] + [b for b in range(1, bits("chan"))])
-    summed = (list(range(bits("space"))), chan_sum_order())
-    plane = shifted(volume[:, -1:], (1, 0))
-    row = shifted(jnp.concatenate([plane, volume], axis=1)[:, :, -1:], (0, 1))
-    first_full = gather_filters(w_first)
-    second_full = gather_filters(w_second)
-    grad_ext = spread_cells(cotangent)
-    grad_cells = grad_ext[:, :-1, :-1]
+    far = list(range(1, bits("chan")))
+    gathered = (list(range(bits("space"))), [0] + far)
+    summed = (list(range(bits("space"))), [0] + far[::-1])
+    cells = CellExchange(cotangent)
+    with jax.named_scope("plane"):
+        plane = shifted(volume[:, -1:], (1, 0))
+    part = own_part(w_first)
+    for step, bit in enumerate(far_bits() + [0]):
+        part = doubled(part, "chan", bit, "first_zx")
+        cells.stage(step)
+    row = jnp.concatenate([plane, volume], axis=1)[:, :, -1:]
+    with jax.named_scope("row"):
+        row = shifted(after(row, part), (0, 1))
+    first_full = finish_gather(part, "first")
+    second_full = mixed_gather(after(own_part(w_second), part), "second")
+    grad_cells, grad_ext = cells.finish()
     vol_parts = parted(volume, plane, row)
     hidden, hid_plane, hid_row = forward(here, vol_parts, first_full, gathered, True)
-    plane = shifted(hid_plane, (1, 0))
-    row = shifted(hid_row, (0, 1))
-    corner = shifted(hid_row[:, -1:], (1, 1))
+    with jax.named_scope("hidden_halo"):
+        row = shifted(hid_row, (0, 1))
+        plane = shifted(hid_plane, (1, 0))
+        corner = shifted(hid_row[:, -1:], (1, 1))
     act_parts = parted(hidden, plane, jnp.concatenate([corner, row], axis=1))
-    second_grad = sum_filters(*filter_grads(here, act_parts, grad_cells, summed))
+    second_terms = core_sum(*filter_grads(here, act_parts, grad_cells, summed), "sum_second")
+    second_grad = sum_filters(second_terms, "sum_second")
+    grad_ext = after(grad_ext, second_terms)
     pre_back, pre_plane, pre_row = hidden_back(here, grad_ext, second_full, hidden, gathered)
-    first_grad = sum_filters(*filter_grads(here, vol_parts, pre_back, summed))
-    local_out = forward(here, act_parts, second_full, gathered, False)[0]
-    second_out = lax.all_to_all(local_out, "chan", split_axis=4, concat_axis=2, tiled=True)
-    plane = shifted(pre_plane, (-1, 0))
-    row = shifted(jnp.concatenate([pre_row, plane[:, :, :1]], axis=1), (0, -1))
+    first_terms = core_sum(*filter_grads(here, vol_parts, pre_back, summed), "sum_first")
+    first_grad = sum_filters(first_terms, "sum_first")
+    with jax.named_scope("back_plane"):
+        plane = shifted(pre_plane, (-1, 0))
+    with jax.named_scope("back_row"):
+        row = shifted(jnp.concatenate([pre_row, plane[:, :, :1]], axis=1), (0, -1))
+    local_out = forward(here, after(act_parts, first_terms), second_full, gathered, False)[0]
+    with jax.named_scope("out"):
+        second_out = lax.all_to_all(local_out, "chan", split_axis=4, concat_axis=2, tiled=True)
     volume_grad = volume_grads(here, pre_back, plane, row, first_full, gathered)
     return (second_out, volume_grad, first_grad, second_grad)
 

time: 220 us -> 248 us (1.13)
  waiting for transfers between devices: 30.8 us -> 74.5 us
  starting transfers between devices: 84.7 us -> 76 us
  other arithmetic: 27.8 us -> 21.5 us
    ppermute x27 -> x34, waiting for transfers between devices: 26.9 us -> 66.1 us  [swapped(): return lax.ppermute(value, axis, [(i, i ^ 1 << bit) for i in range(count)])]
    another operation x20 -> x26, other arithmetic: 16.3 us -> 5.84 us  [the longest x18 4.71 us: doubled(): return jnp.stack([value, other])]
    ppermute x27 -> x34, starting transfers between devices: 58.7 us -> 50.8 us  [swapped(): return lax.ppermute(value, axis, [(i, i ^ 1 << bit) for i in range(count)])]
    ppermute x8 -> x9, waiting for transfers between devices: 2.43 us -> 6.81 us  [shifted(): return lax.ppermute(value, ('space', 'chan'), pairs)]
    all_to_all x1, starting transfers between devices: 6.83 us -> 3.61 us  [local(): lax.all_to_all(local_out, 'chan', split_axis=4, concat_axis=2, tiled=True)]
    ppermute x8 -> x9, starting transfers between devices: 19.2 us -> 21.6 us  [shifted(): return lax.ppermute(value, ('space', 'chan'), pairs)]
    add x8 -> x12, other arithmetic: 4.8 us -> 6.23 us  [the longest x2 3.7 us: core_sum(): total = keep.astype(F32) + other.astype(F32)]
  transfers between devices with their start and end apart: 36 -> 44, of which waited for: 15 -> 16; matrix products, arithmetic and copies ran while one was open for 18% -> 12% of each run, Pallas kernels for 24% -> 21%
where the time goes in v1:
time: 248 us; the launch traced here: 247 us
  starting transfers between devices  76 us (31%)
  waiting for transfers between devices  74.5 us (30%)
  Pallas kernels  52.6 us (21%)
  other arithmetic  21.5 us (9%)
  local copies, waits for them, and re-layouts  15.5 us (6%)
  between operations  6.43 us (3%)
    ppermute x34, waiting for transfers between devices, swapped(): return lax.ppermute(value, axis, [(i, i ^ 1 << bit) for i in range(count)])  66.1 us
    pallas_call x8, Pallas kernels, call(): pl.pallas_call(kernel, out_shape=outs, grid=grid or (), in_specs=specs, o...  52.6 us
    ppermute x34, starting transfers between devices, swapped(): return lax.ppermute(value, axis, [(i, i ^ 1 << bit) for i in range(count)])  50.8 us
    ppermute x9, starting transfers between devices, shifted(): return lax.ppermute(value, ('space', 'chan'), pairs)  21.6 us
    ppermute x9, waiting for transfers between devices, shifted(): return lax.ppermute(value, ('space', 'chan'), pairs)  6.81 us
  transfers between devices with their start and end apart: 44, of which 16 were waited for; matrix products, arithmetic and copies ran while one was open for 12% of the time, Pallas kernels for 21%

profile of v1, /device:TPU:0, one launch (start us, length us, event | category | flops | bytes accessed | tf_op | source)
XLA Modules:
  0.0 246.5 jit_solution(8252626197384170211)
XLA Ops:
  13.5 3.7 %collective-permute-done.2 = bf16[2,7,32,128]{3,2,1,0:T(8,128)(2,1)S(1)} collective-permute-done((bf16[2,7,32,128]{3,2,1,0:T(8,128)(2,1)S(1)}, bf16[2,7,32,128]{3,2,1,0:T(8,128)(2,1)S(1)}, u32[]{:S(2)}, u32[]{:S(2)}) %collective-permute-start.2) | collective-permute-done | bytes 114720 | tf_op jit(solution)/shard_map/first_zx/ppermute | solution.py:44
  21.2 3.7 %collective-permute-done.3 = bf16[2,2,7,32,128]{4,3,2,1,0:T(8,128)(2,1)S(1)} collective-permute-done((bf16[2,2,7,32,128]{4,3,2,1,0:T(8,128)(2,1)S(1)}, bf16[2,2,7,32,128]{4,3,2,1,0:T(8,128)(2,1)S(1)}, u32[]{:S(2)}, u32[]{:S(2)}) %collective-permute-start.3) | collective-permute-done | bytes 229408 | tf_op jit(solution)/shard_map/first_zx/ppermute | solution.py:44
  27.0 9.8 %collective-permute-done.5 = bf16[2,2,2,7,32,128]{5,4,3,2,1,0:T(8,128)(2,1)S(1)} collective-permute-done((bf16[2,2,2,7,32,128]{5,4,3,2,1,0:T(8,128)(2,1)S(1)}, bf16[2,2,2,7,32,128]{5,4,3,2,1,0:T(8,128)(2,1)S(1)}, u32[]{:S(2)}, u32[]{:S(2)}) %collective-permute-start.5) | collective-permute-done | bytes 458784 | tf_op jit(solution)/shard_map/first_y/ppermute | solution.py:44
  42.3 3.5 %collective-permute-start.16 = (bf16[7,32,256]{2,1,0:T(8,128)(2,1)S(1)}, bf16[7,32,256]{2,1,0:T(8,128)(2,1)S(1)}, u32[]{:S(2)}, u32[]{:S(2)}) collective-permute-start(bf16[7,32,256]{2,1,0:T(8,128)(2,1)S(1)} %pad_dynamic-slice_fusion), channel_id=1, source_target_pairs={{0,4},{1,5},{2,6},{3,7},{4,0},{5,1},{6,2},{7,3},{8,12},{9,13},{10,... | collective-permute-start | bytes 344072 | tf_op jit(solution)/shard_map/second_z/ppermute | solution.py:44
  45.9 5.9 %collective-permute-done.16 = bf16[7,32,256]{2,1,0:T(8,128)(2,1)S(1)} collective-permute-done((bf16[7,32,256]{2,1,0:T(8,128)(2,1)S(1)}, bf16[7,32,256]{2,1,0:T(8,128)(2,1)S(1)}, u32[]{:S(2)}, u32[]{:S(2)}) %collective-permute-start.16) | collective-permute-done | bytes 114720 | tf_op jit(solution)/shard_map/second_z/ppermute | solution.py:44
  54.3 5.5 %collective-permute-done.17 = bf16[2,7,32,256]{3,2,1,0:T(8,128)(2,1)S(1)} collective-permute-done((bf16[2,7,32,256]{3,2,1,0:T(8,128)(2,1)}, bf16[2,7,32,256]{3,2,1,0:T(8,128)(2,1)S(1)}, u32[]{:S(2)}, u32[]{:S(2)}) %collective-permute-start.17) | collective-permute-done | bytes 229408 | tf_op jit(solution)/shard_map/second_z/ppermute | solution.py:44
  59.9 11.2 %collective-permute-start.18 = (bf16[2,2,4,32,256]{4,3,2,1,0:T(8,128)(2,1)S(1)}, bf16[2,2,4,32,256]{4,3,2,1,0:T(8,128)(2,1)S(1)}, u32[]{:S(2)}, u32[]{:S(2)}) collective-permute-start(bf16[2,2,4,32,256]{4,3,2,1,0:T(8,128)(2,1)S(1)} %fusion.10), channel_id=1, source_target_pairs={{0,1},{1,0},{2,3},{3,2},{4,5},{5,4},{6,7},{7,6},{8,9},{9,8},{10,11... | collective-permute-start | bytes 786440 | tf_op jit(solution)/shard_map/second_x1/ppermute | solution.py:44
  71.9 4.7 %shard_map.75.ref = bf16[3,4,9,5,32,128]{5,4,3,2,1,0:T(8,128)(2,1)} custom-call(bf16[4,8,4,64,128]{4,3,2,1,0:T(8,128)(2,1)} %own.1, bf16[4,1,4,64,128]{4,3,2,1,0:T(8,128)(2,1)} %copy-done.2, bf16[4,9,1,64,128]{4,3,2,1,0:T(8,128)(2,1)} %copy-done.5), custom_call_target="tpu_custom_call" | custom-call | bytes 7372800 | tf_op jit(solution)/shard_map/pallas_call | solution.py:132
  77.9 8.2 %shard_map.76 = (bf16[4,4,2,32,256]{4,3,2,1,0:T(8,128)(2,1)}, bf16[4,1,2,32,256]{4,3,2,1,0:T(8,128)(2,1)}, bf16[4,4,1,32,256]{4,3,2,1,0:T(8,128)(2,1)}) custom-call(s32[2]{0:T(128)} %pad_add_fusion.here, bf16[3,4,9,5,32,128]{5,4,3,2,1,0:T(8,128)(2,1)} %shard_map.75.ref, bf16[4,8,7,32,128]{4,3,2,1,0:T(8,128)(2,1)} %bitcast.208), custom_call_target="tpu_custom_call" | custom-call | flops 1811939328 | bytes 7176200 | tf_op jit(solution)/shard_map/pallas_call | solution.py:132
  90.7 7.1 %collective-permute-start.8 = (bf16[4,1,1,32,256]{4,3,2,1,0:T(8,128)(2,1)S(1)}, bf16[4,1,1,32,256]{4,3,2,1,0:T(8,128)(2,1)S(1)}, u32[]{:S(2)}, u32[]{:S(2)}) collective-permute-start(bf16[4,1,1,32,256]{4,3,2,1,0:T(8,128)(2,1)S(1)} %slice.149), channel_id=1, source_target_pairs={{0,9},{1,10},{2,11},{3,12},{4,13},{5,14},{6,15},{8,17},{9,18},{10,... | collective-permute-start | bytes 196616 | tf_op jit(solution)/shard_map/hidden_halo/ppermute | solution.py:39
  101.1 3.6 %shard_map.77.ref = bf16[3,4,5,3,16,256]{5,4,3,2,1,0:T(8,128)(2,1)} custom-call(bf16[4,4,2,32,256]{4,3,2,1,0:T(8,128)(2,1)} %get-tuple-element.19.own.hidden, bf16[4,1,2,32,256]{4,3,2,1,0:T(8,128)(2,1)} %copy-done.9, bf16[4,5,1,32,256]{4,3,2,1,0:T(8,128)(2,1)} %pad_maximum_fusion.14.row), custom_call_target="tpu_custom_call" | custom-call | bytes 2457600 | tf_op jit(solution)/shard_map/pallas_call | solution.py:132
  104.8 8.8 %shard_map.78 = (bf16[2,8,7,32,256]{4,3,2,1,0:T(8,128)(2,1)}, bf16[2,8,7,32,256]{4,3,2,1,0:T(8,128)(2,1)}) custom-call(s32[2]{0:T(128)} %pad_add_fusion.here, bf16[3,4,5,3,16,256]{5,4,3,2,1,0:T(8,128)(2,1)} %shard_map.77.ref, bf16[4,2,1,16,256]{4,3,2,1,0:T(8,128)(2,1)} %reshape.141.grads), custom_call_target="tpu_custom_call" | custom-call | flops 452984832 | bytes 5210120 | tf_op jit(solution)/shard_map/pallas_call | solution.py:132
  116.4 9.0 %collective-permute-done.22 = bf16[2,2,2,3,32,256]{5,4,3,2,1,0:T(8,128)(2,1)S(1)} collective-permute-done((bf16[2,2,2,3,32,256]{5,4,3,2,1,0:T(8,128)(2,1)S(1)}, bf16[2,2,2,3,32,256]{5,4,3,2,1,0:T(8,128)(2,1)S(1)}, u32[]{:S(2)}, u32[]{:S(2)}) %collective-permute-start.22) | collective-permute-done | bytes 393248 | tf_op jit(solution)/shard_map/second_x2/ppermute | solution.py:44
  127.8 5.1 %collective-permute-done.13 = bf16[4,2,1,16,256]{4,3,2,1,0:T(8,128)(2,1)S(1)} collective-permute-done((bf16[4,2,1,16,256]{4,3,2,1,0:T(8,128)(2,1)S(1)}, bf16[4,2,1,16,256]{4,3,2,1,0:T(8,128)(2,1)S(1)}, u32[]{:S(2)}, u32[]{:S(2)}) %collective-permute-start.13) | collective-permute-done | bytes 65568 | tf_op jit(solution)/shard_map/cells_row/ppermute | solution.py:39
  150.2 3.8 %shard_map.79 = (bf16[4,4,2,32,256]{4,3,2,1,0:T(8,128)(2,1)}, bf16[4,1,2,32,256]{4,3,2,1,0:T(8,128)(2,1)}, bf16[4,4,1,32,256]{4,3,2,1,0:T(8,128)(2,1)}) custom-call(s32[2]{0:T(128)} %pad_add_fusion.here, bf16[4,3,2,16,256]{4,3,2,1,0:T(8,128)(2,1)} %pad_maximum_fusion.25.cells, bf16[4,8,7,32,256]{4,3,2,1,0:T(8,128)(2,1)} %bitcast.192, ...), custom_call_target="tpu_custom_call" | custom-call | flops 452984832 | bytes 5308424 | tf_op jit(solution)/shard_map/pallas_call | solution.py:132
  154.0 10.9 %shard_map.80 = (bf16[2,8,7,32,128]{4,3,2,1,0:T(8,128)(2,1)}, bf16[2,8,7,32,128]{4,3,2,1,0:T(8,128)(2,1)}) custom-call(s32[2]{0:T(128)} %pad_add_fusion.here, bf16[3,4,9,5,32,128]{5,4,3,2,1,0:T(8,128)(2,1)} %shard_map.75.ref, bf16[4,4,2,32,256]{4,3,2,1,0:T(8,128)(2,1)} %get-tuple-element.26.grads.cells), custom_call_target="tpu_custom_call" | custom-call | flops 1811939328 | bytes 6782984 | tf_op jit(solution)/shard_map/pallas_call | solution.py:132
  171.2 3.7 %collective-permute-start.38 = (bf16[4,3,32,256]{3,2,1,0:T(8,128)(2,1)S(1)}, bf16[4,3,32,256]{3,2,1,0:T(8,128)(2,1)S(1)}, u32[]{:S(2)}, u32[]{:S(2)}) collective-permute-start(bf16[4,3,32,256]{3,2,1,0:T(8,128)(2,1)S(1)} %fusion.18), channel_id=1, source_target_pairs={{0,16},{8,24},{16,0},{24,8},{1,17},{9,25},{17,1},{25,9},{2,18},{10... | collective-permute-start | bytes 589832 | tf_op jit(solution)/shard_map/sum_second_y2/ppermute | solution.py:44
  174.9 9.9 %collective-permute-done.35 = bf16[2,4,4,32,256]{4,3,2,1,0:T(8,128)(2,1)S(1)} collective-permute-done((bf16[2,4,4,32,256]{4,3,2,1,0:T(8,128)(2,1)S(1)}, bf16[2,4,4,32,256]{4,3,2,1,0:T(8,128)(2,1)S(1)}, u32[]{:S(2)}, u32[]{:S(2)}) %collective-permute-start.35) | collective-permute-done | bytes 524320 | tf_op jit(solution)/shard_map/sum_second_y1/ppermute | solution.py:44
  186.2 6.6 %shard_map.82 = bf16[4,8,4,64,128]{4,3,2,1,0:T(8,128)(2,1)} custom-call(s32[2]{0:T(128)} %pad_add_fusion.here, bf16[4,4,2,32,256]{4,3,2,1,0:T(8,128)(2,1)} %get-tuple-element.26.grads.cells, bf16[4,1,2,32,256]{4,3,2,1,0:T(8,128)(2,1)} %copy-done.10, bf16[4,5,1,32,256]{4,3,2,1,0:T(8,128)(2,1)} %copy-done.11, bf16[4,8,7,32,128]{4,3,2,1,0:T(8,128)(2,1)} %bitcast.209), custom_call_target="tpu_custom_call" | custom-call | flops 1811939328 | bytes 4915208 | tf_op jit(solution)/shard_map/pallas_call | solution.py:132
  200.1 5.9 %shard_map.81 = bf16[4,2,1,16,256]{4,3,2,1,0:T(8,128)(2,1)} custom-call(s32[2]{0:T(128)} %pad_add_fusion.here, bf16[3,4,5,3,16,256]{5,4,3,2,1,0:T(8,128)(2,1)} %shard_map.77.ref, bf16[4,8,7,32,256]{4,3,2,1,0:T(8,128)(2,1)} %bitcast.193), custom_call_target="tpu_custom_call" | custom-call | flops 452984832 | bytes 5210120 | tf_op jit(solution)/shard_map/pallas_call | solution.py:132
  208.3 3.6 %all-to-all-start = ((bf16[8,2,2048]{2,1,0:T(2,128)(2,1)}), bf16[8,2,2048]{2,1,0:T(2,128)(2,1)S(1)}, u32[]{:S(2)}, u32[]{:S(2)}) async-start(bf16[8,2,2048]{2,1,0:T(2,128)(2,1)} %reshape.160), calls=%async_computation | async-start | bytes 131072 | tf_op jit(solution)/shard_map/out/all_to_all | solution.py:583
  230.4 5.3 %collective-permute-done.31 = bf16[2,7,32,128]{3,2,1,0:T(8,128)(2,1)S(1)} collective-permute-done((bf16[2,7,32,128]{3,2,1,0:T(8,128)(2,1)S(1)}, bf16[2,7,32,128]{3,2,1,0:T(8,128)(2,1)S(1)}, u32[]{:S(2)}, u32[]{:S(2)}) %collective-permute-start.31) | collective-permute-done | bytes 114720 | tf_op jit(solution)/shard_map/sum_first_z/ppermute | solution.py:44
  235.9 4.1 %collective-permute-done.32 = bf16[1,7,32,128]{3,2,1,0:T(8,128)(2,1)S(1)} collective-permute-done((bf16[1,7,32,128]{3,2,1,0:T(8,128)(2,1)S(1)}, bf16[1,7,32,128]{3,2,1,0:T(8,128)(2,1)S(1)}, u32[]{:S(2)}, u32[]{:S(2)}) %collective-permute-start.32) | collective-permute-done | bytes 57376 | tf_op jit(solution)/shard_map/sum_first_z/ppermute | solution.py:44
  240.1 4.1 %collective-permute-done.33 = bf16[7,32,128]{2,1,0:T(8,128)(2,1)S(1)} collective-permute-done((bf16[7,32,128]{2,1,0:T(8,128)(2,1)S(1)}, bf16[7,32,128]{2,1,0:T(8,128)(2,1)S(1)}, u32[]{:S(2)}, u32[]{:S(2)}) %collective-permute-start.33) | collective-permute-done | bytes 57376 | tf_op jit(solution)/shard_map/sum_first_end/ppermute | solution.py:44
  (184 shorter events, 92.1 us)
Async XLA Ops:
  1.7 36.2 %collective-permute-start = (bf16[4,1,4,64,128]{4,3,2,1,0:T(8,128)(2,1)S(1)}, bf16[4,1,4,64,128]{4,3,2,1,0:T(8,128)(2,1)S(1)}, u32[]{:S(2)}, u32[]{:S(2)}) collective-permute-start(bf16[4,1,4,64,128]{4,3,2,1,0:T(8,128)(2,1)S(1)} %slice.147), channel_id=1, source_target_pairs={{0,8},{1,9},{2,10},{3,11},{4,12},{5,13},{6,14},{7,15},{8,16},{9,17... | collective-permute-start | bytes 786440 | tf_op jit(solution)/shard_map/plane/ppermute | solution.py:39
  9.7 9.3 %collective-permute-start.10 = (bf16[2,2,1,4,2,512]{5,4,3,1,0,2:T(2,128)(2,1)S(1)}, bf16[2,2,1,4,2,512]{5,4,3,1,0,2:T(2,128)(2,1)S(1)}, u32[]{:S(2)}, u32[]{:S(2)}) collective-permute-start(bf16[2,2,1,4,2,512]{5,4,3,1,0,2:T(2,128)(2,1)S(1)} %bitcast.237), channel_id=1, source_target_pairs={{0,4},{1,5},{2,6},{3,7},{4,0},{5,1},{6,2},{7,3},{8,12},{9,13},{10,... | collective-permute-start | bytes 98312 | tf_op jit(solution)/shard_map/cells/ppermute | solution.py:44
  25.1 11.8 %collective-permute-start.5 = (bf16[2,2,2,7,32,128]{5,4,3,2,1,0:T(8,128)(2,1)S(1)}, bf16[2,2,2,7,32,128]{5,4,3,2,1,0:T(8,128)(2,1)S(1)}, u32[]{:S(2)}, u32[]{:S(2)}) collective-permute-start(bf16[2,2,2,7,32,128]{5,4,3,2,1,0:T(8,128)(2,1)S(1)} %get-tuple-element.57), channel_id=1, source_target_pairs={{0,16},{8,24},{16,0},{24,8},{1,17},{9,25},{17,1},{25,9},{2,18},{10... | collective-permute-start | bytes 1376264 | tf_op jit(solution)/shard_map/first_y/ppermute | solution.py:44
  25.3 20.4 %collective-permute-start.12 = (bf16[2,2,1,4,2,512]{5,4,3,1,0,2:T(2,128)(2,1)S(1)}, bf16[2,2,1,4,2,512]{5,4,3,1,0,2:T(2,128)(2,1)S(1)}, u32[]{:S(2)}, u32[]{:S(2)}) collective-permute-start(bf16[2,2,1,4,2,512]{5,4,3,1,0,2:T(2,128)(2,1)S(1)} %fusion.34), channel_id=1, source_target_pairs={{0,1},{1,0},{2,3},{3,2},{4,5},{5,4},{6,7},{7,6},{8,9},{9,8},{10,11... | collective-permute-start | bytes 98312 | tf_op jit(solution)/shard_map/cells/ppermute | solution.py:44
  37.9 38.7 %collective-permute-start.6 = (bf16[2,2,2,2,7,32,128]{6,5,4,3,2,1,0:T(8,128)(2,1)}, bf16[2,2,2,2,7,32,128]{6,5,4,3,2,1,0:T(8,128)(2,1)S(1)}, u32[]{:S(2)}, u32[]{:S(2)}) collective-permute-start(bf16[2,2,2,2,7,32,128]{6,5,4,3,2,1,0:T(8,128)(2,1)} %get-tuple-element.47), channel_id=1, source_target_pairs={{0,8},{8,0},{16,24},{24,16},{1,9},{9,1},{17,25},{25,17},{2,10},{10... | collective-permute-start | bytes 2752520 | tf_op jit(solution)/shard_map/first_core/ppermute | solution.py:44
  38.8 32.3 %collective-permute-start.4 = (bf16[4,9,1,64,128]{4,3,2,1,0:T(8,128)(2,1)}, bf16[4,9,1,64,128]{4,3,2,1,0:T(8,128)(2,1)S(1)}, u32[]{:S(2)}, u32[]{:S(2)}) collective-permute-start(bf16[4,9,1,64,128]{4,3,2,1,0:T(8,128)(2,1)} %pad_maximum_fusion.5), channel_id=1, source_target_pairs={{0,1},{1,2},{2,3},{3,4},{4,5},{5,6},{6,7},{8,9},{9,10},{10,11},{11... | collective-permute-start | bytes 1769480 | tf_op jit(solution)/shard_map/row/ppermute | solution.py:39
  42.3 9.5 %collective-permute-start.16 = (bf16[7,32,256]{2,1,0:T(8,128)(2,1)S(1)}, bf16[7,32,256]{2,1,0:T(8,128)(2,1)S(1)}, u32[]{:S(2)}, u32[]{:S(2)}) collective-permute-start(bf16[7,32,256]{2,1,0:T(8,128)(2,1)S(1)} %pad_dynamic-slice_fusion), channel_id=1, source_target_pairs={{0,4},{1,5},{2,6},{3,7},{4,0},{5,1},{6,2},{7,3},{8,12},{9,13},{10,... | collective-permute-start | bytes 344072 | tf_op jit(solution)/shard_map/second_z/ppermute | solution.py:44
  59.9 37.9 %collective-permute-start.18 = (bf16[2,2,4,32,256]{4,3,2,1,0:T(8,128)(2,1)S(1)}, bf16[2,2,4,32,256]{4,3,2,1,0:T(8,128)(2,1)S(1)}, u32[]{:S(2)}, u32[]{:S(2)}) collective-permute-start(bf16[2,2,4,32,256]{4,3,2,1,0:T(8,128)(2,1)S(1)} %fusion.10), channel_id=1, source_target_pairs={{0,1},{1,0},{2,3},{3,2},{4,5},{5,4},{6,7},{7,6},{8,9},{9,8},{10,11... | collective-permute-start | bytes 786440 | tf_op jit(solution)/shard_map/second_x1/ppermute | solution.py:44
  86.2 13.5 %collective-permute-start.9 = (bf16[4,4,1,32,256]{4,3,2,1,0:T(8,128)(2,1)}, bf16[4,4,1,32,256]{4,3,2,1,0:T(8,128)(2,1)S(1)}, u32[]{:S(2)}, u32[]{:S(2)}) collective-permute-start(bf16[4,4,1,32,256]{4,3,2,1,0:T(8,128)(2,1)} %get-tuple-element.21), channel_id=1, source_target_pairs={{0,1},{1,2},{2,3},{3,4},{4,5},{5,6},{6,7},{8,9},{9,10},{10,11},{11... | collective-permute-start | bytes 786440 | tf_op jit(solution)/shard_map/hidden_halo/ppermute | solution.py:39
  88.1 25.5 %collective-permute-start.21 = (bf16[2,2,3,32,256]{4,3,2,1,0:T(8,128)(2,1)S(1)}, bf16[2,2,3,32,256]{4,3,2,1,0:T(8,128)(2,1)S(1)}, u32[]{:S(2)}, u32[]{:S(2)}) collective-permute-start(bf16[2,2,3,32,256]{4,3,2,1,0:T(8,128)(2,1)S(1)} %pad_maximum_fusion.24), channel_id=1, source_target_pairs={{0,16},{8,24},{16,0},{24,8},{1,17},{9,25},{17,1},{25,9},{2,18},{10... | collective-permute-start | bytes 589832 | tf_op jit(solution)/shard_map/second_y1/ppermute | solution.py:44
  89.4 11.1 %collective-permute-start.7 = (bf16[4,1,2,32,256]{4,3,2,1,0:T(8,128)(2,1)}, bf16[4,1,2,32,256]{4,3,2,1,0:T(8,128)(2,1)S(1)}, u32[]{:S(2)}, u32[]{:S(2)}) collective-permute-start(bf16[4,1,2,32,256]{4,3,2,1,0:T(8,128)(2,1)} %get-tuple-element.20), channel_id=1, source_target_pairs={{0,8},{1,9},{2,10},{3,11},{4,12},{5,13},{6,14},{7,15},{8,16},{9,17... | collective-permute-start | bytes 393224 | tf_op jit(solution)/shard_map/hidden_halo/ppermute | solution.py:39
  97.9 18.3 %collective-permute-start.19 = (bf16[2,2,2,4,32,256]{5,4,3,2,1,0:T(8,128)(2,1)S(1)}, bf16[2,2,2,4,32,256]{5,4,3,2,1,0:T(8,128)(2,1)S(1)}, u32[]{:S(2)}, u32[]{:S(2)}) collective-permute-start(bf16[2,2,2,4,32,256]{5,4,3,2,1,0:T(8,128)(2,1)S(1)} %get-tuple-element.51), channel_id=1, source_target_pairs={{0,16},{8,24},{16,0},{24,8},{1,17},{9,25},{17,1},{25,9},{2,18},{10... | collective-permute-start | bytes 1572872 | tf_op jit(solution)/shard_map/second_y2/ppermute | solution.py:44
  113.6 31.6 %collective-permute-start.15 = (bf16[2,8,7,32,256]{4,3,2,1,0:T(8,128)(2,1)}, bf16[2,8,7,32,256]{4,3,2,1,0:T(8,128)(2,1)}, u32[]{:S(2)}, u32[]{:S(2)}) collective-permute-start(bf16[2,8,7,32,256]{4,3,2,1,0:T(8,128)(2,1)} %get-tuple-element.23), channel_id=1, source_target_pairs={{0,8},{8,0},{16,24},{24,16},{1,9},{9,1},{17,25},{25,17},{2,10},{10... | collective-permute-start | bytes 5505032 | tf_op jit(solution)/shard_map/sum_second_core/ppermute | solution.py:44
  113.7 11.8 %collective-permute-start.22 = (bf16[2,2,2,3,32,256]{5,4,3,2,1,0:T(8,128)(2,1)S(1)}, bf16[2,2,2,3,32,256]{5,4,3,2,1,0:T(8,128)(2,1)S(1)}, u32[]{:S(2)}, u32[]{:S(2)}) collective-permute-start(bf16[2,2,2,3,32,256]{5,4,3,2,1,0:T(8,128)(2,1)S(1)} %get-tuple-element.59), channel_id=1, source_target_pairs={{0,1},{1,0},{2,3},{3,2},{4,5},{5,4},{6,7},{7,6},{8,9},{9,8},{10,11... | collective-permute-start | bytes 1179656 | tf_op jit(solution)/shard_map/second_x2/ppermute | solution.py:44
  116.4 25.6 %collective-permute-start.20 = (bf16[2,2,2,2,4,32,256]{6,5,4,3,2,1,0:T(8,128)(2,1)S(1)}, bf16[2,2,2,2,4,32,256]{6,5,4,3,2,1,0:T(8,128)(2,1)}, u32[]{:S(2)}, u32[]{:S(2)}) collective-permute-start(bf16[2,2,2,2,4,32,256]{6,5,4,3,2,1,0:T(8,128)(2,1)S(1)} %get-tuple-element.45), channel_id=1, source_target_pairs={{0,8},{8,0},{16,24},{24,16},{1,9},{9,1},{17,25},{25,17},{2,10},{10... | collective-permute-start | bytes 3145736 | tf_op jit(solution)/shard_map/second_core/ppermute | solution.py:44
  126.5 14.2 %collective-permute-start.23 = (bf16[2,2,2,2,3,32,256]{6,5,4,3,2,0,1:T(8,128)(2,1)}, bf16[2,2,2,2,3,32,256]{6,5,4,3,2,0,1:T(8,128)(2,1)}, u32[]{:S(2)}, u32[]{:S(2)}) collective-permute-start(bf16[2,2,2,2,3,32,256]{6,5,4,3,2,0,1:T(8,128)(2,1)} %get-tuple-element.49), channel_id=1, source_target_pairs={{0,8},{8,0},{16,24},{24,16},{1,9},{9,1},{17,25},{25,17},{2,10},{10... | collective-permute-start | bytes 2359304 | tf_op jit(solution)/shard_map/second_core/ppermute | solution.py:44
  147.5 23.5 %collective-permute-start.37 = (bf16[2,4,3,32,256]{4,3,2,1,0:T(8,128)(2,1)S(1)}, bf16[2,4,3,32,256]{4,3,2,1,0:T(8,128)(2,1)S(1)}, u32[]{:S(2)}, u32[]{:S(2)}) collective-permute-start(bf16[2,4,3,32,256]{4,3,2,1,0:T(8,128)(2,1)S(1)} %slice_bitcast_fusion.6), channel_id=1, source_target_pairs={{0,1},{1,0},{2,3},{3,2},{4,5},{5,4},{6,7},{7,6},{8,9},{9,8},{10,11... | collective-permute-start | bytes 1179656 | tf_op jit(solution)/shard_map/sum_second_x1/ppermute | solution.py:44
  165.0 32.0 %collective-permute-start.24 = (bf16[2,8,7,32,128]{4,3,2,1,0:T(8,128)(2,1)}, bf16[2,8,7,32,128]{4,3,2,1,0:T(8,128)(2,1)S(1)}, u32[]{:S(2)}, u32[]{:S(2)}) collective-permute-start(bf16[2,8,7,32,128]{4,3,2,1,0:T(8,128)(2,1)} %get-tuple-element.28), channel_id=1, source_target_pairs={{0,8},{8,0},{16,24},{24,16},{1,9},{9,1},{17,25},{25,17},{2,10},{10... | collective-permute-start | bytes 2752520 | tf_op jit(solution)/shard_map/sum_first_core/ppermute | solution.py:44
  167.2 17.6 %collective-permute-start.35 = (bf16[2,4,4,32,256]{4,3,2,1,0:T(8,128)(2,1)S(1)}, bf16[2,4,4,32,256]{4,3,2,1,0:T(8,128)(2,1)S(1)}, u32[]{:S(2)}, u32[]{:S(2)}) collective-permute-start(bf16[2,4,4,32,256]{4,3,2,1,0:T(8,128)(2,1)S(1)} %slice_bitcast_fusion.3), channel_id=1, source_target_pairs={{0,16},{8,24},{16,0},{24,8},{1,17},{9,25},{17,1},{25,9},{2,18},{10... | collective-permute-start | bytes 1572872 | tf_op jit(solution)/shard_map/sum_second_y1/ppermute | solution.py:44
  169.6 15.9 %collective-permute-start.26 = (bf16[4,5,1,32,256]{4,3,2,1,0:T(8,128)(2,1)S(1)}, bf16[4,5,1,32,256]{4,3,2,1,0:T(8,128)(2,1)S(1)}, u32[]{:S(2)}, u32[]{:S(2)}) collective-permute-start(bf16[4,5,1,32,256]{4,3,2,1,0:T(8,128)(2,1)S(1)} %pad_maximum_fusion.15), channel_id=1, source_target_pairs={{1,0},{2,1},{3,2},{4,3},{5,4},{6,5},{7,6},{9,8},{10,9},{11,10},{12... | collective-permute-start | bytes 983048 | tf_op jit(solution)/shard_map/back_row/ppermute | solution.py:39
  171.2 21.5 %collective-permute-start.38 = (bf16[4,3,32,256]{3,2,1,0:T(8,128)(2,1)S(1)}, bf16[4,3,32,256]{3,2,1,0:T(8,128)(2,1)S(1)}, u32[]{:S(2)}, u32[]{:S(2)}) collective-permute-start(bf16[4,3,32,256]{3,2,1,0:T(8,128)(2,1)S(1)} %fusion.18), channel_id=1, source_target_pairs={{0,16},{8,24},{16,0},{24,8},{1,17},{9,25},{17,1},{25,9},{2,18},{10... | collective-permute-start | bytes 589832 | tf_op jit(solution)/shard_map/sum_second_y2/ppermute | solution.py:44
  193.6 21.1 %collective-permute-start.39 = (bf16[2,7,32,256]{3,2,1,0:T(8,128)(2,1)}, bf16[2,7,32,256]{3,2,1,0:T(8,128)(2,1)}, u32[]{:S(2)}, u32[]{:S(2)}) collective-permute-start(bf16[2,7,32,256]{3,2,1,0:T(8,128)(2,1)} %fusion.6), channel_id=1, source_target_pairs={{0,4},{1,5},{2,6},{3,7},{4,0},{5,1},{6,2},{7,3},{8,12},{9,13},{10,... | collective-permute-start | bytes 688136 | tf_op jit(solution)/shard_map/sum_second_z/ppermute | solution.py:44
  208.3 10.5 %all-to-all-start = ((bf16[8,2,2048]{2,1,0:T(2,128)(2,1)}), bf16[8,2,2048]{2,1,0:T(2,128)(2,1)S(1)}, u32[]{:S(2)}, u32[]{:S(2)}) async-start(bf16[8,2,2048]{2,1,0:T(2,128)(2,1)} %reshape.160), calls=%async_computation | async-start | bytes 131072 | tf_op jit(solution)/shard_map/out/all_to_all | solution.py:583
  211.9 11.6 %collective-permute-start.27 = (bf16[2,4,4,32,128]{4,3,2,1,0:T(8,128)(2,1)}, bf16[2,4,4,32,128]{4,3,2,1,0:T(8,128)(2,1)S(1)}, u32[]{:S(2)}, u32[]{:S(2)}) collective-permute-start(bf16[2,4,4,32,128]{4,3,2,1,0:T(8,128)(2,1)} %slice_bitcast_fusion.9), channel_id=1, source_target_pairs={{0,16},{8,24},{16,0},{24,8},{1,17},{9,25},{17,1},{25,9},{2,18},{10... | collective-permute-start | bytes 786440 | tf_op jit(solution)/shard_map/sum_first_y1/ppermute | solution.py:44
  (33 other events, 226.3 us)

commit v2 on v1

--- a/solution.py
+++ b/solution.py
@@ -6,6 +6,7 @@
 from jax.experimental import pallas as pl
 from jax.experimental.pallas import tpu as pltpu
 from jax.sharding import PartitionSpec as P
+
 
 BF16 = jnp.bfloat16
 F32 = jnp.float32
@@ -22,10 +23,6 @@
 
 def bits(axis):
     return lax.axis_size(axis).bit_length() - 1
-
-
-def chan_sum_order():
-    return [0] + [bit for bit in reversed(range(bits("chan"))) if bit]
 
 
 def shifted(value, steps):
@@ -44,9 +41,8 @@
     return lax.ppermute(value, axis, [(i, i ^ (1 << bit)) for i in range(count)])
 
 
-def doubled(value, axis, bit, name):
-    with jax.named_scope(name):
-        other = swapped(value, axis, bit)
+def doubled(value, axis, bit):
+    other = swapped(value, axis, bit)
     return jnp.stack([value, other])
 
 
@@ -72,34 +68,21 @@
     return list(reversed(range(1, bits("space"))))
 
 
-def after(value, other):
-    return lax.optimization_barrier((value, other))[0]
-
-
-def finish_gather(part, name, gate=None):
-    each, mine, inputs = part.shape[-3:]
-    for bit in high_bits():
-        part = doubled(part, "space", bit, f"{name}_y")
-    part = doubled(part, "space", 0, f"{name}_core")
-    return part.reshape(lax.axis_size("space"), lax.axis_size("chan"), each, mine, inputs)
-
-
-def mixed_gather(part, name):
+def mixed_gather(part):
     each, mine, inputs = part.shape
     for bit in far_bits():
-        part = doubled(part, "chan", bit, f"{name}_z")
-    far = part.shape[:-3]
+        part = doubled(part, "chan", bit)
     highs = len(high_bits())
     cut = (each + 1) // 2
     one, two = part[..., :cut, :, :], part[..., cut:, :, :]
-    one = doubled(one, "chan", 0, f"{name}_x1")
+    one = doubled(one, "chan", 0)
     for bit in high_bits():
-        two = doubled(two, "space", bit, f"{name}_y1")
+        two = doubled(two, "space", bit)
     for bit in high_bits():
-        one = doubled(one, "space", bit, f"{name}_y2")
-    two = doubled(two, "chan", 0, f"{name}_x2")
-    one = doubled(one, "space", 0, f"{name}_core")
-    two = doubled(two, "space", 0, f"{name}_core")
+        one = doubled(one, "space", bit)
+    two = doubled(two, "chan", 0)
+    one = doubled(one, "space", 0)
+    two = doubled(two, "space", 0)
     two = jnp.moveaxis(two, 1, 1 + highs)
     whole = jnp.concatenate([one, two], axis=-3)
     return whole.reshape(lax.axis_size("space"), lax.axis_size("chan"), each, mine, inputs)
@@ -152,196 +135,189 @@
             store(k, part, piece.astype(BF16))
 
 
-def part_kernel(own, plane, row, out, wide):
-    _, wide_a, wide_b, depth, _ = (1, out.shape[2], out.shape[3], own.shape[3], own.shape[4])
+def part_kernel(pick, shape, wide, out_of):
+    wide_a, wide_b, depth = shape
     for a in range(wide_a):
         for b in range(wide_b):
-            if b == 0:
-                tile = row[0, a, 0]
-            elif a == 0:
-                tile = plane[0, 0, b - 1]
-            else:
-                tile = own[0, a - 1, b - 1]
             slot = ((a * wide_b + b) % 8) * (PAD + depth)
 
             def store(k, part, piece):
-                out[k, 0, a, b, :, part * LANES : (part + 1) * LANES] = piece
-
-            parted_tile(tile, wide, slot, store)
-
-
-def parted(own, plane, row):
-    vols, side_a, side_b, depth, lanes = own.shape
-    out = jax.ShapeDtypeStruct((3, vols, side_a + 1, side_b + 1, depth // 2, lanes), BF16)
+                out_of[k, 0, a, b, :, part * LANES : (part + 1) * LANES] = piece
+
+            parted_tile(pick(a, b), wide, slot, store)
+
+
+def parted(blocks, shape, picker):
+    vols, wide_a, wide_b, depth, lanes = shape
+    out = jax.ShapeDtypeStruct((3, vols, wide_a, wide_b, depth // 2, lanes), BF16)
+
+    def kernel(*refs):
+        *ins, out_ref, wide = refs
+        part_kernel(picker(ins), (wide_a, wide_b, depth), wide, out_ref)
 
     def block(shape):
         return pl.BlockSpec((1,) + shape[1:], lambda n: (n, 0, 0, 0, 0))
 
     return call(
-        part_kernel,
+        kernel,
         [out],
-        (own, plane, row),
+        blocks,
         [pltpu.VMEM((lanes // LANES, 8 * (PAD + depth), LANES), F32)],
         (vols,),
-        [block(own.shape), block(plane.shape), block(row.shape)],
+        [block(b.shape) for b in blocks],
         [pl.BlockSpec((3, 1) + out.shape[2:], lambda n: (0, n, 0, 0, 0, 0))],
     )[0]
 
 
-def window(ref, i, j, sides):
-    vols, side_a, side_b = sides
+def window(refs, i, j, sides):
+    vols, side_a, cells_b = sides
     rows = []
     for n in range(vols):
         for a in range(side_a):
-            for b in range(side_b):
-                rows.append(
-                    jnp.concatenate([ref[k, n, 2 * a + i, 2 * b + j] for k in range(3)], axis=1)
-                )
+            for b in cells_b:
+                y = 2 * b + j
+                ref = refs[0]
+                if len(refs) == 2:
+                    ref, y = (refs[1], 0) if y == 0 else (refs[0], y - 1)
+                assert 0 <= y < ref.shape[3]
+                rows.append(jnp.concatenate([ref[k, n, 2 * a + i, y] for k in range(3)], axis=1))
     return jnp.concatenate(rows, axis=0)
 
 
-def forward_kernel(orders, sides, here, ref, filters, *rest):
-    outs, acc = rest[:-1], rest[-1]
-
-    def step(ij, carry):
-        i, j = ij // 3, ij % 3
-        left = window(ref, i, j, sides)
-        right = jnp.concatenate(
-            [filter_tap(filters, here, ij * 3 + k, orders) for k in range(3)], axis=1
-        )
-        part = dot(left, right, NT)
-        acc[...] = jnp.where(ij == 0, part, acc[...] + part)
+def forward_kernel(orders, sides, act, split, here, filters, *rest):
+    *refs, out, acc = rest
+    if split and len(refs) == 1:
+        refs.append(None)
+    acc[...] = jnp.zeros_like(acc)
+
+    def step(i, carry):
+        for j in range(3):
+            right = jnp.concatenate(
+                [filter_tap(filters, here, i * 9 + j * 3 + k, orders) for k in range(3)], axis=1
+            )
+            acc[...] += dot(window(refs, i, j, sides), right, NT)
         return carry
 
-    lax.fori_loop(0, 9, step, 0)
+    lax.fori_loop(0, 3, step, 0)
     total = acc[...]
-    depth = ref.shape[4]
-    vols, side_a, side_b = sides
-    if len(outs) == 1:
-        outs[0][...] = total.astype(BF16).reshape(outs[0].shape)
-        return
-    hidden, plane, row = outs
-    act = jnp.where(total > 0, total, 0.3 * total).astype(BF16)
-    act = act.reshape(vols, side_a, side_b, depth, total.shape[1])
-    hidden[...] = act
-    plane[...] = act[:, side_a - 1 :]
-    row[...] = act[:, :, side_b - 1 :]
-
-
-def forward(here, ref, filters, orders, split):
-    _, vols, wide_a, wide_b, depth, inputs = ref.shape
-    sides = (vols, (wide_a - 1) // 2, (wide_b - 1) // 2)
+    if act:
+        total = jnp.where(total > 0, total, 0.3 * total)
+    out[...] = total.astype(BF16).reshape(out.shape)
+
+
+def forward(here, refs, filters, orders, cells_b, act):
+    _, vols, wide_a, _, depth, inputs = refs[0].shape
+    sides = (vols, (wide_a - 1) // 2, cells_b)
     count = filters.shape[1] * filters.shape[3]
-    cells = vols * sides[1] * sides[2] * depth
-    shape = sides + (depth, count)
-    outs = [jax.ShapeDtypeStruct(shape, BF16)]
-    if split:
-        outs.append(jax.ShapeDtypeStruct((vols, 1) + shape[2:], BF16))
-        outs.append(jax.ShapeDtypeStruct(shape[:2] + (1,) + shape[3:], BF16))
+    cells = vols * sides[1] * len(cells_b) * depth
+    out = jax.ShapeDtypeStruct((vols, sides[1], len(cells_b), depth, count), BF16)
     return call(
-        functools.partial(forward_kernel, orders, sides),
-        outs,
-        (here, ref, filters),
+        functools.partial(forward_kernel, orders, sides, act, len(refs) == 2),
+        [out],
+        (here, filters, *(r for r in refs if r is not None)),
         [pltpu.VMEM((cells, count), F32)],
         flops=2 * cells * 27 * inputs * count,
-    )
-
-
-def grads_kernel(orders, sides, here, ref, grads, keep, send, turned):
+    )[0]
+
+
+def grads_kernel(orders, sides, here, grads, *rest):
+    *refs, keep, send, turned = rest
     cells, count = turned.shape[1], turned.shape[0]
-    inputs = ref.shape[5]
+    inputs = refs[0].shape[5]
     chans = 2 ** len(orders[1])
     mine = count // chans
     each = keep.shape[2]
+    half = keep.shape[0]
     turned[...] = jnp.transpose(grads[...].reshape(cells, count).astype(F32), (1, 0)).astype(BF16)
 
-    def step(ij, carry):
-        part = dot(turned[...], window(ref, ij // 3, ij % 3, sides), NN).astype(BF16)
-        for k in range(3):
-            tap = ij * 3 + k
-            place = relative(tap // each, here[0], orders[0])
-            half = keep.shape[0]
-            for chan in range(chans):
-                block = part[chan * mine : (chan + 1) * mine, k * inputs : (k + 1) * inputs]
-                to = relative(chan, here[1], orders[1])
+    def put(ref, place, tap, part):
+        for chan in range(chans):
+            to = relative(chan, here[1], orders[1])
+            ref[place, to, tap % each] = part[chan * mine : (chan + 1) * mine]
+
+    def step(i, carry):
+        for j in range(3):
+            part = dot(turned[...], window(refs, i, j, sides), NN).astype(BF16)
+            for k in range(3):
+                tap = i * 9 + j * 3 + k
+                place = relative(tap // each, here[0], orders[0])
+                piece = part[:, k * inputs : (k + 1) * inputs]
 
                 @pl.when(place < half)
                 def _():
-                    keep[place, to, tap % each] = block
+                    put(keep, place, tap, piece)
 
                 @pl.when(place >= half)
                 def _():
-                    send[place - half, to, tap % each] = block
+                    put(send, place - half, tap, piece)
 
         return carry
 
-    lax.fori_loop(0, 9, step, 0)
-    for tap in range(27, each * 2 * keep.shape[0]):
+    lax.fori_loop(0, 3, step, 0)
+    for tap in range(27, each * 2 * half):
         place = relative(tap // each, here[0], orders[0])
         blank = jnp.zeros((chans, mine, inputs), BF16)
 
-        @pl.when(place < keep.shape[0])
+        @pl.when(place < half)
         def _():
             keep[place, :, tap % each] = blank
 
-        @pl.when(place >= keep.shape[0])
+        @pl.when(place >= half)
         def _():
-            send[place - keep.shape[0], :, tap % each] = blank
-
-
-def filter_grads(here, ref, grads, orders):
-    _, vols, wide_a, wide_b, depth, inputs = ref.shape
-    sides = (vols, (wide_a - 1) // 2, (wide_b - 1) // 2)
-    cells = vols * sides[1] * sides[2] * depth
-    count = grads.shape[-1]
+            send[place - half, :, tap % each] = blank
+
+
+def filter_grads(here, refs, grads, orders):
+    inputs = refs[0].shape[5]
+    vols, side_a, side_b, depth, count = grads.shape
+    sides = (vols, side_a, range(side_b))
+    cells = vols * side_a * side_b * depth
     space, chans = 2 ** len(orders[0]), 2 ** len(orders[1])
     each = -(-27 // space)
     out = jax.ShapeDtypeStruct((space // 2, chans, each, count // chans, inputs), BF16)
     return call(
         functools.partial(grads_kernel, orders, sides),
         [out, out],
-        (here, ref, grads),
+        (here, grads, *refs),
         [pltpu.VMEM((count, cells), BF16)],
         flops=2 * cells * 27 * inputs * count,
     )
 
 
-def core_sum(keep, send, name):
+def core_sum(keep, send):
     tail = keep.shape[2:]
-    with jax.named_scope(f"{name}_core"):
-        other = swapped(send, "space", 0)
+    other = swapped(send, "space", 0)
     total = keep.astype(F32) + other.astype(F32)
     highs = bits("space") - 1
     return total.reshape((2,) * highs + (2, -1) + tail)
 
 
-def half_sum(value, axis, bit, dim, name):
+def half_sum(value, axis, bit, dim):
     keep = lax.index_in_dim(value, 0, dim, keepdims=False)
     send = lax.index_in_dim(value, 1, dim, keepdims=False)
-    with jax.named_scope(name):
-        other = swapped(send.astype(BF16), axis, bit)
+    other = swapped(send.astype(BF16), axis, bit)
     return keep.astype(F32) + other.astype(F32)
 
 
-def sum_filters(total, name):
+def sum_filters(total):
     each, mine, inputs = total.shape[-3:]
     highs = list(range(1, bits("space")))
     cut = (each + 1) // 2
     one, two = total[..., :cut, :, :], total[..., cut:, :, :]
-    two = half_sum(two, "chan", 0, len(highs), f"{name}_x1")
+    two = half_sum(two, "chan", 0, len(highs))
     for bit in highs:
-        one = half_sum(one, "space", bit, 0, f"{name}_y1")
-    one = half_sum(one, "chan", 0, 0, f"{name}_x2")
+        one = half_sum(one, "space", bit, 0)
+    one = half_sum(one, "chan", 0, 0)
     for bit in highs:
-        two = half_sum(two, "space", bit, 0, f"{name}_y2")
+        two = half_sum(two, "space", bit, 0)
     part = jnp.concatenate([one, two], axis=-3)
     for bit in far_bits():
         part = part.reshape((2, -1, each, mine, inputs))
-        part = half_sum(part, "chan", bit, 0, f"{name}_z")
+        part = half_sum(part, "chan", bit, 0)
     part = part.reshape(each, mine, inputs).astype(BF16)
     for bit in high_bits():
-        part = doubled(part, "space", bit, f"{name}_end")
-    part = doubled(part, "space", 0, f"{name}_end")
+        part = doubled(part, "space", bit)
+    part = doubled(part, "space", 0)
     space = lax.axis_size("space")
     part = part.reshape(space, each, mine, inputs)
     places = jnp.arange(space) ^ lax.axis_index("space")
@@ -366,7 +342,7 @@
         store(part, rows[pl.ds(base + 1, depth), :].astype(BF16))
 
 
-def back_kernel(orders, here, cells, filters, hidden, out, plane, row, wide, moved, spread):
+def back_kernel(orders, here, cells, filters, low, high, out, plane, row, wide, moved, spread):
     vols, wide_a, wide_b, depth, count = cells.shape
     side_a, side_b = wide_a - 1, wide_b - 1
     inputs = filters.shape[4]
@@ -406,17 +382,18 @@
                                 ] = value[n, a, b, :, part * LANES : (part + 1) * LANES]
     for part in range(inputs // LANES):
         lanes = slice(part * LANES, (part + 1) * LANES)
-        act = hidden[:, :, :, :, lanes].astype(F32)
+        act = jnp.concatenate([low[:, :, :, :, lanes], high[:, :, :, :, lanes]], axis=2)
+        act = act.astype(F32)
         value = (spread[part] * jnp.where(act > 0, 1.0, 0.3)).astype(BF16)
         out[:, :, :, :, lanes] = value
         plane[:, :, :, :, lanes] = value[:, :1]
         row[:, :, :, :, lanes] = value[:, :, :1]
 
 
-def hidden_back(here, cells, filters, hidden, orders):
+def hidden_back(here, cells, filters, low, high, orders):
     vols, wide_a, wide_b, depth, count = cells.shape
-    inputs = hidden.shape[-1]
-    shape = hidden.shape
+    inputs = low.shape[-1]
+    shape = low.shape[:2] + (low.shape[2] + high.shape[2],) + low.shape[3:]
     outs = [
         jax.ShapeDtypeStruct(shape, BF16),
         jax.ShapeDtypeStruct((vols, 1) + shape[2:], BF16),
@@ -425,7 +402,7 @@
     return call(
         functools.partial(back_kernel, orders),
         outs,
-        (here, cells, filters, hidden),
+        (here, cells, filters, low, high),
         [
             pltpu.VMEM((count // LANES, 8 * (PAD + depth), LANES), F32),
             pltpu.VMEM(cells.shape, BF16),
@@ -518,29 +495,55 @@
         flat = cotangent.reshape(vols, side_a, side_b, side_c * mine)
         flat = jnp.transpose(flat, (2, 0, 1, 3))
         self.value = flat.reshape((2,) * self.count + (-1,) + flat.shape[1:])
-
-    def stage(self, step):
-        bit = self.count - 1 - step
+        self.open = list(reversed(range(self.count)))
+        self.done = []
+
+    def stage(self, bit):
+        dim = self.open.index(bit)
         mine = (lax.axis_index("chan") >> bit) & 1
-        keep = lax.dynamic_index_in_dim(self.value, mine, 0, keepdims=False)
-        send = lax.dynamic_index_in_dim(self.value, 1 - mine, 0, keepdims=False)
-        with jax.named_scope("cells"):
-            other = swapped(send, "chan", bit)
+        keep = lax.dynamic_index_in_dim(self.value, mine, dim, keepdims=False)
+        send = lax.dynamic_index_in_dim(self.value, 1 - mine, dim, keepdims=False)
+        other = swapped(send, "chan", bit)
         low, high = jnp.where(mine == 1, other, keep), jnp.where(mine == 1, keep, other)
         self.value = jnp.stack([low, high], axis=self.count - 1)
+        self.open.remove(bit)
+        self.done.append(bit)
 
     def finish(self):
         rows, vols, side_a, side_c, mine = self.tail
-        chan = 2**self.count
-        value = self.value.reshape((chan, rows, vols, side_a, side_c, mine))
-        value = jnp.transpose(value, (2, 3, 1, 4, 0, 5))
-        own = value.reshape(vols, side_a, rows, side_c, chan * mine)
-        with jax.named_scope("cells_row"):
-            row = shifted(own[:, :, :1], (0, -1))
+        count = self.count
+        value = self.value.reshape((2,) * count + (rows, vols, side_a, side_c, mine))
+        sources = [self.done.index(bit) for bit in reversed(range(count))]
+        value = jnp.transpose(
+            value, (count + 1, count + 2, count, count + 3, *sources, count + 4)
+        )
+        own = value.reshape(vols, side_a, rows, side_c, 2**count * mine)
+        row = shifted(own[:, :, :1], (0, -1))
         near = jnp.concatenate([own, row], axis=2)
-        with jax.named_scope("cells_plane"):
-            plane = shifted(near[:, :1], (-1, 0))
+        plane = shifted(near[:, :1], (-1, 0))
         return own, jnp.concatenate([near, plane], axis=1)
+
+
+def volume_picker(refs):
+    own, plane = refs
+    return lambda a, b: plane[0, 0, b] if a == 0 else own[0, a - 1, b]
+
+
+def row_picker(refs):
+    return lambda a, b: refs[0][0, a, 0]
+
+
+def hidden_picker(refs):
+    low, high, plane, row, corner = refs
+
+    def pick(a, b):
+        if b == 0:
+            return corner[0, 0, 0] if a == 0 else row[0, a - 1, 0]
+        if a == 0:
+            return plane[0, 0, b - 1]
+        return low[0, a - 1, 0] if b == 1 else high[0, a - 1, b - 2]
+
+    return pick
 
 
 def local(volume, w_first, w_second, cotangent):
@@ -548,39 +551,51 @@
     far = list(range(1, bits("chan")))
     gathered = (list(range(bits("space"))), [0] + far)
     summed = (list(range(bits("space"))), [0] + far[::-1])
+    vols, side_x, side_y, depth, inputs = volume.shape
+    side_b = side_y // 2
+
     cells = CellExchange(cotangent)
-    with jax.named_scope("plane"):
-        plane = shifted(volume[:, -1:], (1, 0))
+    plane = shifted(volume[:, -1:], (1, 0))
     part = own_part(w_first)
-    for step, bit in enumerate(far_bits() + [0]):
-        part = doubled(part, "chan", bit, "first_zx")
-        cells.stage(step)
+    for bit in far_bits():
+        part = doubled(part, "chan", bit)
+    part = doubled(part, "chan", 0)
+    for bit in high_bits():
+        part = doubled(part, "space", bit)
+    part = doubled(part, "space", 0)
+    first_full = part.reshape(lax.axis_size("space"), lax.axis_size("chan"), *part.shape[-3:])
+    for bit in [0] + far_bits():
+        cells.stage(bit)
+    grad_cells, grad_ext = cells.finish()
     row = jnp.concatenate([plane, volume], axis=1)[:, :, -1:]
-    with jax.named_scope("row"):
-        row = shifted(after(row, part), (0, 1))
-    first_full = finish_gather(part, "first")
-    second_full = mixed_gather(after(own_part(w_second), part), "second")
-    grad_cells, grad_ext = cells.finish()
-    vol_parts = parted(volume, plane, row)
-    hidden, hid_plane, hid_row = forward(here, vol_parts, first_full, gathered, True)
-    with jax.named_scope("hidden_halo"):
-        row = shifted(hid_row, (0, 1))
-        plane = shifted(hid_plane, (1, 0))
-        corner = shifted(hid_row[:, -1:], (1, 1))
-    act_parts = parted(hidden, plane, jnp.concatenate([corner, row], axis=1))
-    second_terms = core_sum(*filter_grads(here, act_parts, grad_cells, summed), "sum_second")
-    second_grad = sum_filters(second_terms, "sum_second")
-    grad_ext = after(grad_ext, second_terms)
-    pre_back, pre_plane, pre_row = hidden_back(here, grad_ext, second_full, hidden, gathered)
-    first_terms = core_sum(*filter_grads(here, vol_parts, pre_back, summed), "sum_first")
-    first_grad = sum_filters(first_terms, "sum_first")
-    with jax.named_scope("back_plane"):
-        plane = shifted(pre_plane, (-1, 0))
-    with jax.named_scope("back_row"):
-        row = shifted(jnp.concatenate([pre_row, plane[:, :, :1]], axis=1), (0, -1))
-    local_out = forward(here, after(act_parts, first_terms), second_full, gathered, False)[0]
-    with jax.named_scope("out"):
-        second_out = lax.all_to_all(local_out, "chan", split_axis=4, concat_axis=2, tiled=True)
+    row = shifted(row, (0, 1))
+    second_full = mixed_gather(own_part(w_second))
+
+    wide = (vols, side_x + 1, side_y, depth, inputs)
+    vol_main = parted((volume, plane), wide, volume_picker)
+    high = forward(here, (vol_main, None), first_full, gathered, range(1, side_b), True)
+    hid_row = shifted(high[:, :, -1:], (0, 1))
+    hid_corner = shifted(high[:, -1:, -1:], (1, 1))
+    vol_row = parted((row,), wide[:2] + (1, depth, inputs), row_picker)
+    vol_parts = (vol_main, vol_row)
+    low = forward(here, vol_parts, first_full, gathered, range(1), True)
+    hid_plane = jnp.concatenate([low[:, -1:], high[:, -1:]], axis=2)
+    hid_plane = shifted(hid_plane, (1, 0))
+    shape = (vols, side_x // 2 + 1, side_b + 1) + low.shape[3:]
+    act_blocks = (low, high, hid_plane, hid_row, hid_corner)
+    act_parts = (parted(act_blocks, shape, hidden_picker),)
+    second_terms = core_sum(*filter_grads(here, act_parts, grad_cells, summed))
+    second_grad = sum_filters(second_terms)
+
+    pre_back, pre_plane, pre_row = hidden_back(here, grad_ext, second_full, low, high, gathered)
+    first_terms = core_sum(*filter_grads(here, vol_parts, pre_back, summed))
+    first_grad = sum_filters(first_terms)
+    plane = shifted(pre_plane, (-1, 0))
+    row = jnp.concatenate([pre_row, plane[:, :, :1]], axis=1)
+    row = shifted(row, (0, -1))
+    out_b = (shape[2] - 1) // 2
+    local_out = forward(here, act_parts, second_full, gathered, range(out_b), False)
+    second_out = lax.all_to_all(local_out, "chan", split_axis=4, concat_axis=2, tiled=True)
     volume_grad = volume_grads(here, pre_back, plane, row, first_full, gathered)
     return (second_out, volume_grad, first_grad, second_grad)
 

time: 248 us -> 239 us (0.964)
  waiting for transfers between devices: 74.5 us -> 62.3 us
  starting transfers between devices: 76 us -> 79.6 us
    ppermute x34, waiting for transfers between devices: 66.1 us -> 48.4 us  [swapped(): return lax.ppermute(value, axis, [(i, i ^ 1 << bit) for i in range(count)])]
    ppermute x9, starting transfers between devices: 21.6 us -> 29.9 us  [shifted(): return lax.ppermute(value, ('space', 'chan'), pairs)]
    ppermute x9, waiting for transfers between devices: 6.81 us -> 13.9 us  [shifted(): return lax.ppermute(value, ('space', 'chan'), pairs)]
    another operation x18, other arithmetic: 4.71 us -> 10.6 us  [doubled(): return jnp.stack([value, other])]
    ppermute x34, starting transfers between devices: 50.8 us -> 45.8 us  [swapped(): return lax.ppermute(value, axis, [(i, i ^ 1 << bit) for i in range(count)])]
    add x2, other arithmetic: 3.7 us -> 1.02 us  [core_sum(): total = keep.astype(F32) + other.astype(F32)]
    pallas_call x8 -> x10, Pallas kernels: 52.6 us -> 53.5 us  [call(): pl.pallas_call(kernel, out_shape=outs, grid=grid or (), in_specs=specs, o...]
  transfers between devices with their start and end apart: 44 -> 44, of which waited for: 16 -> 20; matrix products, arithmetic and copies ran while one was open for 12% -> 12% of each run, Pallas kernels for 21% -> 17%
where the time goes in v2:
time: 239 us; the launch traced here: 238 us
  starting transfers between devices  79.6 us (33%)
  waiting for transfers between devices  62.3 us (26%)
  Pallas kernels  53.5 us (22%)
  other arithmetic  22.6 us (9%)
  local copies, waits for them, and re-layouts  13.1 us (5%)
  between operations  6.34 us (3%)
    pallas_call x10, Pallas kernels, call(): pl.pallas_call(kernel, out_shape=outs, grid=grid or (), in_specs=specs, o...  53.5 us
    ppermute x34, waiting for transfers between devices, swapped(): return lax.ppermute(value, axis, [(i, i ^ 1 << bit) for i in range(count)])  48.4 us
    ppermute x34, starting transfers between devices, swapped(): return lax.ppermute(value, axis, [(i, i ^ 1 << bit) for i in range(count)])  45.8 us
    ppermute x9, starting transfers between devices, shifted(): return lax.ppermute(value, ('space', 'chan'), pairs)  29.9 us
    ppermute x9, waiting for transfers between devices, shifted(): return lax.ppermute(value, ('space', 'chan'), pairs)  13.9 us
    another operation x18, other arithmetic, doubled(): return jnp.stack([value, other])  10.6 us
  transfers between devices with their start and end apart: 44, of which 20 were waited for; matrix products, arithmetic and copies ran while one was open for 12% of the time, Pallas kernels for 17%

profile of v2, /device:TPU:0, one launch (start us, length us, event | category | flops | bytes accessed | tf_op | source)
XLA Modules:
  0.0 237.5 jit_solution(3307305838444229290)
XLA Ops:
  1.6 4.1 %collective-permute-start = (bf16[7,32,256]{2,1,0:T(8,128)(2,1)S(1)}, bf16[7,32,256]{2,1,0:T(8,128)(2,1)S(1)}, u32[]{:S(2)}, u32[]{:S(2)}) collective-permute-start(bf16[7,32,256]{2,1,0:T(8,128)(2,1)S(1)} %pad_dynamic-slice_fusion), channel_id=1, source_target_pairs={{0,4},{1,5},{2,6},{3,7},{4,0},{5,1},{6,2},{7,3},{8,12},{9,13},{10,... | collective-permute-start | bytes 344072 | tf_op jit(solution)/shard_map/ppermute | solution.py:41
  33.1 4.0 %collective-permute-done.5 = bf16[2,2,3,32,256]{4,3,2,1,0:T(8,128)(2,1)S(1)} collective-permute-done((bf16[2,2,3,32,256]{4,3,2,1,0:T(8,128)(2,1)S(1)}, bf16[2,2,3,32,256]{4,3,2,1,0:T(8,128)(2,1)S(1)}, u32[]{:S(2)}, u32[]{:S(2)}) %collective-permute-start.5) | collective-permute-done | bytes 196640 | tf_op jit(solution)/shard_map/ppermute | solution.py:41
  42.1 4.9 %collective-permute-done.11 = bf16[2,2,2,7,32,128]{5,4,3,2,1,0:T(8,128)(2,1)S(1)} collective-permute-done((bf16[2,2,2,7,32,128]{5,4,3,2,1,0:T(8,128)(2,1)S(1)}, bf16[2,2,2,7,32,128]{5,4,3,2,1,0:T(8,128)(2,1)S(1)}, u32[]{:S(2)}, u32[]{:S(2)}) %collective-permute-start.11) | collective-permute-done | bytes 458784 | tf_op jit(solution)/shard_map/ppermute | solution.py:41
  52.7 4.4 %collective-permute-start.14 = (bf16[4,9,1,64,128]{4,3,2,1,0:T(8,128)(2,1)}, bf16[4,9,1,64,128]{4,3,2,1,0:T(8,128)(2,1)}, u32[]{:S(2)}, u32[]{:S(2)}) collective-permute-start(bf16[4,9,1,64,128]{4,3,2,1,0:T(8,128)(2,1)} %pad_maximum_fusion.5), channel_id=1, source_target_pairs={{0,1},{1,2},{2,3},{3,4},{4,5},{5,6},{6,7},{8,9},{9,10},{10,11},{11... | collective-permute-start | bytes 1769480 | tf_op jit(solution)/shard_map/ppermute | solution.py:36
  61.1 5.1 %collective-permute-done.21 = bf16[4,2,1,16,256]{4,3,2,1,0:T(8,128)(2,1)S(1)} collective-permute-done((bf16[4,2,1,16,256]{4,3,2,1,0:T(8,128)(2,1)S(1)}, bf16[4,2,1,16,256]{4,3,2,1,0:T(8,128)(2,1)S(1)}, u32[]{:S(2)}, u32[]{:S(2)}) %collective-permute-start.21) | collective-permute-done | bytes 65568 | tf_op jit(solution)/shard_map/ppermute | solution.py:36
  70.0 4.3 %shard_map.75.rest_0_ = bf16[3,4,9,4,32,128]{5,4,3,2,1,0:T(8,128)(2,1)} custom-call(bf16[4,8,4,64,128]{4,3,2,1,0:T(8,128)(2,1)} %refs_0_.1, bf16[4,1,4,64,128]{4,3,2,1,0:T(8,128)(2,1)} %collective-permute-done.13.refs_1_), custom_call_target="tpu_custom_call" | custom-call | bytes 5898240 | tf_op jit(solution)/shard_map/pallas_call | solution.py:115
  74.4 3.4 %shard_map.76.rest_1_ = bf16[3,4,9,1,32,128]{5,4,3,2,1,0:T(8,128)(2,1)} custom-call(bf16[4,9,1,64,128]{4,3,2,1,0:T(8,128)(2,1)} %collective-permute-done.14.refs_0_), custom_call_target="tpu_custom_call" | custom-call | bytes 1474560 | tf_op jit(solution)/shard_map/pallas_call | solution.py:115
  81.7 5.2 %shard_map.78.refs_1_.high = bf16[4,4,1,32,256]{4,3,2,1,0:T(8,128)(2,1)} custom-call(s32[2]{0:T(128)} %pad_add_fusion.here, bf16[4,8,7,32,128]{4,3,2,1,0:T(8,128)(2,1)} %bitcast.187, bf16[3,4,9,4,32,128]{5,4,3,2,1,0:T(8,128)(2,1)} %shard_map.75.rest_0_), custom_call_target="tpu_custom_call" | custom-call | flops 905969664 | bytes 5636104 | tf_op jit(solution)/shard_map/pallas_call | solution.py:115
  86.9 5.5 %shard_map.77.refs_0_.low = bf16[4,4,1,32,256]{4,3,2,1,0:T(8,128)(2,1)} custom-call(s32[2]{0:T(128)} %pad_add_fusion.here, bf16[4,8,7,32,128]{4,3,2,1,0:T(8,128)(2,1)} %bitcast.188, bf16[3,4,9,4,32,128]{5,4,3,2,1,0:T(8,128)(2,1)} %shard_map.75.rest_0_, bf16[3,4,9,1,32,128]{5,4,3,2,1,0:T(8,128)(2,1)} %shard_map.76.rest_1_), custom_call_target="tpu_custom_call" | custom-call | flops 905969664 | bytes 6520840 | tf_op jit(solution)/shard_map/pallas_call | solution.py:115
  95.4 3.8 %shard_map.81 = (bf16[4,4,2,32,256]{4,3,2,1,0:T(8,128)(2,1)}, bf16[4,1,2,32,256]{4,3,2,1,0:T(8,128)(2,1)}, bf16[4,4,1,32,256]{4,3,2,1,0:T(8,128)(2,1)}) custom-call(s32[2]{0:T(128)} %pad_add_fusion.here, bf16[4,3,2,16,256]{4,3,2,1,0:T(8,128)(2,1)} %pad_maximum_fusion.24.cells, bf16[4,8,7,32,256]{4,3,2,1,0:T(8,128)(2,1)} %bitcast.185, ...), custom_call_target="tpu_custom_call" | custom-call | flops 452984832 | bytes 5308424 | tf_op jit(solution)/shard_map/pallas_call | solution.py:115
  99.2 9.1 %shard_map.83 = (bf16[2,8,7,32,128]{4,3,2,1,0:T(8,128)(2,1)}, bf16[2,8,7,32,128]{4,3,2,1,0:T(8,128)(2,1)}) custom-call(s32[2]{0:T(128)} %pad_add_fusion.here, bf16[4,4,2,32,256]{4,3,2,1,0:T(8,128)(2,1)} %get-tuple-element.11.cells.grads, bf16[3,4,9,4,32,128]{5,4,3,2,1,0:T(8,128)(2,1)} %shard_map.75.rest_0_, bf16[3,4,9,1,32,128]{5,4,3,2,1,0:T(8,128)(2,1)} %shard_map.76.rest_1_), custom_call_target="tpu_custom_call" | custom-call | flops 1811939328 | bytes 6782984 | tf_op jit(solution)/shard_map/pallas_call | solution.py:115
  111.7 3.9 %collective-permute-start.16 = (bf16[4,4,1,32,256]{4,3,2,1,0:T(8,128)(2,1)S(1)}, bf16[4,4,1,32,256]{4,3,2,1,0:T(8,128)(2,1)S(1)}, u32[]{:S(2)}, u32[]{:S(2)}) collective-permute-start(bf16[4,4,1,32,256]{4,3,2,1,0:T(8,128)(2,1)S(1)} %copy-done.2), channel_id=1, source_target_pairs={{0,1},{1,2},{2,3},{3,4},{4,5},{5,6},{6,7},{8,9},{9,10},{10,11},{11... | collective-permute-start | bytes 786440 | tf_op jit(solution)/shard_map/ppermute | solution.py:36
  120.6 11.6 %collective-permute-start.17 = (bf16[4,1,1,32,256]{4,3,2,1,0:T(8,128)(2,1)S(1)}, bf16[4,1,1,32,256]{4,3,2,1,0:T(8,128)(2,1)S(1)}, u32[]{:S(2)}, u32[]{:S(2)}) collective-permute-start(bf16[4,1,1,32,256]{4,3,2,1,0:T(8,128)(2,1)S(1)} %slice.192), channel_id=1, source_target_pairs={{0,9},{1,10},{2,11},{3,12},{4,13},{5,14},{6,15},{8,17},{9,18},{10,... | collective-permute-start | bytes 196616 | tf_op jit(solution)/shard_map/ppermute | solution.py:36
  132.2 7.5 %collective-permute-done.17.refs_4_ = bf16[4,1,1,32,256]{4,3,2,1,0:T(8,128)(2,1)S(1)} collective-permute-done((bf16[4,1,1,32,256]{4,3,2,1,0:T(8,128)(2,1)S(1)}, bf16[4,1,1,32,256]{4,3,2,1,0:T(8,128)(2,1)S(1)}, u32[]{:S(2)}, u32[]{:S(2)}) %collective-permute-start.17) | collective-permute-done | bytes 65568 | tf_op jit(solution)/shard_map/ppermute | solution.py:36
  141.1 3.5 %shard_map.79.rest_0_ = bf16[3,4,5,3,16,256]{5,4,3,2,1,0:T(8,128)(2,1)} custom-call(bf16[4,4,1,32,256]{4,3,2,1,0:T(8,128)(2,1)} %shard_map.77.refs_0_.low, bf16[4,4,1,32,256]{4,3,2,1,0:T(8,128)(2,1)} %shard_map.78.refs_1_.high, bf16[4,1,2,32,256]{4,3,2,1,0:T(8,128)(2,1)} %copy-done.12, bf16[4,4,1,32,256]{4,3,2,1,0:T(8,128)(2,1)} %copy-done.9, ...), custom_call_target="tpu_custom_call" | custom-call | bytes 2457600 | tf_op jit(solution)/shard_map/pallas_call | solution.py:115
  144.6 4.8 %shard_map.80 = bf16[4,2,1,16,256]{4,3,2,1,0:T(8,128)(2,1)} custom-call(s32[2]{0:T(128)} %pad_add_fusion.here, bf16[4,8,7,32,256]{4,3,2,1,0:T(8,128)(2,1)} %bitcast.186, bf16[3,4,5,3,16,256]{5,4,3,2,1,0:T(8,128)(2,1)} %shard_map.79.rest_0_), custom_call_target="tpu_custom_call" | custom-call | flops 452984832 | bytes 5210120 | tf_op jit(solution)/shard_map/pallas_call | solution.py:115
  151.8 3.9 %all-to-all-start = ((bf16[8,2,2048]{2,1,0:T(2,128)(2,1)}), bf16[8,2,2048]{2,1,0:T(2,128)(2,1)S(1)}, u32[]{:S(2)}, u32[]{:S(2)}) async-start(bf16[8,2,2048]{2,1,0:T(2,128)(2,1)} %reshape.161), calls=%async_computation | async-start | bytes 131072 | tf_op jit(solution)/shard_map/all_to_all | solution.py:598
  161.3 7.2 %shard_map.84 = (bf16[2,8,7,32,256]{4,3,2,1,0:T(8,128)(2,1)}, bf16[2,8,7,32,256]{4,3,2,1,0:T(8,128)(2,1)}) custom-call(s32[2]{0:T(128)} %pad_add_fusion.here, bf16[4,2,1,16,256]{4,3,2,1,0:T(8,128)(2,1)} %copy-done.10, bf16[3,4,5,3,16,256]{5,4,3,2,1,0:T(8,128)(2,1)} %shard_map.79.rest_0_), custom_call_target="tpu_custom_call" | custom-call | flops 452984832 | bytes 5210120 | tf_op jit(solution)/shard_map/pallas_call | solution.py:115
  171.4 6.7 %shard_map.82 = bf16[4,8,4,64,128]{4,3,2,1,0:T(8,128)(2,1)} custom-call(s32[2]{0:T(128)} %pad_add_fusion.here, bf16[4,4,2,32,256]{4,3,2,1,0:T(8,128)(2,1)} %get-tuple-element.11.cells.grads, bf16[4,1,2,32,256]{4,3,2,1,0:T(8,128)(2,1)} %copy-done.14, bf16[4,5,1,32,256]{4,3,2,1,0:T(8,128)(2,1)} %collective-permute-done.24.row, ...), custom_call_target="tpu_custom_call" | custom-call | flops 1811939328 | bytes 4915208 | tf_op jit(solution)/shard_map/pallas_call | solution.py:115
  204.9 3.9 %collective-permute-done.35 = bf16[2,4,4,32,256]{4,3,2,1,0:T(8,128)(2,1)S(1)} collective-permute-done((bf16[2,4,4,32,256]{4,3,2,1,0:T(8,128)(2,1)S(1)}, bf16[2,4,4,32,256]{4,3,2,1,0:T(8,128)(2,1)S(1)}, u32[]{:S(2)}, u32[]{:S(2)}) %collective-permute-start.35) | collective-permute-done | bytes 524320 | tf_op jit(solution)/shard_map/ppermute | solution.py:41
  211.4 4.1 %collective-permute-done.36 = bf16[4,4,32,256]{3,2,1,0:T(8,128)(2,1)S(1)} collective-permute-done((bf16[4,4,32,256]{3,2,1,0:T(8,128)(2,1)S(1)}, bf16[4,4,32,256]{3,2,1,0:T(8,128)(2,1)S(1)}, u32[]{:S(2)}, u32[]{:S(2)}) %collective-permute-start.36) | collective-permute-done | bytes 262176 | tf_op jit(solution)/shard_map/ppermute | solution.py:41
  219.2 5.8 %collective-permute-done.39 = bf16[2,7,32,256]{3,2,1,0:T(8,128)(2,1)S(1)} collective-permute-done((bf16[2,7,32,256]{3,2,1,0:T(8,128)(2,1)S(1)}, bf16[2,7,32,256]{3,2,1,0:T(8,128)(2,1)S(1)}, u32[]{:S(2)}, u32[]{:S(2)}) %collective-permute-start.39) | collective-permute-done | bytes 229408 | tf_op jit(solution)/shard_map/ppermute | solution.py:41
  225.7 4.2 %collective-permute-done.40 = bf16[1,7,32,256]{3,2,1,0:T(8,128)(2,1)S(1)} collective-permute-done((bf16[1,7,32,256]{3,2,1,0:T(8,128)(2,1)S(1)}, bf16[1,7,32,256]{3,2,1,0:T(8,128)(2,1)S(1)}, u32[]{:S(2)}, u32[]{:S(2)}) %collective-permute-start.40) | collective-permute-done | bytes 114720 | tf_op jit(solution)/shard_map/ppermute | solution.py:41
  231.3 3.6 %collective-permute-done.41 = bf16[7,32,256]{2,1,0:T(8,128)(2,1)S(1)} collective-permute-done((bf16[7,32,256]{2,1,0:T(8,128)(2,1)S(1)}, bf16[7,32,256]{2,1,0:T(8,128)(2,1)S(1)}, u32[]{:S(2)}, u32[]{:S(2)}) %collective-permute-start.41) | collective-permute-done | bytes 114720 | tf_op jit(solution)/shard_map/ppermute | solution.py:41
  (194 shorter events, 106.7 us)
Async XLA Ops:
  1.6 19.2 %collective-permute-start = (bf16[7,32,256]{2,1,0:T(8,128)(2,1)S(1)}, bf16[7,32,256]{2,1,0:T(8,128)(2,1)S(1)}, u32[]{:S(2)}, u32[]{:S(2)}) collective-permute-start(bf16[7,32,256]{2,1,0:T(8,128)(2,1)S(1)} %pad_dynamic-slice_fusion), channel_id=1, source_target_pairs={{0,4},{1,5},{2,6},{3,7},{4,0},{5,1},{6,2},{7,3},{8,12},{9,13},{10,... | collective-permute-start | bytes 344072 | tf_op jit(solution)/shard_map/ppermute | solution.py:41
  6.6 12.1 %collective-permute-start.8 = (bf16[7,32,128]{2,1,0:T(8,128)(2,1)S(1)}, bf16[7,32,128]{2,1,0:T(8,128)(2,1)S(1)}, u32[]{:S(2)}, u32[]{:S(2)}) collective-permute-start(bf16[7,32,128]{2,1,0:T(8,128)(2,1)S(1)} %pad_dynamic-slice_fusion.1), channel_id=1, source_target_pairs={{0,4},{1,5},{2,6},{3,7},{4,0},{5,1},{6,2},{7,3},{8,12},{9,13},{10,... | collective-permute-start | bytes 172040 | tf_op jit(solution)/shard_map/ppermute | solution.py:41
  8.3 42.7 %collective-permute-start.13 = (bf16[4,1,4,64,128]{4,3,2,1,0:T(8,128)(2,1)}, bf16[4,1,4,64,128]{4,3,2,1,0:T(8,128)(2,1)}, u32[]{:S(2)}, u32[]{:S(2)}) collective-permute-start(bf16[4,1,4,64,128]{4,3,2,1,0:T(8,128)(2,1)} %slice.153), channel_id=1, source_target_pairs={{0,8},{1,9},{2,10},{3,11},{4,12},{5,13},{6,14},{7,15},{8,16},{9,17... | collective-permute-start | bytes 786440 | tf_op jit(solution)/shard_map/ppermute | solution.py:36
  23.2 17.3 %collective-permute-start.20 = (bf16[2,2,1,4,2,512]{5,4,3,1,0,2:T(2,128)(2,1)S(1)}, bf16[2,2,1,4,2,512]{5,4,3,1,0,2:T(2,128)(2,1)S(1)}, u32[]{:S(2)}, u32[]{:S(2)}) collective-permute-start(bf16[2,2,1,4,2,512]{5,4,3,1,0,2:T(2,128)(2,1)S(1)} %bitcast.228), channel_id=1, source_target_pairs={{0,2},{1,3},{2,0},{3,1},{4,6},{5,7},{6,4},{7,5},{8,10},{9,11},{10,... | collective-permute-start | bytes 98312 | tf_op jit(solution)/shard_map/ppermute | solution.py:41
  29.4 10.2 %collective-permute-start.2 = (bf16[2,2,4,32,256]{4,3,2,1,0:T(8,128)(2,1)S(1)}, bf16[2,2,4,32,256]{4,3,2,1,0:T(8,128)(2,1)S(1)}, u32[]{:S(2)}, u32[]{:S(2)}) collective-permute-start(bf16[2,2,4,32,256]{4,3,2,1,0:T(8,128)(2,1)S(1)} %fusion.10), channel_id=1, source_target_pairs={{0,1},{1,0},{2,3},{3,2},{4,5},{5,4},{6,7},{7,6},{8,9},{9,8},{10,11... | collective-permute-start | bytes 786440 | tf_op jit(solution)/shard_map/ppermute | solution.py:41
  31.1 15.9 %collective-permute-start.11 = (bf16[2,2,2,7,32,128]{5,4,3,2,1,0:T(8,128)(2,1)S(1)}, bf16[2,2,2,7,32,128]{5,4,3,2,1,0:T(8,128)(2,1)S(1)}, u32[]{:S(2)}, u32[]{:S(2)}) collective-permute-start(bf16[2,2,2,7,32,128]{5,4,3,2,1,0:T(8,128)(2,1)S(1)} %get-tuple-element.39), channel_id=1, source_target_pairs={{0,16},{8,24},{16,0},{24,8},{1,17},{9,25},{17,1},{25,9},{2,18},{10... | collective-permute-start | bytes 1376264 | tf_op jit(solution)/shard_map/ppermute | solution.py:41
  38.1 10.0 %collective-permute-start.6 = (bf16[2,2,2,3,32,256]{5,4,3,2,1,0:T(8,128)(2,1)}, bf16[2,2,2,3,32,256]{5,4,3,2,1,0:T(8,128)(2,1)}, u32[]{:S(2)}, u32[]{:S(2)}) collective-permute-start(bf16[2,2,2,3,32,256]{5,4,3,2,1,0:T(8,128)(2,1)} %get-tuple-element.41), channel_id=1, source_target_pairs={{0,1},{1,0},{2,3},{3,2},{4,5},{5,4},{6,7},{7,6},{8,9},{9,8},{10,11... | collective-permute-start | bytes 1179656 | tf_op jit(solution)/shard_map/ppermute | solution.py:41
  40.5 16.6 %collective-permute-start.3 = (bf16[2,2,2,4,32,256]{5,4,3,2,1,0:T(8,128)(2,1)}, bf16[2,2,2,4,32,256]{5,4,3,2,1,0:T(8,128)(2,1)}, u32[]{:S(2)}, u32[]{:S(2)}) collective-permute-start(bf16[2,2,2,4,32,256]{5,4,3,2,1,0:T(8,128)(2,1)} %get-tuple-element.33), channel_id=1, source_target_pairs={{0,16},{8,24},{16,0},{24,8},{1,17},{9,25},{17,1},{25,9},{2,18},{10... | collective-permute-start | bytes 1572872 | tf_op jit(solution)/shard_map/ppermute | solution.py:41
  48.1 30.9 %collective-permute-start.12 = (bf16[2,2,2,2,7,32,128]{6,5,4,3,2,1,0:T(8,128)(2,1)}, bf16[2,2,2,2,7,32,128]{6,5,4,3,2,1,0:T(8,128)(2,1)}, u32[]{:S(2)}, u32[]{:S(2)}) collective-permute-start(bf16[2,2,2,2,7,32,128]{6,5,4,3,2,1,0:T(8,128)(2,1)} %get-tuple-element.29), channel_id=1, source_target_pairs={{0,8},{8,0},{16,24},{24,16},{1,9},{9,1},{17,25},{25,17},{2,10},{10... | collective-permute-start | bytes 2752520 | tf_op jit(solution)/shard_map/ppermute | solution.py:41
  50.6 27.1 %collective-permute-start.7 = (bf16[2,2,2,2,3,32,256]{6,5,4,3,2,0,1:T(8,128)(2,1)}, bf16[2,2,2,2,3,32,256]{6,5,4,3,2,0,1:T(8,128)(2,1)}, u32[]{:S(2)}, u32[]{:S(2)}) collective-permute-start(bf16[2,2,2,2,3,32,256]{6,5,4,3,2,0,1:T(8,128)(2,1)} %get-tuple-element.31), channel_id=1, source_target_pairs={{0,8},{8,0},{16,24},{24,16},{1,9},{9,1},{17,25},{25,17},{2,10},{10... | collective-permute-start | bytes 2359304 | tf_op jit(solution)/shard_map/ppermute | solution.py:41
  52.7 21.6 %collective-permute-start.14 = (bf16[4,9,1,64,128]{4,3,2,1,0:T(8,128)(2,1)}, bf16[4,9,1,64,128]{4,3,2,1,0:T(8,128)(2,1)}, u32[]{:S(2)}, u32[]{:S(2)}) collective-permute-start(bf16[4,9,1,64,128]{4,3,2,1,0:T(8,128)(2,1)} %pad_maximum_fusion.5), channel_id=1, source_target_pairs={{0,1},{1,2},{2,3},{3,4},{4,5},{5,6},{6,7},{8,9},{9,10},{10,11},{11... | collective-permute-start | bytes 1769480 | tf_op jit(solution)/shard_map/ppermute | solution.py:36
  59.2 33.1 %collective-permute-start.4 = (bf16[2,2,2,2,4,32,256]{6,5,4,3,2,1,0:T(8,128)(2,1)}, bf16[2,2,2,2,4,32,256]{6,5,4,3,2,1,0:T(8,128)(2,1)}, u32[]{:S(2)}, u32[]{:S(2)}) collective-permute-start(bf16[2,2,2,2,4,32,256]{6,5,4,3,2,1,0:T(8,128)(2,1)} %get-tuple-element.27), channel_id=1, source_target_pairs={{0,8},{8,0},{16,24},{24,16},{1,9},{9,1},{17,25},{25,17},{2,10},{10... | collective-permute-start | bytes 3145736 | tf_op jit(solution)/shard_map/ppermute | solution.py:41
  108.3 69.7 %collective-permute-start.25 = (bf16[2,8,7,32,128]{4,3,2,1,0:T(8,128)(2,1)}, bf16[2,8,7,32,128]{4,3,2,1,0:T(8,128)(2,1)S(1)}, u32[]{:S(2)}, u32[]{:S(2)}) collective-permute-start(bf16[2,8,7,32,128]{4,3,2,1,0:T(8,128)(2,1)} %get-tuple-element.15), channel_id=1, source_target_pairs={{0,8},{8,0},{16,24},{24,16},{1,9},{9,1},{17,25},{25,17},{2,10},{10... | collective-permute-start | bytes 2752520 | tf_op jit(solution)/shard_map/ppermute | solution.py:41
  111.7 28.0 %collective-permute-start.16 = (bf16[4,4,1,32,256]{4,3,2,1,0:T(8,128)(2,1)S(1)}, bf16[4,4,1,32,256]{4,3,2,1,0:T(8,128)(2,1)S(1)}, u32[]{:S(2)}, u32[]{:S(2)}) collective-permute-start(bf16[4,4,1,32,256]{4,3,2,1,0:T(8,128)(2,1)S(1)} %copy-done.2), channel_id=1, source_target_pairs={{0,1},{1,2},{2,3},{3,4},{4,5},{5,6},{6,7},{8,9},{9,10},{10,11},{11... | collective-permute-start | bytes 786440 | tf_op jit(solution)/shard_map/ppermute | solution.py:36
  115.7 24.0 %collective-permute-start.15 = (bf16[4,1,2,32,256]{4,3,2,1,0:T(8,128)(2,1)S(1)}, bf16[4,1,2,32,256]{4,3,2,1,0:T(8,128)(2,1)S(1)}, u32[]{:S(2)}, u32[]{:S(2)}) collective-permute-start(bf16[4,1,2,32,256]{4,3,2,1,0:T(8,128)(2,1)S(1)} %pad_maximum_fusion.25), channel_id=1, source_target_pairs={{0,8},{1,9},{2,10},{3,11},{4,12},{5,13},{6,14},{7,15},{8,16},{9,17... | collective-permute-start | bytes 393224 | tf_op jit(solution)/shard_map/ppermute | solution.py:36
  119.3 52.1 %collective-permute-start.24 = (bf16[4,5,1,32,256]{4,3,2,1,0:T(8,128)(2,1)}, bf16[4,5,1,32,256]{4,3,2,1,0:T(8,128)(2,1)}, u32[]{:S(2)}, u32[]{:S(2)}) collective-permute-start(bf16[4,5,1,32,256]{4,3,2,1,0:T(8,128)(2,1)} %pad_maximum_fusion.14), channel_id=1, source_target_pairs={{1,0},{2,1},{3,2},{4,3},{5,4},{6,5},{7,6},{9,8},{10,9},{11,10},{12... | collective-permute-start | bytes 983048 | tf_op jit(solution)/shard_map/ppermute | solution.py:36
  120.6 19.1 %collective-permute-start.17 = (bf16[4,1,1,32,256]{4,3,2,1,0:T(8,128)(2,1)S(1)}, bf16[4,1,1,32,256]{4,3,2,1,0:T(8,128)(2,1)S(1)}, u32[]{:S(2)}, u32[]{:S(2)}) collective-permute-start(bf16[4,1,1,32,256]{4,3,2,1,0:T(8,128)(2,1)S(1)} %slice.192), channel_id=1, source_target_pairs={{0,9},{1,10},{2,11},{3,12},{4,13},{5,14},{6,15},{8,17},{9,18},{10,... | collective-permute-start | bytes 196616 | tf_op jit(solution)/shard_map/ppermute | solution.py:36
  151.8 18.2 %all-to-all-start = ((bf16[8,2,2048]{2,1,0:T(2,128)(2,1)}), bf16[8,2,2048]{2,1,0:T(2,128)(2,1)S(1)}, u32[]{:S(2)}, u32[]{:S(2)}) async-start(bf16[8,2,2048]{2,1,0:T(2,128)(2,1)} %reshape.161), calls=%async_computation | async-start | bytes 131072 | tf_op jit(solution)/shard_map/all_to_all | solution.py:598
  168.5 22.8 %collective-permute-start.34 = (bf16[2,8,7,32,256]{4,3,2,1,0:T(8,128)(2,1)}, bf16[2,8,7,32,256]{4,3,2,1,0:T(8,128)(2,1)S(1)}, u32[]{:S(2)}, u32[]{:S(2)}) collective-permute-start(bf16[2,8,7,32,256]{4,3,2,1,0:T(8,128)(2,1)} %get-tuple-element.17), channel_id=1, source_target_pairs={{0,8},{8,0},{16,24},{24,16},{1,9},{9,1},{17,25},{25,17},{2,10},{10... | collective-permute-start | bytes 5505032 | tf_op jit(solution)/shard_map/ppermute | solution.py:41
  180.3 9.2 %collective-permute-start.26 = (bf16[2,4,4,32,128]{4,3,2,1,0:T(8,128)(2,1)S(1)}, bf16[2,4,4,32,128]{4,3,2,1,0:T(8,128)(2,1)S(1)}, u32[]{:S(2)}, u32[]{:S(2)}) collective-permute-start(bf16[2,4,4,32,128]{4,3,2,1,0:T(8,128)(2,1)S(1)} %slice_bitcast_fusion.9), channel_id=1, source_target_pairs={{0,16},{8,24},{16,0},{24,8},{1,17},{9,25},{17,1},{25,9},{2,18},{10... | collective-permute-start | bytes 786440 | tf_op jit(solution)/shard_map/ppermute | solution.py:41
  192.1 10.9 %collective-permute-start.37 = (bf16[2,4,3,32,256]{4,3,2,1,0:T(8,128)(2,1)S(1)}, bf16[2,4,3,32,256]{4,3,2,1,0:T(8,128)(2,1)S(1)}, u32[]{:S(2)}, u32[]{:S(2)}) collective-permute-start(bf16[2,4,3,32,256]{4,3,2,1,0:T(8,128)(2,1)S(1)} %slice_bitcast_fusion.6), channel_id=1, source_target_pairs={{0,1},{1,0},{2,3},{3,2},{4,5},{5,4},{6,7},{7,6},{8,9},{9,8},{10,11... | collective-permute-start | bytes 1179656 | tf_op jit(solution)/shard_map/ppermute | solution.py:41
  194.8 14.0 %collective-permute-start.35 = (bf16[2,4,4,32,256]{4,3,2,1,0:T(8,128)(2,1)S(1)}, bf16[2,4,4,32,256]{4,3,2,1,0:T(8,128)(2,1)S(1)}, u32[]{:S(2)}, u32[]{:S(2)}) collective-permute-start(bf16[2,4,4,32,256]{4,3,2,1,0:T(8,128)(2,1)S(1)} %slice_bitcast_fusion.3), channel_id=1, source_target_pairs={{0,16},{8,24},{16,0},{24,8},{1,17},{9,25},{17,1},{25,9},{2,18},{10... | collective-permute-start | bytes 1572872 | tf_op jit(solution)/shard_map/ppermute | solution.py:41
  196.9 13.0 %collective-permute-start.30 = (bf16[2,7,32,128]{3,2,1,0:T(8,128)(2,1)S(1)}, bf16[2,7,32,128]{3,2,1,0:T(8,128)(2,1)S(1)}, u32[]{:S(2)}, u32[]{:S(2)}) collective-permute-start(bf16[2,7,32,128]{3,2,1,0:T(8,128)(2,1)S(1)} %fusion.16), channel_id=1, source_target_pairs={{0,4},{1,5},{2,6},{3,7},{4,0},{5,1},{6,2},{7,3},{8,12},{9,13},{10,... | collective-permute-start | bytes 344072 | tf_op jit(solution)/shard_map/ppermute | solution.py:41
  215.6 9.4 %collective-permute-start.39 = (bf16[2,7,32,256]{3,2,1,0:T(8,128)(2,1)S(1)}, bf16[2,7,32,256]{3,2,1,0:T(8,128)(2,1)S(1)}, u32[]{:S(2)}, u32[]{:S(2)}) collective-permute-start(bf16[2,7,32,256]{3,2,1,0:T(8,128)(2,1)S(1)} %fusion.6), channel_id=1, source_target_pairs={{0,4},{1,5},{2,6},{3,7},{4,0},{5,1},{6,2},{7,3},{8,12},{9,13},{10,... | collective-permute-start | bytes 688136 | tf_op jit(solution)/shard_map/ppermute | solution.py:41
  (37 other events, 291.5 us)

commit v3 on v2

--- a/solution.py
+++ b/solution.py
@@ -68,24 +68,22 @@
     return list(reversed(range(1, bits("space"))))
 
 
-def mixed_gather(part):
-    each, mine, inputs = part.shape
-    for bit in far_bits():
-        part = doubled(part, "chan", bit)
-    highs = len(high_bits())
-    cut = (each + 1) // 2
-    one, two = part[..., :cut, :, :], part[..., cut:, :, :]
-    one = doubled(one, "chan", 0)
+def far_swapped(value, mask):
+    count = lax.axis_size("chan")
+    return lax.ppermute(value, "chan", [(i, i ^ (mask << 1)) for i in range(count)])
+
+
+def far_gather(part):
+    others = [far_swapped(part, m) for m in range(1, lax.axis_size("chan") // 2)]
+    return jnp.stack([part, *others])
+
+
+def near_gather(part):
+    each, mine, inputs = part.shape[-3:]
     for bit in high_bits():
-        two = doubled(two, "space", bit)
-    for bit in high_bits():
-        one = doubled(one, "space", bit)
-    two = doubled(two, "chan", 0)
-    one = doubled(one, "space", 0)
-    two = doubled(two, "space", 0)
-    two = jnp.moveaxis(two, 1, 1 + highs)
-    whole = jnp.concatenate([one, two], axis=-3)
-    return whole.reshape(lax.axis_size("space"), lax.axis_size("chan"), each, mine, inputs)
+        part = doubled(part, "space", bit)
+    part = doubled(part, "space", 0)
+    return part.reshape(lax.axis_size("space"), lax.axis_size("chan"), each, mine, inputs)
 
 
 def relative(index, mine, order):
@@ -106,9 +104,15 @@
     return jnp.concatenate(rows, axis=0)
 
 
+def scratch_avals(scratch):
+    return [jax.ShapeDtypeStruct(ref.inner_aval.shape, ref.inner_aval.dtype) for ref in scratch]
+
+
 def call(kernel, outs, args, scratch=(), grid=None, in_specs=None, out_specs=None, flops=0):
     moved = sum(a.size * a.dtype.itemsize for a in args)
     moved += sum(o.size * o.dtype.itemsize for o in outs)
+    used = sum(v.size * v.dtype.itemsize for v in scratch_avals(scratch))
+    grant = min(56 * 2**20, moved + used + 6 * 2**20)
     whole = pl.BlockSpec(memory_space=pltpu.VMEM)
     smem = pl.BlockSpec(memory_space=pltpu.SMEM)
     specs = in_specs or [smem if a.dtype == jnp.int32 else whole for a in args]
@@ -120,7 +124,7 @@
         out_specs=out_specs or [whole] * len(outs),
         scratch_shapes=scratch,
         cost_estimate=pl.CostEstimate(flops=flops, bytes_accessed=moved, transcendentals=0),
-        compiler_params=pltpu.CompilerParams(vmem_limit_bytes=56 * 2**20),
+        compiler_params=pltpu.CompilerParams(vmem_limit_bytes=grant),
     )(*args)
 
 
@@ -135,25 +139,31 @@
             store(k, part, piece.astype(BF16))
 
 
-def part_kernel(pick, shape, wide, out_of):
+def part_block(pick, out, n, shape, wide):
     wide_a, wide_b, depth = shape
     for a in range(wide_a):
         for b in range(wide_b):
             slot = ((a * wide_b + b) % 8) * (PAD + depth)
 
             def store(k, part, piece):
-                out_of[k, 0, a, b, :, part * LANES : (part + 1) * LANES] = piece
+                out[k, n, a, b, :, part * LANES : (part + 1) * LANES] = piece
 
             parted_tile(pick(a, b), wide, slot, store)
 
 
-def parted(blocks, shape, picker):
-    vols, wide_a, wide_b, depth, lanes = shape
-    out = jax.ShapeDtypeStruct((3, vols, wide_a, wide_b, depth // 2, lanes), BF16)
-
-    def kernel(*refs):
-        *ins, out_ref, wide = refs
-        part_kernel(picker(ins), (wide_a, wide_b, depth), wide, out_ref)
+def part_scratch(depth, lanes):
+    return pltpu.VMEM((lanes // LANES, 8 * (PAD + depth), LANES), F32)
+
+
+def parted_volume(own, plane):
+    vols, side_a, side_b, depth, lanes = own.shape
+    out = jax.ShapeDtypeStruct((3, vols, side_a + 1, side_b, depth // 2, lanes), BF16)
+
+    def kernel(own, plane, out, wide):
+        def pick(a, b):
+            return plane[0, 0, b] if a == 0 else own[0, a - 1, b]
+
+        part_block(pick, out, 0, (side_a + 1, side_b, depth), wide)
 
     def block(shape):
         return pl.BlockSpec((1,) + shape[1:], lambda n: (n, 0, 0, 0, 0))
@@ -161,10 +171,10 @@
     return call(
         kernel,
         [out],
-        blocks,
-        [pltpu.VMEM((lanes // LANES, 8 * (PAD + depth), LANES), F32)],
+        (own, plane),
+        [part_scratch(depth, lanes)],
         (vols,),
-        [block(b.shape) for b in blocks],
+        [block(own.shape), block(plane.shape)],
         [pl.BlockSpec((3, 1) + out.shape[2:], lambda n: (0, n, 0, 0, 0, 0))],
     )[0]
 
@@ -184,10 +194,7 @@
     return jnp.concatenate(rows, axis=0)
 
 
-def forward_kernel(orders, sides, act, split, here, filters, *rest):
-    *refs, out, acc = rest
-    if split and len(refs) == 1:
-        refs.append(None)
+def forward_total(orders, sides, refs, here, filters, acc):
     acc[...] = jnp.zeros_like(acc)
 
     def step(i, carry):
@@ -199,41 +206,68 @@
         return carry
 
     lax.fori_loop(0, 3, step, 0)
-    total = acc[...]
-    if act:
-        total = jnp.where(total > 0, total, 0.3 * total)
-    out[...] = total.astype(BF16).reshape(out.shape)
-
-
-def forward(here, refs, filters, orders, cells_b, act):
-    _, vols, wide_a, _, depth, inputs = refs[0].shape
+    return acc[...]
+
+
+def leaky(total):
+    return jnp.where(total > 0, total, 0.3 * total)
+
+
+def forward(here, parts, filters, orders, cells_b, kind):
+    main = parts[0]
+    _, vols, wide_a, _, depth, inputs = main.shape
     sides = (vols, (wide_a - 1) // 2, cells_b)
     count = filters.shape[1] * filters.shape[3]
     cells = vols * sides[1] * len(cells_b) * depth
-    out = jax.ShapeDtypeStruct((vols, sides[1], len(cells_b), depth, count), BF16)
+    outs = [jax.ShapeDtypeStruct((vols, sides[1], len(cells_b), depth, count), BF16)]
+    scratch = [pltpu.VMEM((cells, count), F32)]
+    if kind == "low":
+        outs.append(jax.ShapeDtypeStruct(main.shape[:3] + (1,) + main.shape[4:], BF16))
+        scratch.append(part_scratch(2 * depth, inputs))
+
+    def kernel(here, filters, main, *rest):
+        if kind == "low":
+            row, out, row_parts, acc, wide = rest
+
+            def split(n, carry):
+                part_block(lambda a, b: row[n, a, 0], row_parts, n, (wide_a, 1, 2 * depth), wide)
+                return carry
+
+            lax.fori_loop(0, vols, split, 0)
+            refs = (main, row_parts)
+        else:
+            out, acc = rest
+            refs = (main, None) if kind == "high" else (main,)
+        total = forward_total(orders, sides, refs, here, filters, acc)
+        if kind != "out":
+            total = leaky(total)
+        out[...] = total.astype(BF16).reshape(out.shape)
+
     return call(
-        functools.partial(forward_kernel, orders, sides, act, len(refs) == 2),
-        [out],
-        (here, filters, *(r for r in refs if r is not None)),
-        [pltpu.VMEM((cells, count), F32)],
+        kernel,
+        outs,
+        (here, filters, *parts),
+        scratch,
         flops=2 * cells * 27 * inputs * count,
-    )[0]
-
-
-def grads_kernel(orders, sides, here, grads, *rest):
-    *refs, keep, send, turned = rest
+    )
+
+
+def grads_body(orders, sides, here, grads, refs, keep, send, turned):
     cells, count = turned.shape[1], turned.shape[0]
     inputs = refs[0].shape[5]
+    pieces = inputs // LANES
     chans = 2 ** len(orders[1])
     mine = count // chans
-    each = keep.shape[2]
+    each = keep.shape[2] // pieces
     half = keep.shape[0]
     turned[...] = jnp.transpose(grads[...].reshape(cells, count).astype(F32), (1, 0)).astype(BF16)
 
     def put(ref, place, tap, part):
         for chan in range(chans):
             to = relative(chan, here[1], orders[1])
-            ref[place, to, tap % each] = part[chan * mine : (chan + 1) * mine]
+            for piece in range(pieces):
+                lanes = slice(piece * LANES, (piece + 1) * LANES)
+                ref[place, to, (tap % each) * pieces + piece] = part[chan * mine : (chan + 1) * mine, lanes]
 
     def step(i, carry):
         for j in range(3):
@@ -254,32 +288,74 @@
         return carry
 
     lax.fori_loop(0, 3, step, 0)
+    blank = jnp.zeros((count, inputs), BF16)
     for tap in range(27, each * 2 * half):
         place = relative(tap // each, here[0], orders[0])
-        blank = jnp.zeros((chans, mine, inputs), BF16)
 
         @pl.when(place < half)
         def _():
-            keep[place, :, tap % each] = blank
+            put(keep, place, tap, blank)
 
         @pl.when(place >= half)
         def _():
-            send[place - half, :, tap % each] = blank
-
-
-def filter_grads(here, refs, grads, orders):
+            put(send, place - half, tap, blank)
+
+
+def grads_out(count, inputs, orders):
+    space, chans = 2 ** len(orders[0]), 2 ** len(orders[1])
+    each = -(-27 // space) * (inputs // LANES)
+    return jax.ShapeDtypeStruct((space // 2, chans, each, count // chans, LANES), BF16)
+
+
+def first_grads(here, refs, grads, orders):
     inputs = refs[0].shape[5]
     vols, side_a, side_b, depth, count = grads.shape
     sides = (vols, side_a, range(side_b))
     cells = vols * side_a * side_b * depth
-    space, chans = 2 ** len(orders[0]), 2 ** len(orders[1])
-    each = -(-27 // space)
-    out = jax.ShapeDtypeStruct((space // 2, chans, each, count // chans, inputs), BF16)
+    out = grads_out(count, inputs, orders)
+
+    def kernel(here, grads, main, row, keep, send, turned):
+        grads_body(orders, sides, here, grads, (main, row), keep, send, turned)
+
     return call(
-        functools.partial(grads_kernel, orders, sides),
+        kernel,
         [out, out],
         (here, grads, *refs),
         [pltpu.VMEM((count, cells), BF16)],
+        flops=2 * cells * 27 * inputs * count,
+    )
+
+
+def second_grads(here, blocks, grads, orders):
+    low, high = blocks[:2]
+    side_x, deep, inputs = low.shape[1], low.shape[3], low.shape[4]
+    wide_b = low.shape[2] + high.shape[2] + 1
+    vols, side_a, side_b, depth, count = grads.shape
+    sides = (vols, side_a, range(side_b))
+    cells = vols * side_a * side_b * depth
+    out = grads_out(count, inputs, orders)
+    parts = jax.ShapeDtypeStruct((3, vols, side_x + 1, wide_b, depth, inputs), BF16)
+
+    def kernel(here, grads, low, high, plane, row, corner, keep, send, parts, turned, wide):
+        def split(n, carry):
+            def pick(a, b):
+                if b == 0:
+                    return corner[n, 0, 0] if a == 0 else row[n, a - 1, 0]
+                if a == 0:
+                    return plane[n, 0, b - 1]
+                return low[n, a - 1, 0] if b == 1 else high[n, a - 1, b - 2]
+
+            part_block(pick, parts, n, (side_x + 1, wide_b, deep), wide)
+            return carry
+
+        lax.fori_loop(0, vols, split, 0)
+        grads_body(orders, sides, here, grads, (parts,), keep, send, turned)
+
+    return call(
+        kernel,
+        [out, out, parts],
+        (here, grads, *blocks),
+        [pltpu.VMEM((count, cells), BF16), part_scratch(deep, inputs)],
         flops=2 * cells * 27 * inputs * count,
     )
 
@@ -299,10 +375,15 @@
     return keep.astype(F32) + other.astype(F32)
 
 
-def sum_filters(total):
-    each, mine, inputs = total.shape[-3:]
+def plain_sum(total):
+    for bit in range(1, bits("space")):
+        total = half_sum(total, "space", bit, 0)
+    return half_sum(total, "chan", 0, 0)
+
+
+def mixed_sum(total):
     highs = list(range(1, bits("space")))
-    cut = (each + 1) // 2
+    cut = (total.shape[-3] + 1) // 2
     one, two = total[..., :cut, :, :], total[..., cut:, :, :]
     two = half_sum(two, "chan", 0, len(highs))
     for bit in highs:
@@ -310,20 +391,34 @@
     one = half_sum(one, "chan", 0, 0)
     for bit in highs:
         two = half_sum(two, "space", bit, 0)
-    part = jnp.concatenate([one, two], axis=-3)
-    for bit in far_bits():
-        part = part.reshape((2, -1, each, mine, inputs))
-        part = half_sum(part, "chan", bit, 0)
-    part = part.reshape(each, mine, inputs).astype(BF16)
+    return jnp.concatenate([one, two], axis=-3)
+
+
+def finish_sum(totals):
+    count = lax.axis_size("chan") // 2
+    space = lax.axis_size("space")
+    merged = jnp.concatenate(totals, axis=1)
+    part = merged[0].astype(F32)
+    for m in range(1, count):
+        part = part + far_swapped(merged[m].astype(BF16), m).astype(F32)
+    part = part.astype(BF16)
     for bit in high_bits():
         part = doubled(part, "space", bit)
     part = doubled(part, "space", 0)
-    space = lax.axis_size("space")
-    part = part.reshape(space, each, mine, inputs)
-    places = jnp.arange(space) ^ lax.axis_index("space")
-    taps = [lax.dynamic_index_in_dim(part, space_order(places[s]), 0, keepdims=False) for s in range(space)]
-    full = jnp.concatenate(taps, axis=0)[:27].astype(F32)
-    return jnp.transpose(full, (0, 2, 1)).reshape(3, 3, 3, inputs, mine)
+    part = part.reshape((space,) + merged.shape[1:])
+    apart = [jnp.int32(s) ^ lax.axis_index("space") for s in range(space)]
+    ordered = [lax.dynamic_index_in_dim(part, space_order(a), 0, keepdims=False) for a in apart]
+    outs, begin = [], 0
+    taps = -(-27 // space)
+    for total in totals:
+        rows, mine = total.shape[1], total.shape[2]
+        pieces = rows // taps
+        full = jnp.concatenate([o[begin : begin + rows] for o in ordered], axis=0)
+        full = full.reshape(space * taps, pieces, mine, LANES)[:27].astype(F32)
+        full = jnp.transpose(full, (0, 1, 3, 2)).reshape(3, 3, 3, pieces * LANES, mine)
+        outs.append(full)
+        begin += rows
+    return outs
 
 
 def space_order(apart):
@@ -487,116 +582,66 @@
     )[0]
 
 
-class CellExchange:
-    def __init__(self, cotangent):
-        vols, side_a, side_b, side_c, mine = cotangent.shape
-        self.count = bits("chan")
-        self.tail = (side_b // 2**self.count, vols, side_a, side_c, mine)
-        flat = cotangent.reshape(vols, side_a, side_b, side_c * mine)
-        flat = jnp.transpose(flat, (2, 0, 1, 3))
-        self.value = flat.reshape((2,) * self.count + (-1,) + flat.shape[1:])
-        self.open = list(reversed(range(self.count)))
-        self.done = []
-
-    def stage(self, bit):
-        dim = self.open.index(bit)
-        mine = (lax.axis_index("chan") >> bit) & 1
-        keep = lax.dynamic_index_in_dim(self.value, mine, dim, keepdims=False)
-        send = lax.dynamic_index_in_dim(self.value, 1 - mine, dim, keepdims=False)
-        other = swapped(send, "chan", bit)
-        low, high = jnp.where(mine == 1, other, keep), jnp.where(mine == 1, keep, other)
-        self.value = jnp.stack([low, high], axis=self.count - 1)
-        self.open.remove(bit)
-        self.done.append(bit)
-
-    def finish(self):
-        rows, vols, side_a, side_c, mine = self.tail
-        count = self.count
-        value = self.value.reshape((2,) * count + (rows, vols, side_a, side_c, mine))
-        sources = [self.done.index(bit) for bit in reversed(range(count))]
-        value = jnp.transpose(
-            value, (count + 1, count + 2, count, count + 3, *sources, count + 4)
-        )
-        own = value.reshape(vols, side_a, rows, side_c, 2**count * mine)
-        row = shifted(own[:, :, :1], (0, -1))
-        near = jnp.concatenate([own, row], axis=2)
-        plane = shifted(near[:, :1], (-1, 0))
-        return own, jnp.concatenate([near, plane], axis=1)
-
-
-def volume_picker(refs):
-    own, plane = refs
-    return lambda a, b: plane[0, 0, b] if a == 0 else own[0, a - 1, b]
-
-
-def row_picker(refs):
-    return lambda a, b: refs[0][0, a, 0]
-
-
-def hidden_picker(refs):
-    low, high, plane, row, corner = refs
-
-    def pick(a, b):
-        if b == 0:
-            return corner[0, 0, 0] if a == 0 else row[0, a - 1, 0]
-        if a == 0:
-            return plane[0, 0, b - 1]
-        return low[0, a - 1, 0] if b == 1 else high[0, a - 1, b - 2]
-
-    return pick
+def near_cells(value, shape):
+    chan = lax.axis_size("chan")
+    vols, side_a, side_b, side_c, mine = shape
+    rows = side_b // chan
+    value = value.reshape(chan, vols, side_a, side_b, side_c * mine)
+    value = jnp.pad(value, ((0, 0), (0, 0), (0, 0), (0, 1), (0, 0)))
+    value = lax.dynamic_slice_in_dim(value, lax.axis_index("chan") * rows, rows + 1, 3)
+    count = bits("chan")
+    value = value.reshape((2,) * count + value.shape[1:])
+    for dim, bit in enumerate([0] + far_bits()):
+        mine_bit = (lax.axis_index("chan") >> bit) & 1
+        value = jnp.where(mine_bit == 1, jnp.flip(value, dim), value)
+    value = jnp.transpose(value, (*range(1, count), 0, *range(count, value.ndim)))
+    value = value.reshape(chan, vols, side_a, rows + 1, side_c, mine)
+    value = jnp.transpose(value, (1, 2, 3, 4, 0, 5))
+    near = value.reshape(vols, side_a, rows + 1, side_c, chan * mine)
+    plane = shifted(near[:, :1], (-1, 0))
+    return near[:, :, :rows], jnp.concatenate([near, plane], axis=1)
 
 
 def local(volume, w_first, w_second, cotangent):
     here = position()
-    far = list(range(1, bits("chan")))
-    gathered = (list(range(bits("space"))), [0] + far)
-    summed = (list(range(bits("space"))), [0] + far[::-1])
-    vols, side_x, side_y, depth, inputs = volume.shape
-    side_b = side_y // 2
-
-    cells = CellExchange(cotangent)
+    orders = (list(range(bits("space"))), [0] + far_bits())
+    side_b = volume.shape[2] // 2
+
     plane = shifted(volume[:, -1:], (1, 0))
-    part = own_part(w_first)
-    for bit in far_bits():
-        part = doubled(part, "chan", bit)
-    part = doubled(part, "chan", 0)
-    for bit in high_bits():
-        part = doubled(part, "space", bit)
-    part = doubled(part, "space", 0)
-    first_full = part.reshape(lax.axis_size("space"), lax.axis_size("chan"), *part.shape[-3:])
-    for bit in [0] + far_bits():
-        cells.stage(bit)
-    grad_cells, grad_ext = cells.finish()
+    part = far_gather(own_part(w_first))
+    first_full = near_gather(doubled(part, "chan", 0))
     row = jnp.concatenate([plane, volume], axis=1)[:, :, -1:]
     row = shifted(row, (0, 1))
-    second_full = mixed_gather(own_part(w_second))
-
-    wide = (vols, side_x + 1, side_y, depth, inputs)
-    vol_main = parted((volume, plane), wide, volume_picker)
-    high = forward(here, (vol_main, None), first_full, gathered, range(1, side_b), True)
+    second = own_part(w_second)
+    taps = second.shape[0]
+    riders = cotangent.reshape((-1,) + second.shape[1:])
+    part = far_gather(jnp.concatenate([second, riders], axis=0))
+    part = doubled(part, "chan", 0)
+    second_full = near_gather(part[:, :, :taps])
+    grad_cells, grad_ext = near_cells(part[:, :, taps:], cotangent.shape)
+
+    vol_main = parted_volume(volume, plane)
+    (high,) = forward(here, (vol_main,), first_full, orders, range(1, side_b), "high")
+    low, vol_row = forward(here, (vol_main, row), first_full, orders, range(1), "low")
     hid_row = shifted(high[:, :, -1:], (0, 1))
     hid_corner = shifted(high[:, -1:, -1:], (1, 1))
-    vol_row = parted((row,), wide[:2] + (1, depth, inputs), row_picker)
-    vol_parts = (vol_main, vol_row)
-    low = forward(here, vol_parts, first_full, gathered, range(1), True)
     hid_plane = jnp.concatenate([low[:, -1:], high[:, -1:]], axis=2)
     hid_plane = shifted(hid_plane, (1, 0))
-    shape = (vols, side_x // 2 + 1, side_b + 1) + low.shape[3:]
-    act_blocks = (low, high, hid_plane, hid_row, hid_corner)
-    act_parts = (parted(act_blocks, shape, hidden_picker),)
-    second_terms = core_sum(*filter_grads(here, act_parts, grad_cells, summed))
-    second_grad = sum_filters(second_terms)
-
-    pre_back, pre_plane, pre_row = hidden_back(here, grad_ext, second_full, low, high, gathered)
-    first_terms = core_sum(*filter_grads(here, vol_parts, pre_back, summed))
-    first_grad = sum_filters(first_terms)
+    blocks = (low, high, hid_plane, hid_row, hid_corner)
+    keep, send, act_parts = second_grads(here, blocks, grad_cells, orders)
+    second_sum = mixed_sum(core_sum(keep, send))
+
+    pre_back, pre_plane, pre_row = hidden_back(here, grad_ext, second_full, low, high, orders)
+    keep, send = first_grads(here, (vol_main, vol_row), pre_back, orders)
+    first_sum = plain_sum(core_sum(keep, send))
+    first_grad, second_grad = finish_sum([first_sum, second_sum])
     plane = shifted(pre_plane, (-1, 0))
     row = jnp.concatenate([pre_row, plane[:, :, :1]], axis=1)
     row = shifted(row, (0, -1))
-    out_b = (shape[2] - 1) // 2
-    local_out = forward(here, act_parts, second_full, gathered, range(out_b), False)
+    out_b = range(grad_cells.shape[2])
+    (local_out,) = forward(here, (act_parts,), second_full, orders, out_b, "out")
     second_out = lax.all_to_all(local_out, "chan", split_axis=4, concat_axis=2, tiled=True)
-    volume_grad = volume_grads(here, pre_back, plane, row, first_full, gathered)
+    volume_grad = volume_grads(here, pre_back, plane, row, first_full, orders)
     return (second_out, volume_grad, first_grad, second_grad)
 
 

time: 239 us -> 204 us (0.85)
  Pallas kernels: 53.5 us -> 28.4 us
  starting transfers between devices: 79.6 us -> 67.9 us
  local copies, waits for them, and re-layouts: 13.1 us -> 24.1 us
  between operations: 6.34 us -> 1.24 us
  waiting for transfers between devices: 62.3 us -> 59.2 us
    pallas_call x10 -> x8, Pallas kernels: 53.5 us -> 28.4 us  [call(): pl.pallas_call(kernel, out_shape=outs, grid=grid or (), in_specs=specs, o...]
    ppermute x34 -> x16, starting transfers between devices: 45.8 us -> 23.6 us  [swapped(): return lax.ppermute(value, axis, [(i, i ^ 1 << bit) for i in range(count)])]
    ppermute x0 -> x9, waiting for transfers between devices: none -> 20.5 us  [far_swapped(): lax.ppermute(value, 'chan', [(i, i ^ mask << 1) for i in range(count)])]
    ppermute x34 -> x16, waiting for transfers between devices: 48.4 us -> 28.8 us  [swapped(): return lax.ppermute(value, axis, [(i, i ^ 1 << bit) for i in range(count)])]
    ppermute x0 -> x9, starting transfers between devices: none -> 14 us  [far_swapped(): lax.ppermute(value, 'chan', [(i, i ^ mask << 1) for i in range(count)])]
    ppermute x9 -> x8, waiting for transfers between devices: 13.9 us -> 2.93 us  [shifted(): return lax.ppermute(value, ('space', 'chan'), pairs)]
    reshape x3 -> x6, local copies, waits for them, and re-layouts: 1.42 us -> 9.67 us  [the longest x2 2.31 us: finish_sum(): jnp.transpose(full, (0, 1, 3, 2)).reshape(3, 3, 3, pieces * LANES, mine)]
    all_to_all x1, waiting for transfers between devices: 0.01 us -> 6.9 us  [local(): lax.all_to_all(local_out, 'chan', split_axis=4, concat_axis=2, tiled=True)]
  transfers between devices with their start and end apart: 44 -> 34, of which waited for: 20 -> 14; matrix products, arithmetic and copies ran while one was open for 12% -> 18% of each run, Pallas kernels for 17% -> 14%
where the time goes in v3:
time: 204 us; the launch traced here: 203 us
  starting transfers between devices  67.9 us (33%)
  waiting for transfers between devices  59.2 us (29%)
  Pallas kernels  28.4 us (14%)
  local copies, waits for them, and re-layouts  24.1 us (12%)
  other arithmetic  22.4 us (11%)
    ppermute x16, waiting for transfers between devices, swapped(): return lax.ppermute(value, axis, [(i, i ^ 1 << bit) for i in range(count)])  28.8 us
    pallas_call x8, Pallas kernels, call(): pl.pallas_call(kernel, out_shape=outs, grid=grid or (), in_specs=specs, o...  28.4 us
    ppermute x8, starting transfers between devices, shifted(): return lax.ppermute(value, ('space', 'chan'), pairs)  27 us
    ppermute x16, starting transfers between devices, swapped(): return lax.ppermute(value, axis, [(i, i ^ 1 << bit) for i in range(count)])  23.6 us
    ppermute x9, waiting for transfers between devices, far_swapped(): lax.ppermute(value, 'chan', [(i, i ^ mask << 1) for i in range(count)])  20.5 us
    another operation x11, other arithmetic, doubled(): return jnp.stack([value, other])  14.9 us
    ppermute x9, starting transfers between devices, far_swapped(): lax.ppermute(value, 'chan', [(i, i ^ mask << 1) for i in range(count)])  14 us
    all_to_all x1, waiting for transfers between devices, local(): lax.all_to_all(local_out, 'chan', split_axis=4, concat_axis=2, tiled=True)  6.9 us
  transfers between devices with their start and end apart: 34, of which 14 were waited for; matrix products, arithmetic and copies ran while one was open for 18% of the time, Pallas kernels for 14%

profile of v3, /device:TPU:0, one launch (start us, length us, event | category | flops | bytes accessed | tf_op | source)
XLA Modules:
  0.0 203.2 jit_solution(4353494366870800125)
XLA Ops:
  1.5 4.1 %collective-permute-start.7 = (bf16[7,32,128]{2,1,0:T(8,128)(2,1)S(1)}, bf16[7,32,128]{2,1,0:T(8,128)(2,1)S(1)}, u32[]{:S(2)}, u32[]{:S(2)}) collective-permute-start(bf16[7,32,128]{2,1,0:T(8,128)(2,1)S(1)} %pad_dynamic-slice_fusion.2), channel_id=1, source_target_pairs={{0,4},{1,5},{2,6},{3,7},{4,0},{5,1},{6,2},{7,3},{8,12},{9,13},{10,... | collective-permute-start | bytes 172040 | tf_op jit(solution)/shard_map/ppermute | solution.py:73
  11.3 2.5 %collective-permute-start = (bf16[11,32,256]{2,1,0:T(8,128)(2,1)S(1)}, bf16[11,32,256]{2,1,0:T(8,128)(2,1)S(1)}, u32[]{:S(2)}, u32[]{:S(2)}) collective-permute-start(bf16[11,32,256]{2,1,0:T(8,128)(2,1)S(1)} %get-tuple-element.58), channel_id=1, source_target_pairs={{0,2},{1,3},{2,0},{3,1},{4,6},{5,7},{6,4},{7,5},{8,10},{9,11},{10,... | collective-permute-start | bytes 540680 | tf_op jit(solution)/shard_map/ppermute | solution.py:73
  15.7 9.1 %collective-permute-done.1 = bf16[11,32,256]{2,1,0:T(8,128)(2,1)S(1)} collective-permute-done((bf16[11,32,256]{2,1,0:T(8,128)(2,1)S(1)}, bf16[11,32,256]{2,1,0:T(8,128)(2,1)S(1)}, u32[]{:S(2)}, u32[]{:S(2)}) %collective-permute-start.1) | collective-permute-done | bytes 180256 | tf_op jit(solution)/shard_map/ppermute | solution.py:73
  33.5 3.3 %collective-permute-start.13 = (bf16[4,9,1,64,128]{4,3,2,1,0:T(8,128)(2,1)}, bf16[4,9,1,64,128]{4,3,2,1,0:T(8,128)(2,1)}, u32[]{:S(2)}, u32[]{:S(2)}) collective-permute-start(bf16[4,9,1,64,128]{4,3,2,1,0:T(8,128)(2,1)} %pad_maximum_fusion.7), channel_id=1, source_target_pairs={{0,1},{1,2},{2,3},{3,4},{4,5},{5,6},{6,7},{8,9},{9,10},{10,11},{11... | collective-permute-start | bytes 1769480 | tf_op jit(solution)/shard_map/ppermute | solution.py:36
  38.6 2.7 %collective-permute-done.10 = bf16[2,4,7,32,128]{4,3,2,1,0:T(8,128)(2,1)} collective-permute-done((bf16[2,4,7,32,128]{4,3,2,1,0:T(8,128)(2,1)}, bf16[2,4,7,32,128]{4,3,2,1,0:T(8,128)(2,1)}, u32[]{:S(2)}, u32[]{:S(2)}) %collective-permute-start.10) | collective-permute-done | bytes 458784 | tf_op jit(solution)/shard_map/ppermute | solution.py:41
  43.7 6.0 %collective-permute-start.11 = (bf16[2,2,4,7,32,128]{5,4,3,2,1,0:T(8,128)(2,1)}, bf16[2,2,4,7,32,128]{5,4,3,2,1,0:T(8,128)(2,1)}, u32[]{:S(2)}, u32[]{:S(2)}) collective-permute-start(bf16[2,2,4,7,32,128]{5,4,3,2,1,0:T(8,128)(2,1)} %get-tuple-element.37), channel_id=1, source_target_pairs={{0,8},{8,0},{16,24},{24,16},{1,9},{9,1},{17,25},{25,17},{2,10},{10... | collective-permute-start | bytes 2752520 | tf_op jit(solution)/shard_map/ppermute | solution.py:41
  54.8 2.7 %collective-permute-start.4 = (bf16[2,4,7,32,256]{4,3,2,1,0:T(8,128)(2,1)S(1)}, bf16[2,4,7,32,256]{4,3,2,1,0:T(8,128)(2,1)S(1)}, u32[]{:S(2)}, u32[]{:S(2)}) collective-permute-start(bf16[2,4,7,32,256]{4,3,2,1,0:T(8,128)(2,1)S(1)} %fusion), channel_id=1, source_target_pairs={{0,16},{8,24},{16,0},{24,8},{1,17},{9,25},{17,1},{25,9},{2,18},{10... | collective-permute-start | bytes 2752520 | tf_op jit(solution)/shard_map/ppermute | solution.py:41
  60.5 3.2 %shard_map.77.high = bf16[4,4,1,32,256]{4,3,2,1,0:T(8,128)(2,1)} custom-call(s32[2]{0:T(128)S(1)} %pad_add_fusion.here, bf16[4,8,7,32,128]{4,3,2,1,0:T(8,128)(2,1)S(1)} %bitcast.141, bf16[3,4,9,4,32,128]{5,4,3,2,1,0:T(8,128)(2,1)S(1)} %shard_map.75.main), custom_call_target="tpu_custom_call" | custom-call | flops 905969664 | bytes 5636104 | tf_op jit(solution)/shard_map/pallas_call | solution.py:119
  65.2 7.8 %collective-permute-start.15 = (bf16[4,4,1,32,256]{4,3,2,1,0:T(8,128)(2,1)}, bf16[4,4,1,32,256]{4,3,2,1,0:T(8,128)(2,1)}, u32[]{:S(2)}, u32[]{:S(2)}) collective-permute-start(bf16[4,4,1,32,256]{4,3,2,1,0:T(8,128)(2,1)} %shard_map.77.high), channel_id=1, source_target_pairs={{0,1},{1,2},{2,3},{3,4},{4,5},{5,6},{6,7},{8,9},{9,10},{10,11},{11... | collective-permute-start | bytes 786440 | tf_op jit(solution)/shard_map/ppermute | solution.py:36
  74.9 3.3 %shard_map.76 = (bf16[4,4,1,32,256]{4,3,2,1,0:T(8,128)(2,1)S(1)}, bf16[3,4,9,1,32,128]{5,4,3,2,1,0:T(8,128)(2,1)S(1)}) custom-call(s32[2]{0:T(128)S(1)} %pad_add_fusion.here, bf16[4,8,7,32,128]{4,3,2,1,0:T(8,128)(2,1)S(1)} %bitcast.142, bf16[3,4,9,4,32,128]{5,4,3,2,1,0:T(8,128)(2,1)S(1)} %shard_map.75.main, ...), custom_call_target="tpu_custom_call" | custom-call | flops 905969664 | bytes 7110664 | tf_op jit(solution)/shard_map/pallas_call | solution.py:119
  81.2 8.7 %collective-permute-start.14 = (bf16[4,1,2,32,256]{4,3,2,1,0:T(8,128)(2,1)}, bf16[4,1,2,32,256]{4,3,2,1,0:T(8,128)(2,1)}, u32[]{:S(2)}, u32[]{:S(2)}) collective-permute-start(bf16[4,1,2,32,256]{4,3,2,1,0:T(8,128)(2,1)} %pad_maximum_fusion.21), channel_id=1, source_target_pairs={{0,8},{1,9},{2,10},{3,11},{4,12},{5,13},{6,14},{7,15},{8,16},{9,17... | collective-permute-start | bytes 393224 | tf_op jit(solution)/shard_map/ppermute | solution.py:36
  101.1 5.7 %shard_map.78 = (bf16[2,8,14,32,128]{4,3,2,1,0:T(8,128)(2,1)S(1)}, bf16[2,8,14,32,128]{4,3,2,1,0:T(8,128)(2,1)S(1)}, bf16[3,4,5,3,16,256]{5,4,3,2,1,0:T(8,128)(2,1)S(1)}) custom-call(s32[2]{0:T(128)S(1)} %pad_add_fusion.here, bf16[4,2,1,16,256]{4,3,2,1,0:T(8,128)(2,1)S(1)} %slice.194.grads, bf16[4,4,1,32,256]{4,3,2,1,0:T(8,128)(2,1)S(1)} %copy-done.7, ...), custom_call_target="tpu_custom_call" | custom-call | flops 452984832 | bytes 6193160 | tf_op jit(solution)/shard_map/pallas_call | solution.py:119
  117.5 6.0 %shard_map.82 = (bf16[2,8,7,32,128]{4,3,2,1,0:T(8,128)(2,1)S(1)}, bf16[2,8,7,32,128]{4,3,2,1,0:T(8,128)(2,1)S(1)}) custom-call(s32[2]{0:T(128)S(1)} %pad_add_fusion.here, bf16[4,4,2,32,256]{4,3,2,1,0:T(8,128)(2,1)S(1)} %get-tuple-element.16.cells.grads, bf16[3,4,9,4,32,128]{5,4,3,2,1,0:T(8,128)(2,1)S(1)} %shard_map.75.main, ...), custom_call_target="tpu_custom_call" | custom-call | flops 1811939328 | bytes 6782984 | tf_op jit(solution)/shard_map/pallas_call | solution.py:119
  124.7 3.2 %collective-permute-done.24 = bf16[2,4,7,32,128]{4,3,2,1,0:T(8,128)(2,1)S(1)} collective-permute-done((bf16[2,4,7,32,128]{4,3,2,1,0:T(8,128)(2,1)S(1)}, bf16[2,4,7,32,128]{4,3,2,1,0:T(8,128)(2,1)S(1)}, u32[]{:S(2)}, u32[]{:S(2)}) %collective-permute-start.24) | collective-permute-done | bytes 458784 | tf_op jit(solution)/shard_map/ppermute | solution.py:41
  133.4 5.6 %collective-permute-done.27 = bf16[4,7,32,128]{3,2,1,0:T(8,128)(2,1)S(1)} collective-permute-done((bf16[4,7,32,128]{3,2,1,0:T(8,128)(2,1)S(1)}, bf16[4,7,32,128]{3,2,1,0:T(8,128)(2,1)S(1)}, u32[]{:S(2)}, u32[]{:S(2)}) %collective-permute-start.27) | collective-permute-done | bytes 229408 | tf_op jit(solution)/shard_map/ppermute | solution.py:41
  139.1 8.1 %collective-permute-done.21 = bf16[2,4,7,32,128]{4,3,2,1,0:T(8,128)(2,1)S(1)} collective-permute-done((bf16[2,4,7,32,128]{4,3,2,1,0:T(8,128)(2,1)S(1)}, bf16[2,4,7,32,128]{4,3,2,1,0:T(8,128)(2,1)S(1)}, u32[]{:S(2)}, u32[]{:S(2)}) %collective-permute-start.21) | collective-permute-done | bytes 458784 | tf_op jit(solution)/shard_map/ppermute | solution.py:41
  148.1 5.4 %collective-permute-done.22 = bf16[4,7,32,128]{3,2,1,0:T(8,128)(2,1)S(1)} collective-permute-done((bf16[4,7,32,128]{3,2,1,0:T(8,128)(2,1)S(1)}, bf16[4,7,32,128]{3,2,1,0:T(8,128)(2,1)S(1)}, u32[]{:S(2)}, u32[]{:S(2)}) %collective-permute-start.22) | collective-permute-done | bytes 229408 | tf_op jit(solution)/shard_map/ppermute | solution.py:41
  154.4 2.9 %collective-permute-start.29 = (bf16[21,32,128]{2,1,0:T(8,128)(2,1)S(1)}, bf16[21,32,128]{2,1,0:T(8,128)(2,1)S(1)}, u32[]{:S(2)}, u32[]{:S(2)}) collective-permute-start(bf16[21,32,128]{2,1,0:T(8,128)(2,1)S(1)} %get-tuple-element.50), channel_id=1, source_target_pairs={{0,4},{1,5},{2,6},{3,7},{4,0},{5,1},{6,2},{7,3},{8,12},{9,13},{10,... | collective-permute-start | bytes 516104 | tf_op jit(solution)/shard_map/ppermute | solution.py:73
  158.7 2.7 %collective-permute-done.28 = bf16[21,32,128]{2,1,0:T(8,128)(2,1)S(1)} collective-permute-done((bf16[21,32,128]{2,1,0:T(8,128)(2,1)S(1)}, bf16[21,32,128]{2,1,0:T(8,128)(2,1)S(1)}, u32[]{:S(2)}, u32[]{:S(2)}) %collective-permute-start.28) | collective-permute-done | bytes 172064 | tf_op jit(solution)/shard_map/ppermute | solution.py:73
  162.8 7.2 %collective-permute-done.29 = bf16[21,32,128]{2,1,0:T(8,128)(2,1)S(1)} collective-permute-done((bf16[21,32,128]{2,1,0:T(8,128)(2,1)S(1)}, bf16[21,32,128]{2,1,0:T(8,128)(2,1)S(1)}, u32[]{:S(2)}, u32[]{:S(2)}) %collective-permute-start.29) | collective-permute-done | bytes 172064 | tf_op jit(solution)/shard_map/ppermute | solution.py:73
  170.1 3.4 %collective-permute-start.31 = (bf16[21,32,128]{2,1,0:T(8,128)(2,1)S(1)}, bf16[21,32,128]{2,1,0:T(8,128)(2,1)S(1)}, u32[]{:S(2)}, u32[]{:S(2)}) collective-permute-start(bf16[21,32,128]{2,1,0:T(8,128)(2,1)S(1)} %fusion.9), channel_id=1, source_target_pairs={{0,16},{8,24},{16,0},{24,8},{1,17},{9,25},{17,1},{25,9},{2,18},{10... | collective-permute-start | bytes 516104 | tf_op jit(solution)/shard_map/ppermute | solution.py:41
  181.8 3.4 %all-to-all-start = ((bf16[8,2,2048]{2,1,0:T(2,128)(2,1)}), bf16[8,2,2048]{2,1,0:T(2,128)(2,1)S(1)}, u32[]{:S(2)}, u32[]{:S(2)}) async-start(bf16[8,2,2048]{2,1,0:T(2,128)(2,1)} %reshape.108), calls=%async_computation | async-start | bytes 131072 | tf_op jit(solution)/shard_map/all_to_all | solution.py:643
  185.2 6.9 %all-to-all-done = bf16[8,2,2048]{2,1,0:T(2,128)(2,1)S(1)} async-done(((bf16[8,2,2048]{2,1,0:T(2,128)(2,1)}), bf16[8,2,2048]{2,1,0:T(2,128)(2,1)S(1)}, u32[]{:S(2)}, u32[]{:S(2)}) %all-to-all-start) | async-done | bytes 65568 | tf_op jit(solution)/shard_map/all_to_all | solution.py:643
  193.5 5.2 %shard_map.81 = bf16[4,8,4,64,128]{4,3,2,1,0:T(8,128)(2,1)} custom-call(s32[2]{0:T(128)S(1)} %pad_add_fusion.here, bf16[4,4,2,32,256]{4,3,2,1,0:T(8,128)(2,1)S(1)} %copy-done.12, bf16[4,1,2,32,256]{4,3,2,1,0:T(8,128)(2,1)S(1)} %collective-permute-done.18.plane, bf16[4,5,1,32,256]{4,3,2,1,0:T(8,128)(2,1)S(1)} %collective-permute-done.19.row, ...), custom_call_target="tpu_custom_call" | custom-call | flops 1811939328 | bytes 4915208 | tf_op jit(solution)/shard_map/pallas_call | solution.py:119
  (162 shorter events, 83.1 us)
Async XLA Ops:
  1.5 12.3 %collective-permute-start.7 = (bf16[7,32,128]{2,1,0:T(8,128)(2,1)S(1)}, bf16[7,32,128]{2,1,0:T(8,128)(2,1)S(1)}, u32[]{:S(2)}, u32[]{:S(2)}) collective-permute-start(bf16[7,32,128]{2,1,0:T(8,128)(2,1)S(1)} %pad_dynamic-slice_fusion.2), channel_id=1, source_target_pairs={{0,4},{1,5},{2,6},{3,7},{4,0},{5,1},{6,2},{7,3},{8,12},{9,13},{10,... | collective-permute-start | bytes 172040 | tf_op jit(solution)/shard_map/ppermute | solution.py:73
  9.3 15.6 %collective-permute-start.1 = (bf16[11,32,256]{2,1,0:T(8,128)(2,1)S(1)}, bf16[11,32,256]{2,1,0:T(8,128)(2,1)S(1)}, u32[]{:S(2)}, u32[]{:S(2)}) collective-permute-start(bf16[11,32,256]{2,1,0:T(8,128)(2,1)S(1)} %get-tuple-element.58), channel_id=1, source_target_pairs={{0,4},{1,5},{2,6},{3,7},{4,0},{5,1},{6,2},{7,3},{8,12},{9,13},{10,... | collective-permute-start | bytes 540680 | tf_op jit(solution)/shard_map/ppermute | solution.py:73
  11.3 13.6 %collective-permute-start = (bf16[11,32,256]{2,1,0:T(8,128)(2,1)S(1)}, bf16[11,32,256]{2,1,0:T(8,128)(2,1)S(1)}, u32[]{:S(2)}, u32[]{:S(2)}) collective-permute-start(bf16[11,32,256]{2,1,0:T(8,128)(2,1)S(1)} %get-tuple-element.58), channel_id=1, source_target_pairs={{0,2},{1,3},{2,0},{3,1},{4,6},{5,7},{6,4},{7,5},{8,10},{9,11},{10,... | collective-permute-start | bytes 540680 | tf_op jit(solution)/shard_map/ppermute | solution.py:73
  13.8 11.1 %collective-permute-start.2 = (bf16[11,32,256]{2,1,0:T(8,128)(2,1)S(1)}, bf16[11,32,256]{2,1,0:T(8,128)(2,1)S(1)}, u32[]{:S(2)}, u32[]{:S(2)}) collective-permute-start(bf16[11,32,256]{2,1,0:T(8,128)(2,1)S(1)} %get-tuple-element.58), channel_id=1, source_target_pairs={{0,6},{1,7},{2,4},{3,5},{4,2},{5,3},{6,0},{7,1},{8,14},{9,15},{10,... | collective-permute-start | bytes 540680 | tf_op jit(solution)/shard_map/ppermute | solution.py:73
  14.2 13.4 %collective-permute-start.9 = (bf16[4,7,32,128]{3,2,1,0:T(8,128)(2,1)S(1)}, bf16[4,7,32,128]{3,2,1,0:T(8,128)(2,1)S(1)}, u32[]{:S(2)}, u32[]{:S(2)}) collective-permute-start(bf16[4,7,32,128]{3,2,1,0:T(8,128)(2,1)S(1)} %get-tuple-element.56), channel_id=1, source_target_pairs={{0,1},{1,0},{2,3},{3,2},{4,5},{5,4},{6,7},{7,6},{8,9},{9,8},{10,11... | collective-permute-start | bytes 688136 | tf_op jit(solution)/shard_map/ppermute | solution.py:41
  26.1 23.5 %collective-permute-start.3 = (bf16[4,11,32,256]{3,2,1,0:T(8,128)(2,1)}, bf16[4,11,32,256]{3,2,1,0:T(8,128)(2,1)}, u32[]{:S(2)}, u32[]{:S(2)}) collective-permute-start(bf16[4,11,32,256]{3,2,1,0:T(8,128)(2,1)} %get-tuple-element.38), channel_id=1, source_target_pairs={{0,1},{1,0},{2,3},{3,2},{4,5},{5,4},{6,7},{7,6},{8,9},{9,8},{10,11... | collective-permute-start | bytes 2162696 | tf_op jit(solution)/shard_map/ppermute | solution.py:41
  28.6 12.7 %collective-permute-start.10 = (bf16[2,4,7,32,128]{4,3,2,1,0:T(8,128)(2,1)}, bf16[2,4,7,32,128]{4,3,2,1,0:T(8,128)(2,1)}, u32[]{:S(2)}, u32[]{:S(2)}) collective-permute-start(bf16[2,4,7,32,128]{4,3,2,1,0:T(8,128)(2,1)} %get-tuple-element.52), channel_id=1, source_target_pairs={{0,16},{8,24},{16,0},{24,8},{1,17},{9,25},{17,1},{25,9},{2,18},{10... | collective-permute-start | bytes 1376264 | tf_op jit(solution)/shard_map/ppermute | solution.py:41
  33.5 41.4 %collective-permute-start.13 = (bf16[4,9,1,64,128]{4,3,2,1,0:T(8,128)(2,1)}, bf16[4,9,1,64,128]{4,3,2,1,0:T(8,128)(2,1)}, u32[]{:S(2)}, u32[]{:S(2)}) collective-permute-start(bf16[4,9,1,64,128]{4,3,2,1,0:T(8,128)(2,1)} %pad_maximum_fusion.7), channel_id=1, source_target_pairs={{0,1},{1,2},{2,3},{3,4},{4,5},{5,6},{6,7},{8,9},{9,10},{10,11},{11... | collective-permute-start | bytes 1769480 | tf_op jit(solution)/shard_map/ppermute | solution.py:36
  43.7 15.4 %collective-permute-start.11 = (bf16[2,2,4,7,32,128]{5,4,3,2,1,0:T(8,128)(2,1)}, bf16[2,2,4,7,32,128]{5,4,3,2,1,0:T(8,128)(2,1)}, u32[]{:S(2)}, u32[]{:S(2)}) collective-permute-start(bf16[2,2,4,7,32,128]{5,4,3,2,1,0:T(8,128)(2,1)} %get-tuple-element.37), channel_id=1, source_target_pairs={{0,8},{8,0},{16,24},{24,16},{1,9},{9,1},{17,25},{25,17},{2,10},{10... | collective-permute-start | bytes 2752520 | tf_op jit(solution)/shard_map/ppermute | solution.py:41
  54.8 35.1 %collective-permute-start.4 = (bf16[2,4,7,32,256]{4,3,2,1,0:T(8,128)(2,1)S(1)}, bf16[2,4,7,32,256]{4,3,2,1,0:T(8,128)(2,1)S(1)}, u32[]{:S(2)}, u32[]{:S(2)}) collective-permute-start(bf16[2,4,7,32,256]{4,3,2,1,0:T(8,128)(2,1)S(1)} %fusion), channel_id=1, source_target_pairs={{0,16},{8,24},{16,0},{24,8},{1,17},{9,25},{17,1},{25,9},{2,18},{10... | collective-permute-start | bytes 2752520 | tf_op jit(solution)/shard_map/ppermute | solution.py:41
  65.2 35.0 %collective-permute-start.15 = (bf16[4,4,1,32,256]{4,3,2,1,0:T(8,128)(2,1)}, bf16[4,4,1,32,256]{4,3,2,1,0:T(8,128)(2,1)}, u32[]{:S(2)}, u32[]{:S(2)}) collective-permute-start(bf16[4,4,1,32,256]{4,3,2,1,0:T(8,128)(2,1)} %shard_map.77.high), channel_id=1, source_target_pairs={{0,1},{1,2},{2,3},{3,4},{4,5},{5,6},{6,7},{8,9},{9,10},{10,11},{11... | collective-permute-start | bytes 786440 | tf_op jit(solution)/shard_map/ppermute | solution.py:36
  72.9 27.2 %collective-permute-start.16 = (bf16[4,1,1,32,256]{4,3,2,1,0:T(8,128)(2,1)}, bf16[4,1,1,32,256]{4,3,2,1,0:T(8,128)(2,1)}, u32[]{:S(2)}, u32[]{:S(2)}) collective-permute-start(bf16[4,1,1,32,256]{4,3,2,1,0:T(8,128)(2,1)} %slice.195), channel_id=1, source_target_pairs={{0,9},{1,10},{2,11},{3,12},{4,13},{5,14},{6,15},{8,17},{9,18},{10,... | collective-permute-start | bytes 196616 | tf_op jit(solution)/shard_map/ppermute | solution.py:36
  81.2 18.9 %collective-permute-start.14 = (bf16[4,1,2,32,256]{4,3,2,1,0:T(8,128)(2,1)}, bf16[4,1,2,32,256]{4,3,2,1,0:T(8,128)(2,1)}, u32[]{:S(2)}, u32[]{:S(2)}) collective-permute-start(bf16[4,1,2,32,256]{4,3,2,1,0:T(8,128)(2,1)} %pad_maximum_fusion.21), channel_id=1, source_target_pairs={{0,8},{1,9},{2,10},{3,11},{4,12},{5,13},{6,14},{7,15},{8,16},{9,17... | collective-permute-start | bytes 393224 | tf_op jit(solution)/shard_map/ppermute | solution.py:36
  92.0 18.8 %collective-permute-start.5 = (bf16[2,2,4,7,32,256]{5,4,3,2,1,0:T(8,128)(2,1)}, bf16[2,2,4,7,32,256]{5,4,3,2,1,0:T(8,128)(2,1)}, u32[]{:S(2)}, u32[]{:S(2)}) collective-permute-start(bf16[2,2,4,7,32,256]{5,4,3,2,1,0:T(8,128)(2,1)} %get-tuple-element.35), channel_id=1, source_target_pairs={{0,8},{8,0},{16,24},{24,16},{1,9},{9,1},{17,25},{25,17},{2,10},{10... | collective-permute-start | bytes 5505032 | tf_op jit(solution)/shard_map/ppermute | solution.py:41
  115.3 12.5 %collective-permute-start.24 = (bf16[2,4,7,32,128]{4,3,2,1,0:T(8,128)(2,1)S(1)}, bf16[2,4,7,32,128]{4,3,2,1,0:T(8,128)(2,1)S(1)}, u32[]{:S(2)}, u32[]{:S(2)}) collective-permute-start(bf16[2,4,7,32,128]{4,3,2,1,0:T(8,128)(2,1)S(1)} %slice_bitcast_fusion.5), channel_id=1, source_target_pairs={{0,16},{8,24},{16,0},{24,8},{1,17},{9,25},{17,1},{25,9},{2,18},{10... | collective-permute-start | bytes 1376264 | tf_op jit(solution)/shard_map/ppermute | solution.py:41
  117.5 12.7 %collective-permute-start.26 = (bf16[2,4,7,32,128]{4,3,2,1,0:T(8,128)(2,1)S(1)}, bf16[2,4,7,32,128]{4,3,2,1,0:T(8,128)(2,1)S(1)}, u32[]{:S(2)}, u32[]{:S(2)}) collective-permute-start(bf16[2,4,7,32,128]{4,3,2,1,0:T(8,128)(2,1)S(1)} %slice_bitcast_fusion.3), channel_id=1, source_target_pairs={{0,1},{1,0},{2,3},{3,2},{4,5},{5,4},{6,7},{7,6},{8,9},{9,8},{10,11... | collective-permute-start | bytes 1376264 | tf_op jit(solution)/shard_map/ppermute | solution.py:41
  130.5 8.5 %collective-permute-start.27 = (bf16[4,7,32,128]{3,2,1,0:T(8,128)(2,1)S(1)}, bf16[4,7,32,128]{3,2,1,0:T(8,128)(2,1)S(1)}, u32[]{:S(2)}, u32[]{:S(2)}) collective-permute-start(bf16[4,7,32,128]{3,2,1,0:T(8,128)(2,1)S(1)} %fusion.12), channel_id=1, source_target_pairs={{0,16},{8,24},{16,0},{24,8},{1,17},{9,25},{17,1},{25,9},{2,18},{10... | collective-permute-start | bytes 688136 | tf_op jit(solution)/shard_map/ppermute | solution.py:41
  131.1 16.1 %collective-permute-start.21 = (bf16[2,4,7,32,128]{4,3,2,1,0:T(8,128)(2,1)S(1)}, bf16[2,4,7,32,128]{4,3,2,1,0:T(8,128)(2,1)S(1)}, u32[]{:S(2)}, u32[]{:S(2)}) collective-permute-start(bf16[2,4,7,32,128]{4,3,2,1,0:T(8,128)(2,1)S(1)} %bitcast.159), channel_id=1, source_target_pairs={{0,16},{8,24},{16,0},{24,8},{1,17},{9,25},{17,1},{25,9},{2,18},{10... | collective-permute-start | bytes 1376264 | tf_op jit(solution)/shard_map/ppermute | solution.py:41
  133.0 15.1 %collective-permute-start.25 = (bf16[4,7,32,128]{3,2,1,0:T(8,128)(2,1)S(1)}, bf16[4,7,32,128]{3,2,1,0:T(8,128)(2,1)S(1)}, u32[]{:S(2)}, u32[]{:S(2)}) collective-permute-start(bf16[4,7,32,128]{3,2,1,0:T(8,128)(2,1)S(1)} %fusion.11), channel_id=1, source_target_pairs={{0,1},{1,0},{2,3},{3,2},{4,5},{5,4},{6,7},{7,6},{8,9},{9,8},{10,11... | collective-permute-start | bytes 688136 | tf_op jit(solution)/shard_map/ppermute | solution.py:41
  154.4 15.6 %collective-permute-start.29 = (bf16[21,32,128]{2,1,0:T(8,128)(2,1)S(1)}, bf16[21,32,128]{2,1,0:T(8,128)(2,1)S(1)}, u32[]{:S(2)}, u32[]{:S(2)}) collective-permute-start(bf16[21,32,128]{2,1,0:T(8,128)(2,1)S(1)} %get-tuple-element.50), channel_id=1, source_target_pairs={{0,4},{1,5},{2,6},{3,7},{4,0},{5,1},{6,2},{7,3},{8,12},{9,13},{10,... | collective-permute-start | bytes 516104 | tf_op jit(solution)/shard_map/ppermute | solution.py:73
  157.3 16.2 %collective-permute-start.18 = (bf16[4,1,2,32,256]{4,3,2,1,0:T(8,128)(2,1)S(1)}, bf16[4,1,2,32,256]{4,3,2,1,0:T(8,128)(2,1)S(1)}, u32[]{:S(2)}, u32[]{:S(2)}) collective-permute-start(bf16[4,1,2,32,256]{4,3,2,1,0:T(8,128)(2,1)S(1)} %get-tuple-element.17), channel_id=1, source_target_pairs={{8,0},{9,1},{10,2},{11,3},{12,4},{13,5},{14,6},{15,7},{16,8},{17,9... | collective-permute-start | bytes 393224 | tf_op jit(solution)/shard_map/ppermute | solution.py:36
  174.3 19.2 %collective-permute-start.19 = (bf16[4,5,1,32,256]{4,3,2,1,0:T(8,128)(2,1)}, bf16[4,5,1,32,256]{4,3,2,1,0:T(8,128)(2,1)S(1)}, u32[]{:S(2)}, u32[]{:S(2)}) collective-permute-start(bf16[4,5,1,32,256]{4,3,2,1,0:T(8,128)(2,1)} %pad_maximum_fusion.14), channel_id=1, source_target_pairs={{1,0},{2,1},{3,2},{4,3},{5,4},{6,5},{7,6},{9,8},{10,9},{11,10},{12... | collective-permute-start | bytes 983048 | tf_op jit(solution)/shard_map/ppermute | solution.py:36
  178.0 20.8 %collective-permute-start.32 = (bf16[2,21,32,128]{3,2,1,0:T(8,128)(2,1)}, bf16[2,21,32,128]{3,2,1,0:T(8,128)(2,1)}, u32[]{:S(2)}, u32[]{:S(2)}) collective-permute-start(bf16[2,21,32,128]{3,2,1,0:T(8,128)(2,1)} %get-tuple-element.54), channel_id=1, source_target_pairs={{0,8},{8,0},{16,24},{24,16},{1,9},{9,1},{17,25},{25,17},{2,10},{10... | collective-permute-start | bytes 1032200 | tf_op jit(solution)/shard_map/ppermute | solution.py:41
  181.8 10.3 %all-to-all-start = ((bf16[8,2,2048]{2,1,0:T(2,128)(2,1)}), bf16[8,2,2048]{2,1,0:T(2,128)(2,1)S(1)}, u32[]{:S(2)}, u32[]{:S(2)}) async-start(bf16[8,2,2048]{2,1,0:T(2,128)(2,1)} %reshape.108), calls=%async_computation | async-start | bytes 131072 | tf_op jit(solution)/shard_map/all_to_all | solution.py:643
  (32 other events, 202.8 us)

commit v4 on v3

--- a/solution.py
+++ b/solution.py
@@ -582,24 +582,41 @@
     )[0]
 
 
-def near_cells(value, shape):
-    chan = lax.axis_size("chan")
-    vols, side_a, side_b, side_c, mine = shape
-    rows = side_b // chan
-    value = value.reshape(chan, vols, side_a, side_b, side_c * mine)
-    value = jnp.pad(value, ((0, 0), (0, 0), (0, 0), (0, 1), (0, 0)))
-    value = lax.dynamic_slice_in_dim(value, lax.axis_index("chan") * rows, rows + 1, 3)
-    count = bits("chan")
-    value = value.reshape((2,) * count + value.shape[1:])
-    for dim, bit in enumerate([0] + far_bits()):
-        mine_bit = (lax.axis_index("chan") >> bit) & 1
-        value = jnp.where(mine_bit == 1, jnp.flip(value, dim), value)
-    value = jnp.transpose(value, (*range(1, count), 0, *range(count, value.ndim)))
-    value = value.reshape(chan, vols, side_a, rows + 1, side_c, mine)
-    value = jnp.transpose(value, (1, 2, 3, 4, 0, 5))
-    near = value.reshape(vols, side_a, rows + 1, side_c, chan * mine)
-    plane = shifted(near[:, :1], (-1, 0))
-    return near[:, :, :rows], jnp.concatenate([near, plane], axis=1)
+class CellExchange:
+    def __init__(self, cotangent):
+        vols, side_a, side_b, side_c, mine = cotangent.shape
+        self.count = bits("chan")
+        self.tail = (side_b // 2**self.count, vols, side_a, side_c, mine)
+        flat = cotangent.reshape(vols, side_a, side_b, side_c * mine)
+        flat = jnp.transpose(flat, (2, 0, 1, 3))
+        self.value = flat.reshape((2,) * self.count + (-1,) + flat.shape[1:])
+        self.open = list(reversed(range(self.count)))
+        self.done = []
+
+    def stage(self, bit):
+        dim = self.open.index(bit)
+        mine = (lax.axis_index("chan") >> bit) & 1
+        keep = lax.dynamic_index_in_dim(self.value, mine, dim, keepdims=False)
+        send = lax.dynamic_index_in_dim(self.value, 1 - mine, dim, keepdims=False)
+        other = swapped(send, "chan", bit)
+        low, high = jnp.where(mine == 1, other, keep), jnp.where(mine == 1, keep, other)
+        self.value = jnp.stack([low, high], axis=self.count - 1)
+        self.open.remove(bit)
+        self.done.append(bit)
+
+    def finish(self):
+        rows, vols, side_a, side_c, mine = self.tail
+        count = self.count
+        value = self.value.reshape((2,) * count + (rows, vols, side_a, side_c, mine))
+        sources = [self.done.index(bit) for bit in reversed(range(count))]
+        value = jnp.transpose(
+            value, (count + 1, count + 2, count, count + 3, *sources, count + 4)
+        )
+        own = value.reshape(vols, side_a, rows, side_c, 2**count * mine)
+        row = shifted(own[:, :, :1], (0, -1))
+        near = jnp.concatenate([own, row], axis=2)
+        plane = shifted(near[:, :1], (-1, 0))
+        return own, jnp.concatenate([near, plane], axis=1)
 
 
 def local(volume, w_first, w_second, cotangent):
@@ -612,13 +629,12 @@
     first_full = near_gather(doubled(part, "chan", 0))
     row = jnp.concatenate([plane, volume], axis=1)[:, :, -1:]
     row = shifted(row, (0, 1))
-    second = own_part(w_second)
-    taps = second.shape[0]
-    riders = cotangent.reshape((-1,) + second.shape[1:])
-    part = far_gather(jnp.concatenate([second, riders], axis=0))
-    part = doubled(part, "chan", 0)
-    second_full = near_gather(part[:, :, :taps])
-    grad_cells, grad_ext = near_cells(part[:, :, taps:], cotangent.shape)
+    part = far_gather(own_part(w_second))
+    second_full = near_gather(doubled(part, "chan", 0))
+    cells = CellExchange(cotangent)
+    for bit in far_bits() + [0]:
+        cells.stage(bit)
+    grad_cells, grad_ext = cells.finish()
 
     vol_main = parted_volume(volume, plane)
     (high,) = forward(here, (vol_main,), first_full, orders, range(1, side_b), "high")
@@ -636,8 +652,9 @@
     first_sum = plain_sum(core_sum(keep, send))
     first_grad, second_grad = finish_sum([first_sum, second_sum])
     plane = shifted(pre_plane, (-1, 0))
-    row = jnp.concatenate([pre_row, plane[:, :, :1]], axis=1)
-    row = shifted(row, (0, -1))
+    row = shifted(pre_row, (0, -1))
+    corner = shifted(pre_row[:, :1], (-1, -1))
+    row = jnp.concatenate([row, corner], axis=1)
     out_b = range(grad_cells.shape[2])
     (local_out,) = forward(here, (act_parts,), second_full, orders, out_b, "out")
     second_out = lax.all_to_all(local_out, "chan", split_axis=4, concat_axis=2, tiled=True)

time: 204 us -> 204 us (level)
  waiting for transfers between devices: 59.2 us -> 69.2 us
  other arithmetic: 22.4 us -> 14.5 us
  starting transfers between devices: 67.9 us -> 65.5 us
    ppermute x16 -> x19, waiting for transfers between devices: 28.8 us -> 44.2 us  [swapped(): return lax.ppermute(value, axis, [(i, i ^ 1 << bit) for i in range(count)])]
    another operation x11 -> x10, other arithmetic: 14.9 us -> 7.27 us  [doubled(): return jnp.stack([value, other])]
    ppermute x8 -> x10, starting transfers between devices: 27 us -> 21.8 us  [shifted(): return lax.ppermute(value, ('space', 'chan'), pairs)]
    ppermute x9, waiting for transfers between devices: 20.5 us -> 15.4 us  [far_swapped(): lax.ppermute(value, 'chan', [(i, i ^ mask << 1) for i in range(count)])]
    reshape x4 -> x3, local copies, waits for them, and re-layouts: 7.35 us -> 3.03 us  [the longest x1 1.8 us: finish(): own = value.reshape(vols, side_a, rows, side_c, 2 ** count * mine)]
    all_to_all x1, waiting for transfers between devices: 6.9 us -> 2.91 us  [local(): lax.all_to_all(local_out, 'chan', split_axis=4, concat_axis=2, tiled=True)]
    ppermute x8 -> x10, waiting for transfers between devices: 2.93 us -> 6.72 us  [shifted(): return lax.ppermute(value, ('space', 'chan'), pairs)]
    all_to_all x1, starting transfers between devices: 3.35 us -> 6.65 us  [local(): lax.all_to_all(local_out, 'chan', split_axis=4, concat_axis=2, tiled=True)]
  transfers between devices with their start and end apart: 34 -> 39, of which waited for: 14 -> 15; matrix products, arithmetic and copies ran while one was open for 18% -> 13% of each run, Pallas kernels for 14% -> 14%
where the time goes in v4:
time: 204 us; the launch traced here: 203 us
  waiting for transfers between devices  69.2 us (34%)
  starting transfers between devices  65.5 us (32%)
  Pallas kernels  28.4 us (14%)
  local copies, waits for them, and re-layouts  23.8 us (12%)
  other arithmetic  14.5 us (7%)
    ppermute x19, waiting for transfers between devices, swapped(): return lax.ppermute(value, axis, [(i, i ^ 1 << bit) for i in range(count)])  44.2 us
    pallas_call x8, Pallas kernels, call(): pl.pallas_call(kernel, out_shape=outs, grid=grid or (), in_specs=specs, o...  28.4 us
    ppermute x10, starting transfers between devices, shifted(): return lax.ppermute(value, ('space', 'chan'), pairs)  21.8 us
    ppermute x19, starting transfers between devices, swapped(): return lax.ppermute(value, axis, [(i, i ^ 1 << bit) for i in range(count)])  21.7 us
    ppermute x9, waiting for transfers between devices, far_swapped(): lax.ppermute(value, 'chan', [(i, i ^ mask << 1) for i in range(count)])  15.4 us
    ppermute x9, starting transfers between devices, far_swapped(): lax.ppermute(value, 'chan', [(i, i ^ mask << 1) for i in range(count)])  15.3 us
    another operation x10, other arithmetic, doubled(): return jnp.stack([value, other])  7.27 us
    unnamed x39, local copies, waits for them, and re-layouts  7.18 us
  transfers between devices with their start and end apart: 39, of which 15 were waited for; matrix products, arithmetic and copies ran while one was open for 13% of the time, Pallas kernels for 14%

profile of v4, /device:TPU:0, one launch (start us, length us, event | category | flops | bytes accessed | tf_op | source)
XLA Modules:
  0.0 202.7 jit_solution(5532561647837496461)
XLA Ops:
  1.6 4.1 %collective-permute-start.10 = (bf16[7,32,128]{2,1,0:T(8,128)(2,1)S(1)}, bf16[7,32,128]{2,1,0:T(8,128)(2,1)S(1)}, u32[]{:S(2)}, u32[]{:S(2)}) collective-permute-start(bf16[7,32,128]{2,1,0:T(8,128)(2,1)S(1)} %pad_dynamic-slice_fusion.1), channel_id=1, source_target_pairs={{0,4},{1,5},{2,6},{3,7},{4,0},{5,1},{6,2},{7,3},{8,12},{9,13},{10,... | collective-permute-start | bytes 172040 | tf_op jit(solution)/shard_map/ppermute | solution.py:73
  10.2 2.5 %collective-permute-start = (bf16[7,32,256]{2,1,0:T(8,128)(2,1)S(1)}, bf16[7,32,256]{2,1,0:T(8,128)(2,1)S(1)}, u32[]{:S(2)}, u32[]{:S(2)}) collective-permute-start(bf16[7,32,256]{2,1,0:T(8,128)(2,1)S(1)} %pad_dynamic-slice_fusion), channel_id=1, source_target_pairs={{0,2},{1,3},{2,0},{3,1},{4,6},{5,7},{6,4},{7,5},{8,10},{9,11},{10,... | collective-permute-start | bytes 344072 | tf_op jit(solution)/shard_map/ppermute | solution.py:73
  27.5 6.8 %collective-permute-done.3 = bf16[4,7,32,256]{3,2,1,0:T(8,128)(2,1)S(1)} collective-permute-done((bf16[4,7,32,256]{3,2,1,0:T(8,128)(2,1)S(1)}, bf16[4,7,32,256]{3,2,1,0:T(8,128)(2,1)S(1)}, u32[]{:S(2)}, u32[]{:S(2)}) %collective-permute-start.3) | collective-permute-done | bytes 458784 | tf_op jit(solution)/shard_map/ppermute | solution.py:41
  37.4 2.5 %collective-permute-start.16 = (bf16[4,9,1,64,128]{4,3,2,1,0:T(8,128)(2,1)S(1)}, bf16[4,9,1,64,128]{4,3,2,1,0:T(8,128)(2,1)S(1)}, u32[]{:S(2)}, u32[]{:S(2)}) collective-permute-start(bf16[4,9,1,64,128]{4,3,2,1,0:T(8,128)(2,1)S(1)} %pad_maximum_fusion.7), channel_id=1, source_target_pairs={{0,1},{1,2},{2,3},{3,4},{4,5},{5,6},{6,7},{8,9},{9,10},{10,11},{11... | collective-permute-start | bytes 1769480 | tf_op jit(solution)/shard_map/ppermute | solution.py:36
  41.6 14.4 %collective-permute-done.4 = bf16[2,4,7,32,256]{4,3,2,1,0:T(8,128)(2,1)S(1)} collective-permute-done((bf16[2,4,7,32,256]{4,3,2,1,0:T(8,128)(2,1)S(1)}, bf16[2,4,7,32,256]{4,3,2,1,0:T(8,128)(2,1)S(1)}, u32[]{:S(2)}, u32[]{:S(2)}) %collective-permute-start.4) | collective-permute-done | bytes 917536 | tf_op jit(solution)/shard_map/ppermute | solution.py:41
  58.2 3.2 %shard_map.77.high = bf16[4,4,1,32,256]{4,3,2,1,0:T(8,128)(2,1)} custom-call(s32[2]{0:T(128)S(1)} %pad_add_fusion.here, bf16[4,8,7,32,128]{4,3,2,1,0:T(8,128)(2,1)S(1)} %bitcast.174, bf16[3,4,9,4,32,128]{5,4,3,2,1,0:T(8,128)(2,1)S(1)} %shard_map.75.main), custom_call_target="tpu_custom_call" | custom-call | flops 905969664 | bytes 5636104 | tf_op jit(solution)/shard_map/pallas_call | solution.py:119
  62.3 3.4 %collective-permute-start.18 = (bf16[4,4,1,32,256]{4,3,2,1,0:T(8,128)(2,1)}, bf16[4,4,1,32,256]{4,3,2,1,0:T(8,128)(2,1)}, u32[]{:S(2)}, u32[]{:S(2)}) collective-permute-start(bf16[4,4,1,32,256]{4,3,2,1,0:T(8,128)(2,1)} %shard_map.77.high), channel_id=1, source_target_pairs={{0,1},{1,2},{2,3},{3,4},{4,5},{5,6},{6,7},{8,9},{9,10},{10,11},{11... | collective-permute-start | bytes 786440 | tf_op jit(solution)/shard_map/ppermute | solution.py:36
  65.7 2.7 %shard_map.76 = (bf16[4,4,1,32,256]{4,3,2,1,0:T(8,128)(2,1)S(1)}, bf16[3,4,9,1,32,128]{5,4,3,2,1,0:T(8,128)(2,1)S(1)}) custom-call(s32[2]{0:T(128)S(1)} %pad_add_fusion.here, bf16[4,8,7,32,128]{4,3,2,1,0:T(8,128)(2,1)S(1)} %bitcast.175, bf16[3,4,9,4,32,128]{5,4,3,2,1,0:T(8,128)(2,1)S(1)} %shard_map.75.main, ...), custom_call_target="tpu_custom_call" | custom-call | flops 905969664 | bytes 7110664 | tf_op jit(solution)/shard_map/pallas_call | solution.py:119
  70.7 2.8 %collective-permute-start.17 = (bf16[4,1,2,32,256]{4,3,2,1,0:T(8,128)(2,1)}, bf16[4,1,2,32,256]{4,3,2,1,0:T(8,128)(2,1)}, u32[]{:S(2)}, u32[]{:S(2)}) collective-permute-start(bf16[4,1,2,32,256]{4,3,2,1,0:T(8,128)(2,1)} %pad_maximum_fusion.20), channel_id=1, source_target_pairs={{0,8},{1,9},{2,10},{3,11},{4,12},{5,13},{6,14},{7,15},{8,16},{9,17... | collective-permute-start | bytes 393224 | tf_op jit(solution)/shard_map/ppermute | solution.py:36
  77.3 5.2 %collective-permute-start.19 = (bf16[4,1,1,32,256]{4,3,2,1,0:T(8,128)(2,1)}, bf16[4,1,1,32,256]{4,3,2,1,0:T(8,128)(2,1)}, u32[]{:S(2)}, u32[]{:S(2)}) collective-permute-start(bf16[4,1,1,32,256]{4,3,2,1,0:T(8,128)(2,1)} %copy-done.16), channel_id=1, source_target_pairs={{0,9},{1,10},{2,11},{3,12},{4,13},{5,14},{6,15},{8,17},{9,18},{10,... | collective-permute-start | bytes 196616 | tf_op jit(solution)/shard_map/ppermute | solution.py:36
  88.1 5.7 %shard_map.78 = (bf16[2,8,14,32,128]{4,3,2,1,0:T(8,128)(2,1)S(1)}, bf16[2,8,14,32,128]{4,3,2,1,0:T(8,128)(2,1)S(1)}, bf16[3,4,5,3,16,256]{5,4,3,2,1,0:T(8,128)(2,1)S(1)}) custom-call(s32[2]{0:T(128)S(1)} %pad_add_fusion.here, bf16[4,2,1,16,256]{4,3,2,1,0:T(8,128)(2,1)S(1)} %copy-done.7, bf16[4,4,1,32,256]{4,3,2,1,0:T(8,128)(2,1)S(1)} %copy-done.5, ...), custom_call_target="tpu_custom_call" | custom-call | flops 452984832 | bytes 6193160 | tf_op jit(solution)/shard_map/pallas_call | solution.py:119
  95.2 5.0 %collective-permute-done.20 = bf16[4,2,1,16,256]{4,3,2,1,0:T(8,128)(2,1)S(1)} collective-permute-done((bf16[4,2,1,16,256]{4,3,2,1,0:T(8,128)(2,1)S(1)}, bf16[4,2,1,16,256]{4,3,2,1,0:T(8,128)(2,1)S(1)}, u32[]{:S(2)}, u32[]{:S(2)}) %collective-permute-start.20) | collective-permute-done | bytes 65568 | tf_op jit(solution)/shard_map/ppermute | solution.py:36
  113.1 6.0 %shard_map.82 = (bf16[2,8,7,32,128]{4,3,2,1,0:T(8,128)(2,1)S(1)}, bf16[2,8,7,32,128]{4,3,2,1,0:T(8,128)(2,1)S(1)}) custom-call(s32[2]{0:T(128)S(1)} %pad_add_fusion.here, bf16[4,4,2,32,256]{4,3,2,1,0:T(8,128)(2,1)S(1)} %get-tuple-element.16.cells.grads, bf16[3,4,9,4,32,128]{5,4,3,2,1,0:T(8,128)(2,1)S(1)} %shard_map.75.main, ...), custom_call_target="tpu_custom_call" | custom-call | flops 1811939328 | bytes 6782984 | tf_op jit(solution)/shard_map/pallas_call | solution.py:119
  121.5 2.5 %collective-permute-done.31 = bf16[2,4,7,32,128]{4,3,2,1,0:T(8,128)(2,1)S(1)} collective-permute-done((bf16[2,4,7,32,128]{4,3,2,1,0:T(8,128)(2,1)S(1)}, bf16[2,4,7,32,128]{4,3,2,1,0:T(8,128)(2,1)S(1)}, u32[]{:S(2)}, u32[]{:S(2)}) %collective-permute-start.31) | collective-permute-done | bytes 458784 | tf_op jit(solution)/shard_map/ppermute | solution.py:41
  128.7 4.1 %collective-permute-done.32 = bf16[4,7,32,128]{3,2,1,0:T(8,128)(2,1)S(1)} collective-permute-done((bf16[4,7,32,128]{3,2,1,0:T(8,128)(2,1)S(1)}, bf16[4,7,32,128]{3,2,1,0:T(8,128)(2,1)S(1)}, u32[]{:S(2)}, u32[]{:S(2)}) %collective-permute-start.32) | collective-permute-done | bytes 229408 | tf_op jit(solution)/shard_map/ppermute | solution.py:41
  132.9 8.5 %collective-permute-done.26 = bf16[2,4,7,32,128]{4,3,2,1,0:T(8,128)(2,1)S(1)} collective-permute-done((bf16[2,4,7,32,128]{4,3,2,1,0:T(8,128)(2,1)S(1)}, bf16[2,4,7,32,128]{4,3,2,1,0:T(8,128)(2,1)S(1)}, u32[]{:S(2)}, u32[]{:S(2)}) %collective-permute-start.26) | collective-permute-done | bytes 458784 | tf_op jit(solution)/shard_map/ppermute | solution.py:41
  143.2 4.8 %collective-permute-done.27 = bf16[4,7,32,128]{3,2,1,0:T(8,128)(2,1)S(1)} collective-permute-done((bf16[4,7,32,128]{3,2,1,0:T(8,128)(2,1)S(1)}, bf16[4,7,32,128]{3,2,1,0:T(8,128)(2,1)S(1)}, u32[]{:S(2)}, u32[]{:S(2)}) %collective-permute-start.27) | collective-permute-done | bytes 229408 | tf_op jit(solution)/shard_map/ppermute | solution.py:41
  149.9 3.0 %collective-permute-start.35 = (bf16[21,32,128]{2,1,0:T(8,128)(2,1)S(1)}, bf16[21,32,128]{2,1,0:T(8,128)(2,1)S(1)}, u32[]{:S(2)}, u32[]{:S(2)}) collective-permute-start(bf16[21,32,128]{2,1,0:T(8,128)(2,1)S(1)} %get-tuple-element.53), channel_id=1, source_target_pairs={{0,6},{1,7},{2,4},{3,5},{4,2},{5,3},{6,0},{7,1},{8,14},{9,15},{10,... | collective-permute-start | bytes 516104 | tf_op jit(solution)/shard_map/ppermute | solution.py:73
  153.0 2.6 %collective-permute-done.33 = bf16[21,32,128]{2,1,0:T(8,128)(2,1)S(1)} collective-permute-done((bf16[21,32,128]{2,1,0:T(8,128)(2,1)S(1)}, bf16[21,32,128]{2,1,0:T(8,128)(2,1)S(1)}, u32[]{:S(2)}, u32[]{:S(2)}) %collective-permute-start.33) | collective-permute-done | bytes 172064 | tf_op jit(solution)/shard_map/ppermute | solution.py:73
  155.6 5.0 %collective-permute-done.35 = bf16[21,32,128]{2,1,0:T(8,128)(2,1)S(1)} collective-permute-done((bf16[21,32,128]{2,1,0:T(8,128)(2,1)S(1)}, bf16[21,32,128]{2,1,0:T(8,128)(2,1)S(1)}, u32[]{:S(2)}, u32[]{:S(2)}) %collective-permute-start.35) | collective-permute-done | bytes 172064 | tf_op jit(solution)/shard_map/ppermute | solution.py:73
  160.7 5.5 %collective-permute-done.34 = bf16[21,32,128]{2,1,0:T(8,128)(2,1)S(1)} collective-permute-done((bf16[21,32,128]{2,1,0:T(8,128)(2,1)S(1)}, bf16[21,32,128]{2,1,0:T(8,128)(2,1)S(1)}, u32[]{:S(2)}, u32[]{:S(2)}) %collective-permute-start.34) | collective-permute-done | bytes 172064 | tf_op jit(solution)/shard_map/ppermute | solution.py:73
  176.0 6.6 %all-to-all-start = ((bf16[8,2,2048]{2,1,0:T(2,128)(2,1)}), bf16[8,2,2048]{2,1,0:T(2,128)(2,1)}, u32[]{:S(2)}, u32[]{:S(2)}) async-start(bf16[8,2,2048]{2,1,0:T(2,128)(2,1)} %reshape.105), calls=%async_computation | async-start | bytes 131072 | tf_op jit(solution)/shard_map/all_to_all | solution.py:660
  186.7 2.9 %all-to-all-done = bf16[8,2,2048]{2,1,0:T(2,128)(2,1)} async-done(((bf16[8,2,2048]{2,1,0:T(2,128)(2,1)}), bf16[8,2,2048]{2,1,0:T(2,128)(2,1)}, u32[]{:S(2)}, u32[]{:S(2)}) %all-to-all-start) | async-done | bytes 65568 | tf_op jit(solution)/shard_map/all_to_all | solution.py:660
  193.0 5.2 %shard_map.81 = bf16[4,8,4,64,128]{4,3,2,1,0:T(8,128)(2,1)} custom-call(s32[2]{0:T(128)S(1)} %pad_add_fusion.here, bf16[4,4,2,32,256]{4,3,2,1,0:T(8,128)(2,1)S(1)} %copy-done.11, bf16[4,1,2,32,256]{4,3,2,1,0:T(8,128)(2,1)S(1)} %collective-permute-done.22.plane, bf16[4,5,1,32,256]{4,3,2,1,0:T(8,128)(2,1)S(1)} %pad_maximum_fusion.14.row, ...), custom_call_target="tpu_custom_call" | custom-call | flops 1811939328 | bytes 4915208 | tf_op jit(solution)/shard_map/pallas_call | solution.py:119
  (169 shorter events, 86.2 us)
Async XLA Ops:
  1.6 13.3 %collective-permute-start.10 = (bf16[7,32,128]{2,1,0:T(8,128)(2,1)S(1)}, bf16[7,32,128]{2,1,0:T(8,128)(2,1)S(1)}, u32[]{:S(2)}, u32[]{:S(2)}) collective-permute-start(bf16[7,32,128]{2,1,0:T(8,128)(2,1)S(1)} %pad_dynamic-slice_fusion.1), channel_id=1, source_target_pairs={{0,4},{1,5},{2,6},{3,7},{4,0},{5,1},{6,2},{7,3},{8,12},{9,13},{10,... | collective-permute-start | bytes 172040 | tf_op jit(solution)/shard_map/ppermute | solution.py:73
  8.2 10.0 %collective-permute-start.1 = (bf16[7,32,256]{2,1,0:T(8,128)(2,1)S(1)}, bf16[7,32,256]{2,1,0:T(8,128)(2,1)S(1)}, u32[]{:S(2)}, u32[]{:S(2)}) collective-permute-start(bf16[7,32,256]{2,1,0:T(8,128)(2,1)S(1)} %pad_dynamic-slice_fusion), channel_id=1, source_target_pairs={{0,4},{1,5},{2,6},{3,7},{4,0},{5,1},{6,2},{7,3},{8,12},{9,13},{10,... | collective-permute-start | bytes 344072 | tf_op jit(solution)/shard_map/ppermute | solution.py:73
  18.2 19.2 %collective-permute-start.15 = (bf16[4,1,4,64,128]{4,3,2,1,0:T(8,128)(2,1)S(1)}, bf16[4,1,4,64,128]{4,3,2,1,0:T(8,128)(2,1)S(1)}, u32[]{:S(2)}, u32[]{:S(2)}) collective-permute-start(bf16[4,1,4,64,128]{4,3,2,1,0:T(8,128)(2,1)S(1)} %slice.140), channel_id=1, source_target_pairs={{0,8},{1,9},{2,10},{3,11},{4,12},{5,13},{6,14},{7,15},{8,16},{9,17... | collective-permute-start | bytes 786440 | tf_op jit(solution)/shard_map/ppermute | solution.py:36
  21.8 12.5 %collective-permute-start.3 = (bf16[4,7,32,256]{3,2,1,0:T(8,128)(2,1)S(1)}, bf16[4,7,32,256]{3,2,1,0:T(8,128)(2,1)S(1)}, u32[]{:S(2)}, u32[]{:S(2)}) collective-permute-start(bf16[4,7,32,256]{3,2,1,0:T(8,128)(2,1)S(1)} %get-tuple-element.58), channel_id=1, source_target_pairs={{0,1},{1,0},{2,3},{3,2},{4,5},{5,4},{6,7},{7,6},{8,9},{9,8},{10,11... | collective-permute-start | bytes 1376264 | tf_op jit(solution)/shard_map/ppermute | solution.py:41
  23.4 12.0 %collective-permute-start.13 = (bf16[2,4,7,32,128]{4,3,2,1,0:T(8,128)(2,1)S(1)}, bf16[2,4,7,32,128]{4,3,2,1,0:T(8,128)(2,1)S(1)}, u32[]{:S(2)}, u32[]{:S(2)}) collective-permute-start(bf16[2,4,7,32,128]{4,3,2,1,0:T(8,128)(2,1)S(1)} %get-tuple-element.56), channel_id=1, source_target_pairs={{0,16},{8,24},{16,0},{24,8},{1,17},{9,25},{17,1},{25,9},{2,18},{10... | collective-permute-start | bytes 1376264 | tf_op jit(solution)/shard_map/ppermute | solution.py:41
  25.4 10.3 %collective-permute-start.7 = (bf16[2,2,1,4,2,512]{5,4,3,1,0,2:T(2,128)(2,1)S(1)}, bf16[2,2,1,4,2,512]{5,4,3,1,0,2:T(2,128)(2,1)S(1)}, u32[]{:S(2)}, u32[]{:S(2)}) collective-permute-start(bf16[2,2,1,4,2,512]{5,4,3,1,0,2:T(2,128)(2,1)S(1)} %fusion.22), channel_id=1, source_target_pairs={{0,2},{1,3},{2,0},{3,1},{4,6},{5,7},{6,4},{7,5},{8,10},{9,11},{10,... | collective-permute-start | bytes 98312 | tf_op jit(solution)/shard_map/ppermute | solution.py:41
  34.5 21.5 %collective-permute-start.4 = (bf16[2,4,7,32,256]{4,3,2,1,0:T(8,128)(2,1)S(1)}, bf16[2,4,7,32,256]{4,3,2,1,0:T(8,128)(2,1)S(1)}, u32[]{:S(2)}, u32[]{:S(2)}) collective-permute-start(bf16[2,4,7,32,256]{4,3,2,1,0:T(8,128)(2,1)S(1)} %get-tuple-element.43), channel_id=1, source_target_pairs={{0,16},{8,24},{16,0},{24,8},{1,17},{9,25},{17,1},{25,9},{2,18},{10... | collective-permute-start | bytes 2752520 | tf_op jit(solution)/shard_map/ppermute | solution.py:41
  35.5 22.5 %collective-permute-start.14 = (bf16[2,2,4,7,32,128]{5,4,3,2,1,0:T(8,128)(2,1)S(1)}, bf16[2,2,4,7,32,128]{5,4,3,2,1,0:T(8,128)(2,1)S(1)}, u32[]{:S(2)}, u32[]{:S(2)}) collective-permute-start(bf16[2,2,4,7,32,128]{5,4,3,2,1,0:T(8,128)(2,1)S(1)} %get-tuple-element.41), channel_id=1, source_target_pairs={{0,8},{8,0},{16,24},{24,16},{1,9},{9,1},{17,25},{25,17},{2,10},{10... | collective-permute-start | bytes 2752520 | tf_op jit(solution)/shard_map/ppermute | solution.py:41
  37.4 28.2 %collective-permute-start.16 = (bf16[4,9,1,64,128]{4,3,2,1,0:T(8,128)(2,1)S(1)}, bf16[4,9,1,64,128]{4,3,2,1,0:T(8,128)(2,1)S(1)}, u32[]{:S(2)}, u32[]{:S(2)}) collective-permute-start(bf16[4,9,1,64,128]{4,3,2,1,0:T(8,128)(2,1)S(1)} %pad_maximum_fusion.7), channel_id=1, source_target_pairs={{0,1},{1,2},{2,3},{3,4},{4,5},{5,6},{6,7},{8,9},{9,10},{10,11},{11... | collective-permute-start | bytes 1769480 | tf_op jit(solution)/shard_map/ppermute | solution.py:36
  58.0 45.4 %collective-permute-start.5 = (bf16[2,2,4,7,32,256]{5,4,3,2,1,0:T(8,128)(2,1)}, bf16[2,2,4,7,32,256]{5,4,3,2,1,0:T(8,128)(2,1)}, u32[]{:S(2)}, u32[]{:S(2)}) collective-permute-start(bf16[2,2,4,7,32,256]{5,4,3,2,1,0:T(8,128)(2,1)} %get-tuple-element.39), channel_id=1, source_target_pairs={{0,8},{8,0},{16,24},{24,16},{1,9},{9,1},{17,25},{25,17},{2,10},{10... | collective-permute-start | bytes 5505032 | tf_op jit(solution)/shard_map/ppermute | solution.py:41
  62.3 24.0 %collective-permute-start.18 = (bf16[4,4,1,32,256]{4,3,2,1,0:T(8,128)(2,1)}, bf16[4,4,1,32,256]{4,3,2,1,0:T(8,128)(2,1)}, u32[]{:S(2)}, u32[]{:S(2)}) collective-permute-start(bf16[4,4,1,32,256]{4,3,2,1,0:T(8,128)(2,1)} %shard_map.77.high), channel_id=1, source_target_pairs={{0,1},{1,2},{2,3},{3,4},{4,5},{5,6},{6,7},{8,9},{9,10},{10,11},{11... | collective-permute-start | bytes 786440 | tf_op jit(solution)/shard_map/ppermute | solution.py:36
  70.7 15.6 %collective-permute-start.17 = (bf16[4,1,2,32,256]{4,3,2,1,0:T(8,128)(2,1)}, bf16[4,1,2,32,256]{4,3,2,1,0:T(8,128)(2,1)}, u32[]{:S(2)}, u32[]{:S(2)}) collective-permute-start(bf16[4,1,2,32,256]{4,3,2,1,0:T(8,128)(2,1)} %pad_maximum_fusion.20), channel_id=1, source_target_pairs={{0,8},{1,9},{2,10},{3,11},{4,12},{5,13},{6,14},{7,15},{8,16},{9,17... | collective-permute-start | bytes 393224 | tf_op jit(solution)/shard_map/ppermute | solution.py:36
  93.8 14.5 %collective-permute-start.28 = (bf16[2,8,14,32,128]{4,3,2,1,0:T(8,128)(2,1)S(1)}, bf16[2,8,14,32,128]{4,3,2,1,0:T(8,128)(2,1)S(1)}, u32[]{:S(2)}, u32[]{:S(2)}) collective-permute-start(bf16[2,8,14,32,128]{4,3,2,1,0:T(8,128)(2,1)S(1)} %get-tuple-element.23), channel_id=1, source_target_pairs={{0,8},{8,0},{16,24},{24,16},{1,9},{9,1},{17,25},{25,17},{2,10},{10... | collective-permute-start | bytes 5505032 | tf_op jit(solution)/shard_map/ppermute | solution.py:41
  109.1 12.4 %collective-permute-start.29 = (bf16[2,4,7,32,128]{4,3,2,1,0:T(8,128)(2,1)S(1)}, bf16[2,4,7,32,128]{4,3,2,1,0:T(8,128)(2,1)S(1)}, u32[]{:S(2)}, u32[]{:S(2)}) collective-permute-start(bf16[2,4,7,32,128]{4,3,2,1,0:T(8,128)(2,1)S(1)} %slice_bitcast_fusion.5), channel_id=1, source_target_pairs={{0,16},{8,24},{16,0},{24,8},{1,17},{9,25},{17,1},{25,9},{2,18},{10... | collective-permute-start | bytes 1376264 | tf_op jit(solution)/shard_map/ppermute | solution.py:41
  111.0 12.9 %collective-permute-start.31 = (bf16[2,4,7,32,128]{4,3,2,1,0:T(8,128)(2,1)S(1)}, bf16[2,4,7,32,128]{4,3,2,1,0:T(8,128)(2,1)S(1)}, u32[]{:S(2)}, u32[]{:S(2)}) collective-permute-start(bf16[2,4,7,32,128]{4,3,2,1,0:T(8,128)(2,1)S(1)} %slice_bitcast_fusion.3), channel_id=1, source_target_pairs={{0,1},{1,0},{2,3},{3,2},{4,5},{5,4},{6,7},{7,6},{8,9},{9,8},{10,11... | collective-permute-start | bytes 1376264 | tf_op jit(solution)/shard_map/ppermute | solution.py:41
  124.8 16.6 %collective-permute-start.26 = (bf16[2,4,7,32,128]{4,3,2,1,0:T(8,128)(2,1)S(1)}, bf16[2,4,7,32,128]{4,3,2,1,0:T(8,128)(2,1)S(1)}, u32[]{:S(2)}, u32[]{:S(2)}) collective-permute-start(bf16[2,4,7,32,128]{4,3,2,1,0:T(8,128)(2,1)S(1)} %bitcast.193), channel_id=1, source_target_pairs={{0,16},{8,24},{16,0},{24,8},{1,17},{9,25},{17,1},{25,9},{2,18},{10... | collective-permute-start | bytes 1376264 | tf_op jit(solution)/shard_map/ppermute | solution.py:41
  126.9 16.2 %collective-permute-start.30 = (bf16[4,7,32,128]{3,2,1,0:T(8,128)(2,1)S(1)}, bf16[4,7,32,128]{3,2,1,0:T(8,128)(2,1)S(1)}, u32[]{:S(2)}, u32[]{:S(2)}) collective-permute-start(bf16[4,7,32,128]{3,2,1,0:T(8,128)(2,1)S(1)} %fusion.10), channel_id=1, source_target_pairs={{0,1},{1,0},{2,3},{3,2},{4,5},{5,4},{6,7},{7,6},{8,9},{9,8},{10,11... | collective-permute-start | bytes 688136 | tf_op jit(solution)/shard_map/ppermute | solution.py:41
  149.9 10.8 %collective-permute-start.35 = (bf16[21,32,128]{2,1,0:T(8,128)(2,1)S(1)}, bf16[21,32,128]{2,1,0:T(8,128)(2,1)S(1)}, u32[]{:S(2)}, u32[]{:S(2)}) collective-permute-start(bf16[21,32,128]{2,1,0:T(8,128)(2,1)S(1)} %get-tuple-element.53), channel_id=1, source_target_pairs={{0,6},{1,7},{2,4},{3,5},{4,2},{5,3},{6,0},{7,1},{8,14},{9,15},{10,... | collective-permute-start | bytes 516104 | tf_op jit(solution)/shard_map/ppermute | solution.py:73
  152.9 13.3 %collective-permute-start.34 = (bf16[21,32,128]{2,1,0:T(8,128)(2,1)S(1)}, bf16[21,32,128]{2,1,0:T(8,128)(2,1)S(1)}, u32[]{:S(2)}, u32[]{:S(2)}) collective-permute-start(bf16[21,32,128]{2,1,0:T(8,128)(2,1)S(1)} %get-tuple-element.54), channel_id=1, source_target_pairs={{0,4},{1,5},{2,6},{3,7},{4,0},{5,1},{6,2},{7,3},{8,12},{9,13},{10,... | collective-permute-start | bytes 516104 | tf_op jit(solution)/shard_map/ppermute | solution.py:73
  166.3 16.4 %collective-permute-start.36 = (bf16[21,32,128]{2,1,0:T(8,128)(2,1)S(1)}, bf16[21,32,128]{2,1,0:T(8,128)(2,1)S(1)}, u32[]{:S(2)}, u32[]{:S(2)}) collective-permute-start(bf16[21,32,128]{2,1,0:T(8,128)(2,1)S(1)} %fusion.8), channel_id=1, source_target_pairs={{0,16},{8,24},{16,0},{24,8},{1,17},{9,25},{17,1},{25,9},{2,18},{10... | collective-permute-start | bytes 516104 | tf_op jit(solution)/shard_map/ppermute | solution.py:41
  168.1 23.8 %collective-permute-start.23 = (bf16[4,4,1,32,256]{4,3,2,1,0:T(8,128)(2,1)}, bf16[4,4,1,32,256]{4,3,2,1,0:T(8,128)(2,1)}, u32[]{:S(2)}, u32[]{:S(2)}) collective-permute-start(bf16[4,4,1,32,256]{4,3,2,1,0:T(8,128)(2,1)} %get-tuple-element.18), channel_id=1, source_target_pairs={{1,0},{2,1},{3,2},{4,3},{5,4},{6,5},{7,6},{9,8},{10,9},{11,10},{12... | collective-permute-start | bytes 786440 | tf_op jit(solution)/shard_map/ppermute | solution.py:36
  170.9 21.0 %collective-permute-start.24 = (bf16[4,1,1,32,256]{4,3,2,1,0:T(8,128)(2,1)}, bf16[4,1,1,32,256]{4,3,2,1,0:T(8,128)(2,1)}, u32[]{:S(2)}, u32[]{:S(2)}) collective-permute-start(bf16[4,1,1,32,256]{4,3,2,1,0:T(8,128)(2,1)} %slice.145), channel_id=1, source_target_pairs={{9,0},{10,1},{11,2},{12,3},{13,4},{14,5},{15,6},{17,8},{18,9},{19,... | collective-permute-start | bytes 196616 | tf_op jit(solution)/shard_map/ppermute | solution.py:36
  176.0 13.7 %all-to-all-start = ((bf16[8,2,2048]{2,1,0:T(2,128)(2,1)}), bf16[8,2,2048]{2,1,0:T(2,128)(2,1)}, u32[]{:S(2)}, u32[]{:S(2)}) async-start(bf16[8,2,2048]{2,1,0:T(2,128)(2,1)} %reshape.105), calls=%async_computation | async-start | bytes 131072 | tf_op jit(solution)/shard_map/all_to_all | solution.py:660
  185.0 13.3 %collective-permute-start.37 = (bf16[2,21,32,128]{3,2,1,0:T(8,128)(2,1)}, bf16[2,21,32,128]{3,2,1,0:T(8,128)(2,1)}, u32[]{:S(2)}, u32[]{:S(2)}) collective-permute-start(bf16[2,21,32,128]{3,2,1,0:T(8,128)(2,1)} %get-tuple-element.60), channel_id=1, source_target_pairs={{0,8},{8,0},{16,24},{24,16},{1,9},{9,1},{17,25},{25,17},{2,10},{10... | collective-permute-start | bytes 1032200 | tf_op jit(solution)/shard_map/ppermute | solution.py:41
  (33 other events, 236.1 us)

commit v5 on v4

--- a/solution.py
+++ b/solution.py
@@ -221,13 +221,17 @@
     cells = vols * sides[1] * len(cells_b) * depth
     outs = [jax.ShapeDtypeStruct((vols, sides[1], len(cells_b), depth, count), BF16)]
     scratch = [pltpu.VMEM((cells, count), F32)]
+    if kind == "high":
+        outs.append(jax.ShapeDtypeStruct((vols, 1, 1, depth, count), BF16))
     if kind == "low":
+        high_b = parts[2].shape[2]
+        outs.append(jax.ShapeDtypeStruct((vols, 1, 1 + high_b, depth, count), BF16))
         outs.append(jax.ShapeDtypeStruct(main.shape[:3] + (1,) + main.shape[4:], BF16))
         scratch.append(part_scratch(2 * depth, inputs))
 
     def kernel(here, filters, main, *rest):
         if kind == "low":
-            row, out, row_parts, acc, wide = rest
+            row, above, out, plane, row_parts, acc, wide = rest
 
             def split(n, carry):
                 part_block(lambda a, b: row[n, a, 0], row_parts, n, (wide_a, 1, 2 * depth), wide)
@@ -236,12 +240,18 @@
             lax.fori_loop(0, vols, split, 0)
             refs = (main, row_parts)
         else:
-            out, acc = rest
+            out, acc = rest[0], rest[-1]
             refs = (main, None) if kind == "high" else (main,)
         total = forward_total(orders, sides, refs, here, filters, acc)
         if kind != "out":
             total = leaky(total)
-        out[...] = total.astype(BF16).reshape(out.shape)
+        value = total.astype(BF16).reshape(out.shape)
+        out[...] = value
+        if kind == "high":
+            rest[1][...] = value[:, -1:, -1:]
+        if kind == "low":
+            plane[:, :, :1] = value[:, -1:]
+            plane[:, :, 1:] = above[:, above.shape[1] - 1 :]
 
     return call(
         kernel,
@@ -252,15 +262,14 @@
     )
 
 
-def grads_body(orders, sides, here, grads, refs, keep, send, turned):
-    cells, count = turned.shape[1], turned.shape[0]
+def grads_body(orders, sides, here, refs, keep, send, turned):
+    count = turned.shape[0]
     inputs = refs[0].shape[5]
     pieces = inputs // LANES
     chans = 2 ** len(orders[1])
     mine = count // chans
     each = keep.shape[2] // pieces
     half = keep.shape[0]
-    turned[...] = jnp.transpose(grads[...].reshape(cells, count).astype(F32), (1, 0)).astype(BF16)
 
     def put(ref, place, tap, part):
         for chan in range(chans):
@@ -315,7 +324,9 @@
     out = grads_out(count, inputs, orders)
 
     def kernel(here, grads, main, row, keep, send, turned):
-        grads_body(orders, sides, here, grads, (main, row), keep, send, turned)
+        flat = grads[...].reshape(cells, count).astype(F32)
+        turned[...] = jnp.transpose(flat, (1, 0)).astype(BF16)
+        grads_body(orders, sides, here, (main, row), keep, send, turned)
 
     return call(
         kernel,
@@ -330,9 +341,10 @@
     low, high = blocks[:2]
     side_x, deep, inputs = low.shape[1], low.shape[3], low.shape[4]
     wide_b = low.shape[2] + high.shape[2] + 1
-    vols, side_a, side_b, depth, count = grads.shape
+    vols, side_a, side_b, depth = low.shape[0], side_x // 2, wide_b // 2, deep // 2
+    chans, mine, cells = grads.shape
+    count = chans * mine
     sides = (vols, side_a, range(side_b))
-    cells = vols * side_a * side_b * depth
     out = grads_out(count, inputs, orders)
     parts = jax.ShapeDtypeStruct((3, vols, side_x + 1, wide_b, depth, inputs), BF16)
 
@@ -349,7 +361,9 @@
             return carry
 
         lax.fori_loop(0, vols, split, 0)
-        grads_body(orders, sides, here, grads, (parts,), keep, send, turned)
+        for chan in range(chans):
+            turned[chan * mine : (chan + 1) * mine] = grads[chan ^ here[1]]
+        grads_body(orders, sides, here, (parts,), keep, send, turned)
 
     return call(
         kernel,
@@ -376,9 +390,17 @@
 
 
 def plain_sum(total):
+    total = half_sum(total, "chan", 0, bits("space") - 1)
     for bit in range(1, bits("space")):
         total = half_sum(total, "space", bit, 0)
-    return half_sum(total, "chan", 0, 0)
+    return total
+
+
+def far_sum(total):
+    part = total[0].astype(F32)
+    for m in range(1, lax.axis_size("chan") // 2):
+        part = part + far_swapped(total[m].astype(BF16), m).astype(F32)
+    return part.astype(BF16)
 
 
 def mixed_sum(total):
@@ -395,23 +417,18 @@
 
 
 def finish_sum(totals):
-    count = lax.axis_size("chan") // 2
     space = lax.axis_size("space")
-    merged = jnp.concatenate(totals, axis=1)
-    part = merged[0].astype(F32)
-    for m in range(1, count):
-        part = part + far_swapped(merged[m].astype(BF16), m).astype(F32)
-    part = part.astype(BF16)
+    part = merged = jnp.concatenate(totals, axis=0)
     for bit in high_bits():
         part = doubled(part, "space", bit)
     part = doubled(part, "space", 0)
-    part = part.reshape((space,) + merged.shape[1:])
+    part = part.reshape((space,) + merged.shape)
     apart = [jnp.int32(s) ^ lax.axis_index("space") for s in range(space)]
     ordered = [lax.dynamic_index_in_dim(part, space_order(a), 0, keepdims=False) for a in apart]
     outs, begin = [], 0
     taps = -(-27 // space)
     for total in totals:
-        rows, mine = total.shape[1], total.shape[2]
+        rows, mine = total.shape[0], total.shape[1]
         pieces = rows // taps
         full = jnp.concatenate([o[begin : begin + rows] for o in ordered], axis=0)
         full = full.reshape(space * taps, pieces, mine, LANES)[:27].astype(F32)
@@ -437,10 +454,22 @@
         store(part, rows[pl.ds(base + 1, depth), :].astype(BF16))
 
 
-def back_kernel(orders, here, cells, filters, low, high, out, plane, row, wide, moved, spread):
+def back_kernel(
+    orders, here, near, beyond, filters, low, high, out, plane, row, corner, wide, cells, moved, spread
+):
     vols, wide_a, wide_b, depth, count = cells.shape
     side_a, side_b = wide_a - 1, wide_b - 1
     inputs = filters.shape[4]
+    chans = near.shape[1]
+    for b in range(2):
+        owner = (here[1] + b) & (chans - 1)
+        for ref in (near, beyond):
+            rows = jnp.concatenate([ref[b, chan ^ owner] for chan in range(chans)], axis=0)
+            flat = jnp.transpose(rows.astype(F32), (1, 0)).astype(BF16)
+            for n in range(vols):
+                for a in range(side_a if ref is near else 1):
+                    begin = (n * side_a + a) * depth
+                    cells[n, a if ref is near else side_a, b] = flat[begin : begin + depth]
     for n in range(vols):
         for a in range(wide_a):
             for b in range(wide_b):
@@ -483,27 +512,32 @@
         out[:, :, :, :, lanes] = value
         plane[:, :, :, :, lanes] = value[:, :1]
         row[:, :, :, :, lanes] = value[:, :, :1]
-
-
-def hidden_back(here, cells, filters, low, high, orders):
-    vols, wide_a, wide_b, depth, count = cells.shape
+        corner[:, :, :, :, lanes] = value[:, :1, :1]
+
+
+def hidden_back(here, near, beyond, filters, low, high, orders):
     inputs = low.shape[-1]
     shape = low.shape[:2] + (low.shape[2] + high.shape[2],) + low.shape[3:]
+    vols, depth = shape[0], shape[3] // 2
+    count = near.shape[1] * near.shape[2]
+    ext = (vols, shape[1] // 2 + 1, shape[2] // 2 + 1, depth, count)
     outs = [
         jax.ShapeDtypeStruct(shape, BF16),
         jax.ShapeDtypeStruct((vols, 1) + shape[2:], BF16),
         jax.ShapeDtypeStruct(shape[:2] + (1,) + shape[3:], BF16),
+        jax.ShapeDtypeStruct((vols, 1, 1) + shape[3:], BF16),
     ]
     return call(
         functools.partial(back_kernel, orders),
         outs,
-        (here, cells, filters, low, high),
+        (here, near, beyond, filters, low, high),
         [
             pltpu.VMEM((count // LANES, 8 * (PAD + depth), LANES), F32),
-            pltpu.VMEM(cells.shape, BF16),
+            pltpu.VMEM(ext, BF16),
+            pltpu.VMEM(ext, BF16),
             pltpu.VMEM((inputs // LANES,) + shape[:4] + (LANES,), F32),
         ],
-        flops=2 * vols * (wide_a - 1) * (wide_b - 1) * depth * 27 * inputs * count,
+        flops=2 * vols * (ext[1] - 1) * (ext[2] - 1) * depth * 27 * inputs * count,
     )
 
 
@@ -586,12 +620,10 @@
     def __init__(self, cotangent):
         vols, side_a, side_b, side_c, mine = cotangent.shape
         self.count = bits("chan")
-        self.tail = (side_b // 2**self.count, vols, side_a, side_c, mine)
-        flat = cotangent.reshape(vols, side_a, side_b, side_c * mine)
-        flat = jnp.transpose(flat, (2, 0, 1, 3))
-        self.value = flat.reshape((2,) * self.count + (-1,) + flat.shape[1:])
+        assert side_b == 2**self.count
+        flat = jnp.transpose(cotangent, (2, 4, 0, 1, 3))
+        self.value = flat.reshape((2,) * self.count + (mine, vols * side_a * side_c))
         self.open = list(reversed(range(self.count)))
-        self.done = []
 
     def stage(self, bit):
         dim = self.open.index(bit)
@@ -599,24 +631,13 @@
         keep = lax.dynamic_index_in_dim(self.value, mine, dim, keepdims=False)
         send = lax.dynamic_index_in_dim(self.value, 1 - mine, dim, keepdims=False)
         other = swapped(send, "chan", bit)
-        low, high = jnp.where(mine == 1, other, keep), jnp.where(mine == 1, keep, other)
-        self.value = jnp.stack([low, high], axis=self.count - 1)
+        self.value = jnp.stack([keep, other], axis=self.count - 1)
         self.open.remove(bit)
-        self.done.append(bit)
 
     def finish(self):
-        rows, vols, side_a, side_c, mine = self.tail
-        count = self.count
-        value = self.value.reshape((2,) * count + (rows, vols, side_a, side_c, mine))
-        sources = [self.done.index(bit) for bit in reversed(range(count))]
-        value = jnp.transpose(
-            value, (count + 1, count + 2, count, count + 3, *sources, count + 4)
-        )
-        own = value.reshape(vols, side_a, rows, side_c, 2**count * mine)
-        row = shifted(own[:, :, :1], (0, -1))
-        near = jnp.concatenate([own, row], axis=2)
-        plane = shifted(near[:, :1], (-1, 0))
-        return own, jnp.concatenate([near, plane], axis=1)
+        own = self.value.reshape((2**self.count,) + self.value.shape[self.count :])
+        near = jnp.stack([own, shifted(own, (0, -1))])
+        return own, near, shifted(near, (-1, 0))
 
 
 def local(volume, w_first, w_second, cotangent):
@@ -634,28 +655,27 @@
     cells = CellExchange(cotangent)
     for bit in far_bits() + [0]:
         cells.stage(bit)
-    grad_cells, grad_ext = cells.finish()
+    own_cells, near_cells, beyond_cells = cells.finish()
 
     vol_main = parted_volume(volume, plane)
-    (high,) = forward(here, (vol_main,), first_full, orders, range(1, side_b), "high")
-    low, vol_row = forward(here, (vol_main, row), first_full, orders, range(1), "low")
+    high, corner = forward(here, (vol_main,), first_full, orders, range(1, side_b), "high")
+    low, hid_plane, vol_row = forward(here, (vol_main, row, high), first_full, orders, range(1), "low")
     hid_row = shifted(high[:, :, -1:], (0, 1))
-    hid_corner = shifted(high[:, -1:, -1:], (1, 1))
-    hid_plane = jnp.concatenate([low[:, -1:], high[:, -1:]], axis=2)
+    hid_corner = shifted(corner, (1, 1))
     hid_plane = shifted(hid_plane, (1, 0))
     blocks = (low, high, hid_plane, hid_row, hid_corner)
-    keep, send, act_parts = second_grads(here, blocks, grad_cells, orders)
-    second_sum = mixed_sum(core_sum(keep, send))
-
-    pre_back, pre_plane, pre_row = hidden_back(here, grad_ext, second_full, low, high, orders)
+    keep, send, act_parts = second_grads(here, blocks, own_cells, orders)
+    second_sum = far_sum(mixed_sum(core_sum(keep, send)))
+
+    pre_back, pre_plane, pre_row, corner = hidden_back(here, near_cells, beyond_cells, second_full, low, high, orders)
     keep, send = first_grads(here, (vol_main, vol_row), pre_back, orders)
-    first_sum = plain_sum(core_sum(keep, send))
+    first_sum = far_sum(plain_sum(core_sum(keep, send)))
     first_grad, second_grad = finish_sum([first_sum, second_sum])
     plane = shifted(pre_plane, (-1, 0))
     row = shifted(pre_row, (0, -1))
-    corner = shifted(pre_row[:, :1], (-1, -1))
+    corner = shifted(corner, (-1, -1))
     row = jnp.concatenate([row, corner], axis=1)
-    out_b = range(grad_cells.shape[2])
+    out_b = range(act_parts.shape[3] // 2)
     (local_out,) = forward(here, (act_parts,), second_full, orders, out_b, "out")
     second_out = lax.all_to_all(local_out, "chan", split_axis=4, concat_axis=2, tiled=True)
     volume_grad = volume_grads(here, pre_back, plane, row, first_full, orders)

time: 204 us -> 196 us (0.961)
  local copies, waits for them, and re-layouts: 23.8 us -> 10.3 us
  starting transfers between devices: 65.5 us -> 68.9 us
  waiting for transfers between devices: 69.2 us -> 72.1 us
    ppermute x19, starting transfers between devices: 21.7 us -> 28.7 us  [swapped(): return lax.ppermute(value, axis, [(i, i ^ 1 << bit) for i in range(count)])]
    unnamed x39 -> x12, local copies, waits for them, and re-layouts: 7.18 us -> 1.57 us
    ppermute x10, starting transfers between devices: 21.8 us -> 17.7 us  [shifted(): return lax.ppermute(value, ('space', 'chan'), pairs)]
    another operation x2 -> x1, local copies, waits for them, and re-layouts: 3.13 us -> 0.01 us  [stage(): self.value = jnp.stack([keep, other], axis=self.count - 1)]
    reshape x3 -> x0, local copies, waits for them, and re-layouts: 3.03 us -> none  [the longest x1 1.8 us: finish(): own = value.reshape(vols, side_a, rows, side_c, 2 ** count * mine)]
    another operation x10 -> x11, other arithmetic: 7.27 us -> 9.87 us  [doubled(): return jnp.stack([value, other])]
    slice x6 -> x0, local copies, waits for them, and re-layouts: 2.46 us -> none  [the longest x1 1.47 us: local(): corner = shifted(pre_row[:, :1], (-1, -1))]
    ppermute x9 -> x12, starting transfers between devices: 15.3 us -> 17.1 us  [far_swapped(): lax.ppermute(value, 'chan', [(i, i ^ mask << 1) for i in range(count)])]
  transfers between devices with their start and end apart: 39 -> 42, of which waited for: 15 -> 19; matrix products, arithmetic and copies ran while one was open for 13% -> 10% of each run, Pallas kernels for 14% -> 14%
where the time goes in v5:
time: 196 us
  waiting for transfers between devices  72.1 us (37%)
  starting transfers between devices  68.9 us (35%)
  Pallas kernels  26.6 us (14%)
  other arithmetic  16.3 us (8%)
  local copies, waits for them, and re-layouts  10.3 us (5%)
    ppermute x19, waiting for transfers between devices, swapped(): return lax.ppermute(value, axis, [(i, i ^ 1 << bit) for i in range(count)])  45.9 us
    ppermute x19, starting transfers between devices, swapped(): return lax.ppermute(value, axis, [(i, i ^ 1 << bit) for i in range(count)])  28.7 us
    pallas_call x8, Pallas kernels, call(): pl.pallas_call(kernel, out_shape=outs, grid=grid or (), in_specs=specs, o...  26.6 us
    ppermute x10, starting transfers between devices, shifted(): return lax.ppermute(value, ('space', 'chan'), pairs)  17.7 us
    ppermute x12, starting transfers between devices, far_swapped(): lax.ppermute(value, 'chan', [(i, i ^ mask << 1) for i in range(count)])  17.1 us
    ppermute x12, waiting for transfers between devices, far_swapped(): lax.ppermute(value, 'chan', [(i, i ^ mask << 1) for i in range(count)])  14.7 us
    another operation x11, other arithmetic, doubled(): return jnp.stack([value, other])  9.87 us
    ppermute x10, waiting for transfers between devices, shifted(): return lax.ppermute(value, ('space', 'chan'), pairs)  8.19 us
  transfers between devices with their start and end apart: 42, of which 19 were waited for; matrix products, arithmetic and copies ran while one was open for 10% of the time, Pallas kernels for 14%

profile of v5, /device:TPU:0, one launch (start us, length us, event | category | flops | bytes accessed | tf_op | source)
XLA Modules:
  0.0 195.5 jit_solution(2875531168747382258)
XLA Ops:
  1.5 4.1 %collective-permute-start.10 = (bf16[7,32,128]{2,1,0:T(8,128)(2,1)S(1)}, bf16[7,32,128]{2,1,0:T(8,128)(2,1)S(1)}, u32[]{:S(2)}, u32[]{:S(2)}) collective-permute-start(bf16[7,32,128]{2,1,0:T(8,128)(2,1)S(1)} %pad_dynamic-slice_fusion.1), channel_id=1, source_target_pairs={{0,4},{1,5},{2,6},{3,7},{4,0},{5,1},{6,2},{7,3},{8,12},{9,13},{10,... | collective-permute-start | bytes 172040 | tf_op jit(solution)/shard_map/ppermute | solution.py:73
  9.7 3.4 %collective-permute-done.11 = bf16[7,32,128]{2,1,0:T(8,128)(2,1)S(1)} collective-permute-done((bf16[7,32,128]{2,1,0:T(8,128)(2,1)S(1)}, bf16[7,32,128]{2,1,0:T(8,128)(2,1)S(1)}, u32[]{:S(2)}, u32[]{:S(2)}) %collective-permute-start.11) | collective-permute-done | bytes 57376 | tf_op jit(solution)/shard_map/ppermute | solution.py:73
  14.7 4.5 %collective-permute-done.12 = bf16[4,7,32,128]{3,2,1,0:T(8,128)(2,1)S(1)} collective-permute-done((bf16[4,7,32,128]{3,2,1,0:T(8,128)(2,1)S(1)}, bf16[4,7,32,128]{3,2,1,0:T(8,128)(2,1)S(1)}, u32[]{:S(2)}, u32[]{:S(2)}) %collective-permute-start.12) | collective-permute-done | bytes 229408 | tf_op jit(solution)/shard_map/ppermute | solution.py:41
  20.9 8.0 %collective-permute-done.13 = bf16[2,4,7,32,128]{4,3,2,1,0:T(8,128)(2,1)S(1)} collective-permute-done((bf16[2,4,7,32,128]{4,3,2,1,0:T(8,128)(2,1)S(1)}, bf16[2,4,7,32,128]{4,3,2,1,0:T(8,128)(2,1)S(1)}, u32[]{:S(2)}, u32[]{:S(2)}) %collective-permute-start.13) | collective-permute-done | bytes 458784 | tf_op jit(solution)/shard_map/ppermute | solution.py:41
  30.9 2.6 %collective-permute-start.1 = (bf16[7,32,256]{2,1,0:T(8,128)(2,1)}, bf16[7,32,256]{2,1,0:T(8,128)(2,1)}, u32[]{:S(2)}, u32[]{:S(2)}) collective-permute-start(bf16[7,32,256]{2,1,0:T(8,128)(2,1)} %pad_dynamic-slice_fusion), channel_id=1, source_target_pairs={{0,4},{1,5},{2,6},{3,7},{4,0},{5,1},{6,2},{7,3},{8,12},{9,13},{10,... | collective-permute-start | bytes 344072 | tf_op jit(solution)/shard_map/ppermute | solution.py:73
  37.0 4.5 %collective-permute-done.6 = bf16[2,2,32,128]{3,2,1,0:T(8,128)(2,1)S(1)} collective-permute-done((bf16[2,2,32,128]{3,2,1,0:T(8,128)(2,1)S(1)}, bf16[2,2,32,128]{3,2,1,0:T(8,128)(2,1)S(1)}, u32[]{:S(2)}, u32[]{:S(2)}) %collective-permute-start.6) | collective-permute-done | bytes 32800 | tf_op jit(solution)/shard_map/ppermute | solution.py:41
  46.1 3.4 %collective-permute-start.16 = (bf16[4,9,1,64,128]{4,3,2,1,0:T(8,128)(2,1)}, bf16[4,9,1,64,128]{4,3,2,1,0:T(8,128)(2,1)S(1)}, u32[]{:S(2)}, u32[]{:S(2)}) collective-permute-start(bf16[4,9,1,64,128]{4,3,2,1,0:T(8,128)(2,1)} %pad_maximum_fusion.7), channel_id=1, source_target_pairs={{0,1},{1,2},{2,3},{3,4},{4,5},{5,6},{6,7},{8,9},{9,10},{10,11},{11... | collective-permute-start | bytes 1769480 | tf_op jit(solution)/shard_map/ppermute | solution.py:36
  57.3 2.5 %shard_map.76 = (bf16[4,4,1,32,256]{4,3,2,1,0:T(8,128)(2,1)S(1)}, bf16[4,1,1,32,256]{4,3,2,1,0:T(8,128)(2,1)S(1)}) custom-call(s32[2]{0:T(128)S(1)} %pad_add_fusion.here, bf16[4,8,7,32,128]{4,3,2,1,0:T(8,128)(2,1)S(1)} %bitcast.178, bf16[3,4,9,4,32,128]{5,4,3,2,1,0:T(8,128)(2,1)S(1)} %shard_map.75.main), custom_call_target="tpu_custom_call" | custom-call | flops 905969664 | bytes 5701640 | tf_op jit(solution)/shard_map/pallas_call | solution.py:119
  59.9 3.1 %collective-permute-start.18 = (bf16[4,4,1,32,256]{4,3,2,1,0:T(8,128)(2,1)S(1)}, bf16[4,4,1,32,256]{4,3,2,1,0:T(8,128)(2,1)S(1)}, u32[]{:S(2)}, u32[]{:S(2)}) collective-permute-start(bf16[4,4,1,32,256]{4,3,2,1,0:T(8,128)(2,1)S(1)} %get-tuple-element.18.rest_1_.high), channel_id=1, source_target_pairs={{0,1},{1,2},{2,3},{3,4},{4,5},{5,6},{6,7},{8,9},{9,10},{10,11},{11... | collective-permute-start | bytes 786440 | tf_op jit(solution)/shard_map/ppermute | solution.py:36
  63.5 2.7 %shard_map.77 = (bf16[4,4,1,32,256]{4,3,2,1,0:T(8,128)(2,1)S(1)}, bf16[4,1,2,32,256]{4,3,2,1,0:T(8,128)(2,1)S(1)}, bf16[3,4,9,1,32,128]{5,4,3,2,1,0:T(8,128)(2,1)S(1)}) custom-call(s32[2]{0:T(128)S(1)} %pad_add_fusion.here, bf16[4,8,7,32,128]{4,3,2,1,0:T(8,128)(2,1)S(1)} %bitcast.179, bf16[3,4,9,4,32,128]{5,4,3,2,1,0:T(8,128)(2,1)S(1)} %shard_map.75.main, ...), custom_call_target="tpu_custom_call" | custom-call | flops 905969664 | bytes 7503880 | tf_op jit(solution)/shard_map/pallas_call | solution.py:119
  67.5 5.8 %collective-permute-done.3 = bf16[4,7,32,256]{3,2,1,0:T(8,128)(2,1)} collective-permute-done((bf16[4,7,32,256]{3,2,1,0:T(8,128)(2,1)}, bf16[4,7,32,256]{3,2,1,0:T(8,128)(2,1)}, u32[]{:S(2)}, u32[]{:S(2)}) %collective-permute-start.3) | collective-permute-done | bytes 458784 | tf_op jit(solution)/shard_map/ppermute | solution.py:41
  79.1 4.9 %shard_map.78 = (bf16[2,8,14,32,128]{4,3,2,1,0:T(8,128)(2,1)S(1)}, bf16[2,8,14,32,128]{4,3,2,1,0:T(8,128)(2,1)S(1)}, bf16[3,4,5,3,16,256]{5,4,3,2,1,0:T(8,128)(2,1)S(1)}) custom-call(s32[2]{0:T(128)S(1)} %pad_add_fusion.here, bf16[8,32,128]{2,1,0:T(8,128)(2,1)S(1)} %bitcast.181, bf16[4,4,1,32,256]{4,3,2,1,0:T(8,128)(2,1)S(1)} %get-tuple-element.19.low, ...), custom_call_target="tpu_custom_call" | custom-call | flops 452984832 | bytes 6193160 | tf_op jit(solution)/shard_map/pallas_call | solution.py:119
  84.1 2.7 %collective-permute-start.31 = (bf16[2,8,14,32,128]{4,3,2,1,0:T(8,128)(2,1)S(1)}, bf16[2,8,14,32,128]{4,3,2,1,0:T(8,128)(2,1)S(1)}, u32[]{:S(2)}, u32[]{:S(2)}) collective-permute-start(bf16[2,8,14,32,128]{4,3,2,1,0:T(8,128)(2,1)S(1)} %get-tuple-element.31), channel_id=1, source_target_pairs={{0,8},{8,0},{16,24},{24,16},{1,9},{9,1},{17,25},{25,17},{2,10},{10... | collective-permute-start | bytes 5505032 | tf_op jit(solution)/shard_map/ppermute | solution.py:41
  86.8 7.1 %collective-permute-done.4 = bf16[2,4,7,32,256]{4,3,2,1,0:T(8,128)(2,1)S(1)} collective-permute-done((bf16[2,4,7,32,256]{4,3,2,1,0:T(8,128)(2,1)S(1)}, bf16[2,4,7,32,256]{4,3,2,1,0:T(8,128)(2,1)S(1)}, u32[]{:S(2)}, u32[]{:S(2)}) %collective-permute-start.4) | collective-permute-done | bytes 917536 | tf_op jit(solution)/shard_map/ppermute | solution.py:41
  95.5 5.8 %collective-permute-done.20 = bf16[8,32,128]{2,1,0:T(8,128)(2,1)S(1)} collective-permute-done((bf16[8,32,128]{2,1,0:T(8,128)(2,1)S(1)}, bf16[8,32,128]{2,1,0:T(8,128)(2,1)S(1)}, u32[]{:S(2)}, u32[]{:S(2)}) %collective-permute-start.20) | collective-permute-done | bytes 65568 | tf_op jit(solution)/shard_map/ppermute | solution.py:36
  106.0 9.7 %collective-permute-start.34 = (bf16[2,4,7,32,128]{4,3,2,1,0:T(8,128)(2,1)S(1)}, bf16[2,4,7,32,128]{4,3,2,1,0:T(8,128)(2,1)S(1)}, u32[]{:S(2)}, u32[]{:S(2)}) collective-permute-start(bf16[2,4,7,32,128]{4,3,2,1,0:T(8,128)(2,1)S(1)} %slice_bitcast_fusion.4), channel_id=1, source_target_pairs={{0,1},{1,0},{2,3},{3,2},{4,5},{5,4},{6,7},{7,6},{8,9},{9,8},{10,11... | collective-permute-start | bytes 1376264 | tf_op jit(solution)/shard_map/ppermute | solution.py:41
  118.0 6.2 %shard_map.82 = (bf16[2,8,7,32,128]{4,3,2,1,0:T(8,128)(2,1)S(1)}, bf16[2,8,7,32,128]{4,3,2,1,0:T(8,128)(2,1)S(1)}) custom-call(s32[2]{0:T(128)S(1)} %pad_add_fusion.here, bf16[4,4,2,32,256]{4,3,2,1,0:T(8,128)(2,1)S(1)} %get-tuple-element.23.cells.grads, bf16[3,4,9,4,32,128]{5,4,3,2,1,0:T(8,128)(2,1)S(1)} %shard_map.75.main, ...), custom_call_target="tpu_custom_call" | custom-call | flops 1811939328 | bytes 6782984 | tf_op jit(solution)/shard_map/pallas_call | solution.py:119
  130.1 4.9 %collective-permute-done.33 = bf16[4,7,32,128]{3,2,1,0:T(8,128)(2,1)S(1)} collective-permute-done((bf16[4,7,32,128]{3,2,1,0:T(8,128)(2,1)S(1)}, bf16[4,7,32,128]{3,2,1,0:T(8,128)(2,1)S(1)}, u32[]{:S(2)}, u32[]{:S(2)}) %collective-permute-start.33) | collective-permute-done | bytes 229408 | tf_op jit(solution)/shard_map/ppermute | solution.py:41
  135.2 8.0 %collective-permute-done.26 = bf16[2,4,7,32,128]{4,3,2,1,0:T(8,128)(2,1)S(1)} collective-permute-done((bf16[2,4,7,32,128]{4,3,2,1,0:T(8,128)(2,1)S(1)}, bf16[2,4,7,32,128]{4,3,2,1,0:T(8,128)(2,1)S(1)}, u32[]{:S(2)}, u32[]{:S(2)}) %collective-permute-start.26) | collective-permute-done | bytes 458784 | tf_op jit(solution)/shard_map/ppermute | solution.py:41
  155.6 6.8 %collective-permute-done.37 = bf16[14,32,128]{2,1,0:T(8,128)(2,1)S(1)} collective-permute-done((bf16[14,32,128]{2,1,0:T(8,128)(2,1)S(1)}, bf16[14,32,128]{2,1,0:T(8,128)(2,1)S(1)}, u32[]{:S(2)}, u32[]{:S(2)}) %collective-permute-start.37) | collective-permute-done | bytes 114720 | tf_op jit(solution)/shard_map/ppermute | solution.py:73
  167.4 2.2 %shard_map.79 = bf16[4,2,1,16,256]{4,3,2,1,0:T(8,128)(2,1)S(1)} custom-call(s32[2]{0:T(128)S(1)} %pad_add_fusion.here, bf16[4,8,7,32,256]{4,3,2,1,0:T(8,128)(2,1)S(1)} %bitcast.177, bf16[3,4,5,3,16,256]{5,4,3,2,1,0:T(8,128)(2,1)S(1)} %get-tuple-element.22.main), custom_call_target="tpu_custom_call" | custom-call | flops 452984832 | bytes 5210120 | tf_op jit(solution)/shard_map/pallas_call | solution.py:119
  171.1 5.4 %all-to-all-start = ((bf16[8,2,2048]{2,1,0:T(2,128)(2,1)}), bf16[8,2,2048]{2,1,0:T(2,128)(2,1)S(1)}, u32[]{:S(2)}, u32[]{:S(2)}) async-start(bf16[8,2,2048]{2,1,0:T(2,128)(2,1)} %reshape.101), calls=%async_computation | async-start | bytes 131072 | tf_op jit(solution)/shard_map/all_to_all | solution.py:680
  180.1 3.3 %all-to-all-done = bf16[8,2,2048]{2,1,0:T(2,128)(2,1)S(1)} async-done(((bf16[8,2,2048]{2,1,0:T(2,128)(2,1)}), bf16[8,2,2048]{2,1,0:T(2,128)(2,1)S(1)}, u32[]{:S(2)}, u32[]{:S(2)}) %all-to-all-start) | async-done | bytes 65568 | tf_op jit(solution)/shard_map/all_to_all | solution.py:680
  185.9 5.2 %shard_map.81 = bf16[4,8,4,64,128]{4,3,2,1,0:T(8,128)(2,1)} custom-call(s32[2]{0:T(128)S(1)} %pad_add_fusion.here, bf16[4,4,2,32,256]{4,3,2,1,0:T(8,128)(2,1)S(1)} %get-tuple-element.23.cells.grads, bf16[4,1,2,32,256]{4,3,2,1,0:T(8,128)(2,1)S(1)} %collective-permute-done.22.plane, bf16[4,5,1,32,256]{4,3,2,1,0:T(8,128)(2,1)S(1)} %pad_maximum_fusion.14.row, ...), custom_call_target="tpu_custom_call" | custom-call | flops 1811939328 | bytes 4915208 | tf_op jit(solution)/shard_map/pallas_call | solution.py:119
  (140 shorter events, 77.3 us)
Async XLA Ops:
  30.2 25.7 %collective-permute-start.14 = (bf16[2,2,4,7,32,128]{5,4,3,2,1,0:T(8,128)(2,1)}, bf16[2,2,4,7,32,128]{5,4,3,2,1,0:T(8,128)(2,1)}, u32[]{:S(2)}, u32[]{:S(2)}) collective-permute-start(bf16[2,2,4,7,32,128]{5,4,3,2,1,0:T(8,128)(2,1)} %get-tuple-element.47), channel_id=1, source_target_pairs={{0,8},{8,0},{16,24},{24,16},{1,9},{9,1},{17,25},{25,17},{2,10},{10... | collective-permute-start | bytes 2752520 | tf_op jit(solution)/shard_map/ppermute | solution.py:41
  30.9 15.2 %collective-permute-start.1 = (bf16[7,32,256]{2,1,0:T(8,128)(2,1)}, bf16[7,32,256]{2,1,0:T(8,128)(2,1)}, u32[]{:S(2)}, u32[]{:S(2)}) collective-permute-start(bf16[7,32,256]{2,1,0:T(8,128)(2,1)} %pad_dynamic-slice_fusion), channel_id=1, source_target_pairs={{0,4},{1,5},{2,6},{3,7},{4,0},{5,1},{6,2},{7,3},{8,12},{9,13},{10,... | collective-permute-start | bytes 344072 | tf_op jit(solution)/shard_map/ppermute | solution.py:73
  33.5 16.0 %collective-permute-start = (bf16[7,32,256]{2,1,0:T(8,128)(2,1)}, bf16[7,32,256]{2,1,0:T(8,128)(2,1)}, u32[]{:S(2)}, u32[]{:S(2)}) collective-permute-start(bf16[7,32,256]{2,1,0:T(8,128)(2,1)} %pad_dynamic-slice_fusion), channel_id=1, source_target_pairs={{0,2},{1,3},{2,0},{3,1},{4,6},{5,7},{6,4},{7,5},{8,10},{9,11},{10,... | collective-permute-start | bytes 344072 | tf_op jit(solution)/shard_map/ppermute | solution.py:73
  34.3 9.9 %collective-permute-start.15 = (bf16[4,1,4,64,128]{4,3,2,1,0:T(8,128)(2,1)}, bf16[4,1,4,64,128]{4,3,2,1,0:T(8,128)(2,1)S(1)}, u32[]{:S(2)}, u32[]{:S(2)}) collective-permute-start(bf16[4,1,4,64,128]{4,3,2,1,0:T(8,128)(2,1)} %slice.140), channel_id=1, source_target_pairs={{0,8},{1,9},{2,10},{3,11},{4,12},{5,13},{6,14},{7,15},{8,16},{9,17... | collective-permute-start | bytes 786440 | tf_op jit(solution)/shard_map/ppermute | solution.py:36
  46.1 17.4 %collective-permute-start.16 = (bf16[4,9,1,64,128]{4,3,2,1,0:T(8,128)(2,1)}, bf16[4,9,1,64,128]{4,3,2,1,0:T(8,128)(2,1)S(1)}, u32[]{:S(2)}, u32[]{:S(2)}) collective-permute-start(bf16[4,9,1,64,128]{4,3,2,1,0:T(8,128)(2,1)} %pad_maximum_fusion.7), channel_id=1, source_target_pairs={{0,1},{1,2},{2,3},{3,4},{4,5},{5,6},{6,7},{8,9},{9,10},{10,11},{11... | collective-permute-start | bytes 1769480 | tf_op jit(solution)/shard_map/ppermute | solution.py:36
  51.3 22.0 %collective-permute-start.3 = (bf16[4,7,32,256]{3,2,1,0:T(8,128)(2,1)}, bf16[4,7,32,256]{3,2,1,0:T(8,128)(2,1)}, u32[]{:S(2)}, u32[]{:S(2)}) collective-permute-start(bf16[4,7,32,256]{3,2,1,0:T(8,128)(2,1)} %get-tuple-element.64), channel_id=1, source_target_pairs={{0,1},{1,0},{2,3},{3,2},{4,5},{5,4},{6,7},{7,6},{8,9},{9,8},{10,11... | collective-permute-start | bytes 1376264 | tf_op jit(solution)/shard_map/ppermute | solution.py:41
  54.1 23.2 %collective-permute-start.8 = (bf16[2,2,32,128]{3,2,1,0:T(8,128)(2,1)S(1)}, bf16[2,2,32,128]{3,2,1,0:T(8,128)(2,1)S(1)}, u32[]{:S(2)}, u32[]{:S(2)}) collective-permute-start(bf16[2,2,32,128]{3,2,1,0:T(8,128)(2,1)S(1)} %bitcast.214), channel_id=1, source_target_pairs={{0,1},{1,0},{2,3},{3,2},{4,5},{5,4},{6,7},{7,6},{8,9},{9,8},{10,11... | collective-permute-start | bytes 98312 | tf_op jit(solution)/shard_map/ppermute | solution.py:41
  59.9 19.3 %collective-permute-start.18 = (bf16[4,4,1,32,256]{4,3,2,1,0:T(8,128)(2,1)S(1)}, bf16[4,4,1,32,256]{4,3,2,1,0:T(8,128)(2,1)S(1)}, u32[]{:S(2)}, u32[]{:S(2)}) collective-permute-start(bf16[4,4,1,32,256]{4,3,2,1,0:T(8,128)(2,1)S(1)} %get-tuple-element.18.rest_1_.high), channel_id=1, source_target_pairs={{0,1},{1,2},{2,3},{3,4},{4,5},{5,6},{6,7},{8,9},{9,10},{10,11},{11... | collective-permute-start | bytes 786440 | tf_op jit(solution)/shard_map/ppermute | solution.py:36
  66.2 13.0 %collective-permute-start.17 = (bf16[4,1,2,32,256]{4,3,2,1,0:T(8,128)(2,1)S(1)}, bf16[4,1,2,32,256]{4,3,2,1,0:T(8,128)(2,1)S(1)}, u32[]{:S(2)}, u32[]{:S(2)}) collective-permute-start(bf16[4,1,2,32,256]{4,3,2,1,0:T(8,128)(2,1)S(1)} %get-tuple-element.20), channel_id=1, source_target_pairs={{0,8},{1,9},{2,10},{3,11},{4,12},{5,13},{6,14},{7,15},{8,16},{9,17... | collective-permute-start | bytes 393224 | tf_op jit(solution)/shard_map/ppermute | solution.py:36
  74.4 19.4 %collective-permute-start.4 = (bf16[2,4,7,32,256]{4,3,2,1,0:T(8,128)(2,1)S(1)}, bf16[2,4,7,32,256]{4,3,2,1,0:T(8,128)(2,1)S(1)}, u32[]{:S(2)}, u32[]{:S(2)}) collective-permute-start(bf16[2,4,7,32,256]{4,3,2,1,0:T(8,128)(2,1)S(1)} %get-tuple-element.49), channel_id=1, source_target_pairs={{0,16},{8,24},{16,0},{24,8},{1,17},{9,25},{17,1},{25,9},{2,18},{10... | collective-permute-start | bytes 2752520 | tf_op jit(solution)/shard_map/ppermute | solution.py:41
  84.1 18.6 %collective-permute-start.31 = (bf16[2,8,14,32,128]{4,3,2,1,0:T(8,128)(2,1)S(1)}, bf16[2,8,14,32,128]{4,3,2,1,0:T(8,128)(2,1)S(1)}, u32[]{:S(2)}, u32[]{:S(2)}) collective-permute-start(bf16[2,8,14,32,128]{4,3,2,1,0:T(8,128)(2,1)S(1)} %get-tuple-element.31), channel_id=1, source_target_pairs={{0,8},{8,0},{16,24},{24,16},{1,9},{9,1},{17,25},{25,17},{2,10},{10... | collective-permute-start | bytes 5505032 | tf_op jit(solution)/shard_map/ppermute | solution.py:41
  94.1 21.6 %collective-permute-start.5 = (bf16[2,2,4,7,32,256]{5,4,3,2,1,0:T(8,128)(2,1)S(1)}, bf16[2,2,4,7,32,256]{5,4,3,2,1,0:T(8,128)(2,1)S(1)}, u32[]{:S(2)}, u32[]{:S(2)}) collective-permute-start(bf16[2,2,4,7,32,256]{5,4,3,2,1,0:T(8,128)(2,1)S(1)} %get-tuple-element.45), channel_id=1, source_target_pairs={{0,8},{8,0},{16,24},{24,16},{1,9},{9,1},{17,25},{25,17},{2,10},{10... | collective-permute-start | bytes 5505032 | tf_op jit(solution)/shard_map/ppermute | solution.py:41
  101.3 14.7 %collective-permute-start.21 = (bf16[2,8,32,128]{3,2,1,0:T(8,128)(2,1)S(1)}, bf16[2,8,32,128]{3,2,1,0:T(8,128)(2,1)S(1)}, u32[]{:S(2)}, u32[]{:S(2)}) collective-permute-start(bf16[2,8,32,128]{3,2,1,0:T(8,128)(2,1)S(1)} %pad_maximum_fusion.20.near), channel_id=1, source_target_pairs={{8,0},{9,1},{10,2},{11,3},{12,4},{13,5},{14,6},{15,7},{16,8},{17,9... | collective-permute-start | bytes 393224 | tf_op jit(solution)/shard_map/ppermute | solution.py:36
  103.8 20.5 %collective-permute-start.32 = (bf16[2,4,7,32,128]{4,3,2,1,0:T(8,128)(2,1)S(1)}, bf16[2,4,7,32,128]{4,3,2,1,0:T(8,128)(2,1)S(1)}, u32[]{:S(2)}, u32[]{:S(2)}) collective-permute-start(bf16[2,4,7,32,128]{4,3,2,1,0:T(8,128)(2,1)S(1)} %slice_bitcast_fusion.6), channel_id=1, source_target_pairs={{0,16},{8,24},{16,0},{24,8},{1,17},{9,25},{17,1},{25,9},{2,18},{10... | collective-permute-start | bytes 1376264 | tf_op jit(solution)/shard_map/ppermute | solution.py:41
  106.0 20.1 %collective-permute-start.34 = (bf16[2,4,7,32,128]{4,3,2,1,0:T(8,128)(2,1)S(1)}, bf16[2,4,7,32,128]{4,3,2,1,0:T(8,128)(2,1)S(1)}, u32[]{:S(2)}, u32[]{:S(2)}) collective-permute-start(bf16[2,4,7,32,128]{4,3,2,1,0:T(8,128)(2,1)S(1)} %slice_bitcast_fusion.4), channel_id=1, source_target_pairs={{0,1},{1,0},{2,3},{3,2},{4,5},{5,4},{6,7},{7,6},{8,9},{9,8},{10,11... | collective-permute-start | bytes 1376264 | tf_op jit(solution)/shard_map/ppermute | solution.py:41
  129.8 13.4 %collective-permute-start.26 = (bf16[2,4,7,32,128]{4,3,2,1,0:T(8,128)(2,1)S(1)}, bf16[2,4,7,32,128]{4,3,2,1,0:T(8,128)(2,1)S(1)}, u32[]{:S(2)}, u32[]{:S(2)}) collective-permute-start(bf16[2,4,7,32,128]{4,3,2,1,0:T(8,128)(2,1)S(1)} %fusion.4), channel_id=1, source_target_pairs={{0,1},{1,0},{2,3},{3,2},{4,5},{5,4},{6,7},{7,6},{8,9},{9,8},{10,11... | collective-permute-start | bytes 1376264 | tf_op jit(solution)/shard_map/ppermute | solution.py:41
  149.1 13.3 %collective-permute-start.37 = (bf16[14,32,128]{2,1,0:T(8,128)(2,1)S(1)}, bf16[14,32,128]{2,1,0:T(8,128)(2,1)S(1)}, u32[]{:S(2)}, u32[]{:S(2)}) collective-permute-start(bf16[14,32,128]{2,1,0:T(8,128)(2,1)S(1)} %get-tuple-element.60), channel_id=1, source_target_pairs={{0,4},{1,5},{2,6},{3,7},{4,0},{5,1},{6,2},{7,3},{8,12},{9,13},{10,... | collective-permute-start | bytes 344072 | tf_op jit(solution)/shard_map/ppermute | solution.py:73
  150.4 12.0 %collective-permute-start.28 = (bf16[7,32,128]{2,1,0:T(8,128)(2,1)S(1)}, bf16[7,32,128]{2,1,0:T(8,128)(2,1)S(1)}, u32[]{:S(2)}, u32[]{:S(2)}) collective-permute-start(bf16[7,32,128]{2,1,0:T(8,128)(2,1)S(1)} %get-tuple-element.69), channel_id=1, source_target_pairs={{0,2},{1,3},{2,0},{3,1},{4,6},{5,7},{6,4},{7,5},{8,10},{9,11},{10,... | collective-permute-start | bytes 172040 | tf_op jit(solution)/shard_map/ppermute | solution.py:73
  152.3 10.2 %collective-permute-start.30 = (bf16[7,32,128]{2,1,0:T(8,128)(2,1)S(1)}, bf16[7,32,128]{2,1,0:T(8,128)(2,1)S(1)}, u32[]{:S(2)}, u32[]{:S(2)}) collective-permute-start(bf16[7,32,128]{2,1,0:T(8,128)(2,1)S(1)} %get-tuple-element.70), channel_id=1, source_target_pairs={{0,6},{1,7},{2,4},{3,5},{4,2},{5,3},{6,0},{7,1},{8,14},{9,15},{10,... | collective-permute-start | bytes 172040 | tf_op jit(solution)/shard_map/ppermute | solution.py:73
  164.5 12.0 %collective-permute-start.39 = (bf16[21,32,128]{2,1,0:T(8,128)(2,1)}, bf16[21,32,128]{2,1,0:T(8,128)(2,1)}, u32[]{:S(2)}, u32[]{:S(2)}) collective-permute-start(bf16[21,32,128]{2,1,0:T(8,128)(2,1)} %get-tuple-element.75), channel_id=1, source_target_pairs={{0,16},{8,24},{16,0},{24,8},{1,17},{9,25},{17,1},{25,9},{2,18},{10... | collective-permute-start | bytes 516104 | tf_op jit(solution)/shard_map/ppermute | solution.py:41
  164.8 20.1 %collective-permute-start.23 = (bf16[4,4,1,32,256]{4,3,2,1,0:T(8,128)(2,1)}, bf16[4,4,1,32,256]{4,3,2,1,0:T(8,128)(2,1)}, u32[]{:S(2)}, u32[]{:S(2)}) collective-permute-start(bf16[4,4,1,32,256]{4,3,2,1,0:T(8,128)(2,1)} %get-tuple-element.25), channel_id=1, source_target_pairs={{1,0},{2,1},{3,2},{4,3},{5,4},{6,5},{7,6},{9,8},{10,9},{11,10},{12... | collective-permute-start | bytes 786440 | tf_op jit(solution)/shard_map/ppermute | solution.py:36
  166.1 18.8 %collective-permute-start.24 = (bf16[4,1,1,32,256]{4,3,2,1,0:T(8,128)(2,1)S(1)}, bf16[4,1,1,32,256]{4,3,2,1,0:T(8,128)(2,1)S(1)}, u32[]{:S(2)}, u32[]{:S(2)}) collective-permute-start(bf16[4,1,1,32,256]{4,3,2,1,0:T(8,128)(2,1)S(1)} %get-tuple-element.26), channel_id=1, source_target_pairs={{9,0},{10,1},{11,2},{12,3},{13,4},{14,5},{15,6},{17,8},{18,9},{19,... | collective-permute-start | bytes 196616 | tf_op jit(solution)/shard_map/ppermute | solution.py:36
  171.1 12.3 %all-to-all-start = ((bf16[8,2,2048]{2,1,0:T(2,128)(2,1)}), bf16[8,2,2048]{2,1,0:T(2,128)(2,1)S(1)}, u32[]{:S(2)}, u32[]{:S(2)}) async-start(bf16[8,2,2048]{2,1,0:T(2,128)(2,1)} %reshape.101), calls=%async_computation | async-start | bytes 131072 | tf_op jit(solution)/shard_map/all_to_all | solution.py:680
  178.3 12.8 %collective-permute-start.40 = (bf16[2,21,32,128]{3,2,1,0:T(8,128)(2,1)}, bf16[2,21,32,128]{3,2,1,0:T(8,128)(2,1)}, u32[]{:S(2)}, u32[]{:S(2)}) collective-permute-start(bf16[2,21,32,128]{3,2,1,0:T(8,128)(2,1)} %get-tuple-element.66), channel_id=1, source_target_pairs={{0,8},{8,0},{16,24},{24,16},{1,9},{9,1},{17,25},{25,17},{2,10},{10... | collective-permute-start | bytes 1032200 | tf_op jit(solution)/shard_map/ppermute | solution.py:41
  (23 other events, 166.1 us)

commit v6 on v5

--- a/solution.py
+++ b/solution.py
@@ -8,6 +8,7 @@
 from jax.sharding import PartitionSpec as P
 
 
+SPACE, CHAN = ("space", "chan")
 BF16 = jnp.bfloat16
 F32 = jnp.float32
 LANES = 128
@@ -27,13 +28,13 @@
 
 def shifted(value, steps):
     pairs = []
-    sizes = (lax.axis_size("space"), lax.axis_size("chan"))
+    sizes = (lax.axis_size(SPACE), lax.axis_size(CHAN))
     for a in range(sizes[0]):
         for b in range(sizes[1]):
             to = (a + steps[0], b + steps[1])
             if 0 <= to[0] < sizes[0] and 0 <= to[1] < sizes[1]:
                 pairs.append((a * sizes[1] + b, to[0] * sizes[1] + to[1]))
-    return lax.ppermute(value, ("space", "chan"), pairs)
+    return lax.ppermute(value, (SPACE, CHAN), pairs)
 
 
 def swapped(value, axis, bit):
@@ -47,43 +48,59 @@
 
 
 def position():
-    return jnp.stack([lax.axis_index("space"), lax.axis_index("chan")]).astype(jnp.int32)
+    return jnp.stack([lax.axis_index(SPACE), lax.axis_index(CHAN)]).astype(jnp.int32)
 
 
 def own_part(shard):
-    space = lax.axis_size("space")
+    space = lax.axis_size(SPACE)
     edge, inputs, mine = shard.shape[0], shard.shape[3], shard.shape[4]
     taps = edge**3
     each = -(-taps // space)
     flat = jnp.transpose(shard.reshape(taps, inputs, mine), (0, 2, 1))
     flat = jnp.pad(flat, ((0, each * space - taps), (0, 0), (0, 0)))
-    return lax.dynamic_slice_in_dim(flat, lax.axis_index("space") * each, each, 0)
+    return lax.dynamic_slice_in_dim(flat, lax.axis_index(SPACE) * each, each, 0)
 
 
 def far_bits():
-    return list(reversed(range(1, bits("chan"))))
+    return list(reversed(range(1, bits(CHAN))))
 
 
 def high_bits():
-    return list(reversed(range(1, bits("space"))))
+    return list(reversed(range(1, bits(SPACE))))
 
 
 def far_swapped(value, mask):
-    count = lax.axis_size("chan")
-    return lax.ppermute(value, "chan", [(i, i ^ (mask << 1)) for i in range(count)])
+    count = lax.axis_size(CHAN)
+    return lax.ppermute(value, CHAN, [(i, i ^ (mask << 1)) for i in range(count)])
 
 
 def far_gather(part):
-    others = [far_swapped(part, m) for m in range(1, lax.axis_size("chan") // 2)]
+    others = [far_swapped(part, m) for m in range(1, lax.axis_size(CHAN) // 2)]
     return jnp.stack([part, *others])
 
 
 def near_gather(part):
     each, mine, inputs = part.shape[-3:]
     for bit in high_bits():
-        part = doubled(part, "space", bit)
-    part = doubled(part, "space", 0)
-    return part.reshape(lax.axis_size("space"), lax.axis_size("chan"), each, mine, inputs)
+        part = doubled(part, SPACE, bit)
+    part = doubled(part, SPACE, 0)
+    return part.reshape(lax.axis_size(SPACE), lax.axis_size(CHAN), each, mine, inputs)
+
+
+def mixed_gather(part):
+    each, mine, inputs = part.shape[-3:]
+    highs = len(high_bits())
+    cut = (each + 1) // 2
+    one, two = part[..., :cut, :, :], part[..., cut:, :, :]
+    one = doubled(one, CHAN, 0)
+    for bit in high_bits():
+        two = doubled(two, SPACE, bit)
+    for bit in high_bits():
+        one = doubled(one, SPACE, bit)
+    two = doubled(two, CHAN, 0)
+    whole = jnp.concatenate([one, jnp.moveaxis(two, 0, highs)], axis=-3)
+    whole = doubled(whole, SPACE, 0)
+    return whole.reshape(lax.axis_size(SPACE), lax.axis_size(CHAN), each, mine, inputs)
 
 
 def relative(index, mine, order):
@@ -221,16 +238,16 @@
     cells = vols * sides[1] * len(cells_b) * depth
     outs = [jax.ShapeDtypeStruct((vols, sides[1], len(cells_b), depth, count), BF16)]
     scratch = [pltpu.VMEM((cells, count), F32)]
-    if kind == "high":
+    if kind == "h":
         outs.append(jax.ShapeDtypeStruct((vols, 1, 1, depth, count), BF16))
-    if kind == "low":
+    if kind == "l":
         high_b = parts[2].shape[2]
         outs.append(jax.ShapeDtypeStruct((vols, 1, 1 + high_b, depth, count), BF16))
         outs.append(jax.ShapeDtypeStruct(main.shape[:3] + (1,) + main.shape[4:], BF16))
         scratch.append(part_scratch(2 * depth, inputs))
 
     def kernel(here, filters, main, *rest):
-        if kind == "low":
+        if kind == "l":
             row, above, out, plane, row_parts, acc, wide = rest
 
             def split(n, carry):
@@ -241,15 +258,15 @@
             refs = (main, row_parts)
         else:
             out, acc = rest[0], rest[-1]
-            refs = (main, None) if kind == "high" else (main,)
+            refs = (main, None) if kind == "h" else (main,)
         total = forward_total(orders, sides, refs, here, filters, acc)
-        if kind != "out":
+        if kind != "u":
             total = leaky(total)
         value = total.astype(BF16).reshape(out.shape)
         out[...] = value
-        if kind == "high":
+        if kind == "h":
             rest[1][...] = value[:, -1:, -1:]
-        if kind == "low":
+        if kind == "l":
             plane[:, :, :1] = value[:, -1:]
             plane[:, :, 1:] = above[:, above.shape[1] - 1 :]
 
@@ -376,9 +393,9 @@
 
 def core_sum(keep, send):
     tail = keep.shape[2:]
-    other = swapped(send, "space", 0)
+    other = swapped(send, SPACE, 0)
     total = keep.astype(F32) + other.astype(F32)
-    highs = bits("space") - 1
+    highs = bits(SPACE) - 1
     return total.reshape((2,) * highs + (2, -1) + tail)
 
 
@@ -390,40 +407,40 @@
 
 
 def plain_sum(total):
-    total = half_sum(total, "chan", 0, bits("space") - 1)
-    for bit in range(1, bits("space")):
-        total = half_sum(total, "space", bit, 0)
+    total = half_sum(total, CHAN, 0, bits(SPACE) - 1)
+    for bit in range(1, bits(SPACE)):
+        total = half_sum(total, SPACE, bit, 0)
     return total
 
 
 def far_sum(total):
     part = total[0].astype(F32)
-    for m in range(1, lax.axis_size("chan") // 2):
+    for m in range(1, lax.axis_size(CHAN) // 2):
         part = part + far_swapped(total[m].astype(BF16), m).astype(F32)
     return part.astype(BF16)
 
 
 def mixed_sum(total):
-    highs = list(range(1, bits("space")))
+    highs = list(range(1, bits(SPACE)))
     cut = (total.shape[-3] + 1) // 2
     one, two = total[..., :cut, :, :], total[..., cut:, :, :]
-    two = half_sum(two, "chan", 0, len(highs))
+    two = half_sum(two, CHAN, 0, len(highs))
     for bit in highs:
-        one = half_sum(one, "space", bit, 0)
-    one = half_sum(one, "chan", 0, 0)
+        one = half_sum(one, SPACE, bit, 0)
+    one = half_sum(one, CHAN, 0, 0)
     for bit in highs:
-        two = half_sum(two, "space", bit, 0)
+        two = half_sum(two, SPACE, bit, 0)
     return jnp.concatenate([one, two], axis=-3)
 
 
 def finish_sum(totals):
-    space = lax.axis_size("space")
+    space = lax.axis_size(SPACE)
     part = merged = jnp.concatenate(totals, axis=0)
     for bit in high_bits():
-        part = doubled(part, "space", bit)
-    part = doubled(part, "space", 0)
+        part = doubled(part, SPACE, bit)
+    part = doubled(part, SPACE, 0)
     part = part.reshape((space,) + merged.shape)
-    apart = [jnp.int32(s) ^ lax.axis_index("space") for s in range(space)]
+    apart = [jnp.int32(s) ^ lax.axis_index(SPACE) for s in range(space)]
     ordered = [lax.dynamic_index_in_dim(part, space_order(a), 0, keepdims=False) for a in apart]
     outs, begin = [], 0
     taps = -(-27 // space)
@@ -440,7 +457,7 @@
 
 def space_order(apart):
     place = 0
-    for bit in range(bits("space")):
+    for bit in range(bits(SPACE)):
         place = place * 2 + ((apart >> bit) & 1)
     return place
 
@@ -619,7 +636,7 @@
 class CellExchange:
     def __init__(self, cotangent):
         vols, side_a, side_b, side_c, mine = cotangent.shape
-        self.count = bits("chan")
+        self.count = bits(CHAN)
         assert side_b == 2**self.count
         flat = jnp.transpose(cotangent, (2, 4, 0, 1, 3))
         self.value = flat.reshape((2,) * self.count + (mine, vols * side_a * side_c))
@@ -627,10 +644,10 @@
 
     def stage(self, bit):
         dim = self.open.index(bit)
-        mine = (lax.axis_index("chan") >> bit) & 1
+        mine = (lax.axis_index(CHAN) >> bit) & 1
         keep = lax.dynamic_index_in_dim(self.value, mine, dim, keepdims=False)
         send = lax.dynamic_index_in_dim(self.value, 1 - mine, dim, keepdims=False)
-        other = swapped(send, "chan", bit)
+        other = swapped(send, CHAN, bit)
         self.value = jnp.stack([keep, other], axis=self.count - 1)
         self.open.remove(bit)
 
@@ -642,24 +659,24 @@
 
 def local(volume, w_first, w_second, cotangent):
     here = position()
-    orders = (list(range(bits("space"))), [0] + far_bits())
+    orders = (list(range(bits(SPACE))), [0] + far_bits())
     side_b = volume.shape[2] // 2
 
     plane = shifted(volume[:, -1:], (1, 0))
     part = far_gather(own_part(w_first))
-    first_full = near_gather(doubled(part, "chan", 0))
+    first_full = near_gather(doubled(part, CHAN, 0))
     row = jnp.concatenate([plane, volume], axis=1)[:, :, -1:]
     row = shifted(row, (0, 1))
     part = far_gather(own_part(w_second))
-    second_full = near_gather(doubled(part, "chan", 0))
+    second_full = mixed_gather(part)
     cells = CellExchange(cotangent)
     for bit in far_bits() + [0]:
         cells.stage(bit)
     own_cells, near_cells, beyond_cells = cells.finish()
 
     vol_main = parted_volume(volume, plane)
-    high, corner = forward(here, (vol_main,), first_full, orders, range(1, side_b), "high")
-    low, hid_plane, vol_row = forward(here, (vol_main, row, high), first_full, orders, range(1), "low")
+    high, corner = forward(here, (vol_main,), first_full, orders, range(1, side_b), "h")
+    low, hid_plane, vol_row = forward(here, (vol_main, row, high), first_full, orders, range(1), "l")
     hid_row = shifted(high[:, :, -1:], (0, 1))
     hid_corner = shifted(corner, (1, 1))
     hid_plane = shifted(hid_plane, (1, 0))
@@ -667,7 +684,9 @@
     keep, send, act_parts = second_grads(here, blocks, own_cells, orders)
     second_sum = far_sum(mixed_sum(core_sum(keep, send)))
 
-    pre_back, pre_plane, pre_row, corner = hidden_back(here, near_cells, beyond_cells, second_full, low, high, orders)
+    pre_back, pre_plane, pre_row, corner = hidden_back(
+        here, near_cells, beyond_cells, second_full, low, high, orders
+    )
     keep, send = first_grads(here, (vol_main, vol_row), pre_back, orders)
     first_sum = far_sum(plain_sum(core_sum(keep, send)))
     first_grad, second_grad = finish_sum([first_sum, second_sum])
@@ -676,8 +695,8 @@
     corner = shifted(corner, (-1, -1))
     row = jnp.concatenate([row, corner], axis=1)
     out_b = range(act_parts.shape[3] // 2)
-    (local_out,) = forward(here, (act_parts,), second_full, orders, out_b, "out")
-    second_out = lax.all_to_all(local_out, "chan", split_axis=4, concat_axis=2, tiled=True)
+    (local_out,) = forward(here, (act_parts,), second_full, orders, out_b, "u")
+    second_out = lax.all_to_all(local_out, CHAN, split_axis=4, concat_axis=2, tiled=True)
     volume_grad = volume_grads(here, pre_back, plane, row, first_full, orders)
     return (second_out, volume_grad, first_grad, second_grad)
 
@@ -687,16 +706,16 @@
         local,
         mesh=mesh,
         in_specs=(
-            P(None, "space", "chan", None, None),
-            P(None, None, None, None, "chan"),
-            P(None, None, None, None, "chan"),
-            P(None, "space", None, None, "chan"),
+            P(None, SPACE, CHAN, None, None),
+            P(None, None, None, None, CHAN),
+            P(None, None, None, None, CHAN),
+            P(None, SPACE, None, None, CHAN),
         ),
         out_specs=(
-            P(None, "space", None, None, "chan"),
-            P(None, "space", "chan", None, None),
-            P(None, None, None, None, "chan"),
-            P(None, None, None, None, "chan"),
+            P(None, SPACE, None, None, CHAN),
+            P(None, SPACE, CHAN, None, None),
+            P(None, None, None, None, CHAN),
+            P(None, None, None, None, CHAN),
         ),
         check_vma=False,
     )

time: 196 us -> 197 us (level)
  waiting for transfers between devices: 72.1 us -> 61.5 us
  starting transfers between devices: 68.9 us -> 78.1 us
    ppermute x22, waiting for transfers between devices: 22.9 us -> 15.4 us  [the longest x12 14.8 us: far_swapped(): return lax.ppermute(value, CHAN, [(i, i ^ mask << 1) for i in range(count)])]
    ppermute x22, starting transfers between devices: 34.8 us -> 40.6 us  [the longest x10 21.8 us: shifted(): return lax.ppermute(value, (SPACE, CHAN), pairs)]
    ppermute x19 -> x21, starting transfers between devices: 28.7 us -> 32.3 us  [swapped(): return lax.ppermute(value, axis, [(i, i ^ 1 << bit) for i in range(count)])]
    ppermute x19 -> x21, waiting for transfers between devices: 45.9 us -> 43.9 us  [swapped(): return lax.ppermute(value, axis, [(i, i ^ 1 << bit) for i in range(count)])]
    another operation x11 -> x12, other arithmetic: 9.87 us -> 10.5 us  [doubled(): return jnp.stack([value, other])]
  transfers between devices with their start and end apart: 42 -> 44, of which waited for: 19 -> 19; matrix products, arithmetic and copies ran while one was open for 10% -> 11% of each run, Pallas kernels for 14% -> 14%
where the time goes in v6:
time: 197 us; the launch traced here: 196 us
  starting transfers between devices  78.1 us (40%)
  waiting for transfers between devices  61.5 us (31%)
  Pallas kernels  26.7 us (14%)
  other arithmetic  17 us (9%)
  local copies, waits for them, and re-layouts  11.3 us (6%)
    ppermute x21, waiting for transfers between devices, swapped(): return lax.ppermute(value, axis, [(i, i ^ 1 << bit) for i in range(count)])  43.9 us
    ppermute x21, starting transfers between devices, swapped(): return lax.ppermute(value, axis, [(i, i ^ 1 << bit) for i in range(count)])  32.3 us
    pallas_call x8, Pallas kernels, call(): pl.pallas_call(kernel, out_shape=outs, grid=grid or (), in_specs=specs, o...  26.7 us
    ppermute x10, starting transfers between devices, shifted(): return lax.ppermute(value, (SPACE, CHAN), pairs)  21.8 us
    ppermute x12, starting transfers between devices, far_swapped(): return lax.ppermute(value, CHAN, [(i, i ^ mask << 1) for i in range(count)])  18.8 us
    ppermute x12, waiting for transfers between devices, far_swapped(): return lax.ppermute(value, CHAN, [(i, i ^ mask << 1) for i in range(count)])  14.8 us
    another operation x12, other arithmetic, doubled(): return jnp.stack([value, other])  10.5 us
    all_to_all x1, starting transfers between devices, local(): lax.all_to_all(local_out, CHAN, split_axis=4, concat_axis=2, tiled=True)  5.16 us
  transfers between devices with their start and end apart: 44, of which 19 were waited for; matrix products, arithmetic and copies ran while one was open for 11% of the time, Pallas kernels for 14%

profile of v6, /device:TPU:0, one launch (start us, length us, event | category | flops | bytes accessed | tf_op | source)
XLA Modules:
  0.0 195.8 jit_solution(14103612410948422125)
XLA Ops:
  1.5 4.1 %collective-permute-start.12 = (bf16[7,32,128]{2,1,0:T(8,128)(2,1)S(1)}, bf16[7,32,128]{2,1,0:T(8,128)(2,1)S(1)}, u32[]{:S(2)}, u32[]{:S(2)}) collective-permute-start(bf16[7,32,128]{2,1,0:T(8,128)(2,1)S(1)} %pad_dynamic-slice_fusion.1), channel_id=1, source_target_pairs={{0,4},{1,5},{2,6},{3,7},{4,0},{5,1},{6,2},{7,3},{8,12},{9,13},{10,... | collective-permute-start | bytes 172040 | tf_op jit(solution)/shard_map/ppermute | solution.py:74
  8.7 3.9 %collective-permute-start.2 = (bf16[7,32,256]{2,1,0:T(8,128)(2,1)S(1)}, bf16[7,32,256]{2,1,0:T(8,128)(2,1)S(1)}, u32[]{:S(2)}, u32[]{:S(2)}) collective-permute-start(bf16[7,32,256]{2,1,0:T(8,128)(2,1)S(1)} %pad_dynamic-slice_fusion), channel_id=1, source_target_pairs={{0,6},{1,7},{2,4},{3,5},{4,2},{5,3},{6,0},{7,1},{8,14},{9,15},{10,... | collective-permute-start | bytes 344072 | tf_op jit(solution)/shard_map/ppermute | solution.py:74
  13.5 5.2 %collective-permute-done.1 = bf16[7,32,256]{2,1,0:T(8,128)(2,1)S(1)} collective-permute-done((bf16[7,32,256]{2,1,0:T(8,128)(2,1)S(1)}, bf16[7,32,256]{2,1,0:T(8,128)(2,1)S(1)}, u32[]{:S(2)}, u32[]{:S(2)}) %collective-permute-start.1) | collective-permute-done | bytes 114720 | tf_op jit(solution)/shard_map/ppermute | solution.py:74
  23.5 3.0 %collective-permute-done.5 = bf16[4,3,32,256]{3,2,1,0:T(8,128)(2,1)S(1)} collective-permute-done((bf16[4,3,32,256]{3,2,1,0:T(8,128)(2,1)S(1)}, bf16[4,3,32,256]{3,2,1,0:T(8,128)(2,1)S(1)}, u32[]{:S(2)}, u32[]{:S(2)}) %collective-permute-start.5) | collective-permute-done | bytes 196640 | tf_op jit(solution)/shard_map/ppermute | solution.py:42
  28.1 3.1 %collective-permute-done.3 = bf16[4,4,32,256]{3,2,1,0:T(8,128)(2,1)S(1)} collective-permute-done((bf16[4,4,32,256]{3,2,1,0:T(8,128)(2,1)S(1)}, bf16[4,4,32,256]{3,2,1,0:T(8,128)(2,1)S(1)}, u32[]{:S(2)}, u32[]{:S(2)}) %collective-permute-start.3) | collective-permute-done | bytes 262176 | tf_op jit(solution)/shard_map/ppermute | solution.py:42
  33.5 6.6 %collective-permute-done.14 = bf16[4,7,32,128]{3,2,1,0:T(8,128)(2,1)S(1)} collective-permute-done((bf16[4,7,32,128]{3,2,1,0:T(8,128)(2,1)S(1)}, bf16[4,7,32,128]{3,2,1,0:T(8,128)(2,1)S(1)}, u32[]{:S(2)}, u32[]{:S(2)}) %collective-permute-start.14) | collective-permute-done | bytes 229408 | tf_op jit(solution)/shard_map/ppermute | solution.py:42
  44.5 5.8 %collective-permute-done.15 = bf16[2,4,7,32,128]{4,3,2,1,0:T(8,128)(2,1)S(1)} collective-permute-done((bf16[2,4,7,32,128]{4,3,2,1,0:T(8,128)(2,1)S(1)}, bf16[2,4,7,32,128]{4,3,2,1,0:T(8,128)(2,1)S(1)}, u32[]{:S(2)}, u32[]{:S(2)}) %collective-permute-start.15) | collective-permute-done | bytes 458784 | tf_op jit(solution)/shard_map/ppermute | solution.py:42
  55.0 4.8 %collective-permute-start.8 = (bf16[2,2,32,128]{3,2,1,0:T(8,128)(2,1)}, bf16[2,2,32,128]{3,2,1,0:T(8,128)(2,1)}, u32[]{:S(2)}, u32[]{:S(2)}) collective-permute-start(bf16[2,2,32,128]{3,2,1,0:T(8,128)(2,1)} %bitcast.24), channel_id=1, source_target_pairs={{0,4},{1,5},{2,6},{3,7},{4,0},{5,1},{6,2},{7,3},{8,12},{9,13},{10,... | collective-permute-start | bytes 98312 | tf_op jit(solution)/shard_map/ppermute | solution.py:42
  60.5 3.4 %collective-permute-start.18 = (bf16[4,9,1,64,128]{4,3,2,1,0:T(8,128)(2,1)S(1)}, bf16[4,9,1,64,128]{4,3,2,1,0:T(8,128)(2,1)S(1)}, u32[]{:S(2)}, u32[]{:S(2)}) collective-permute-start(bf16[4,9,1,64,128]{4,3,2,1,0:T(8,128)(2,1)S(1)} %pad_maximum_fusion.6), channel_id=1, source_target_pairs={{0,1},{1,2},{2,3},{3,4},{4,5},{5,6},{6,7},{8,9},{9,10},{10,11},{11... | collective-permute-start | bytes 1769480 | tf_op jit(solution)/shard_map/ppermute | solution.py:37
  66.9 3.4 %collective-permute-done.9 = bf16[2,2,32,128]{3,2,1,0:T(8,128)(2,1)} collective-permute-done((bf16[2,2,32,128]{3,2,1,0:T(8,128)(2,1)}, bf16[2,2,32,128]{3,2,1,0:T(8,128)(2,1)}, u32[]{:S(2)}, u32[]{:S(2)}) %collective-permute-start.9) | collective-permute-done | bytes 32800 | tf_op jit(solution)/shard_map/ppermute | solution.py:42
  71.0 8.2 %collective-permute-start.10 = (bf16[2,2,32,128]{3,2,1,0:T(8,128)(2,1)S(1)}, bf16[2,2,32,128]{3,2,1,0:T(8,128)(2,1)S(1)}, u32[]{:S(2)}, u32[]{:S(2)}) collective-permute-start(bf16[2,2,32,128]{3,2,1,0:T(8,128)(2,1)S(1)} %bitcast.233), channel_id=1, source_target_pairs={{0,1},{1,0},{2,3},{3,2},{4,5},{5,4},{6,7},{7,6},{8,9},{9,8},{10,11... | collective-permute-start | bytes 98312 | tf_op jit(solution)/shard_map/ppermute | solution.py:42
  81.6 2.5 %shard_map.76 = (bf16[4,4,1,32,256]{4,3,2,1,0:T(8,128)(2,1)S(1)}, bf16[4,1,1,32,256]{4,3,2,1,0:T(8,128)(2,1)S(1)}) custom-call(s32[2]{0:T(128)S(1)} %pad_add_fusion.here, bf16[4,8,7,32,128]{4,3,2,1,0:T(8,128)(2,1)S(1)} %bitcast.188, bf16[3,4,9,4,32,128]{5,4,3,2,1,0:T(8,128)(2,1)S(1)} %shard_map.75.main), custom_call_target="tpu_custom_call" | custom-call | flops 905969664 | bytes 5701640 | tf_op jit(solution)/shard_map/pallas_call | solution.py:136
  87.5 2.7 %shard_map.77 = (bf16[4,4,1,32,256]{4,3,2,1,0:T(8,128)(2,1)S(1)}, bf16[4,1,2,32,256]{4,3,2,1,0:T(8,128)(2,1)S(1)}, bf16[3,4,9,1,32,128]{5,4,3,2,1,0:T(8,128)(2,1)S(1)}) custom-call(s32[2]{0:T(128)S(1)} %pad_add_fusion.here, bf16[4,8,7,32,128]{4,3,2,1,0:T(8,128)(2,1)S(1)} %bitcast.189, bf16[3,4,9,4,32,128]{5,4,3,2,1,0:T(8,128)(2,1)S(1)} %shard_map.75.main, ...), custom_call_target="tpu_custom_call" | custom-call | flops 905969664 | bytes 7503880 | tf_op jit(solution)/shard_map/pallas_call | solution.py:136
  92.1 5.7 %collective-permute-start.21 = (bf16[4,1,1,32,256]{4,3,2,1,0:T(8,128)(2,1)S(1)}, bf16[4,1,1,32,256]{4,3,2,1,0:T(8,128)(2,1)S(1)}, u32[]{:S(2)}, u32[]{:S(2)}) collective-permute-start(bf16[4,1,1,32,256]{4,3,2,1,0:T(8,128)(2,1)S(1)} %get-tuple-element.21), channel_id=1, source_target_pairs={{0,9},{1,10},{2,11},{3,12},{4,13},{5,14},{6,15},{8,17},{9,18},{10,... | collective-permute-start | bytes 196616 | tf_op jit(solution)/shard_map/ppermute | solution.py:37
  99.6 4.9 %shard_map.78 = (bf16[2,8,14,32,128]{4,3,2,1,0:T(8,128)(2,1)S(1)}, bf16[2,8,14,32,128]{4,3,2,1,0:T(8,128)(2,1)S(1)}, bf16[3,4,5,3,16,256]{5,4,3,2,1,0:T(8,128)(2,1)S(1)}) custom-call(s32[2]{0:T(128)S(1)} %pad_add_fusion.here, bf16[8,32,128]{2,1,0:T(8,128)(2,1)S(1)} %bitcast.193, bf16[4,4,1,32,256]{4,3,2,1,0:T(8,128)(2,1)S(1)} %get-tuple-element.19.low, ...), custom_call_target="tpu_custom_call" | custom-call | flops 452984832 | bytes 6193160 | tf_op jit(solution)/shard_map/pallas_call | solution.py:136
  109.0 6.2 %shard_map.82 = (bf16[2,8,7,32,128]{4,3,2,1,0:T(8,128)(2,1)S(1)}, bf16[2,8,7,32,128]{4,3,2,1,0:T(8,128)(2,1)S(1)}) custom-call(s32[2]{0:T(128)S(1)} %pad_add_fusion.here, bf16[4,4,2,32,256]{4,3,2,1,0:T(8,128)(2,1)S(1)} %get-tuple-element.23.cells.grads, bf16[3,4,9,4,32,128]{5,4,3,2,1,0:T(8,128)(2,1)S(1)} %shard_map.75.main, ...), custom_call_target="tpu_custom_call" | custom-call | flops 1811939328 | bytes 6782984 | tf_op jit(solution)/shard_map/pallas_call | solution.py:136
  118.2 2.7 %collective-permute-start.28 = (bf16[2,4,7,32,128]{4,3,2,1,0:T(8,128)(2,1)S(1)}, bf16[2,4,7,32,128]{4,3,2,1,0:T(8,128)(2,1)S(1)}, u32[]{:S(2)}, u32[]{:S(2)}) collective-permute-start(bf16[2,4,7,32,128]{4,3,2,1,0:T(8,128)(2,1)S(1)} %fusion.4), channel_id=1, source_target_pairs={{0,1},{1,0},{2,3},{3,2},{4,5},{5,4},{6,7},{7,6},{8,9},{9,8},{10,11... | collective-permute-start | bytes 1376264 | tf_op jit(solution)/shard_map/ppermute | solution.py:42
  123.0 9.2 %collective-permute-done.28 = bf16[2,4,7,32,128]{4,3,2,1,0:T(8,128)(2,1)S(1)} collective-permute-done((bf16[2,4,7,32,128]{4,3,2,1,0:T(8,128)(2,1)S(1)}, bf16[2,4,7,32,128]{4,3,2,1,0:T(8,128)(2,1)S(1)}, u32[]{:S(2)}, u32[]{:S(2)}) %collective-permute-start.28) | collective-permute-done | bytes 458784 | tf_op jit(solution)/shard_map/ppermute | solution.py:42
  134.6 6.9 %collective-permute-done.36 = bf16[2,4,7,32,128]{4,3,2,1,0:T(8,128)(2,1)S(1)} collective-permute-done((bf16[2,4,7,32,128]{4,3,2,1,0:T(8,128)(2,1)S(1)}, bf16[2,4,7,32,128]{4,3,2,1,0:T(8,128)(2,1)S(1)}, u32[]{:S(2)}, u32[]{:S(2)}) %collective-permute-start.36) | collective-permute-done | bytes 458784 | tf_op jit(solution)/shard_map/ppermute | solution.py:42
  154.4 2.5 %collective-permute-done.38 = bf16[14,32,128]{2,1,0:T(8,128)(2,1)S(1)} collective-permute-done((bf16[14,32,128]{2,1,0:T(8,128)(2,1)S(1)}, bf16[14,32,128]{2,1,0:T(8,128)(2,1)S(1)}, u32[]{:S(2)}, u32[]{:S(2)}) %collective-permute-start.38) | collective-permute-done | bytes 114720 | tf_op jit(solution)/shard_map/ppermute | solution.py:74
  157.0 2.6 %collective-permute-done.40 = bf16[14,32,128]{2,1,0:T(8,128)(2,1)S(1)} collective-permute-done((bf16[14,32,128]{2,1,0:T(8,128)(2,1)S(1)}, bf16[14,32,128]{2,1,0:T(8,128)(2,1)S(1)}, u32[]{:S(2)}, u32[]{:S(2)}) %collective-permute-start.40) | collective-permute-done | bytes 114720 | tf_op jit(solution)/shard_map/ppermute | solution.py:74
  159.5 4.1 %collective-permute-done.39 = bf16[14,32,128]{2,1,0:T(8,128)(2,1)S(1)} collective-permute-done((bf16[14,32,128]{2,1,0:T(8,128)(2,1)S(1)}, bf16[14,32,128]{2,1,0:T(8,128)(2,1)S(1)}, u32[]{:S(2)}, u32[]{:S(2)}) %collective-permute-start.39) | collective-permute-done | bytes 114720 | tf_op jit(solution)/shard_map/ppermute | solution.py:74
  171.6 5.2 %all-to-all-start = ((bf16[8,2,2048]{2,1,0:T(2,128)(2,1)}), bf16[8,2,2048]{2,1,0:T(2,128)(2,1)S(1)}, u32[]{:S(2)}, u32[]{:S(2)}) async-start(bf16[8,2,2048]{2,1,0:T(2,128)(2,1)} %reshape.101), calls=%async_computation | async-start | bytes 131072 | tf_op jit(solution)/shard_map/all_to_all | solution.py:699
  186.2 5.2 %shard_map.81 = bf16[4,8,4,64,128]{4,3,2,1,0:T(8,128)(2,1)} custom-call(s32[2]{0:T(128)S(1)} %pad_add_fusion.here, bf16[4,4,2,32,256]{4,3,2,1,0:T(8,128)(2,1)S(1)} %get-tuple-element.23.cells.grads, bf16[4,1,2,32,256]{4,3,2,1,0:T(8,128)(2,1)S(1)} %collective-permute-done.24.plane, bf16[4,5,1,32,256]{4,3,2,1,0:T(8,128)(2,1)S(1)} %pad_maximum_fusion.15.row, ...), custom_call_target="tpu_custom_call" | custom-call | flops 1811939328 | bytes 4915208 | tf_op jit(solution)/shard_map/pallas_call | solution.py:136
  (153 shorter events, 82.7 us)
Async XLA Ops:
  1.5 30.3 %collective-permute-start.12 = (bf16[7,32,128]{2,1,0:T(8,128)(2,1)S(1)}, bf16[7,32,128]{2,1,0:T(8,128)(2,1)S(1)}, u32[]{:S(2)}, u32[]{:S(2)}) collective-permute-start(bf16[7,32,128]{2,1,0:T(8,128)(2,1)S(1)} %pad_dynamic-slice_fusion.1), channel_id=1, source_target_pairs={{0,4},{1,5},{2,6},{3,7},{4,0},{5,1},{6,2},{7,3},{8,12},{9,13},{10,... | collective-permute-start | bytes 172040 | tf_op jit(solution)/shard_map/ppermute | solution.py:74
  5.6 26.2 %collective-permute-start.11 = (bf16[7,32,128]{2,1,0:T(8,128)(2,1)S(1)}, bf16[7,32,128]{2,1,0:T(8,128)(2,1)S(1)}, u32[]{:S(2)}, u32[]{:S(2)}) collective-permute-start(bf16[7,32,128]{2,1,0:T(8,128)(2,1)S(1)} %pad_dynamic-slice_fusion.1), channel_id=1, source_target_pairs={{0,2},{1,3},{2,0},{3,1},{4,6},{5,7},{6,4},{7,5},{8,10},{9,11},{10,... | collective-permute-start | bytes 172040 | tf_op jit(solution)/shard_map/ppermute | solution.py:74
  8.1 10.6 %collective-permute-start.1 = (bf16[7,32,256]{2,1,0:T(8,128)(2,1)S(1)}, bf16[7,32,256]{2,1,0:T(8,128)(2,1)S(1)}, u32[]{:S(2)}, u32[]{:S(2)}) collective-permute-start(bf16[7,32,256]{2,1,0:T(8,128)(2,1)S(1)} %pad_dynamic-slice_fusion), channel_id=1, source_target_pairs={{0,4},{1,5},{2,6},{3,7},{4,0},{5,1},{6,2},{7,3},{8,12},{9,13},{10,... | collective-permute-start | bytes 344072 | tf_op jit(solution)/shard_map/ppermute | solution.py:74
  8.5 11.8 %collective-permute-start = (bf16[7,32,256]{2,1,0:T(8,128)(2,1)S(1)}, bf16[7,32,256]{2,1,0:T(8,128)(2,1)S(1)}, u32[]{:S(2)}, u32[]{:S(2)}) collective-permute-start(bf16[7,32,256]{2,1,0:T(8,128)(2,1)S(1)} %pad_dynamic-slice_fusion), channel_id=1, source_target_pairs={{0,2},{1,3},{2,0},{3,1},{4,6},{5,7},{6,4},{7,5},{8,10},{9,11},{10,... | collective-permute-start | bytes 344072 | tf_op jit(solution)/shard_map/ppermute | solution.py:74
  8.7 11.6 %collective-permute-start.2 = (bf16[7,32,256]{2,1,0:T(8,128)(2,1)S(1)}, bf16[7,32,256]{2,1,0:T(8,128)(2,1)S(1)}, u32[]{:S(2)}, u32[]{:S(2)}) collective-permute-start(bf16[7,32,256]{2,1,0:T(8,128)(2,1)S(1)} %pad_dynamic-slice_fusion), channel_id=1, source_target_pairs={{0,6},{1,7},{2,4},{3,5},{4,2},{5,3},{6,0},{7,1},{8,14},{9,15},{10,... | collective-permute-start | bytes 344072 | tf_op jit(solution)/shard_map/ppermute | solution.py:74
  18.7 13.1 %collective-permute-start.13 = (bf16[7,32,128]{2,1,0:T(8,128)(2,1)S(1)}, bf16[7,32,128]{2,1,0:T(8,128)(2,1)S(1)}, u32[]{:S(2)}, u32[]{:S(2)}) collective-permute-start(bf16[7,32,128]{2,1,0:T(8,128)(2,1)S(1)} %pad_dynamic-slice_fusion.1), channel_id=1, source_target_pairs={{0,6},{1,7},{2,4},{3,5},{4,2},{5,3},{6,0},{7,1},{8,14},{9,15},{10,... | collective-permute-start | bytes 172040 | tf_op jit(solution)/shard_map/ppermute | solution.py:74
  26.6 15.1 %collective-permute-start.6 = (bf16[2,4,3,32,256]{4,3,2,1,0:T(8,128)(2,1)S(1)}, bf16[2,4,3,32,256]{4,3,2,1,0:T(8,128)(2,1)S(1)}, u32[]{:S(2)}, u32[]{:S(2)}) collective-permute-start(bf16[2,4,3,32,256]{4,3,2,1,0:T(8,128)(2,1)S(1)} %get-tuple-element.66), channel_id=1, source_target_pairs={{0,1},{1,0},{2,3},{3,2},{4,5},{5,4},{6,7},{7,6},{8,9},{9,8},{10,11... | collective-permute-start | bytes 1179656 | tf_op jit(solution)/shard_map/ppermute | solution.py:42
  31.2 11.2 %collective-permute-start.4 = (bf16[2,4,4,32,256]{4,3,2,1,0:T(8,128)(2,1)S(1)}, bf16[2,4,4,32,256]{4,3,2,1,0:T(8,128)(2,1)S(1)}, u32[]{:S(2)}, u32[]{:S(2)}) collective-permute-start(bf16[2,4,4,32,256]{4,3,2,1,0:T(8,128)(2,1)S(1)} %get-tuple-element.57), channel_id=1, source_target_pairs={{0,16},{8,24},{16,0},{24,8},{1,17},{9,25},{17,1},{25,9},{2,18},{10... | collective-permute-start | bytes 1572872 | tf_op jit(solution)/shard_map/ppermute | solution.py:42
  44.5 60.8 %collective-permute-start.7 = (bf16[2,2,4,7,32,256]{5,4,3,2,1,0:T(8,128)(2,1)}, bf16[2,2,4,7,32,256]{5,4,3,2,1,0:T(8,128)(2,1)}, u32[]{:S(2)}, u32[]{:S(2)}) collective-permute-start(bf16[2,2,4,7,32,256]{5,4,3,2,1,0:T(8,128)(2,1)} %get-tuple-element.45), channel_id=1, source_target_pairs={{0,8},{8,0},{16,24},{24,16},{1,9},{9,1},{17,25},{25,17},{2,10},{10... | collective-permute-start | bytes 5505032 | tf_op jit(solution)/shard_map/ppermute | solution.py:42
  51.7 28.5 %collective-permute-start.16 = (bf16[2,2,4,7,32,128]{5,4,3,2,1,0:T(8,128)(2,1)}, bf16[2,2,4,7,32,128]{5,4,3,2,1,0:T(8,128)(2,1)}, u32[]{:S(2)}, u32[]{:S(2)}) collective-permute-start(bf16[2,2,4,7,32,128]{5,4,3,2,1,0:T(8,128)(2,1)} %get-tuple-element.47), channel_id=1, source_target_pairs={{0,8},{8,0},{16,24},{24,16},{1,9},{9,1},{17,25},{25,17},{2,10},{10... | collective-permute-start | bytes 2752520 | tf_op jit(solution)/shard_map/ppermute | solution.py:42
  60.5 27.0 %collective-permute-start.18 = (bf16[4,9,1,64,128]{4,3,2,1,0:T(8,128)(2,1)S(1)}, bf16[4,9,1,64,128]{4,3,2,1,0:T(8,128)(2,1)S(1)}, u32[]{:S(2)}, u32[]{:S(2)}) collective-permute-start(bf16[4,9,1,64,128]{4,3,2,1,0:T(8,128)(2,1)S(1)} %pad_maximum_fusion.6), channel_id=1, source_target_pairs={{0,1},{1,2},{2,3},{3,4},{4,5},{5,6},{6,7},{8,9},{9,10},{10,11},{11... | collective-permute-start | bytes 1769480 | tf_op jit(solution)/shard_map/ppermute | solution.py:37
  71.0 15.2 %collective-permute-start.10 = (bf16[2,2,32,128]{3,2,1,0:T(8,128)(2,1)S(1)}, bf16[2,2,32,128]{3,2,1,0:T(8,128)(2,1)S(1)}, u32[]{:S(2)}, u32[]{:S(2)}) collective-permute-start(bf16[2,2,32,128]{3,2,1,0:T(8,128)(2,1)S(1)} %bitcast.233), channel_id=1, source_target_pairs={{0,1},{1,0},{2,3},{3,2},{4,5},{5,4},{6,7},{7,6},{8,9},{9,8},{10,11... | collective-permute-start | bytes 98312 | tf_op jit(solution)/shard_map/ppermute | solution.py:42
  84.1 15.5 %collective-permute-start.20 = (bf16[4,4,1,32,256]{4,3,2,1,0:T(8,128)(2,1)S(1)}, bf16[4,4,1,32,256]{4,3,2,1,0:T(8,128)(2,1)S(1)}, u32[]{:S(2)}, u32[]{:S(2)}) collective-permute-start(bf16[4,4,1,32,256]{4,3,2,1,0:T(8,128)(2,1)S(1)} %get-tuple-element.18.rest_1_.high), channel_id=1, source_target_pairs={{0,1},{1,2},{2,3},{3,4},{4,5},{5,6},{6,7},{8,9},{9,10},{10,11},{11... | collective-permute-start | bytes 786440 | tf_op jit(solution)/shard_map/ppermute | solution.py:37
  86.2 11.6 %collective-permute-start.22 = (bf16[8,32,128]{2,1,0:T(8,128)(2,1)S(1)}, bf16[8,32,128]{2,1,0:T(8,128)(2,1)S(1)}, u32[]{:S(2)}, u32[]{:S(2)}) collective-permute-start(bf16[8,32,128]{2,1,0:T(8,128)(2,1)S(1)} %bitcast.191), channel_id=1, source_target_pairs={{1,0},{2,1},{3,2},{4,3},{5,4},{6,5},{7,6},{9,8},{10,9},{11,10},{12... | collective-permute-start | bytes 196616 | tf_op jit(solution)/shard_map/ppermute | solution.py:37
  104.6 16.3 %collective-permute-start.33 = (bf16[2,8,14,32,128]{4,3,2,1,0:T(8,128)(2,1)S(1)}, bf16[2,8,14,32,128]{4,3,2,1,0:T(8,128)(2,1)S(1)}, u32[]{:S(2)}, u32[]{:S(2)}) collective-permute-start(bf16[2,8,14,32,128]{4,3,2,1,0:T(8,128)(2,1)S(1)} %get-tuple-element.31), channel_id=1, source_target_pairs={{0,8},{8,0},{16,24},{24,16},{1,9},{9,1},{17,25},{25,17},{2,10},{10... | collective-permute-start | bytes 5505032 | tf_op jit(solution)/shard_map/ppermute | solution.py:42
  118.2 14.1 %collective-permute-start.28 = (bf16[2,4,7,32,128]{4,3,2,1,0:T(8,128)(2,1)S(1)}, bf16[2,4,7,32,128]{4,3,2,1,0:T(8,128)(2,1)S(1)}, u32[]{:S(2)}, u32[]{:S(2)}) collective-permute-start(bf16[2,4,7,32,128]{4,3,2,1,0:T(8,128)(2,1)S(1)} %fusion.4), channel_id=1, source_target_pairs={{0,1},{1,0},{2,3},{3,2},{4,5},{5,4},{6,7},{7,6},{8,9},{9,8},{10,11... | collective-permute-start | bytes 1376264 | tf_op jit(solution)/shard_map/ppermute | solution.py:42
  122.0 12.6 %collective-permute-start.34 = (bf16[2,4,7,32,128]{4,3,2,1,0:T(8,128)(2,1)S(1)}, bf16[2,4,7,32,128]{4,3,2,1,0:T(8,128)(2,1)S(1)}, u32[]{:S(2)}, u32[]{:S(2)}) collective-permute-start(bf16[2,4,7,32,128]{4,3,2,1,0:T(8,128)(2,1)S(1)} %slice_bitcast_fusion.6), channel_id=1, source_target_pairs={{0,16},{8,24},{16,0},{24,8},{1,17},{9,25},{17,1},{25,9},{2,18},{10... | collective-permute-start | bytes 1376264 | tf_op jit(solution)/shard_map/ppermute | solution.py:42
  123.0 18.5 %collective-permute-start.36 = (bf16[2,4,7,32,128]{4,3,2,1,0:T(8,128)(2,1)S(1)}, bf16[2,4,7,32,128]{4,3,2,1,0:T(8,128)(2,1)S(1)}, u32[]{:S(2)}, u32[]{:S(2)}) collective-permute-start(bf16[2,4,7,32,128]{4,3,2,1,0:T(8,128)(2,1)S(1)} %slice_bitcast_fusion.4), channel_id=1, source_target_pairs={{0,1},{1,0},{2,3},{3,2},{4,5},{5,4},{6,7},{7,6},{8,9},{9,8},{10,11... | collective-permute-start | bytes 1376264 | tf_op jit(solution)/shard_map/ppermute | solution.py:42
  132.4 12.4 %collective-permute-start.29 = (bf16[4,7,32,128]{3,2,1,0:T(8,128)(2,1)S(1)}, bf16[4,7,32,128]{3,2,1,0:T(8,128)(2,1)S(1)}, u32[]{:S(2)}, u32[]{:S(2)}) collective-permute-start(bf16[4,7,32,128]{3,2,1,0:T(8,128)(2,1)S(1)} %fusion.8), channel_id=1, source_target_pairs={{0,16},{8,24},{16,0},{24,8},{1,17},{9,25},{17,1},{25,9},{2,18},{10... | collective-permute-start | bytes 688136 | tf_op jit(solution)/shard_map/ppermute | solution.py:42
  164.4 12.4 %collective-permute-start.41 = (bf16[21,32,128]{2,1,0:T(8,128)(2,1)}, bf16[21,32,128]{2,1,0:T(8,128)(2,1)}, u32[]{:S(2)}, u32[]{:S(2)}) collective-permute-start(bf16[21,32,128]{2,1,0:T(8,128)(2,1)} %get-tuple-element.77), channel_id=1, source_target_pairs={{0,16},{8,24},{16,0},{24,8},{1,17},{9,25},{17,1},{25,9},{2,18},{10... | collective-permute-start | bytes 516104 | tf_op jit(solution)/shard_map/ppermute | solution.py:42
  165.3 19.9 %collective-permute-start.25 = (bf16[4,4,1,32,256]{4,3,2,1,0:T(8,128)(2,1)}, bf16[4,4,1,32,256]{4,3,2,1,0:T(8,128)(2,1)}, u32[]{:S(2)}, u32[]{:S(2)}) collective-permute-start(bf16[4,4,1,32,256]{4,3,2,1,0:T(8,128)(2,1)} %get-tuple-element.25), channel_id=1, source_target_pairs={{1,0},{2,1},{3,2},{4,3},{5,4},{6,5},{7,6},{9,8},{10,9},{11,10},{12... | collective-permute-start | bytes 786440 | tf_op jit(solution)/shard_map/ppermute | solution.py:37
  166.6 18.6 %collective-permute-start.26 = (bf16[4,1,1,32,256]{4,3,2,1,0:T(8,128)(2,1)S(1)}, bf16[4,1,1,32,256]{4,3,2,1,0:T(8,128)(2,1)S(1)}, u32[]{:S(2)}, u32[]{:S(2)}) collective-permute-start(bf16[4,1,1,32,256]{4,3,2,1,0:T(8,128)(2,1)S(1)} %get-tuple-element.26), channel_id=1, source_target_pairs={{9,0},{10,1},{11,2},{12,3},{13,4},{14,5},{15,6},{17,8},{18,9},{19,... | collective-permute-start | bytes 196616 | tf_op jit(solution)/shard_map/ppermute | solution.py:37
  171.6 12.1 %all-to-all-start = ((bf16[8,2,2048]{2,1,0:T(2,128)(2,1)}), bf16[8,2,2048]{2,1,0:T(2,128)(2,1)S(1)}, u32[]{:S(2)}, u32[]{:S(2)}) async-start(bf16[8,2,2048]{2,1,0:T(2,128)(2,1)} %reshape.101), calls=%async_computation | async-start | bytes 131072 | tf_op jit(solution)/shard_map/all_to_all | solution.py:699
  178.6 12.8 %collective-permute-start.42 = (bf16[2,21,32,128]{3,2,1,0:T(8,128)(2,1)}, bf16[2,21,32,128]{3,2,1,0:T(8,128)(2,1)}, u32[]{:S(2)}, u32[]{:S(2)}) collective-permute-start(bf16[2,21,32,128]{3,2,1,0:T(8,128)(2,1)} %get-tuple-element.68), channel_id=1, source_target_pairs={{0,8},{8,0},{16,24},{24,16},{1,9},{9,1},{17,25},{25,17},{2,10},{10... | collective-permute-start | bytes 1032200 | tf_op jit(solution)/shard_map/ppermute | solution.py:42
  (27 other events, 223.5 us)

commit v7 on v6

--- a/solution.py
+++ b/solution.py
@@ -238,6 +238,8 @@
     cells = vols * sides[1] * len(cells_b) * depth
     outs = [jax.ShapeDtypeStruct((vols, sides[1], len(cells_b), depth, count), BF16)]
     scratch = [pltpu.VMEM((cells, count), F32)]
+    if kind == "u":
+        outs = [jax.ShapeDtypeStruct((count, cells), BF16)]
     if kind == "h":
         outs.append(jax.ShapeDtypeStruct((vols, 1, 1, depth, count), BF16))
     if kind == "l":
@@ -262,6 +264,9 @@
         total = forward_total(orders, sides, refs, here, filters, acc)
         if kind != "u":
             total = leaky(total)
+        if kind == "u":
+            out[...] = jnp.transpose(total, (1, 0)).astype(BF16)
+            return
         value = total.astype(BF16).reshape(out.shape)
         out[...] = value
         if kind == "h":
@@ -433,26 +438,20 @@
     return jnp.concatenate([one, two], axis=-3)
 
 
-def finish_sum(totals):
+def finish_sum(part):
     space = lax.axis_size(SPACE)
-    part = merged = jnp.concatenate(totals, axis=0)
+    rows, mine = part.shape[:2]
+    taps = -(-27 // space)
+    pieces = rows // taps
+    shape = part.shape
     for bit in high_bits():
         part = doubled(part, SPACE, bit)
-    part = doubled(part, SPACE, 0)
-    part = part.reshape((space,) + merged.shape)
+    part = doubled(part, SPACE, 0).reshape((space,) + shape)
     apart = [jnp.int32(s) ^ lax.axis_index(SPACE) for s in range(space)]
     ordered = [lax.dynamic_index_in_dim(part, space_order(a), 0, keepdims=False) for a in apart]
-    outs, begin = [], 0
-    taps = -(-27 // space)
-    for total in totals:
-        rows, mine = total.shape[0], total.shape[1]
-        pieces = rows // taps
-        full = jnp.concatenate([o[begin : begin + rows] for o in ordered], axis=0)
-        full = full.reshape(space * taps, pieces, mine, LANES)[:27].astype(F32)
-        full = jnp.transpose(full, (0, 1, 3, 2)).reshape(3, 3, 3, pieces * LANES, mine)
-        outs.append(full)
-        begin += rows
-    return outs
+    full = jnp.concatenate(ordered, axis=0)
+    full = full.reshape(space * taps, pieces, mine, LANES)[:27].astype(F32)
+    return jnp.transpose(full, (0, 1, 3, 2)).reshape(3, 3, 3, pieces * LANES, mine)
 
 
 def space_order(apart):
@@ -689,14 +688,18 @@
     )
     keep, send = first_grads(here, (vol_main, vol_row), pre_back, orders)
     first_sum = far_sum(plain_sum(core_sum(keep, send)))
-    first_grad, second_grad = finish_sum([first_sum, second_sum])
+    first_grad = finish_sum(first_sum)
+    second_grad = finish_sum(second_sum)
     plane = shifted(pre_plane, (-1, 0))
     row = shifted(pre_row, (0, -1))
     corner = shifted(corner, (-1, -1))
     row = jnp.concatenate([row, corner], axis=1)
     out_b = range(act_parts.shape[3] // 2)
     (local_out,) = forward(here, (act_parts,), second_full, orders, out_b, "u")
-    second_out = lax.all_to_all(local_out, CHAN, split_axis=4, concat_axis=2, tiled=True)
+    second_out = lax.all_to_all(local_out, CHAN, split_axis=0, concat_axis=0, tiled=True)
+    vols, side_a, rows, deep, mine = cotangent.shape
+    second_out = second_out.reshape(rows, mine, vols, side_a, deep)
+    second_out = jnp.transpose(second_out, (2, 3, 0, 4, 1))
     volume_grad = volume_grads(here, pre_back, plane, row, first_full, orders)
     return (second_out, volume_grad, first_grad, second_grad)
 

time: 197 us -> 206 us (1.046)
  starting transfers between devices: 78.1 us -> 83.4 us
  Pallas kernels: 26.7 us -> 29.7 us
    another operation x12 -> x13, other arithmetic: 10.5 us -> 7.03 us  [doubled(): return jnp.stack([value, other])]
    all_to_all x1, starting transfers between devices: 5.16 us -> 8.57 us  [local(): lax.all_to_all(local_out, CHAN, split_axis=0, concat_axis=0, tiled=True)]
    ppermute x21 -> x23, waiting for transfers between devices: 43.9 us -> 40.6 us  [swapped(): return lax.ppermute(value, axis, [(i, i ^ 1 << bit) for i in range(count)])]
    pallas_call x8, Pallas kernels: 26.7 us -> 29.7 us  [call(): pl.pallas_call(kernel, out_shape=outs, grid=grid or (), in_specs=specs, o...]
    add x2, other arithmetic: 0.88 us -> 3.63 us  [core_sum(): total = keep.astype(F32) + other.astype(F32)]
    ppermute x21 -> x23, starting transfers between devices: 32.3 us -> 32.5 us  [swapped(): return lax.ppermute(value, axis, [(i, i ^ 1 << bit) for i in range(count)])]
  transfers between devices with their start and end apart: 44 -> 46, of which waited for: 19 -> 19; matrix products, arithmetic and copies ran while one was open for 11% -> 11% of each run, Pallas kernels for 14% -> 14%
where the time goes in v7:
time: 206 us; the launch traced here: 205 us
  starting transfers between devices  83.4 us (40%)
  waiting for transfers between devices  62.2 us (30%)
  Pallas kernels  29.7 us (14%)
  other arithmetic  16.3 us (8%)
  local copies, waits for them, and re-layouts  12.1 us (6%)
    ppermute x23, waiting for transfers between devices, swapped(): return lax.ppermute(value, axis, [(i, i ^ 1 << bit) for i in range(count)])  40.6 us
    ppermute x23, starting transfers between devices, swapped(): return lax.ppermute(value, axis, [(i, i ^ 1 << bit) for i in range(count)])  32.5 us
    pallas_call x8, Pallas kernels, call(): pl.pallas_call(kernel, out_shape=outs, grid=grid or (), in_specs=specs, o...  29.7 us
    ppermute x10, starting transfers between devices, shifted(): return lax.ppermute(value, (SPACE, CHAN), pairs)  22 us
    ppermute x12, starting transfers between devices, far_swapped(): return lax.ppermute(value, CHAN, [(i, i ^ mask << 1) for i in range(count)])  20.2 us
    ppermute x12, waiting for transfers between devices, far_swapped(): return lax.ppermute(value, CHAN, [(i, i ^ mask << 1) for i in range(count)])  16.9 us
    all_to_all x1, starting transfers between devices, local(): lax.all_to_all(local_out, CHAN, split_axis=0, concat_axis=0, tiled=True)  8.57 us
    another operation x13, other arithmetic, doubled(): return jnp.stack([value, other])  7.03 us
  transfers between devices with their start and end apart: 46, of which 19 were waited for; matrix products, arithmetic and copies ran while one was open for 11% of the time, Pallas kernels for 14%

profile of v7, /device:TPU:0, one launch (start us, length us, event | category | flops | bytes accessed | tf_op | source)
XLA Modules:
  0.0 204.9 jit_solution(12467012322004948210)
XLA Ops:
  1.5 4.1 %collective-permute-start.12 = (bf16[7,32,128]{2,1,0:T(8,128)(2,1)S(1)}, bf16[7,32,128]{2,1,0:T(8,128)(2,1)S(1)}, u32[]{:S(2)}, u32[]{:S(2)}) collective-permute-start(bf16[7,32,128]{2,1,0:T(8,128)(2,1)S(1)} %pad_dynamic-slice_fusion.1), channel_id=1, source_target_pairs={{0,4},{1,5},{2,6},{3,7},{4,0},{5,1},{6,2},{7,3},{8,12},{9,13},{10,... | collective-permute-start | bytes 172040 | tf_op jit(solution)/shard_map/ppermute | solution.py:74
  8.7 3.9 %collective-permute-start.2 = (bf16[7,32,256]{2,1,0:T(8,128)(2,1)S(1)}, bf16[7,32,256]{2,1,0:T(8,128)(2,1)S(1)}, u32[]{:S(2)}, u32[]{:S(2)}) collective-permute-start(bf16[7,32,256]{2,1,0:T(8,128)(2,1)S(1)} %pad_dynamic-slice_fusion), channel_id=1, source_target_pairs={{0,6},{1,7},{2,4},{3,5},{4,2},{5,3},{6,0},{7,1},{8,14},{9,15},{10,... | collective-permute-start | bytes 344072 | tf_op jit(solution)/shard_map/ppermute | solution.py:74
  13.5 5.2 %collective-permute-done.1 = bf16[7,32,256]{2,1,0:T(8,128)(2,1)S(1)} collective-permute-done((bf16[7,32,256]{2,1,0:T(8,128)(2,1)S(1)}, bf16[7,32,256]{2,1,0:T(8,128)(2,1)S(1)}, u32[]{:S(2)}, u32[]{:S(2)}) %collective-permute-start.1) | collective-permute-done | bytes 114720 | tf_op jit(solution)/shard_map/ppermute | solution.py:74
  23.5 3.0 %collective-permute-done.5 = bf16[4,3,32,256]{3,2,1,0:T(8,128)(2,1)S(1)} collective-permute-done((bf16[4,3,32,256]{3,2,1,0:T(8,128)(2,1)S(1)}, bf16[4,3,32,256]{3,2,1,0:T(8,128)(2,1)S(1)}, u32[]{:S(2)}, u32[]{:S(2)}) %collective-permute-start.5) | collective-permute-done | bytes 196640 | tf_op jit(solution)/shard_map/ppermute | solution.py:42
  28.1 3.1 %collective-permute-done.3 = bf16[4,4,32,256]{3,2,1,0:T(8,128)(2,1)S(1)} collective-permute-done((bf16[4,4,32,256]{3,2,1,0:T(8,128)(2,1)S(1)}, bf16[4,4,32,256]{3,2,1,0:T(8,128)(2,1)S(1)}, u32[]{:S(2)}, u32[]{:S(2)}) %collective-permute-start.3) | collective-permute-done | bytes 262176 | tf_op jit(solution)/shard_map/ppermute | solution.py:42
  33.5 6.6 %collective-permute-done.14 = bf16[4,7,32,128]{3,2,1,0:T(8,128)(2,1)S(1)} collective-permute-done((bf16[4,7,32,128]{3,2,1,0:T(8,128)(2,1)S(1)}, bf16[4,7,32,128]{3,2,1,0:T(8,128)(2,1)S(1)}, u32[]{:S(2)}, u32[]{:S(2)}) %collective-permute-start.14) | collective-permute-done | bytes 229408 | tf_op jit(solution)/shard_map/ppermute | solution.py:42
  44.5 5.8 %collective-permute-done.15 = bf16[2,4,7,32,128]{4,3,2,1,0:T(8,128)(2,1)S(1)} collective-permute-done((bf16[2,4,7,32,128]{4,3,2,1,0:T(8,128)(2,1)S(1)}, bf16[2,4,7,32,128]{4,3,2,1,0:T(8,128)(2,1)S(1)}, u32[]{:S(2)}, u32[]{:S(2)}) %collective-permute-start.15) | collective-permute-done | bytes 458784 | tf_op jit(solution)/shard_map/ppermute | solution.py:42
  55.0 4.8 %collective-permute-start.8 = (bf16[2,2,32,128]{3,2,1,0:T(8,128)(2,1)}, bf16[2,2,32,128]{3,2,1,0:T(8,128)(2,1)}, u32[]{:S(2)}, u32[]{:S(2)}) collective-permute-start(bf16[2,2,32,128]{3,2,1,0:T(8,128)(2,1)} %bitcast.24), channel_id=1, source_target_pairs={{0,4},{1,5},{2,6},{3,7},{4,0},{5,1},{6,2},{7,3},{8,12},{9,13},{10,... | collective-permute-start | bytes 98312 | tf_op jit(solution)/shard_map/ppermute | solution.py:42
  60.5 3.4 %collective-permute-start.18 = (bf16[4,9,1,64,128]{4,3,2,1,0:T(8,128)(2,1)S(1)}, bf16[4,9,1,64,128]{4,3,2,1,0:T(8,128)(2,1)S(1)}, u32[]{:S(2)}, u32[]{:S(2)}) collective-permute-start(bf16[4,9,1,64,128]{4,3,2,1,0:T(8,128)(2,1)S(1)} %pad_maximum_fusion.5), channel_id=1, source_target_pairs={{0,1},{1,2},{2,3},{3,4},{4,5},{5,6},{6,7},{8,9},{9,10},{10,11},{11... | collective-permute-start | bytes 1769480 | tf_op jit(solution)/shard_map/ppermute | solution.py:37
  66.9 3.4 %collective-permute-done.9 = bf16[2,2,32,128]{3,2,1,0:T(8,128)(2,1)} collective-permute-done((bf16[2,2,32,128]{3,2,1,0:T(8,128)(2,1)}, bf16[2,2,32,128]{3,2,1,0:T(8,128)(2,1)}, u32[]{:S(2)}, u32[]{:S(2)}) %collective-permute-start.9) | collective-permute-done | bytes 32800 | tf_op jit(solution)/shard_map/ppermute | solution.py:42
  71.0 8.2 %collective-permute-start.10 = (bf16[2,2,32,128]{3,2,1,0:T(8,128)(2,1)S(1)}, bf16[2,2,32,128]{3,2,1,0:T(8,128)(2,1)S(1)}, u32[]{:S(2)}, u32[]{:S(2)}) collective-permute-start(bf16[2,2,32,128]{3,2,1,0:T(8,128)(2,1)S(1)} %bitcast.240), channel_id=1, source_target_pairs={{0,1},{1,0},{2,3},{3,2},{4,5},{5,4},{6,7},{7,6},{8,9},{9,8},{10,11... | collective-permute-start | bytes 98312 | tf_op jit(solution)/shard_map/ppermute | solution.py:42
  87.5 2.7 %shard_map.77 = (bf16[4,4,1,32,256]{4,3,2,1,0:T(8,128)(2,1)S(1)}, bf16[4,1,2,32,256]{4,3,2,1,0:T(8,128)(2,1)S(1)}, bf16[3,4,9,1,32,128]{5,4,3,2,1,0:T(8,128)(2,1)S(1)}) custom-call(s32[2]{0:T(128)S(1)} %pad_add_fusion.here, bf16[4,8,7,32,128]{4,3,2,1,0:T(8,128)(2,1)S(1)} %bitcast.192, bf16[3,4,9,4,32,128]{5,4,3,2,1,0:T(8,128)(2,1)S(1)} %shard_map.75.main, ...), custom_call_target="tpu_custom_call" | custom-call | flops 905969664 | bytes 7503880 | tf_op jit(solution)/shard_map/pallas_call | solution.py:136
  92.1 5.7 %collective-permute-start.21 = (bf16[4,1,1,32,256]{4,3,2,1,0:T(8,128)(2,1)S(1)}, bf16[4,1,1,32,256]{4,3,2,1,0:T(8,128)(2,1)S(1)}, u32[]{:S(2)}, u32[]{:S(2)}) collective-permute-start(bf16[4,1,1,32,256]{4,3,2,1,0:T(8,128)(2,1)S(1)} %get-tuple-element.21), channel_id=1, source_target_pairs={{0,9},{1,10},{2,11},{3,12},{4,13},{5,14},{6,15},{8,17},{9,18},{10,... | collective-permute-start | bytes 196616 | tf_op jit(solution)/shard_map/ppermute | solution.py:37
  99.6 6.2 %shard_map.78 = (bf16[2,8,14,32,128]{4,3,2,1,0:T(8,128)(2,1)S(1)}, bf16[2,8,14,32,128]{4,3,2,1,0:T(8,128)(2,1)}, bf16[3,4,5,3,16,256]{5,4,3,2,1,0:T(8,128)(2,1)S(1)}) custom-call(s32[2]{0:T(128)S(1)} %pad_add_fusion.here, bf16[8,32,128]{2,1,0:T(8,128)(2,1)S(1)} %bitcast.196, bf16[4,4,1,32,256]{4,3,2,1,0:T(8,128)(2,1)S(1)} %get-tuple-element.19.low, ...), custom_call_target="tpu_custom_call" | custom-call | flops 452984832 | bytes 6193160 | tf_op jit(solution)/shard_map/pallas_call | solution.py:136
  111.5 7.0 %shard_map.82 = (bf16[2,8,7,32,128]{4,3,2,1,0:T(8,128)(2,1)S(1)}, bf16[2,8,7,32,128]{4,3,2,1,0:T(8,128)(2,1)}) custom-call(s32[2]{0:T(128)S(1)} %pad_add_fusion.here, bf16[4,4,2,32,256]{4,3,2,1,0:T(8,128)(2,1)S(1)} %get-tuple-element.23.cells.grads, bf16[3,4,9,4,32,128]{5,4,3,2,1,0:T(8,128)(2,1)S(1)} %shard_map.75.main, ...), custom_call_target="tpu_custom_call" | custom-call | flops 1811939328 | bytes 6782984 | tf_op jit(solution)/shard_map/pallas_call | solution.py:136
  119.8 3.0 %shard_map.79 = bf16[256,128]{1,0:T(8,128)(2,1)} custom-call(s32[2]{0:T(128)S(1)} %pad_add_fusion.here, bf16[4,8,7,32,256]{4,3,2,1,0:T(8,128)(2,1)S(1)} %bitcast.190, bf16[3,4,5,3,16,256]{5,4,3,2,1,0:T(8,128)(2,1)S(1)} %get-tuple-element.22.main), custom_call_target="tpu_custom_call" | custom-call | flops 452984832 | bytes 5210120 | tf_op jit(solution)/shard_map/pallas_call | solution.py:136
  122.7 8.6 %all-to-all-start = ((bf16[8,32,128]{2,1,0:T(8,128)(2,1)}), bf16[8,32,128]{2,1,0:T(8,128)(2,1)S(1)}, u32[]{:S(2)}, u32[]{:S(2)}) async-start(bf16[8,32,128]{2,1,0:T(8,128)(2,1)} %bitcast.46), calls=%async_computation | async-start | bytes 131072 | tf_op jit(solution)/shard_map/all_to_all | solution.py:699
  134.1 4.1 %all-to-all-done = bf16[8,32,128]{2,1,0:T(8,128)(2,1)S(1)} async-done(((bf16[8,32,128]{2,1,0:T(8,128)(2,1)}), bf16[8,32,128]{2,1,0:T(8,128)(2,1)S(1)}, u32[]{:S(2)}, u32[]{:S(2)}) %all-to-all-start) | async-done | bytes 65568 | tf_op jit(solution)/shard_map/all_to_all | solution.py:699
  141.8 5.4 %shard_map.81 = bf16[4,8,4,64,128]{4,3,2,1,0:T(8,128)(2,1)} custom-call(s32[2]{0:T(128)S(1)} %pad_add_fusion.here, bf16[4,4,2,32,256]{4,3,2,1,0:T(8,128)(2,1)S(1)} %get-tuple-element.23.cells.grads, bf16[4,1,2,32,256]{4,3,2,1,0:T(8,128)(2,1)} %collective-permute-done.24.plane, bf16[4,5,1,32,256]{4,3,2,1,0:T(8,128)(2,1)S(1)} %pad_maximum_fusion.14.row, ...), custom_call_target="tpu_custom_call" | custom-call | flops 1811939328 | bytes 4915208 | tf_op jit(solution)/shard_map/pallas_call | solution.py:136
  155.0 7.3 %collective-permute-done.28 = bf16[2,4,7,32,128]{4,3,2,1,0:T(8,128)(2,1)S(1)} collective-permute-done((bf16[2,4,7,32,128]{4,3,2,1,0:T(8,128)(2,1)S(1)}, bf16[2,4,7,32,128]{4,3,2,1,0:T(8,128)(2,1)S(1)}, u32[]{:S(2)}, u32[]{:S(2)}) %collective-permute-start.28) | collective-permute-done | bytes 458784 | tf_op jit(solution)/shard_map/ppermute | solution.py:42
  165.4 4.6 %collective-permute-done.38 = bf16[2,4,7,32,128]{4,3,2,1,0:T(8,128)(2,1)S(1)} collective-permute-done((bf16[2,4,7,32,128]{4,3,2,1,0:T(8,128)(2,1)S(1)}, bf16[2,4,7,32,128]{4,3,2,1,0:T(8,128)(2,1)S(1)}, u32[]{:S(2)}, u32[]{:S(2)}) %collective-permute-start.38) | collective-permute-done | bytes 458784 | tf_op jit(solution)/shard_map/ppermute | solution.py:42
  182.6 3.0 %collective-permute-start.40 = (bf16[14,32,128]{2,1,0:T(8,128)(2,1)S(1)}, bf16[14,32,128]{2,1,0:T(8,128)(2,1)S(1)}, u32[]{:S(2)}, u32[]{:S(2)}) collective-permute-start(bf16[14,32,128]{2,1,0:T(8,128)(2,1)S(1)} %get-tuple-element.62), channel_id=1, source_target_pairs={{0,2},{1,3},{2,0},{3,1},{4,6},{5,7},{6,4},{7,5},{8,10},{9,11},{10,... | collective-permute-start | bytes 344072 | tf_op jit(solution)/shard_map/ppermute | solution.py:74
  192.3 3.5 %collective-permute-done.41 = bf16[14,32,128]{2,1,0:T(8,128)(2,1)S(1)} collective-permute-done((bf16[14,32,128]{2,1,0:T(8,128)(2,1)S(1)}, bf16[14,32,128]{2,1,0:T(8,128)(2,1)S(1)}, u32[]{:S(2)}, u32[]{:S(2)}) %collective-permute-start.41) | collective-permute-done | bytes 114720 | tf_op jit(solution)/shard_map/ppermute | solution.py:74
  196.7 4.0 %collective-permute-done.43 = bf16[14,32,128]{2,1,0:T(8,128)(2,1)S(1)} collective-permute-done((bf16[14,32,128]{2,1,0:T(8,128)(2,1)S(1)}, bf16[14,32,128]{2,1,0:T(8,128)(2,1)S(1)}, u32[]{:S(2)}, u32[]{:S(2)}) %collective-permute-start.43) | collective-permute-done | bytes 114720 | tf_op jit(solution)/shard_map/ppermute | solution.py:42
  (158 shorter events, 87.1 us)
Async XLA Ops:
  1.5 30.3 %collective-permute-start.12 = (bf16[7,32,128]{2,1,0:T(8,128)(2,1)S(1)}, bf16[7,32,128]{2,1,0:T(8,128)(2,1)S(1)}, u32[]{:S(2)}, u32[]{:S(2)}) collective-permute-start(bf16[7,32,128]{2,1,0:T(8,128)(2,1)S(1)} %pad_dynamic-slice_fusion.1), channel_id=1, source_target_pairs={{0,4},{1,5},{2,6},{3,7},{4,0},{5,1},{6,2},{7,3},{8,12},{9,13},{10,... | collective-permute-start | bytes 172040 | tf_op jit(solution)/shard_map/ppermute | solution.py:74
  5.6 26.2 %collective-permute-start.11 = (bf16[7,32,128]{2,1,0:T(8,128)(2,1)S(1)}, bf16[7,32,128]{2,1,0:T(8,128)(2,1)S(1)}, u32[]{:S(2)}, u32[]{:S(2)}) collective-permute-start(bf16[7,32,128]{2,1,0:T(8,128)(2,1)S(1)} %pad_dynamic-slice_fusion.1), channel_id=1, source_target_pairs={{0,2},{1,3},{2,0},{3,1},{4,6},{5,7},{6,4},{7,5},{8,10},{9,11},{10,... | collective-permute-start | bytes 172040 | tf_op jit(solution)/shard_map/ppermute | solution.py:74
  8.1 10.6 %collective-permute-start.1 = (bf16[7,32,256]{2,1,0:T(8,128)(2,1)S(1)}, bf16[7,32,256]{2,1,0:T(8,128)(2,1)S(1)}, u32[]{:S(2)}, u32[]{:S(2)}) collective-permute-start(bf16[7,32,256]{2,1,0:T(8,128)(2,1)S(1)} %pad_dynamic-slice_fusion), channel_id=1, source_target_pairs={{0,4},{1,5},{2,6},{3,7},{4,0},{5,1},{6,2},{7,3},{8,12},{9,13},{10,... | collective-permute-start | bytes 344072 | tf_op jit(solution)/shard_map/ppermute | solution.py:74
  8.5 11.8 %collective-permute-start = (bf16[7,32,256]{2,1,0:T(8,128)(2,1)S(1)}, bf16[7,32,256]{2,1,0:T(8,128)(2,1)S(1)}, u32[]{:S(2)}, u32[]{:S(2)}) collective-permute-start(bf16[7,32,256]{2,1,0:T(8,128)(2,1)S(1)} %pad_dynamic-slice_fusion), channel_id=1, source_target_pairs={{0,2},{1,3},{2,0},{3,1},{4,6},{5,7},{6,4},{7,5},{8,10},{9,11},{10,... | collective-permute-start | bytes 344072 | tf_op jit(solution)/shard_map/ppermute | solution.py:74
  8.7 11.6 %collective-permute-start.2 = (bf16[7,32,256]{2,1,0:T(8,128)(2,1)S(1)}, bf16[7,32,256]{2,1,0:T(8,128)(2,1)S(1)}, u32[]{:S(2)}, u32[]{:S(2)}) collective-permute-start(bf16[7,32,256]{2,1,0:T(8,128)(2,1)S(1)} %pad_dynamic-slice_fusion), channel_id=1, source_target_pairs={{0,6},{1,7},{2,4},{3,5},{4,2},{5,3},{6,0},{7,1},{8,14},{9,15},{10,... | collective-permute-start | bytes 344072 | tf_op jit(solution)/shard_map/ppermute | solution.py:74
  18.7 13.1 %collective-permute-start.13 = (bf16[7,32,128]{2,1,0:T(8,128)(2,1)S(1)}, bf16[7,32,128]{2,1,0:T(8,128)(2,1)S(1)}, u32[]{:S(2)}, u32[]{:S(2)}) collective-permute-start(bf16[7,32,128]{2,1,0:T(8,128)(2,1)S(1)} %pad_dynamic-slice_fusion.1), channel_id=1, source_target_pairs={{0,6},{1,7},{2,4},{3,5},{4,2},{5,3},{6,0},{7,1},{8,14},{9,15},{10,... | collective-permute-start | bytes 172040 | tf_op jit(solution)/shard_map/ppermute | solution.py:74
  26.6 15.1 %collective-permute-start.6 = (bf16[2,4,3,32,256]{4,3,2,1,0:T(8,128)(2,1)S(1)}, bf16[2,4,3,32,256]{4,3,2,1,0:T(8,128)(2,1)S(1)}, u32[]{:S(2)}, u32[]{:S(2)}) collective-permute-start(bf16[2,4,3,32,256]{4,3,2,1,0:T(8,128)(2,1)S(1)} %get-tuple-element.70), channel_id=1, source_target_pairs={{0,1},{1,0},{2,3},{3,2},{4,5},{5,4},{6,7},{7,6},{8,9},{9,8},{10,11... | collective-permute-start | bytes 1179656 | tf_op jit(solution)/shard_map/ppermute | solution.py:42
  31.2 11.2 %collective-permute-start.4 = (bf16[2,4,4,32,256]{4,3,2,1,0:T(8,128)(2,1)S(1)}, bf16[2,4,4,32,256]{4,3,2,1,0:T(8,128)(2,1)S(1)}, u32[]{:S(2)}, u32[]{:S(2)}) collective-permute-start(bf16[2,4,4,32,256]{4,3,2,1,0:T(8,128)(2,1)S(1)} %get-tuple-element.57), channel_id=1, source_target_pairs={{0,16},{8,24},{16,0},{24,8},{1,17},{9,25},{17,1},{25,9},{2,18},{10... | collective-permute-start | bytes 1572872 | tf_op jit(solution)/shard_map/ppermute | solution.py:42
  40.1 10.2 %collective-permute-start.15 = (bf16[2,4,7,32,128]{4,3,2,1,0:T(8,128)(2,1)S(1)}, bf16[2,4,7,32,128]{4,3,2,1,0:T(8,128)(2,1)S(1)}, u32[]{:S(2)}, u32[]{:S(2)}) collective-permute-start(bf16[2,4,7,32,128]{4,3,2,1,0:T(8,128)(2,1)S(1)} %get-tuple-element.66), channel_id=1, source_target_pairs={{0,16},{8,24},{16,0},{24,8},{1,17},{9,25},{17,1},{25,9},{2,18},{10... | collective-permute-start | bytes 1376264 | tf_op jit(solution)/shard_map/ppermute | solution.py:42
  44.5 63.2 %collective-permute-start.7 = (bf16[2,2,4,7,32,256]{5,4,3,2,1,0:T(8,128)(2,1)}, bf16[2,2,4,7,32,256]{5,4,3,2,1,0:T(8,128)(2,1)}, u32[]{:S(2)}, u32[]{:S(2)}) collective-permute-start(bf16[2,2,4,7,32,256]{5,4,3,2,1,0:T(8,128)(2,1)} %get-tuple-element.53), channel_id=1, source_target_pairs={{0,8},{8,0},{16,24},{24,16},{1,9},{9,1},{17,25},{25,17},{2,10},{10... | collective-permute-start | bytes 5505032 | tf_op jit(solution)/shard_map/ppermute | solution.py:42
  51.7 28.5 %collective-permute-start.16 = (bf16[2,2,4,7,32,128]{5,4,3,2,1,0:T(8,128)(2,1)}, bf16[2,2,4,7,32,128]{5,4,3,2,1,0:T(8,128)(2,1)}, u32[]{:S(2)}, u32[]{:S(2)}) collective-permute-start(bf16[2,2,4,7,32,128]{5,4,3,2,1,0:T(8,128)(2,1)} %get-tuple-element.55), channel_id=1, source_target_pairs={{0,8},{8,0},{16,24},{24,16},{1,9},{9,1},{17,25},{25,17},{2,10},{10... | collective-permute-start | bytes 2752520 | tf_op jit(solution)/shard_map/ppermute | solution.py:42
  60.5 27.0 %collective-permute-start.18 = (bf16[4,9,1,64,128]{4,3,2,1,0:T(8,128)(2,1)S(1)}, bf16[4,9,1,64,128]{4,3,2,1,0:T(8,128)(2,1)S(1)}, u32[]{:S(2)}, u32[]{:S(2)}) collective-permute-start(bf16[4,9,1,64,128]{4,3,2,1,0:T(8,128)(2,1)S(1)} %pad_maximum_fusion.5), channel_id=1, source_target_pairs={{0,1},{1,2},{2,3},{3,4},{4,5},{5,6},{6,7},{8,9},{9,10},{10,11},{11... | collective-permute-start | bytes 1769480 | tf_op jit(solution)/shard_map/ppermute | solution.py:37
  71.0 15.2 %collective-permute-start.10 = (bf16[2,2,32,128]{3,2,1,0:T(8,128)(2,1)S(1)}, bf16[2,2,32,128]{3,2,1,0:T(8,128)(2,1)S(1)}, u32[]{:S(2)}, u32[]{:S(2)}) collective-permute-start(bf16[2,2,32,128]{3,2,1,0:T(8,128)(2,1)S(1)} %bitcast.240), channel_id=1, source_target_pairs={{0,1},{1,0},{2,3},{3,2},{4,5},{5,4},{6,7},{7,6},{8,9},{9,8},{10,11... | collective-permute-start | bytes 98312 | tf_op jit(solution)/shard_map/ppermute | solution.py:42
  84.1 15.5 %collective-permute-start.20 = (bf16[4,4,1,32,256]{4,3,2,1,0:T(8,128)(2,1)S(1)}, bf16[4,4,1,32,256]{4,3,2,1,0:T(8,128)(2,1)S(1)}, u32[]{:S(2)}, u32[]{:S(2)}) collective-permute-start(bf16[4,4,1,32,256]{4,3,2,1,0:T(8,128)(2,1)S(1)} %get-tuple-element.18.rest_1_.high), channel_id=1, source_target_pairs={{0,1},{1,2},{2,3},{3,4},{4,5},{5,6},{6,7},{8,9},{9,10},{10,11},{11... | collective-permute-start | bytes 786440 | tf_op jit(solution)/shard_map/ppermute | solution.py:37
  86.2 11.5 %collective-permute-start.22 = (bf16[8,32,128]{2,1,0:T(8,128)(2,1)S(1)}, bf16[8,32,128]{2,1,0:T(8,128)(2,1)S(1)}, u32[]{:S(2)}, u32[]{:S(2)}) collective-permute-start(bf16[8,32,128]{2,1,0:T(8,128)(2,1)S(1)} %bitcast.194), channel_id=1, source_target_pairs={{1,0},{2,1},{3,2},{4,3},{5,4},{6,5},{7,6},{9,8},{10,9},{11,10},{12... | collective-permute-start | bytes 196616 | tf_op jit(solution)/shard_map/ppermute | solution.py:37
  97.8 11.8 %collective-permute-start.23 = (bf16[2,8,32,128]{3,2,1,0:T(8,128)(2,1)S(1)}, bf16[2,8,32,128]{3,2,1,0:T(8,128)(2,1)S(1)}, u32[]{:S(2)}, u32[]{:S(2)}) collective-permute-start(bf16[2,8,32,128]{3,2,1,0:T(8,128)(2,1)S(1)} %pad_maximum_fusion.22.near), channel_id=1, source_target_pairs={{8,0},{9,1},{10,2},{11,3},{12,4},{13,5},{14,6},{15,7},{16,8},{17,9... | collective-permute-start | bytes 393224 | tf_op jit(solution)/shard_map/ppermute | solution.py:37
  107.1 42.2 %collective-permute-start.35 = (bf16[2,8,14,32,128]{4,3,2,1,0:T(8,128)(2,1)}, bf16[2,8,14,32,128]{4,3,2,1,0:T(8,128)(2,1)}, u32[]{:S(2)}, u32[]{:S(2)}) collective-permute-start(bf16[2,8,14,32,128]{4,3,2,1,0:T(8,128)(2,1)} %get-tuple-element.31), channel_id=1, source_target_pairs={{0,8},{8,0},{16,24},{24,16},{1,9},{9,1},{17,25},{25,17},{2,10},{10... | collective-permute-start | bytes 5505032 | tf_op jit(solution)/shard_map/ppermute | solution.py:42
  118.5 28.7 %collective-permute-start.27 = (bf16[2,8,7,32,128]{4,3,2,1,0:T(8,128)(2,1)}, bf16[2,8,7,32,128]{4,3,2,1,0:T(8,128)(2,1)}, u32[]{:S(2)}, u32[]{:S(2)}) collective-permute-start(bf16[2,8,7,32,128]{4,3,2,1,0:T(8,128)(2,1)} %get-tuple-element.29), channel_id=1, source_target_pairs={{0,8},{8,0},{16,24},{24,16},{1,9},{9,1},{17,25},{25,17},{2,10},{10... | collective-permute-start | bytes 2752520 | tf_op jit(solution)/shard_map/ppermute | solution.py:42
  118.5 22.2 %collective-permute-start.25 = (bf16[4,4,1,32,256]{4,3,2,1,0:T(8,128)(2,1)}, bf16[4,4,1,32,256]{4,3,2,1,0:T(8,128)(2,1)}, u32[]{:S(2)}, u32[]{:S(2)}) collective-permute-start(bf16[4,4,1,32,256]{4,3,2,1,0:T(8,128)(2,1)} %get-tuple-element.25), channel_id=1, source_target_pairs={{1,0},{2,1},{3,2},{4,3},{5,4},{6,5},{7,6},{9,8},{10,9},{11,10},{12... | collective-permute-start | bytes 786440 | tf_op jit(solution)/shard_map/ppermute | solution.py:37
  122.7 15.5 %all-to-all-start = ((bf16[8,32,128]{2,1,0:T(8,128)(2,1)}), bf16[8,32,128]{2,1,0:T(8,128)(2,1)S(1)}, u32[]{:S(2)}, u32[]{:S(2)}) async-start(bf16[8,32,128]{2,1,0:T(8,128)(2,1)} %bitcast.46), calls=%async_computation | async-start | bytes 131072 | tf_op jit(solution)/shard_map/all_to_all | solution.py:699
  148.9 13.5 %collective-permute-start.28 = (bf16[2,4,7,32,128]{4,3,2,1,0:T(8,128)(2,1)S(1)}, bf16[2,4,7,32,128]{4,3,2,1,0:T(8,128)(2,1)S(1)}, u32[]{:S(2)}, u32[]{:S(2)}) collective-permute-start(bf16[2,4,7,32,128]{4,3,2,1,0:T(8,128)(2,1)S(1)} %fusion.4), channel_id=1, source_target_pairs={{0,1},{1,0},{2,3},{3,2},{4,5},{5,4},{6,7},{7,6},{8,9},{9,8},{10,11... | collective-permute-start | bytes 1376264 | tf_op jit(solution)/shard_map/ppermute | solution.py:42
  151.9 13.5 %collective-permute-start.36 = (bf16[2,4,7,32,128]{4,3,2,1,0:T(8,128)(2,1)S(1)}, bf16[2,4,7,32,128]{4,3,2,1,0:T(8,128)(2,1)S(1)}, u32[]{:S(2)}, u32[]{:S(2)}) collective-permute-start(bf16[2,4,7,32,128]{4,3,2,1,0:T(8,128)(2,1)S(1)} %slice_bitcast_fusion.6), channel_id=1, source_target_pairs={{0,16},{8,24},{16,0},{24,8},{1,17},{9,25},{17,1},{25,9},{2,18},{10... | collective-permute-start | bytes 1376264 | tf_op jit(solution)/shard_map/ppermute | solution.py:42
  153.3 16.7 %collective-permute-start.38 = (bf16[2,4,7,32,128]{4,3,2,1,0:T(8,128)(2,1)S(1)}, bf16[2,4,7,32,128]{4,3,2,1,0:T(8,128)(2,1)S(1)}, u32[]{:S(2)}, u32[]{:S(2)}) collective-permute-start(bf16[2,4,7,32,128]{4,3,2,1,0:T(8,128)(2,1)S(1)} %slice_bitcast_fusion.4), channel_id=1, source_target_pairs={{0,1},{1,0},{2,3},{3,2},{4,5},{5,4},{6,7},{7,6},{8,9},{9,8},{10,11... | collective-permute-start | bytes 1376264 | tf_op jit(solution)/shard_map/ppermute | solution.py:42
  187.2 9.5 %collective-permute-start.34 = (bf16[2,7,32,128]{3,2,1,0:T(8,128)(2,1)S(1)}, bf16[2,7,32,128]{3,2,1,0:T(8,128)(2,1)S(1)}, u32[]{:S(2)}, u32[]{:S(2)}) collective-permute-start(bf16[2,7,32,128]{3,2,1,0:T(8,128)(2,1)S(1)} %get-tuple-element.85), channel_id=1, source_target_pairs={{0,8},{8,0},{16,24},{24,16},{1,9},{9,1},{17,25},{25,17},{2,10},{10... | collective-permute-start | bytes 344072 | tf_op jit(solution)/shard_map/ppermute | solution.py:42
  (30 other events, 232.5 us)

commit v8 on v7

--- a/solution.py
+++ b/solution.py
@@ -384,7 +384,7 @@
 
         lax.fori_loop(0, vols, split, 0)
         for chan in range(chans):
-            turned[chan * mine : (chan + 1) * mine] = grads[chan ^ here[1]]
+            turned[chan * mine : (chan + 1) * mine] = grads[relative(chan, here[1], orders[1])]
         grads_body(orders, sides, here, (parts,), keep, send, turned)
 
     return call(
@@ -480,7 +480,7 @@
     for b in range(2):
         owner = (here[1] + b) & (chans - 1)
         for ref in (near, beyond):
-            rows = jnp.concatenate([ref[b, chan ^ owner] for chan in range(chans)], axis=0)
+            rows = jnp.concatenate([ref[b, relative(chan, owner, orders[1])] for chan in range(chans)], axis=0)
             flat = jnp.transpose(rows.astype(F32), (1, 0)).astype(BF16)
             for n in range(vols):
                 for a in range(side_a if ref is near else 1):
@@ -669,7 +669,7 @@
     part = far_gather(own_part(w_second))
     second_full = mixed_gather(part)
     cells = CellExchange(cotangent)
-    for bit in far_bits() + [0]:
+    for bit in [0] + far_bits():
         cells.stage(bit)
     own_cells, near_cells, beyond_cells = cells.finish()
 
@@ -683,9 +683,7 @@
     keep, send, act_parts = second_grads(here, blocks, own_cells, orders)
     second_sum = far_sum(mixed_sum(core_sum(keep, send)))
 
-    pre_back, pre_plane, pre_row, corner = hidden_back(
-        here, near_cells, beyond_cells, second_full, low, high, orders
-    )
+    pre_back, pre_plane, pre_row, corner = hidden_back(here, near_cells, beyond_cells, second_full, low, high, orders)
     keep, send = first_grads(here, (vol_main, vol_row), pre_back, orders)
     first_sum = far_sum(plain_sum(core_sum(keep, send)))
     first_grad = finish_sum(first_sum)

time: 206 us -> 206 us (level)
  starting transfers between devices: 83.4 us -> 86.1 us
    ppermute x10, starting transfers between devices: 22 us -> 29 us  [shifted(): return lax.ppermute(value, (SPACE, CHAN), pairs)]
    ppermute x23, starting transfers between devices: 32.5 us -> 28.1 us  [swapped(): return lax.ppermute(value, axis, [(i, i ^ 1 << bit) for i in range(count)])]
where the time goes in v8:
time: 206 us; the launch traced here: 205 us
  starting transfers between devices  86.1 us (42%)
  waiting for transfers between devices  61 us (30%)
  Pallas kernels  29.7 us (14%)
  other arithmetic  16.4 us (8%)
  local copies, waits for them, and re-layouts  10.7 us (5%)
    ppermute x23, waiting for transfers between devices, swapped(): return lax.ppermute(value, axis, [(i, i ^ 1 << bit) for i in range(count)])  39.4 us
    pallas_call x8, Pallas kernels, call(): pl.pallas_call(kernel, out_shape=outs, grid=grid or (), in_specs=specs, o...  29.7 us
    ppermute x10, starting transfers between devices, shifted(): return lax.ppermute(value, (SPACE, CHAN), pairs)  29 us
    ppermute x23, starting transfers between devices, swapped(): return lax.ppermute(value, axis, [(i, i ^ 1 << bit) for i in range(count)])  28.1 us
    ppermute x12, starting transfers between devices, far_swapped(): return lax.ppermute(value, CHAN, [(i, i ^ mask << 1) for i in range(count)])  20.3 us
    ppermute x12, waiting for transfers between devices, far_swapped(): return lax.ppermute(value, CHAN, [(i, i ^ mask << 1) for i in range(count)])  16.9 us
    all_to_all x1, starting transfers between devices, local(): lax.all_to_all(local_out, CHAN, split_axis=0, concat_axis=0, tiled=True)  8.78 us
    another operation x13, other arithmetic, doubled(): return jnp.stack([value, other])  7.03 us
  transfers between devices with their start and end apart: 46, of which 19 were waited for; matrix products, arithmetic and copies ran while one was open for 11% of the time, Pallas kernels for 14%

profile of v8, /device:TPU:0, one launch (start us, length us, event | category | flops | bytes accessed | tf_op | source)
XLA Modules:
  0.0 205.2 jit_solution(10443781055915102815)
XLA Ops:
  1.5 4.1 %collective-permute-start.12 = (bf16[7,32,128]{2,1,0:T(8,128)(2,1)S(1)}, bf16[7,32,128]{2,1,0:T(8,128)(2,1)S(1)}, u32[]{:S(2)}, u32[]{:S(2)}) collective-permute-start(bf16[7,32,128]{2,1,0:T(8,128)(2,1)S(1)} %pad_dynamic-slice_fusion.1), channel_id=1, source_target_pairs={{0,4},{1,5},{2,6},{3,7},{4,0},{5,1},{6,2},{7,3},{8,12},{9,13},{10,... | collective-permute-start | bytes 172040 | tf_op jit(solution)/shard_map/ppermute | solution.py:74
  8.7 3.9 %collective-permute-start.2 = (bf16[7,32,256]{2,1,0:T(8,128)(2,1)S(1)}, bf16[7,32,256]{2,1,0:T(8,128)(2,1)S(1)}, u32[]{:S(2)}, u32[]{:S(2)}) collective-permute-start(bf16[7,32,256]{2,1,0:T(8,128)(2,1)S(1)} %pad_dynamic-slice_fusion), channel_id=1, source_target_pairs={{0,6},{1,7},{2,4},{3,5},{4,2},{5,3},{6,0},{7,1},{8,14},{9,15},{10,... | collective-permute-start | bytes 344072 | tf_op jit(solution)/shard_map/ppermute | solution.py:74
  13.5 5.2 %collective-permute-done.1 = bf16[7,32,256]{2,1,0:T(8,128)(2,1)S(1)} collective-permute-done((bf16[7,32,256]{2,1,0:T(8,128)(2,1)S(1)}, bf16[7,32,256]{2,1,0:T(8,128)(2,1)S(1)}, u32[]{:S(2)}, u32[]{:S(2)}) %collective-permute-start.1) | collective-permute-done | bytes 114720 | tf_op jit(solution)/shard_map/ppermute | solution.py:74
  23.5 3.0 %collective-permute-done.5 = bf16[4,3,32,256]{3,2,1,0:T(8,128)(2,1)S(1)} collective-permute-done((bf16[4,3,32,256]{3,2,1,0:T(8,128)(2,1)S(1)}, bf16[4,3,32,256]{3,2,1,0:T(8,128)(2,1)S(1)}, u32[]{:S(2)}, u32[]{:S(2)}) %collective-permute-start.5) | collective-permute-done | bytes 196640 | tf_op jit(solution)/shard_map/ppermute | solution.py:42
  28.1 3.1 %collective-permute-done.3 = bf16[4,4,32,256]{3,2,1,0:T(8,128)(2,1)S(1)} collective-permute-done((bf16[4,4,32,256]{3,2,1,0:T(8,128)(2,1)S(1)}, bf16[4,4,32,256]{3,2,1,0:T(8,128)(2,1)S(1)}, u32[]{:S(2)}, u32[]{:S(2)}) %collective-permute-start.3) | collective-permute-done | bytes 262176 | tf_op jit(solution)/shard_map/ppermute | solution.py:42
  33.5 6.6 %collective-permute-done.14 = bf16[4,7,32,128]{3,2,1,0:T(8,128)(2,1)S(1)} collective-permute-done((bf16[4,7,32,128]{3,2,1,0:T(8,128)(2,1)S(1)}, bf16[4,7,32,128]{3,2,1,0:T(8,128)(2,1)S(1)}, u32[]{:S(2)}, u32[]{:S(2)}) %collective-permute-start.14) | collective-permute-done | bytes 229408 | tf_op jit(solution)/shard_map/ppermute | solution.py:42
  44.5 5.8 %collective-permute-done.15 = bf16[2,4,7,32,128]{4,3,2,1,0:T(8,128)(2,1)S(1)} collective-permute-done((bf16[2,4,7,32,128]{4,3,2,1,0:T(8,128)(2,1)S(1)}, bf16[2,4,7,32,128]{4,3,2,1,0:T(8,128)(2,1)S(1)}, u32[]{:S(2)}, u32[]{:S(2)}) %collective-permute-start.15) | collective-permute-done | bytes 458784 | tf_op jit(solution)/shard_map/ppermute | solution.py:42
  61.1 4.8 %collective-permute-start.9 = (bf16[2,2,32,128]{3,2,1,0:T(8,128)(2,1)}, bf16[2,2,32,128]{3,2,1,0:T(8,128)(2,1)}, u32[]{:S(2)}, u32[]{:S(2)}) collective-permute-start(bf16[2,2,32,128]{3,2,1,0:T(8,128)(2,1)} %get-tuple-element.88), channel_id=1, source_target_pairs={{0,4},{1,5},{2,6},{3,7},{4,0},{5,1},{6,2},{7,3},{8,12},{9,13},{10,... | collective-permute-start | bytes 98312 | tf_op jit(solution)/shard_map/ppermute | solution.py:42
  73.7 2.5 %shard_map.76 = (bf16[4,4,1,32,256]{4,3,2,1,0:T(8,128)(2,1)S(1)}, bf16[4,1,1,32,256]{4,3,2,1,0:T(8,128)(2,1)S(1)}) custom-call(s32[2]{0:T(128)S(1)} %pad_add_fusion.here, bf16[4,8,7,32,128]{4,3,2,1,0:T(8,128)(2,1)S(1)} %bitcast.188, bf16[3,4,9,4,32,128]{5,4,3,2,1,0:T(8,128)(2,1)S(1)} %shard_map.75.main), custom_call_target="tpu_custom_call" | custom-call | flops 905969664 | bytes 5701640 | tf_op jit(solution)/shard_map/pallas_call | solution.py:136
  76.2 12.0 %collective-permute-start.20 = (bf16[4,4,1,32,256]{4,3,2,1,0:T(8,128)(2,1)S(1)}, bf16[4,4,1,32,256]{4,3,2,1,0:T(8,128)(2,1)S(1)}, u32[]{:S(2)}, u32[]{:S(2)}) collective-permute-start(bf16[4,4,1,32,256]{4,3,2,1,0:T(8,128)(2,1)S(1)} %get-tuple-element.18.rest_1_.high), channel_id=1, source_target_pairs={{0,1},{1,2},{2,3},{3,4},{4,5},{5,6},{6,7},{8,9},{9,10},{10,11},{11... | collective-permute-start | bytes 786440 | tf_op jit(solution)/shard_map/ppermute | solution.py:37
  89.5 2.7 %shard_map.77 = (bf16[4,4,1,32,256]{4,3,2,1,0:T(8,128)(2,1)S(1)}, bf16[4,1,2,32,256]{4,3,2,1,0:T(8,128)(2,1)S(1)}, bf16[3,4,9,1,32,128]{5,4,3,2,1,0:T(8,128)(2,1)S(1)}) custom-call(s32[2]{0:T(128)S(1)} %pad_add_fusion.here, bf16[4,8,7,32,128]{4,3,2,1,0:T(8,128)(2,1)S(1)} %bitcast.189, bf16[3,4,9,4,32,128]{5,4,3,2,1,0:T(8,128)(2,1)S(1)} %shard_map.75.main, ...), custom_call_target="tpu_custom_call" | custom-call | flops 905969664 | bytes 7503880 | tf_op jit(solution)/shard_map/pallas_call | solution.py:136
  93.7 4.0 %collective-permute-start.21 = (bf16[4,1,1,32,256]{4,3,2,1,0:T(8,128)(2,1)S(1)}, bf16[4,1,1,32,256]{4,3,2,1,0:T(8,128)(2,1)S(1)}, u32[]{:S(2)}, u32[]{:S(2)}) collective-permute-start(bf16[4,1,1,32,256]{4,3,2,1,0:T(8,128)(2,1)S(1)} %get-tuple-element.21), channel_id=1, source_target_pairs={{0,9},{1,10},{2,11},{3,12},{4,13},{5,14},{6,15},{8,17},{9,18},{10,... | collective-permute-start | bytes 196616 | tf_op jit(solution)/shard_map/ppermute | solution.py:37
  99.6 6.2 %shard_map.78 = (bf16[2,8,14,32,128]{4,3,2,1,0:T(8,128)(2,1)S(1)}, bf16[2,8,14,32,128]{4,3,2,1,0:T(8,128)(2,1)}, bf16[3,4,5,3,16,256]{5,4,3,2,1,0:T(8,128)(2,1)S(1)}) custom-call(s32[2]{0:T(128)S(1)} %pad_add_fusion.here, bf16[8,32,128]{2,1,0:T(8,128)(2,1)S(1)} %bitcast.193, bf16[4,4,1,32,256]{4,3,2,1,0:T(8,128)(2,1)S(1)} %get-tuple-element.19.low, ...), custom_call_target="tpu_custom_call" | custom-call | flops 452984832 | bytes 6193160 | tf_op jit(solution)/shard_map/pallas_call | solution.py:136
  111.6 7.0 %shard_map.82 = (bf16[2,8,7,32,128]{4,3,2,1,0:T(8,128)(2,1)S(1)}, bf16[2,8,7,32,128]{4,3,2,1,0:T(8,128)(2,1)}) custom-call(s32[2]{0:T(128)S(1)} %pad_add_fusion.here, bf16[4,4,2,32,256]{4,3,2,1,0:T(8,128)(2,1)S(1)} %get-tuple-element.23.cells.grads, bf16[3,4,9,4,32,128]{5,4,3,2,1,0:T(8,128)(2,1)S(1)} %shard_map.75.main, ...), custom_call_target="tpu_custom_call" | custom-call | flops 1811939328 | bytes 6782984 | tf_op jit(solution)/shard_map/pallas_call | solution.py:136
  119.8 3.0 %shard_map.79 = bf16[256,128]{1,0:T(8,128)(2,1)} custom-call(s32[2]{0:T(128)S(1)} %pad_add_fusion.here, bf16[4,8,7,32,256]{4,3,2,1,0:T(8,128)(2,1)S(1)} %bitcast.187, bf16[3,4,5,3,16,256]{5,4,3,2,1,0:T(8,128)(2,1)S(1)} %get-tuple-element.22.main), custom_call_target="tpu_custom_call" | custom-call | flops 452984832 | bytes 5210120 | tf_op jit(solution)/shard_map/pallas_call | solution.py:136
  122.8 8.8 %all-to-all-start = ((bf16[8,32,128]{2,1,0:T(8,128)(2,1)}), bf16[8,32,128]{2,1,0:T(8,128)(2,1)S(1)}, u32[]{:S(2)}, u32[]{:S(2)}) async-start(bf16[8,32,128]{2,1,0:T(8,128)(2,1)} %bitcast.46), calls=%async_computation | async-start | bytes 131072 | tf_op jit(solution)/shard_map/all_to_all | solution.py:697
  134.4 4.1 %all-to-all-done = bf16[8,32,128]{2,1,0:T(8,128)(2,1)S(1)} async-done(((bf16[8,32,128]{2,1,0:T(8,128)(2,1)}), bf16[8,32,128]{2,1,0:T(8,128)(2,1)S(1)}, u32[]{:S(2)}, u32[]{:S(2)}) %all-to-all-start) | async-done | bytes 65568 | tf_op jit(solution)/shard_map/all_to_all | solution.py:697
  142.0 5.4 %shard_map.81 = bf16[4,8,4,64,128]{4,3,2,1,0:T(8,128)(2,1)} custom-call(s32[2]{0:T(128)S(1)} %pad_add_fusion.here, bf16[4,4,2,32,256]{4,3,2,1,0:T(8,128)(2,1)S(1)} %get-tuple-element.23.cells.grads, bf16[4,1,2,32,256]{4,3,2,1,0:T(8,128)(2,1)} %collective-permute-done.24.plane, bf16[4,5,1,32,256]{4,3,2,1,0:T(8,128)(2,1)S(1)} %pad_maximum_fusion.14.row, ...), custom_call_target="tpu_custom_call" | custom-call | flops 1811939328 | bytes 4915208 | tf_op jit(solution)/shard_map/pallas_call | solution.py:136
  155.3 7.3 %collective-permute-done.28 = bf16[2,4,7,32,128]{4,3,2,1,0:T(8,128)(2,1)S(1)} collective-permute-done((bf16[2,4,7,32,128]{4,3,2,1,0:T(8,128)(2,1)S(1)}, bf16[2,4,7,32,128]{4,3,2,1,0:T(8,128)(2,1)S(1)}, u32[]{:S(2)}, u32[]{:S(2)}) %collective-permute-start.28) | collective-permute-done | bytes 458784 | tf_op jit(solution)/shard_map/ppermute | solution.py:42
  165.6 4.6 %collective-permute-done.38 = bf16[2,4,7,32,128]{4,3,2,1,0:T(8,128)(2,1)S(1)} collective-permute-done((bf16[2,4,7,32,128]{4,3,2,1,0:T(8,128)(2,1)S(1)}, bf16[2,4,7,32,128]{4,3,2,1,0:T(8,128)(2,1)S(1)}, u32[]{:S(2)}, u32[]{:S(2)}) %collective-permute-start.38) | collective-permute-done | bytes 458784 | tf_op jit(solution)/shard_map/ppermute | solution.py:42
  182.8 3.0 %collective-permute-start.40 = (bf16[14,32,128]{2,1,0:T(8,128)(2,1)S(1)}, bf16[14,32,128]{2,1,0:T(8,128)(2,1)S(1)}, u32[]{:S(2)}, u32[]{:S(2)}) collective-permute-start(bf16[14,32,128]{2,1,0:T(8,128)(2,1)S(1)} %get-tuple-element.62), channel_id=1, source_target_pairs={{0,2},{1,3},{2,0},{3,1},{4,6},{5,7},{6,4},{7,5},{8,10},{9,11},{10,... | collective-permute-start | bytes 344072 | tf_op jit(solution)/shard_map/ppermute | solution.py:74
  187.6 2.6 %collective-permute-done.40 = bf16[14,32,128]{2,1,0:T(8,128)(2,1)S(1)} collective-permute-done((bf16[14,32,128]{2,1,0:T(8,128)(2,1)S(1)}, bf16[14,32,128]{2,1,0:T(8,128)(2,1)S(1)}, u32[]{:S(2)}, u32[]{:S(2)}) %collective-permute-start.40) | collective-permute-done | bytes 114720 | tf_op jit(solution)/shard_map/ppermute | solution.py:74
  192.5 3.5 %collective-permute-done.41 = bf16[14,32,128]{2,1,0:T(8,128)(2,1)S(1)} collective-permute-done((bf16[14,32,128]{2,1,0:T(8,128)(2,1)S(1)}, bf16[14,32,128]{2,1,0:T(8,128)(2,1)S(1)}, u32[]{:S(2)}, u32[]{:S(2)}) %collective-permute-start.41) | collective-permute-done | bytes 114720 | tf_op jit(solution)/shard_map/ppermute | solution.py:74
  197.0 4.0 %collective-permute-done.43 = bf16[14,32,128]{2,1,0:T(8,128)(2,1)S(1)} collective-permute-done((bf16[14,32,128]{2,1,0:T(8,128)(2,1)S(1)}, bf16[14,32,128]{2,1,0:T(8,128)(2,1)S(1)}, u32[]{:S(2)}, u32[]{:S(2)}) %collective-permute-start.43) | collective-permute-done | bytes 114720 | tf_op jit(solution)/shard_map/ppermute | solution.py:42
  (153 shorter events, 86.8 us)
Async XLA Ops:
  1.5 30.3 %collective-permute-start.12 = (bf16[7,32,128]{2,1,0:T(8,128)(2,1)S(1)}, bf16[7,32,128]{2,1,0:T(8,128)(2,1)S(1)}, u32[]{:S(2)}, u32[]{:S(2)}) collective-permute-start(bf16[7,32,128]{2,1,0:T(8,128)(2,1)S(1)} %pad_dynamic-slice_fusion.1), channel_id=1, source_target_pairs={{0,4},{1,5},{2,6},{3,7},{4,0},{5,1},{6,2},{7,3},{8,12},{9,13},{10,... | collective-permute-start | bytes 172040 | tf_op jit(solution)/shard_map/ppermute | solution.py:74
  5.6 26.2 %collective-permute-start.11 = (bf16[7,32,128]{2,1,0:T(8,128)(2,1)S(1)}, bf16[7,32,128]{2,1,0:T(8,128)(2,1)S(1)}, u32[]{:S(2)}, u32[]{:S(2)}) collective-permute-start(bf16[7,32,128]{2,1,0:T(8,128)(2,1)S(1)} %pad_dynamic-slice_fusion.1), channel_id=1, source_target_pairs={{0,2},{1,3},{2,0},{3,1},{4,6},{5,7},{6,4},{7,5},{8,10},{9,11},{10,... | collective-permute-start | bytes 172040 | tf_op jit(solution)/shard_map/ppermute | solution.py:74
  8.1 10.6 %collective-permute-start.1 = (bf16[7,32,256]{2,1,0:T(8,128)(2,1)S(1)}, bf16[7,32,256]{2,1,0:T(8,128)(2,1)S(1)}, u32[]{:S(2)}, u32[]{:S(2)}) collective-permute-start(bf16[7,32,256]{2,1,0:T(8,128)(2,1)S(1)} %pad_dynamic-slice_fusion), channel_id=1, source_target_pairs={{0,4},{1,5},{2,6},{3,7},{4,0},{5,1},{6,2},{7,3},{8,12},{9,13},{10,... | collective-permute-start | bytes 344072 | tf_op jit(solution)/shard_map/ppermute | solution.py:74
  8.5 11.8 %collective-permute-start = (bf16[7,32,256]{2,1,0:T(8,128)(2,1)S(1)}, bf16[7,32,256]{2,1,0:T(8,128)(2,1)S(1)}, u32[]{:S(2)}, u32[]{:S(2)}) collective-permute-start(bf16[7,32,256]{2,1,0:T(8,128)(2,1)S(1)} %pad_dynamic-slice_fusion), channel_id=1, source_target_pairs={{0,2},{1,3},{2,0},{3,1},{4,6},{5,7},{6,4},{7,5},{8,10},{9,11},{10,... | collective-permute-start | bytes 344072 | tf_op jit(solution)/shard_map/ppermute | solution.py:74
  8.7 11.6 %collective-permute-start.2 = (bf16[7,32,256]{2,1,0:T(8,128)(2,1)S(1)}, bf16[7,32,256]{2,1,0:T(8,128)(2,1)S(1)}, u32[]{:S(2)}, u32[]{:S(2)}) collective-permute-start(bf16[7,32,256]{2,1,0:T(8,128)(2,1)S(1)} %pad_dynamic-slice_fusion), channel_id=1, source_target_pairs={{0,6},{1,7},{2,4},{3,5},{4,2},{5,3},{6,0},{7,1},{8,14},{9,15},{10,... | collective-permute-start | bytes 344072 | tf_op jit(solution)/shard_map/ppermute | solution.py:74
  18.7 13.1 %collective-permute-start.13 = (bf16[7,32,128]{2,1,0:T(8,128)(2,1)S(1)}, bf16[7,32,128]{2,1,0:T(8,128)(2,1)S(1)}, u32[]{:S(2)}, u32[]{:S(2)}) collective-permute-start(bf16[7,32,128]{2,1,0:T(8,128)(2,1)S(1)} %pad_dynamic-slice_fusion.1), channel_id=1, source_target_pairs={{0,6},{1,7},{2,4},{3,5},{4,2},{5,3},{6,0},{7,1},{8,14},{9,15},{10,... | collective-permute-start | bytes 172040 | tf_op jit(solution)/shard_map/ppermute | solution.py:74
  26.6 15.1 %collective-permute-start.6 = (bf16[2,4,3,32,256]{4,3,2,1,0:T(8,128)(2,1)S(1)}, bf16[2,4,3,32,256]{4,3,2,1,0:T(8,128)(2,1)S(1)}, u32[]{:S(2)}, u32[]{:S(2)}) collective-permute-start(bf16[2,4,3,32,256]{4,3,2,1,0:T(8,128)(2,1)S(1)} %get-tuple-element.70), channel_id=1, source_target_pairs={{0,1},{1,0},{2,3},{3,2},{4,5},{5,4},{6,7},{7,6},{8,9},{9,8},{10,11... | collective-permute-start | bytes 1179656 | tf_op jit(solution)/shard_map/ppermute | solution.py:42
  31.2 11.2 %collective-permute-start.4 = (bf16[2,4,4,32,256]{4,3,2,1,0:T(8,128)(2,1)S(1)}, bf16[2,4,4,32,256]{4,3,2,1,0:T(8,128)(2,1)S(1)}, u32[]{:S(2)}, u32[]{:S(2)}) collective-permute-start(bf16[2,4,4,32,256]{4,3,2,1,0:T(8,128)(2,1)S(1)} %get-tuple-element.57), channel_id=1, source_target_pairs={{0,16},{8,24},{16,0},{24,8},{1,17},{9,25},{17,1},{25,9},{2,18},{10... | collective-permute-start | bytes 1572872 | tf_op jit(solution)/shard_map/ppermute | solution.py:42
  40.1 10.2 %collective-permute-start.15 = (bf16[2,4,7,32,128]{4,3,2,1,0:T(8,128)(2,1)S(1)}, bf16[2,4,7,32,128]{4,3,2,1,0:T(8,128)(2,1)S(1)}, u32[]{:S(2)}, u32[]{:S(2)}) collective-permute-start(bf16[2,4,7,32,128]{4,3,2,1,0:T(8,128)(2,1)S(1)} %get-tuple-element.66), channel_id=1, source_target_pairs={{0,16},{8,24},{16,0},{24,8},{1,17},{9,25},{17,1},{25,9},{2,18},{10... | collective-permute-start | bytes 1376264 | tf_op jit(solution)/shard_map/ppermute | solution.py:42
  44.5 63.2 %collective-permute-start.7 = (bf16[2,2,4,7,32,256]{5,4,3,2,1,0:T(8,128)(2,1)}, bf16[2,2,4,7,32,256]{5,4,3,2,1,0:T(8,128)(2,1)}, u32[]{:S(2)}, u32[]{:S(2)}) collective-permute-start(bf16[2,2,4,7,32,256]{5,4,3,2,1,0:T(8,128)(2,1)} %get-tuple-element.53), channel_id=1, source_target_pairs={{0,8},{8,0},{16,24},{24,16},{1,9},{9,1},{17,25},{25,17},{2,10},{10... | collective-permute-start | bytes 5505032 | tf_op jit(solution)/shard_map/ppermute | solution.py:42
  51.7 20.6 %collective-permute-start.16 = (bf16[2,2,4,7,32,128]{5,4,3,2,1,0:T(8,128)(2,1)}, bf16[2,2,4,7,32,128]{5,4,3,2,1,0:T(8,128)(2,1)}, u32[]{:S(2)}, u32[]{:S(2)}) collective-permute-start(bf16[2,2,4,7,32,128]{5,4,3,2,1,0:T(8,128)(2,1)} %get-tuple-element.55), channel_id=1, source_target_pairs={{0,8},{8,0},{16,24},{24,16},{1,9},{9,1},{17,25},{25,17},{2,10},{10... | collective-permute-start | bytes 2752520 | tf_op jit(solution)/shard_map/ppermute | solution.py:42
  57.2 32.3 %collective-permute-start.18 = (bf16[4,9,1,64,128]{4,3,2,1,0:T(8,128)(2,1)S(1)}, bf16[4,9,1,64,128]{4,3,2,1,0:T(8,128)(2,1)S(1)}, u32[]{:S(2)}, u32[]{:S(2)}) collective-permute-start(bf16[4,9,1,64,128]{4,3,2,1,0:T(8,128)(2,1)S(1)} %pad_maximum_fusion.5), channel_id=1, source_target_pairs={{0,1},{1,2},{2,3},{3,4},{4,5},{5,6},{6,7},{8,9},{9,10},{10,11},{11... | collective-permute-start | bytes 1769480 | tf_op jit(solution)/shard_map/ppermute | solution.py:37
  68.9 19.3 %collective-permute-start.10 = (bf16[2,2,32,128]{3,2,1,0:T(8,128)(2,1)S(1)}, bf16[2,2,32,128]{3,2,1,0:T(8,128)(2,1)S(1)}, u32[]{:S(2)}, u32[]{:S(2)}) collective-permute-start(bf16[2,2,32,128]{3,2,1,0:T(8,128)(2,1)S(1)} %get-tuple-element.87), channel_id=1, source_target_pairs={{0,2},{1,3},{2,0},{3,1},{4,6},{5,7},{6,4},{7,5},{8,10},{9,11},{10,... | collective-permute-start | bytes 98312 | tf_op jit(solution)/shard_map/ppermute | solution.py:42
  76.2 23.5 %collective-permute-start.20 = (bf16[4,4,1,32,256]{4,3,2,1,0:T(8,128)(2,1)S(1)}, bf16[4,4,1,32,256]{4,3,2,1,0:T(8,128)(2,1)S(1)}, u32[]{:S(2)}, u32[]{:S(2)}) collective-permute-start(bf16[4,4,1,32,256]{4,3,2,1,0:T(8,128)(2,1)S(1)} %get-tuple-element.18.rest_1_.high), channel_id=1, source_target_pairs={{0,1},{1,2},{2,3},{3,4},{4,5},{5,6},{6,7},{8,9},{9,10},{10,11},{11... | collective-permute-start | bytes 786440 | tf_op jit(solution)/shard_map/ppermute | solution.py:37
  88.2 9.5 %collective-permute-start.22 = (bf16[8,32,128]{2,1,0:T(8,128)(2,1)S(1)}, bf16[8,32,128]{2,1,0:T(8,128)(2,1)S(1)}, u32[]{:S(2)}, u32[]{:S(2)}) collective-permute-start(bf16[8,32,128]{2,1,0:T(8,128)(2,1)S(1)} %bitcast.191), channel_id=1, source_target_pairs={{1,0},{2,1},{3,2},{4,3},{5,4},{6,5},{7,6},{9,8},{10,9},{11,10},{12... | collective-permute-start | bytes 196616 | tf_op jit(solution)/shard_map/ppermute | solution.py:37
  97.8 11.8 %collective-permute-start.23 = (bf16[2,8,32,128]{3,2,1,0:T(8,128)(2,1)S(1)}, bf16[2,8,32,128]{3,2,1,0:T(8,128)(2,1)S(1)}, u32[]{:S(2)}, u32[]{:S(2)}) collective-permute-start(bf16[2,8,32,128]{3,2,1,0:T(8,128)(2,1)S(1)} %pad_maximum_fusion.22.near), channel_id=1, source_target_pairs={{8,0},{9,1},{10,2},{11,3},{12,4},{13,5},{14,6},{15,7},{16,8},{17,9... | collective-permute-start | bytes 393224 | tf_op jit(solution)/shard_map/ppermute | solution.py:37
  107.1 42.5 %collective-permute-start.35 = (bf16[2,8,14,32,128]{4,3,2,1,0:T(8,128)(2,1)}, bf16[2,8,14,32,128]{4,3,2,1,0:T(8,128)(2,1)}, u32[]{:S(2)}, u32[]{:S(2)}) collective-permute-start(bf16[2,8,14,32,128]{4,3,2,1,0:T(8,128)(2,1)} %get-tuple-element.31), channel_id=1, source_target_pairs={{0,8},{8,0},{16,24},{24,16},{1,9},{9,1},{17,25},{25,17},{2,10},{10... | collective-permute-start | bytes 5505032 | tf_op jit(solution)/shard_map/ppermute | solution.py:42
  118.5 28.9 %collective-permute-start.27 = (bf16[2,8,7,32,128]{4,3,2,1,0:T(8,128)(2,1)}, bf16[2,8,7,32,128]{4,3,2,1,0:T(8,128)(2,1)}, u32[]{:S(2)}, u32[]{:S(2)}) collective-permute-start(bf16[2,8,7,32,128]{4,3,2,1,0:T(8,128)(2,1)} %get-tuple-element.29), channel_id=1, source_target_pairs={{0,8},{8,0},{16,24},{24,16},{1,9},{9,1},{17,25},{25,17},{2,10},{10... | collective-permute-start | bytes 2752520 | tf_op jit(solution)/shard_map/ppermute | solution.py:42
  118.5 22.5 %collective-permute-start.25 = (bf16[4,4,1,32,256]{4,3,2,1,0:T(8,128)(2,1)}, bf16[4,4,1,32,256]{4,3,2,1,0:T(8,128)(2,1)}, u32[]{:S(2)}, u32[]{:S(2)}) collective-permute-start(bf16[4,4,1,32,256]{4,3,2,1,0:T(8,128)(2,1)} %get-tuple-element.25), channel_id=1, source_target_pairs={{1,0},{2,1},{3,2},{4,3},{5,4},{6,5},{7,6},{9,8},{10,9},{11,10},{12... | collective-permute-start | bytes 786440 | tf_op jit(solution)/shard_map/ppermute | solution.py:37
  122.8 15.7 %all-to-all-start = ((bf16[8,32,128]{2,1,0:T(8,128)(2,1)}), bf16[8,32,128]{2,1,0:T(8,128)(2,1)S(1)}, u32[]{:S(2)}, u32[]{:S(2)}) async-start(bf16[8,32,128]{2,1,0:T(8,128)(2,1)} %bitcast.46), calls=%async_computation | async-start | bytes 131072 | tf_op jit(solution)/shard_map/all_to_all | solution.py:697
  149.1 13.5 %collective-permute-start.28 = (bf16[2,4,7,32,128]{4,3,2,1,0:T(8,128)(2,1)S(1)}, bf16[2,4,7,32,128]{4,3,2,1,0:T(8,128)(2,1)S(1)}, u32[]{:S(2)}, u32[]{:S(2)}) collective-permute-start(bf16[2,4,7,32,128]{4,3,2,1,0:T(8,128)(2,1)S(1)} %fusion.4), channel_id=1, source_target_pairs={{0,1},{1,0},{2,3},{3,2},{4,5},{5,4},{6,7},{7,6},{8,9},{9,8},{10,11... | collective-permute-start | bytes 1376264 | tf_op jit(solution)/shard_map/ppermute | solution.py:42
  152.2 13.5 %collective-permute-start.36 = (bf16[2,4,7,32,128]{4,3,2,1,0:T(8,128)(2,1)S(1)}, bf16[2,4,7,32,128]{4,3,2,1,0:T(8,128)(2,1)S(1)}, u32[]{:S(2)}, u32[]{:S(2)}) collective-permute-start(bf16[2,4,7,32,128]{4,3,2,1,0:T(8,128)(2,1)S(1)} %slice_bitcast_fusion.6), channel_id=1, source_target_pairs={{0,16},{8,24},{16,0},{24,8},{1,17},{9,25},{17,1},{25,9},{2,18},{10... | collective-permute-start | bytes 1376264 | tf_op jit(solution)/shard_map/ppermute | solution.py:42
  153.6 16.7 %collective-permute-start.38 = (bf16[2,4,7,32,128]{4,3,2,1,0:T(8,128)(2,1)S(1)}, bf16[2,4,7,32,128]{4,3,2,1,0:T(8,128)(2,1)S(1)}, u32[]{:S(2)}, u32[]{:S(2)}) collective-permute-start(bf16[2,4,7,32,128]{4,3,2,1,0:T(8,128)(2,1)S(1)} %slice_bitcast_fusion.4), channel_id=1, source_target_pairs={{0,1},{1,0},{2,3},{3,2},{4,5},{5,4},{6,7},{7,6},{8,9},{9,8},{10,11... | collective-permute-start | bytes 1376264 | tf_op jit(solution)/shard_map/ppermute | solution.py:42
  187.5 9.5 %collective-permute-start.34 = (bf16[2,7,32,128]{3,2,1,0:T(8,128)(2,1)S(1)}, bf16[2,7,32,128]{3,2,1,0:T(8,128)(2,1)S(1)}, u32[]{:S(2)}, u32[]{:S(2)}) collective-permute-start(bf16[2,7,32,128]{3,2,1,0:T(8,128)(2,1)S(1)} %get-tuple-element.85), channel_id=1, source_target_pairs={{0,8},{8,0},{16,24},{24,16},{1,9},{9,1},{17,25},{25,17},{2,10},{10... | collective-permute-start | bytes 344072 | tf_op jit(solution)/shard_map/ppermute | solution.py:42
  (30 other events, 215.1 us)
